TPU v7x, 512 devices: a whole 4x8x8 slice. The times are simulated.
512 devices in a mesh: sx: 8 (over x, core), sy: 4 (over z_lo), wa: 16 (over y, z_hi).
Axes of the slice: x: 4, y: 8, z: 8 (z_hi: 2, z_lo: 4; z = z_hi * 4 + z_lo), core: 2. Of those that a mesh axis runs over, the one named last changes fastest.
Arguments:
- queries: bfloat16 [16, 16, 16, 16, 2048], P('wa', 'sx', 'sy'), may hold values from -6 to 6
- keys_values: bfloat16 [2, 16, 16, 16, 16, 2048], P(None, 'wa', 'sx', 'sy'), may hold values from -6 to 6
- out_weight: bfloat16 [2048, 2048], P('wa'), may hold values from -0.397747564 to 0.397747564
- gain: float32 [2048], replicated, may hold values from 0.5 to 2
- read_weight: float32 [2048, 2], replicated, may hold values from -0.125 to 0.125
- adjacency: int32 [16, 16, 16, 4], P('wa', 'sx', 'sy'), may hold values from 0 to 7, all different within a row
- boundary: int32 [16, 16, 16], P('wa', 'sx', 'sy'), may hold values 0 or 1
- cotangent: float32 [16, 16, 16, 16, 2], P('wa', 'sx', 'sy'), may hold values from -6 to 6
Outputs:
- prediction: float32 [16, 16, 16, 16, 2], P('wa', 'sx', 'sy')
- grad_queries: bfloat16 [16, 16, 16, 16, 2048], P('wa', 'sx', 'sy')
- grad_keys_values: bfloat16 [2, 16, 16, 16, 16, 2048], P(None, 'wa', 'sx', 'sy')
Inputs may be any that keep to these rules, and one draw needn't show every extreme that they name: `adjacency`: the 4 entries of a block differ; entry e names code e if e < 4 and e + 1 otherwise, code c being the block at offset (c // 3 - 1, c % 3 - 1).
All inputs are finite; a program needn't handle non-finite values. No bound on the sum of `boundary` on one device may be relied on, other than what follows from the above.
Results may differ from a plain program's by a relative error of at most 0.0087.
Values may be sent and summed in bfloat16 or wider, within the bound.
No kernel may reach another device: no remote copies, remote signals or barrier semaphores. Data moves between devices by JAX's collectives and lax.ppermute only.
A program may use at most 128 MiB of HBM per device.

v0:
```python
import jax
import jax.numpy as jnp
from jax import lax
from jax.experimental import pallas as pl
from jax.experimental.pallas import tpu as pltpu
from jax.sharding import PartitionSpec as P

HS = 128
BS = 16
BX = 2
BY = 4
TOK = BX * BY * BS
GROUP = 4
VMEM_LIMIT = 60 * 1024 * 1024

LOCAL = [(x, y) for x in range(BX) for y in range(BY)]
XLOW = [(-1, y) for y in range(BY)]
XHIGH = [(BX, y) for y in range(BY)]
YLOW = [(x, -1) for x in range(BX)]
YHIGH = [(x, BY) for x in range(BX)]
CLOW = [(-1, -1), (-1, BY)]
CHIGH = [(BX, -1), (BX, BY)]
PIECES = [LOCAL, XLOW, XHIGH, YLOW, YHIGH, CLOW, CHIGH]
KEY_BLOCKS = [block for piece in PIECES for block in piece]
KEYS = len(KEY_BLOCKS) * BS


def shift(value, axis, step):
    count = lax.axis_size(axis)
    pairs = [(i, i + step) for i in range(count) if 0 <= i + step < count]
    return lax.ppermute(value, axis, pairs)


def dot(a, b, dims):
    return lax.dot_general(a, b, (dims, ((), ())), preferred_element_type=jnp.float32)


def piece_rows(refs, which, lanes):
    parts = []
    for ref in refs:
        blocks = ref[which, :, :, :, lanes]
        parts.append(blocks.reshape(-1, HS))
    return jnp.concatenate(parts, axis=0)


def allowed_mask(adj_ref, pos_ref):
    lane = lax.broadcasted_iota(jnp.int32, (1, TOK), 1)
    block = lane // BS
    bx = block // BY
    by = block % BY
    entries = []
    for e in range(4):
        vec = jnp.zeros((1, TOK), jnp.int32)
        for b in range(BX * BY):
            vec = jnp.where(block == b, adj_ref[0, b // BY, b % BY, e], vec)
        entries.append(vec)
    rows = []
    for kx, ky in KEY_BLOCKS:
        dx = kx - bx
        dy = ky - by
        near = (jnp.abs(dx) <= 1) & (jnp.abs(dy) <= 1)
        code = 3 * (dx + 1) + dy + 1
        entry = code - (code > 4).astype(jnp.int32)
        listed = code == 4
        for vec in entries:
            listed = listed | ((vec == entry) & (code != 4))
        gx = pos_ref[0] + kx
        gy = pos_ref[1] + ky
        inside = (gx >= 0) & (gx < pos_ref[2]) & (gy >= 0) & (gy < pos_ref[3])
        flag = jnp.where(near & listed, 1.0, 0.0) * jnp.where(inside, 1.0, 0.0)
        rows.append(jnp.broadcast_to(flag, (BS, TOK)))
    return jnp.concatenate(rows, axis=0)


def forward_kernel(adj_ref, pos_ref, q_ref, *rest):
    kv_refs = rest[: len(PIECES)]
    att_ref, prob_ref, mask_ref = rest[len(PIECES) :]

    @pl.when(pl.program_id(0) == 0)
    def _():
        mask_ref[...] = allowed_mask(adj_ref, pos_ref)

    for h in range(GROUP):
        lanes = slice(h * HS, (h + 1) * HS)
        query = q_ref[0, :, :, :, lanes].reshape(TOK, HS)
        keys = piece_rows(kv_refs, 0, lanes)
        values = piece_rows(kv_refs, 1, lanes)
        scores = dot(keys, query, ((1,), (1,))) * (HS**-0.5)
        masked = jnp.where(mask_ref[...] > 0.5, scores, -1e30)
        exponent = jnp.exp(masked - jnp.max(masked, axis=0, keepdims=True))
        prob = exponent / jnp.sum(exponent, axis=0, keepdims=True)
        prob_ref[h] = prob
        att = dot(prob.astype(jnp.bfloat16), values, ((0,), (0,)))
        att_ref[:, lanes] = att.astype(jnp.bfloat16)


def forward(adjacency, position, queries, pieces):
    inner = queries.shape[-1]
    width = GROUP * HS
    smem = pl.BlockSpec(memory_space=pltpu.SMEM)
    specs = [
        pl.BlockSpec(p.shape[:-1] + (width,), lambda g: (0, 0, 0, 0, g))
        for p in pieces
    ]
    return pl.pallas_call(
        forward_kernel,
        grid=(inner // width,),
        in_specs=[smem, smem, pl.BlockSpec(queries.shape[:-1] + (width,), lambda g: (0, 0, 0, 0, g))] + specs,
        out_specs=[
            pl.BlockSpec((TOK, width), lambda g: (0, g)),
            pl.BlockSpec((GROUP, KEYS, TOK), lambda g: (g, 0, 0)),
        ],
        out_shape=[
            jax.ShapeDtypeStruct((TOK, inner), jnp.bfloat16),
            jax.ShapeDtypeStruct((inner // HS, KEYS, TOK), jnp.float32),
        ],
        scratch_shapes=[pltpu.VMEM((KEYS, TOK), jnp.float32)],
        compiler_params=pltpu.CompilerParams(vmem_limit_bytes=VMEM_LIMIT),
        name="attend",
    )(adjacency, position, queries, *pieces)


def project_kernel(bound_ref, pos_ref, att_ref, own_hbm, other_hbm, gain_ref, read_ref, cot_ref, pred_ref, ga_ref, w_ref, proj_ref, gp_ref, sems):
    slabs = w_ref.shape[0]
    cols = w_ref.shape[2]
    core = pos_ref[4]
    copies = [
        pltpu.make_async_copy(own_hbm, w_ref.at[core], sems.at[0]),
        pltpu.make_async_copy(other_hbm, w_ref.at[1 - core], sems.at[1]),
    ]
    for copy in copies:
        copy.start()
    for copy in copies:
        copy.wait()
    att = att_ref[...]
    for s in range(slabs):
        proj_ref[:, s * cols : (s + 1) * cols] = dot(att, w_ref[s], ((1,), (0,)))
    inner = proj_ref.shape[1]
    for half in range(TOK // 32):
        rows = slice(half * 32, (half + 1) * 32)
        x = half * 2 // BY
        y = half * 2 % BY
        proj = proj_ref[rows, :]
        gain = gain_ref[...]
        flag = jnp.where(
            lax.broadcasted_iota(jnp.int32, (32, 1), 0) < BS, bound_ref[0, x, y], bound_ref[0, x, y + 1]
        ).astype(jnp.float32)
        cot = jnp.concatenate([cot_ref[0, x, y], cot_ref[0, x, y + 1]], axis=0) * flag
        inv_rms = lax.rsqrt(jnp.sum(proj * proj, axis=1, keepdims=True) * (1.0 / inner) + 1e-05)
        normed = proj * inv_rms * gain
        pred0 = jnp.sum(normed * read_ref[0:1, :], axis=1, keepdims=True) * flag
        pred1 = jnp.sum(normed * read_ref[1:2, :], axis=1, keepdims=True) * flag
        pred = jnp.where(lax.broadcasted_iota(jnp.int32, (32, 2), 1) == 0, pred0, pred1)
        pred_ref[0, x, y] = pred[:BS]
        pred_ref[0, x, y + 1] = pred[BS:]
        gained = (cot[:, 0:1] * read_ref[0:1, :] + cot[:, 1:2] * read_ref[1:2, :]) * gain
        inner_mean = jnp.sum(gained * proj, axis=1, keepdims=True) * (1.0 / inner)
        gp_ref[rows, :] = (inv_rms * gained - proj * (inv_rms * inv_rms * inv_rms * inner_mean)).astype(jnp.bfloat16)
    chunk = 512
    for r in range(inner // chunk):
        total = None
        for s in range(slabs):
            part = dot(gp_ref[:, s * cols : (s + 1) * cols], w_ref[s, r * chunk : (r + 1) * chunk, :], ((1,), (1,)))
            total = part if total is None else total + part
        ga_ref[:, r * chunk : (r + 1) * chunk] = total.astype(jnp.bfloat16)


def project(boundary, position, att, own_rows, other_rows, gain, read_rows, cotangent):
    vmem = pl.BlockSpec(memory_space=pltpu.VMEM)
    return pl.pallas_call(
        project_kernel,
        in_specs=[
            pl.BlockSpec(memory_space=pltpu.SMEM),
            pl.BlockSpec(memory_space=pltpu.SMEM),
            vmem,
            pl.BlockSpec(memory_space=pl.ANY),
            pl.BlockSpec(memory_space=pl.ANY),
            vmem,
            vmem,
            vmem,
        ],
        out_specs=[vmem, vmem],
        out_shape=[
            jax.ShapeDtypeStruct(cotangent.shape, jnp.float32),
            jax.ShapeDtypeStruct(att.shape, jnp.bfloat16),
        ],
        scratch_shapes=[
            pltpu.VMEM((2,) + own_rows.shape, jnp.bfloat16),
            pltpu.VMEM(att.shape, jnp.float32),
            pltpu.VMEM(att.shape, jnp.bfloat16),
            pltpu.SemaphoreType.DMA((2,)),
        ],
        compiler_params=pltpu.CompilerParams(vmem_limit_bytes=VMEM_LIMIT),
        name="project",
    )(boundary, position, att, own_rows, other_rows, gain, read_rows, cotangent)


def backward_kernel(q_ref, ga_ref, prob_ref, *rest):
    count = len(PIECES)
    kv_refs = rest[:count]
    gq_ref = rest[count]
    gkv_refs = rest[count + 1 :]
    for h in range(GROUP):
        lanes = slice(h * HS, (h + 1) * HS)
        query = q_ref[0, :, :, :, lanes].reshape(TOK, HS)
        keys = piece_rows(kv_refs, 0, lanes)
        values = piece_rows(kv_refs, 1, lanes)
        grad_att = ga_ref[:, lanes]
        prob = prob_ref[h]
        grad_prob = dot(values, grad_att, ((1,), (1,)))
        inner_sum = jnp.sum(prob * grad_prob, axis=0, keepdims=True)
        grad_scores = (prob * (grad_prob - inner_sum) * (HS**-0.5)).astype(jnp.bfloat16)
        grad_query = dot(grad_scores, keys, ((0,), (0,)))
        gq_ref[0, :, :, :, lanes] = grad_query.reshape(BX, BY, BS, HS).astype(gq_ref.dtype)
        grads = (dot(grad_scores, query, ((1,), (0,))), dot(prob.astype(jnp.bfloat16), grad_att, ((1,), (0,))))
        for which, grad in enumerate(grads):
            start = 0
            for ref in gkv_refs:
                shape = ref.shape[1:4]
                rows = shape[0] * shape[1] * shape[2]
                ref[which, :, :, :, lanes] = grad[start : start + rows].reshape(shape + (HS,)).astype(ref.dtype)
                start += rows


def backward(queries, grad_att, prob, pieces):
    inner = queries.shape[-1]
    width = GROUP * HS

    def wide(shape):
        return pl.BlockSpec(tuple(shape[:-1]) + (width,), lambda g: (0,) * (len(shape) - 1) + (g,))

    shapes = [p.shape for p in pieces]
    return pl.pallas_call(
        backward_kernel,
        grid=(inner // width,),
        in_specs=[wide(queries.shape), wide(grad_att.shape), pl.BlockSpec((GROUP, KEYS, TOK), lambda g: (g, 0, 0))]
        + [wide(s) for s in shapes],
        out_specs=[wide(queries.shape)] + [wide(s) for s in shapes],
        out_shape=[jax.ShapeDtypeStruct(queries.shape, jnp.bfloat16)]
        + [jax.ShapeDtypeStruct(s, jnp.float32 if i == 0 else jnp.bfloat16) for i, s in enumerate(shapes)],
        compiler_params=pltpu.CompilerParams(vmem_limit_bytes=VMEM_LIMIT),
        name="attend_back",
    )(queries, grad_att, prob, *pieces)


def finish_kernel(own_ref, xlow_ref, xhigh_ref, ylow_ref, yhigh_ref, out_ref):
    f32 = jnp.float32
    for which in range(2):
        for x in range(BX):
            for y in range(BY):
                total = own_ref[which, x, y]
                if x == 0:
                    total = total + xlow_ref[which, 0, y].astype(f32)
                if x == BX - 1:
                    total = total + xhigh_ref[which, 0, y].astype(f32)
                if y == 0:
                    total = total + ylow_ref[which, x, 0].astype(f32)
                if y == BY - 1:
                    total = total + yhigh_ref[which, x, 0].astype(f32)
                out_ref[which, x, y] = total.astype(out_ref.dtype)


def finish(own, xlow, xhigh, ylow, yhigh):
    inner = own.shape[-1]
    width = inner // 4

    def wide(shape):
        return pl.BlockSpec(tuple(shape[:-1]) + (width,), lambda g: (0, 0, 0, 0, g))

    args = (own, xlow, xhigh, ylow, yhigh)
    return pl.pallas_call(
        finish_kernel,
        grid=(inner // width,),
        in_specs=[wide(a.shape) for a in args],
        out_specs=wide(own.shape),
        out_shape=jax.ShapeDtypeStruct(own.shape, jnp.bfloat16),
        compiler_params=pltpu.CompilerParams(vmem_limit_bytes=VMEM_LIMIT),
        name="finish",
    )(*args)


def gather_weight(out_weight):
    inner = out_weight.shape[1]
    cols = inner // 2
    n_wa = lax.axis_size("wa")
    n_sy = lax.axis_size("sy")
    half = lax.axis_index("wa") % 2
    slab = lax.dynamic_slice_in_dim(out_weight, lax.axis_index("sx") % 2 * cols, cols, axis=1)
    mirror = [(l * n_wa + w, (n_sy - 1 - l) * n_wa + (w ^ 1)) for l in range(n_sy) for w in range(n_wa)]
    other = lax.ppermute(slab, ("sy", "wa"), mirror)
    pair = jnp.where(half == 0, jnp.stack([slab, other]), jnp.stack([other, slab]))
    groups = [list(range(h, n_wa, 2)) for h in range(2)]
    rows = lax.all_gather(pair, "wa", axis=0, axis_index_groups=groups)
    return rows.reshape(-1, cols)


def body(queries, keys_values, out_weight, gain, read_weight, adjacency, boundary, cotangent):
    size_x, size_y = queries.shape[1:3]
    kv = keys_values[:, 0]
    rows = gather_weight(out_weight)
    ylow = shift(kv[:, :, size_y - 1 :], "sy", 1)
    yhigh = shift(kv[:, :, :1], "sy", -1)
    xlow = shift(kv[:, size_x - 1 :], "sx", 1)
    xhigh = shift(kv[:, :1], "sx", -1)
    clow = shift(jnp.concatenate([ylow[:, size_x - 1 :], yhigh[:, size_x - 1 :]], axis=2), "sx", 1)
    chigh = shift(jnp.concatenate([ylow[:, :1], yhigh[:, :1]], axis=2), "sx", -1)
    pieces = (kv, xlow, xhigh, ylow, yhigh, clow, chigh)
    position = jnp.stack(
        [
            lax.axis_index("sx") * size_x,
            lax.axis_index("sy") * size_y,
            jnp.int32(size_x * lax.axis_size("sx")),
            jnp.int32(size_y * lax.axis_size("sy")),
            lax.axis_index("sx") % 2,
        ]
    ).astype(jnp.int32)
    att, prob = forward(adjacency, position, queries, pieces)
    rows, att = lax.optimization_barrier((rows, att))
    other_rows = lax.ppermute(rows, "sx", [(i, i ^ 1) for i in range(lax.axis_size("sx"))])
    prediction, grad_att = project(boundary, position, att, rows, other_rows, gain[None], read_weight.T, cotangent)
    grad_queries, own, gxlow, gxhigh, gylow, gyhigh, gclow, gchigh = backward(queries, grad_att, prob, pieces)
    to_high = shift(jnp.concatenate([gxhigh, gchigh], axis=2), "sx", 1)
    to_low = shift(jnp.concatenate([gxlow, gclow], axis=2), "sx", -1)
    f32 = jnp.float32

    def side(rim, y):
        first = rim[:, :1].astype(f32) + to_high[:, :, size_y + y : size_y + y + 1].astype(f32)
        last = rim[:, 1:].astype(f32) + to_low[:, :, size_y + y : size_y + y + 1].astype(f32)
        return jnp.concatenate([first, last], axis=1).astype(jnp.bfloat16)

    from_low = shift(side(gyhigh, 1), "sy", 1)
    from_high = shift(side(gylow, 0), "sy", -1)
    grad_kv = finish(own, to_high[:, :, :size_y], to_low[:, :, :size_y], from_low, from_high)
    return (prediction, grad_queries, grad_kv[:, None])


def solution(mesh):
    return jax.shard_map(
        body,
        mesh=mesh,
        in_specs=(
            P("wa", "sx", "sy", None, None),
            P(None, "wa", "sx", "sy", None, None),
            P("wa", None),
            P(),
            P(),
            P("wa", "sx", "sy", None),
            P("wa", "sx", "sy"),
            P("wa", "sx", "sy", None, None),
        ),
        out_specs=(
            P("wa", "sx", "sy", None, None),
            P("wa", "sx", "sy", None, None),
            P(None, "wa", "sx", "sy", None, None),
        ),
        check_vma=False,
    )
```

profile of v0, /device:TPU:1, one launch (start us, length us, event | category | flops | bytes accessed | tf_op | source)
XLA Modules:
  0.0 156.6 jit_solution(1606728969335312614)
XLA Ops:
  7.2 0.0 copy-start
  7.2 0.0 copy-start.1
  7.2 0.0 all-gather.2.cloned.1.call-start
  7.3 1.0 copy-done
  8.2 11.5 %collective-permute-start = (bf16[128,1024]{1,0:T(8,128)(2,1)S(1)}, bf16[128,1024]{1,0:T(8,128)(2,1)S(1)}, u32[]{:S(2)}, u32[]{:S(2)}) collective-permute-start(bf16[128,1024]{1,0:T(8,128)(2,1)S(1)} %constant_dynamic-slice_fusion), channel_id=1, source_target_pairs={{0,49},{1,48},{2,51},{3,50},{4,53},{5,52},{6,55},{7,54},{8,57},{9,... | collective-permute-start | bytes 786440 | tf_op jit(solution)/shard_map/ppermute | solution.py:290
  19.8 12.3 %collective-permute-done = bf16[128,1024]{1,0:T(8,128)(2,1)S(1)} collective-permute-done((bf16[128,1024]{1,0:T(8,128)(2,1)S(1)}, bf16[128,1024]{1,0:T(8,128)(2,1)S(1)}, u32[]{:S(2)}, u32[]{:S(2)}) %collective-permute-start) | collective-permute-done | bytes 262176 | tf_op jit(solution)/shard_map/ppermute | solution.py:290
  32.1 0.9 maximum_select_fusion
  33.0 0.0 all-gather.2.cloned.1.call-update
  33.0 1.1 fusion
  34.1 0.0 copy-start.11
  34.1 1.3 collective-permute-start.4
  35.4 4.0 %collective-permute-start.3 = (bf16[2,2,1,16,2048]{4,3,2,1,0:T(8,128)(2,1)S(1)}, bf16[2,2,1,16,2048]{4,3,2,1,0:T(8,128)(2,1)S(1)}, u32[]{:S(2)}, u32[]{:S(2)}) collective-permute-start(bf16[2,2,1,16,2048]{4,3,2,1,0:T(8,128)(2,1)S(1)} %get-tuple-element.38), channel_id=1, source_target_pairs={{0,16},{16,32},{32,48},{1,17},{17,33},{33,49},{2,18},{18,34},{34,5... | collective-permute-start | bytes 786440 | tf_op jit(solution)/shard_map/ppermute | solution.py:31
  39.4 0.0 copy-done.1
  39.4 0.9 fusion.1
  40.3 2.9 %collective-permute-start.2 = (bf16[2,1,4,16,2048]{4,3,2,1,0:T(8,128)(2,1)}, bf16[2,1,4,16,2048]{4,3,2,1,0:T(8,128)(2,1)S(1)}, u32[]{:S(2)}, u32[]{:S(2)}) collective-permute-start(bf16[2,1,4,16,2048]{4,3,2,1,0:T(8,128)(2,1)} %get-tuple-element.39), channel_id=1, source_target_pairs={{64,0},{128,64},{192,128},{256,192},{320,256},{384,320},{448,384},... | collective-permute-start | bytes 1572872 | tf_op jit(solution)/shard_map/ppermute | solution.py:31
  43.3 3.0 %collective-permute-start.1 = (bf16[2,1,4,16,2048]{4,3,2,1,0:T(8,128)(2,1)S(1)}, bf16[2,1,4,16,2048]{4,3,2,1,0:T(8,128)(2,1)S(1)}, u32[]{:S(2)}, u32[]{:S(2)}) collective-permute-start(bf16[2,1,4,16,2048]{4,3,2,1,0:T(8,128)(2,1)S(1)} %get-tuple-element.40), channel_id=1, source_target_pairs={{0,64},{64,128},{128,192},{192,256},{256,320},{320,384},{384,448},... | collective-permute-start | bytes 1572872 | tf_op jit(solution)/shard_map/ppermute | solution.py:31
  46.3 0.0 collective-permute-done.4.rest_4_
  46.3 0.0 copy-start.2
  46.3 0.0 collective-permute-done.3.rest_3_
  46.4 0.0 copy-start.3
  46.4 2.6 %collective-permute-start.5 = (bf16[2,1,2,16,2048]{4,3,2,1,0:T(8,128)(2,1)S(1)}, bf16[2,1,2,16,2048]{4,3,2,1,0:T(8,128)(2,1)S(1)}, u32[]{:S(2)}, u32[]{:S(2)}) collective-permute-start(bf16[2,1,2,16,2048]{4,3,2,1,0:T(8,128)(2,1)S(1)} %pad_maximum_fusion.2), channel_id=1, source_target_pairs={{0,64},{64,128},{128,192},{192,256},{256,320},{320,384},{384,448},... | collective-permute-start | bytes 786440 | tf_op jit(solution)/shard_map/ppermute | solution.py:31
  49.0 0.7 pad_maximum_fusion.3
  49.7 1.9 %collective-permute-start.6 = (bf16[2,1,2,16,2048]{4,3,2,1,0:T(8,128)(2,1)}, bf16[2,1,2,16,2048]{4,3,2,1,0:T(8,128)(2,1)S(1)}, u32[]{:S(2)}, u32[]{:S(2)}) collective-permute-start(bf16[2,1,2,16,2048]{4,3,2,1,0:T(8,128)(2,1)} %pad_maximum_fusion.3), channel_id=1, source_target_pairs={{64,0},{128,64},{192,128},{256,192},{320,256},{384,320},{448,384},... | collective-permute-start | bytes 786440 | tf_op jit(solution)/shard_map/ppermute | solution.py:31
  51.6 0.7 pad_add_fusion.pos_ref
  52.3 2.9 %collective-permute-done.5.rest_5_ = bf16[2,1,2,16,2048]{4,3,2,1,0:T(8,128)(2,1)S(1)} collective-permute-done((bf16[2,1,2,16,2048]{4,3,2,1,0:T(8,128)(2,1)S(1)}, bf16[2,1,2,16,2048]{4,3,2,1,0:T(8,128)(2,1)S(1)}, u32[]{:S(2)}, u32[]{:S(2)}) %collective-permute-start.5) | collective-permute-done | bytes 262176 | tf_op jit(solution)/shard_map/ppermute | solution.py:31
  55.2 0.0 copy-start.6
  55.2 2.8 %collective-permute-done.6.rest_6_ = bf16[2,1,2,16,2048]{4,3,2,1,0:T(8,128)(2,1)S(1)} collective-permute-done((bf16[2,1,2,16,2048]{4,3,2,1,0:T(8,128)(2,1)}, bf16[2,1,2,16,2048]{4,3,2,1,0:T(8,128)(2,1)S(1)}, u32[]{:S(2)}, u32[]{:S(2)}) %collective-permute-start.6) | collective-permute-done | bytes 262176 | tf_op jit(solution)/shard_map/ppermute | solution.py:31
  58.0 0.0 copy-start.7
  58.0 0.0 collective-permute-done.2.rest_2_
  58.0 0.0 copy-start.4
  58.0 0.0 collective-permute-done.1.rest_1_
  58.0 0.0 copy-done.2
  58.0 0.0 copy-done.3
  58.0 0.0 copy-done.6
  58.0 0.7 copy-done.7
  58.7 0.2 copy-done.4
  58.9 0.8 copy-done.5
  59.7 5.6 %attend.1 = (bf16[128,2048]{1,0:T(8,128)(2,1)}, f32[16,384,128]{2,1,0:T(8,128)}) custom-call(s32[1,2,4,4]{3,2,1,0:T(4,128)} %adj_ref.1, s32[5]{0:T(128)} %pad_add_fusion.pos_ref, bf16[1,2,4,16,2048]{4,3,2,1,0:T(8,128)(2,1)} %q_ref.3, bf16[2,2,4,16,2048]{4,3,2,1,0:T(8,128)(2,1)} %bitcast.14, bf16[2,1,4,16,2048]{4,3,2,1,0:T(8,128)(2,1)} %copy-done.5, ...), custom_call_target="tpu_custom_call" | custom-call | tf_op jit(solution)/shard_map/attend/pallas_call | solution.py:105
  65.3 23.4 %all-gather.2.cloned.1.call-done = bf16[8,2,128,1024]{3,2,1,0:T(8,128)(2,1)} async-done(((bf16[1,2,128,1024]{3,2,1,0:T(8,128)(2,1)}), bf16[8,2,128,1024]{3,2,1,0:T(8,128)(2,1)}) %all-gather.2.cloned.1.call-update) | async-done | bytes 4194320 | tf_op jit(solution)/shard_map/all_gather | solution.py:293
  88.7 2.6 %collective-permute-start.7 = (bf16[2048,1024]{1,0:T(8,128)(2,1)}, bf16[2048,1024]{1,0:T(8,128)(2,1)}, u32[]{:S(2)}, u32[]{:S(2)}) collective-permute-start(bf16[2048,1024]{1,0:T(8,128)(2,1)} %bitcast.17), channel_id=1, source_target_pairs={{0,64},{64,0},{128,192},{192,128},{256,320},{320,256},{384,448},{4... | collective-permute-start | bytes 12582920 | tf_op jit(solution)/shard_map/ppermute | solution.py:319
  91.3 0.0 copy-done.11
  91.3 0.7 copy.14.cot_ref
  92.0 6.3 %collective-permute-done.7.other_hbm = bf16[2048,1024]{1,0:T(8,128)(2,1)} collective-permute-done((bf16[2048,1024]{1,0:T(8,128)(2,1)}, bf16[2048,1024]{1,0:T(8,128)(2,1)}, u32[]{:S(2)}, u32[]{:S(2)}) %collective-permute-start.7) | collective-permute-done | bytes 4194336 | tf_op jit(solution)/shard_map/ppermute | solution.py:319
  98.4 9.8 %project.1 = (f32[1,2,4,16,2]{4,3,2,1,0:T(8,128)}, bf16[128,2048]{1,0:T(8,128)(2,1)}) custom-call(s32[1,2,4]{2,1,0:T(2,128)} %bound_ref.1, s32[5]{0:T(128)} %pad_add_fusion.pos_ref, bf16[128,2048]{1,0:T(8,128)(2,1)} %get-tuple-element.18.att_ref, bf16[2048,1024]{1,0:T(8,128)(2,1)} %bitcast.18, bf16[2048,1024]{1,0:T(8,128)(2,1)} %collective-permute-done.7.other_hbm, ...), custom_call_target="tpu_custom_call" | custom-call | tf_op jit(solution)/shard_map/project/pallas_call | solution.py:170
  108.2 8.3 %attend_back.1 = (bf16[1,2,4,16,2048]{4,3,2,1,0:T(8,128)(2,1)}, f32[2,2,4,16,2048]{4,3,2,1,0:T(8,128)}, bf16[2,1,4,16,2048]{4,3,2,1,0:T(8,128)(2,1)}, bf16[2,1,4...) custom-call(bf16[1,2,4,16,2048]{4,3,2,1,0:T(8,128)(2,1)} %q_ref.3, ...), custom_call_target="tpu_custom_call" | custom-call | tf_op jit(solution)/shard_map/attend_back/pallas_call | solution.py:233
  116.5 0.0 copy-start.10
  116.5 1.2 pad_maximum_fusion.1
  117.7 2.3 %collective-permute-start.9 = (bf16[2,1,6,16,2048]{4,3,2,1,0:T(8,128)(2,1)S(1)}, bf16[2,1,6,16,2048]{4,3,2,1,0:T(8,128)(2,1)S(1)}, u32[]{:S(2)}, u32[]{:S(2)}) collective-permute-start(bf16[2,1,6,16,2048]{4,3,2,1,0:T(8,128)(2,1)S(1)} %pad_maximum_fusion.1), channel_id=1, source_target_pairs={{64,0},{128,64},{192,128},{256,192},{320,256},{384,320},{448,384},... | collective-permute-start | bytes 2359304 | tf_op jit(solution)/shard_map/ppermute | solution.py:31
  120.0 1.2 pad_maximum_fusion
  121.2 3.3 %collective-permute-start.8 = (bf16[2,1,6,16,2048]{4,3,2,1,0:T(8,128)(2,1)S(1)}, bf16[2,1,6,16,2048]{4,3,2,1,0:T(8,128)(2,1)S(1)}, u32[]{:S(2)}, u32[]{:S(2)}) collective-permute-start(bf16[2,1,6,16,2048]{4,3,2,1,0:T(8,128)(2,1)S(1)} %pad_maximum_fusion), channel_id=1, source_target_pairs={{0,64},{64,128},{128,192},{192,256},{256,320},{320,384},{384,448},... | collective-permute-start | bytes 2359304 | tf_op jit(solution)/shard_map/ppermute | solution.py:31
  124.5 6.5 %collective-permute-done.9 = bf16[2,1,6,16,2048]{4,3,2,1,0:T(8,128)(2,1)S(1)} collective-permute-done((bf16[2,1,6,16,2048]{4,3,2,1,0:T(8,128)(2,1)S(1)}, bf16[2,1,6,16,2048]{4,3,2,1,0:T(8,128)(2,1)S(1)}, u32[]{:S(2)}, u32[]{:S(2)}) %collective-permute-start.9) | collective-permute-done | bytes 786464 | tf_op jit(solution)/shard_map/ppermute | solution.py:31
  131.0 2.4 %collective-permute-done.8 = bf16[2,1,6,16,2048]{4,3,2,1,0:T(8,128)(2,1)S(1)} collective-permute-done((bf16[2,1,6,16,2048]{4,3,2,1,0:T(8,128)(2,1)S(1)}, bf16[2,1,6,16,2048]{4,3,2,1,0:T(8,128)(2,1)S(1)}, u32[]{:S(2)}, u32[]{:S(2)}) %collective-permute-start.8) | collective-permute-done | bytes 786464 | tf_op jit(solution)/shard_map/ppermute | solution.py:31
  133.4 1.2 add_convert_fusion
  134.7 3.3 %collective-permute-start.10 = (bf16[2,2,1,16,2048]{4,3,2,1,0:T(8,128)(2,1)S(1)}, bf16[2,2,1,16,2048]{4,3,2,1,0:T(8,128)(2,1)S(1)}, u32[]{:S(2)}, u32[]{:S(2)}) collective-permute-start(bf16[2,2,1,16,2048]{4,3,2,1,0:T(8,128)(2,1)S(1)} %pad_maximum_fusion.4), channel_id=1, source_target_pairs={{0,16},{16,32},{32,48},{1,17},{17,33},{33,49},{2,18},{18,34},{34,5... | collective-permute-start | bytes 786440 | tf_op jit(solution)/shard_map/ppermute | solution.py:31
  138.0 1.3 collective-permute-start.11
  139.3 0.0 copy-done.10
  139.3 0.7 copy.15
  140.0 0.8 slice.81.xhigh_ref
  140.8 0.8 slice.80.xlow_ref
  141.7 0.0 collective-permute-done.10.ylow_ref
  141.7 3.4 %collective-permute-done.11.yhigh_ref = bf16[2,2,1,16,2048]{4,3,2,1,0:T(8,128)(2,1)S(1)} collective-permute-done((bf16[2,2,1,16,2048]{4,3,2,1,0:T(8,128)(2,1)S(1)}, bf16[2,2,1,16,2048]{4,3,2,1,0:T(8,128)(2,1)S(1)}, u32[]{:S(2)}, u32[]{:S(2)}) %collective-permute-start.11) | collective-permute-done | bytes 262176 | tf_op jit(solution)/shard_map/ppermute | solution.py:31
  145.1 0.0 copy-done.8
  145.1 0.7 copy-done.9
  145.8 3.9 %finish.1 = bf16[2,2,4,16,2048]{4,3,2,1,0:T(8,128)(2,1)} custom-call(f32[2,2,4,16,2048]{4,3,2,1,0:T(8,128)} %get-tuple-element.24.own_ref, bf16[2,1,4,16,2048]{4,3,2,1,0:T(8,128)(2,1)} %slice.80.xlow_ref, bf16[2,1,4,16,2048]{4,3,2,1,0:T(8,128)(2,1)} %slice.81.xhigh_ref, bf16[2,2,1,16,2048]{4,3,2,1,0:T(8,128)(2,1)} %copy-done.8, ...), custom_call_target="tpu_custom_call" | custom-call | tf_op jit(solution)/shard_map/finish/pallas_call | solution.py:271
  (11 shorter events, 0.2 us)
Async XLA Ops:
  7.2 1.0 copy-start
  7.2 32.3 %copy-start.1 = (bf16[2,1,2,4,16,2048]{5,4,3,2,1,0:T(8,128)(2,1)S(1)}, bf16[2,1,2,4,16,2048]{5,4,3,2,1,0:T(8,128)(2,1)}, u32[]{:S(2)}) copy-start(bf16[2,1,2,4,16,2048]{5,4,3,2,1,0:T(8,128)(2,1)} %param.9) | copy-start | bytes 3145732
  7.2 81.5 %all-gather.2.cloned.1.call-start = ((), (), s32[]{:S(2)}) async-start(), calls=%async_computation | async-start | bytes 4718592 | tf_op jit(solution)/shard_map/all_gather | solution.py:293
  8.2 23.9 %collective-permute-start = (bf16[128,1024]{1,0:T(8,128)(2,1)S(1)}, bf16[128,1024]{1,0:T(8,128)(2,1)S(1)}, u32[]{:S(2)}, u32[]{:S(2)}) collective-permute-start(bf16[128,1024]{1,0:T(8,128)(2,1)S(1)} %constant_dynamic-slice_fusion), channel_id=1, source_target_pairs={{0,49},{1,48},{2,51},{3,50},{4,53},{5,52},{6,55},{7,54},{8,57},{9,... | collective-permute-start | bytes 786440 | tf_op jit(solution)/shard_map/ppermute | solution.py:290
  34.1 57.2 %copy-start.11 = (f32[1,2,4,16,2]{3,4,2,1,0:T(2,128)S(1)}, f32[1,2,4,16,2]{3,4,2,1,0:T(2,128)}, u32[]{:S(2)}) copy-start(f32[1,2,4,16,2]{3,4,2,1,0:T(2,128)} %param.15) | copy-start | bytes 3076
  34.1 12.2 %collective-permute-start.4 = (bf16[2,2,1,16,2048]{4,3,2,1,0:T(8,128)(2,1)S(1)}, bf16[2,2,1,16,2048]{4,3,2,1,0:T(8,128)(2,1)S(1)}, u32[]{:S(2)}, u32[]{:S(2)}) collective-permute-start(bf16[2,2,1,16,2048]{4,3,2,1,0:T(8,128)(2,1)S(1)} %get-tuple-element.37), channel_id=1, source_target_pairs={{16,0},{32,16},{48,32},{17,1},{33,17},{49,33},{18,2},{34,18},{50,3... | collective-permute-start | bytes 786440 | tf_op jit(solution)/shard_map/ppermute | solution.py:31
  35.4 10.9 %collective-permute-start.3 = (bf16[2,2,1,16,2048]{4,3,2,1,0:T(8,128)(2,1)S(1)}, bf16[2,2,1,16,2048]{4,3,2,1,0:T(8,128)(2,1)S(1)}, u32[]{:S(2)}, u32[]{:S(2)}) collective-permute-start(bf16[2,2,1,16,2048]{4,3,2,1,0:T(8,128)(2,1)S(1)} %get-tuple-element.38), channel_id=1, source_target_pairs={{0,16},{16,32},{32,48},{1,17},{17,33},{33,49},{2,18},{18,34},{34,5... | collective-permute-start | bytes 786440 | tf_op jit(solution)/shard_map/ppermute | solution.py:31
  40.3 17.7 %collective-permute-start.2 = (bf16[2,1,4,16,2048]{4,3,2,1,0:T(8,128)(2,1)}, bf16[2,1,4,16,2048]{4,3,2,1,0:T(8,128)(2,1)S(1)}, u32[]{:S(2)}, u32[]{:S(2)}) collective-permute-start(bf16[2,1,4,16,2048]{4,3,2,1,0:T(8,128)(2,1)} %get-tuple-element.39), channel_id=1, source_target_pairs={{64,0},{128,64},{192,128},{256,192},{320,256},{384,320},{448,384},... | collective-permute-start | bytes 1572872 | tf_op jit(solution)/shard_map/ppermute | solution.py:31
  43.3 14.7 %collective-permute-start.1 = (bf16[2,1,4,16,2048]{4,3,2,1,0:T(8,128)(2,1)S(1)}, bf16[2,1,4,16,2048]{4,3,2,1,0:T(8,128)(2,1)S(1)}, u32[]{:S(2)}, u32[]{:S(2)}) collective-permute-start(bf16[2,1,4,16,2048]{4,3,2,1,0:T(8,128)(2,1)S(1)} %get-tuple-element.40), channel_id=1, source_target_pairs={{0,64},{64,128},{128,192},{192,256},{256,320},{320,384},{384,448},... | collective-permute-start | bytes 1572872 | tf_op jit(solution)/shard_map/ppermute | solution.py:31
  46.3 11.7 %copy-start.2 = (bf16[2,2,1,16,2048]{4,3,2,1,0:T(8,128)(2,1)}, bf16[2,2,1,16,2048]{4,3,2,1,0:T(8,128)(2,1)S(1)}, u32[]{:S(2)}) copy-start(bf16[2,2,1,16,2048]{4,3,2,1,0:T(8,128)(2,1)S(1)} %collective-permute-done.4.rest_4_) | copy-start | bytes 786436
  46.4 11.7 %copy-start.3 = (bf16[2,2,1,16,2048]{4,3,2,1,0:T(8,128)(2,1)}, bf16[2,2,1,16,2048]{4,3,2,1,0:T(8,128)(2,1)S(1)}, u32[]{:S(2)}) copy-start(bf16[2,2,1,16,2048]{4,3,2,1,0:T(8,128)(2,1)S(1)} %collective-permute-done.3.rest_3_) | copy-start | bytes 786436
  46.4 8.8 %collective-permute-start.5 = (bf16[2,1,2,16,2048]{4,3,2,1,0:T(8,128)(2,1)S(1)}, bf16[2,1,2,16,2048]{4,3,2,1,0:T(8,128)(2,1)S(1)}, u32[]{:S(2)}, u32[]{:S(2)}) collective-permute-start(bf16[2,1,2,16,2048]{4,3,2,1,0:T(8,128)(2,1)S(1)} %pad_maximum_fusion.2), channel_id=1, source_target_pairs={{0,64},{64,128},{128,192},{192,256},{256,320},{320,384},{384,448},... | collective-permute-start | bytes 786440 | tf_op jit(solution)/shard_map/ppermute | solution.py:31
  49.7 8.3 %collective-permute-start.6 = (bf16[2,1,2,16,2048]{4,3,2,1,0:T(8,128)(2,1)}, bf16[2,1,2,16,2048]{4,3,2,1,0:T(8,128)(2,1)S(1)}, u32[]{:S(2)}, u32[]{:S(2)}) collective-permute-start(bf16[2,1,2,16,2048]{4,3,2,1,0:T(8,128)(2,1)} %pad_maximum_fusion.3), channel_id=1, source_target_pairs={{64,0},{128,64},{192,128},{256,192},{320,256},{384,320},{448,384},... | collective-permute-start | bytes 786440 | tf_op jit(solution)/shard_map/ppermute | solution.py:31
  55.2 2.8 %copy-start.6 = (bf16[2,1,2,16,2048]{4,3,2,1,0:T(8,128)(2,1)}, bf16[2,1,2,16,2048]{4,3,2,1,0:T(8,128)(2,1)S(1)}, u32[]{:S(2)}) copy-start(bf16[2,1,2,16,2048]{4,3,2,1,0:T(8,128)(2,1)S(1)} %collective-permute-done.5.rest_5_) | copy-start | bytes 786436
  58.0 0.7 copy-start.7
  58.0 0.9 copy-start.4
  58.9 0.8 copy-start.5
  88.7 9.7 %collective-permute-start.7 = (bf16[2048,1024]{1,0:T(8,128)(2,1)}, bf16[2048,1024]{1,0:T(8,128)(2,1)}, u32[]{:S(2)}, u32[]{:S(2)}) collective-permute-start(bf16[2048,1024]{1,0:T(8,128)(2,1)} %bitcast.17), channel_id=1, source_target_pairs={{0,64},{64,0},{128,192},{192,128},{256,320},{320,256},{384,448},{4... | collective-permute-start | bytes 12582920 | tf_op jit(solution)/shard_map/ppermute | solution.py:319
  116.5 22.8 %copy-start.10 = (f32[1,2,4,16,2]{4,3,2,1,0:T(8,128)S(1)}, f32[1,2,4,16,2]{4,3,2,1,0:T(8,128)}, u32[]{:S(2)}) copy-start(f32[1,2,4,16,2]{4,3,2,1,0:T(8,128)} %get-tuple-element.34) | copy-start | bytes 3076
  117.7 13.3 %collective-permute-start.9 = (bf16[2,1,6,16,2048]{4,3,2,1,0:T(8,128)(2,1)S(1)}, bf16[2,1,6,16,2048]{4,3,2,1,0:T(8,128)(2,1)S(1)}, u32[]{:S(2)}, u32[]{:S(2)}) collective-permute-start(bf16[2,1,6,16,2048]{4,3,2,1,0:T(8,128)(2,1)S(1)} %pad_maximum_fusion.1), channel_id=1, source_target_pairs={{64,0},{128,64},{192,128},{256,192},{320,256},{384,320},{448,384},... | collective-permute-start | bytes 2359304 | tf_op jit(solution)/shard_map/ppermute | solution.py:31
  121.2 12.2 %collective-permute-start.8 = (bf16[2,1,6,16,2048]{4,3,2,1,0:T(8,128)(2,1)S(1)}, bf16[2,1,6,16,2048]{4,3,2,1,0:T(8,128)(2,1)S(1)}, u32[]{:S(2)}, u32[]{:S(2)}) collective-permute-start(bf16[2,1,6,16,2048]{4,3,2,1,0:T(8,128)(2,1)S(1)} %pad_maximum_fusion), channel_id=1, source_target_pairs={{0,64},{64,128},{128,192},{192,256},{256,320},{320,384},{384,448},... | collective-permute-start | bytes 2359304 | tf_op jit(solution)/shard_map/ppermute | solution.py:31
  134.7 7.0 %collective-permute-start.10 = (bf16[2,2,1,16,2048]{4,3,2,1,0:T(8,128)(2,1)S(1)}, bf16[2,2,1,16,2048]{4,3,2,1,0:T(8,128)(2,1)S(1)}, u32[]{:S(2)}, u32[]{:S(2)}) collective-permute-start(bf16[2,2,1,16,2048]{4,3,2,1,0:T(8,128)(2,1)S(1)} %pad_maximum_fusion.4), channel_id=1, source_target_pairs={{0,16},{16,32},{32,48},{1,17},{17,33},{33,49},{2,18},{18,34},{34,5... | collective-permute-start | bytes 786440 | tf_op jit(solution)/shard_map/ppermute | solution.py:31
  138.0 7.1 %collective-permute-start.11 = (bf16[2,2,1,16,2048]{4,3,2,1,0:T(8,128)(2,1)S(1)}, bf16[2,2,1,16,2048]{4,3,2,1,0:T(8,128)(2,1)S(1)}, u32[]{:S(2)}, u32[]{:S(2)}) collective-permute-start(bf16[2,2,1,16,2048]{4,3,2,1,0:T(8,128)(2,1)S(1)} %pad_maximum_fusion.5), channel_id=1, source_target_pairs={{16,0},{32,16},{48,32},{17,1},{33,17},{49,33},{18,2},{34,18},{50,3... | collective-permute-start | bytes 786440 | tf_op jit(solution)/shard_map/ppermute | solution.py:31
  141.7 3.4 %copy-start.8 = (bf16[2,2,1,16,2048]{4,3,2,1,0:T(8,128)(2,1)}, bf16[2,2,1,16,2048]{4,3,2,1,0:T(8,128)(2,1)S(1)}, u32[]{:S(2)}) copy-start(bf16[2,2,1,16,2048]{4,3,2,1,0:T(8,128)(2,1)S(1)} %collective-permute-done.10.ylow_ref) | copy-start | bytes 786436
  145.1 0.7 copy-start.9
Sparse Core Ops, SparseCore 0:
  33.2 55.4 all-gather.1
where the time goes:
time: 159 us; the launch traced here: 157 us
  waiting for transfers between devices  60.1 us (38%)
  starting transfers between devices  39.9 us (25%)
  Pallas kernels  27.6 us (17%)
  between operations  14.4 us (9%)
  local copies, waits for them, and re-layouts  8.5 us (5%)
  other arithmetic  6.03 us (4%)
    ppermute x10, starting transfers between devices, shift(): return lax.ppermute(value, axis, pairs)  25.8 us
    all_gather x1, waiting for transfers between devices, gather_weight(): rows = lax.all_gather(pair, 'wa', axis=0, axis_index_groups=groups)  23.4 us
    ppermute x10, waiting for transfers between devices, shift(): return lax.ppermute(value, axis, pairs)  18 us
    ppermute x1, waiting for transfers between devices, gather_weight(): other = lax.ppermute(slab, ('sy', 'wa'), mirror)  12.3 us
    ppermute x1, starting transfers between devices, gather_weight(): other = lax.ppermute(slab, ('sy', 'wa'), mirror)  11.5 us
    pallas_call x1, Pallas kernels, project(): pl.pallas_call(project_kernel, in_specs=[pl.BlockSpec(memory_space=pltpu....  9.81 us
    pallas_call x1, Pallas kernels, backward(): pl.pallas_call(backward_kernel, grid=(inner // width,), in_specs=[wide(qu...  8.26 us
    ppermute x1, waiting for transfers between devices, body(): lax.ppermute(rows, 'sx', [(i, i ^ 1) for i in range(lax.axis_size('sx'))])  6.35 us
  transfers between devices with their start and end apart: 13, of which 8 were waited for; matrix products, arithmetic and copies ran while one was open for 5% of the time, Pallas kernels for 4%

commit v1 on v0

--- a/solution.py
+++ b/solution.py
@@ -12,6 +12,7 @@
 TOK = BX * BY * BS
 GROUP = 4
 VMEM_LIMIT = 60 * 1024 * 1024
+SMALL_LIMIT = 24 * 1024 * 1024
 
 LOCAL = [(x, y) for x in range(BX) for y in range(BY)]
 XLOW = [(-1, y) for y in range(BY)]
@@ -20,7 +21,7 @@
 YHIGH = [(x, BY) for x in range(BX)]
 CLOW = [(-1, -1), (-1, BY)]
 CHIGH = [(BX, -1), (BX, BY)]
-PIECES = [LOCAL, XLOW, XHIGH, YLOW, YHIGH, CLOW, CHIGH]
+PIECES = [LOCAL, XLOW, CLOW, XHIGH, CHIGH, YLOW, YHIGH]
 KEY_BLOCKS = [block for piece in PIECES for block in piece]
 KEYS = len(KEY_BLOCKS) * BS
 
@@ -120,79 +121,121 @@
     )(adjacency, position, queries, *pieces)
 
 
-def project_kernel(bound_ref, pos_ref, att_ref, own_hbm, other_hbm, gain_ref, read_ref, cot_ref, pred_ref, ga_ref, w_ref, proj_ref, gp_ref, sems):
-    slabs = w_ref.shape[0]
-    cols = w_ref.shape[2]
-    core = pos_ref[4]
+def head_lanes(index):
+    return pl.ds(pl.multiple_of(index * HS, HS), HS)
+
+
+def far_step(k):
+    return (0, 1, 7, 2)[k // 2] + 4 * (k % 2)
+
+
+def project_kernel(
+    bound_ref, pos_ref, att_ref, near_hbm, near_swap_hbm, far_hbm, far_swap_hbm, gain_ref, read_ref, cot_ref,
+    pred_ref, ga_ref, near_ref, far_ref, own_att_ref, far_att_ref, proj_ref, gp_ref, sems,
+):
     copies = [
-        pltpu.make_async_copy(own_hbm, w_ref.at[core], sems.at[0]),
-        pltpu.make_async_copy(other_hbm, w_ref.at[1 - core], sems.at[1]),
+        pltpu.make_async_copy(near_hbm, near_ref.at[0], sems.at[0]),
+        pltpu.make_async_copy(near_swap_hbm, near_ref.at[1], sems.at[1]),
+        pltpu.make_async_copy(far_hbm, far_ref.at[0], sems.at[2]),
+        pltpu.make_async_copy(far_swap_hbm, far_ref.at[1], sems.at[3]),
     ]
     for copy in copies:
         copy.start()
-    for copy in copies:
-        copy.wait()
-    att = att_ref[...]
-    for s in range(slabs):
-        proj_ref[:, s * cols : (s + 1) * cols] = dot(att, w_ref[s], ((1,), (0,)))
+    core = pos_ref[4]
+    chip = pos_ref[5]
+    ring = pos_ref[6]
+    half = pos_ref[7]
+    n_ring, _, cols = near_ref.shape[1:]
+    n_chip = far_ref.shape[1]
+    part = cols // n_chip
+
+    def near_head(k):
+        return head_lanes(k * 2 + half)
+
+    def far_head(k):
+        return head_lanes(lax.rem(ring + 2 * n_ring - far_step(k), n_ring) * 2 + 1 - half)
+
+    def near_cols(side):
+        return pl.ds(pl.multiple_of((core if side == 0 else 1 - core) * cols, cols), cols)
+
+    def far_cols(side, j):
+        start = (core if side == 0 else 1 - core) * cols + lax.rem(chip + n_chip - j, n_chip) * part
+        return pl.ds(pl.multiple_of(start, part), part)
+
+    for k in range(n_ring):
+        own_att_ref[:, k * HS : (k + 1) * HS] = att_ref[:, near_head(k)]
+        far_att_ref[:, k * HS : (k + 1) * HS] = att_ref[:, far_head(k)]
+    rows = n_ring * HS
+    for side in range(2):
+        copies[side].wait()
+        proj_ref[:, near_cols(side)] = dot(own_att_ref[...], near_ref[side].reshape(rows, cols), ((1,), (0,)))
+    for side in range(2):
+        copies[2 + side].wait()
+        for j in range(n_chip):
+            lanes = far_cols(side, j)
+            proj_ref[:, lanes] += dot(far_att_ref[...], far_ref[side, j].reshape(rows, part), ((1,), (0,)))
     inner = proj_ref.shape[1]
-    for half in range(TOK // 32):
-        rows = slice(half * 32, (half + 1) * 32)
-        x = half * 2 // BY
-        y = half * 2 % BY
-        proj = proj_ref[rows, :]
+    for pair in range(TOK // (2 * BS)):
+        rows_of = slice(pair * 2 * BS, (pair + 1) * 2 * BS)
+        x = pair * 2 // BY
+        y = pair * 2 % BY
+        proj = proj_ref[rows_of, :]
         gain = gain_ref[...]
         flag = jnp.where(
-            lax.broadcasted_iota(jnp.int32, (32, 1), 0) < BS, bound_ref[0, x, y], bound_ref[0, x, y + 1]
+            lax.broadcasted_iota(jnp.int32, (2 * BS, 1), 0) < BS, bound_ref[0, x, y], bound_ref[0, x, y + 1]
         ).astype(jnp.float32)
         cot = jnp.concatenate([cot_ref[0, x, y], cot_ref[0, x, y + 1]], axis=0) * flag
         inv_rms = lax.rsqrt(jnp.sum(proj * proj, axis=1, keepdims=True) * (1.0 / inner) + 1e-05)
         normed = proj * inv_rms * gain
         pred0 = jnp.sum(normed * read_ref[0:1, :], axis=1, keepdims=True) * flag
         pred1 = jnp.sum(normed * read_ref[1:2, :], axis=1, keepdims=True) * flag
-        pred = jnp.where(lax.broadcasted_iota(jnp.int32, (32, 2), 1) == 0, pred0, pred1)
+        pred = jnp.where(lax.broadcasted_iota(jnp.int32, (2 * BS, 2), 1) == 0, pred0, pred1)
         pred_ref[0, x, y] = pred[:BS]
         pred_ref[0, x, y + 1] = pred[BS:]
         gained = (cot[:, 0:1] * read_ref[0:1, :] + cot[:, 1:2] * read_ref[1:2, :]) * gain
         inner_mean = jnp.sum(gained * proj, axis=1, keepdims=True) * (1.0 / inner)
-        gp_ref[rows, :] = (inv_rms * gained - proj * (inv_rms * inv_rms * inv_rms * inner_mean)).astype(jnp.bfloat16)
-    chunk = 512
-    for r in range(inner // chunk):
-        total = None
-        for s in range(slabs):
-            part = dot(gp_ref[:, s * cols : (s + 1) * cols], w_ref[s, r * chunk : (r + 1) * chunk, :], ((1,), (1,)))
-            total = part if total is None else total + part
-        ga_ref[:, r * chunk : (r + 1) * chunk] = total.astype(jnp.bfloat16)
-
-
-def project(boundary, position, att, own_rows, other_rows, gain, read_rows, cotangent):
+        gp_ref[rows_of, :] = (inv_rms * gained - proj * (inv_rms * inv_rms * inv_rms * inner_mean)).astype(jnp.bfloat16)
+    near = None
+    far = None
+    for side in range(2):
+        term = dot(gp_ref[:, near_cols(side)], near_ref[side].reshape(rows, cols), ((1,), (1,)))
+        near = term if near is None else near + term
+        for j in range(n_chip):
+            term = dot(gp_ref[:, far_cols(side, j)], far_ref[side, j].reshape(rows, part), ((1,), (1,)))
+            far = term if far is None else far + term
+    near = near.astype(jnp.bfloat16)
+    far = far.astype(jnp.bfloat16)
+    for k in range(n_ring):
+        ga_ref[:, near_head(k)] = near[:, k * HS : (k + 1) * HS]
+        ga_ref[:, far_head(k)] = far[:, k * HS : (k + 1) * HS]
+
+
+def project(boundary, position, att, weights, gain, read_rows, cotangent):
     vmem = pl.BlockSpec(memory_space=pltpu.VMEM)
+    smem = pl.BlockSpec(memory_space=pltpu.SMEM)
+    hbm = pl.BlockSpec(memory_space=pl.ANY)
+    near, _, far, _ = weights
+    tokens, inner = att.shape
     return pl.pallas_call(
         project_kernel,
-        in_specs=[
-            pl.BlockSpec(memory_space=pltpu.SMEM),
-            pl.BlockSpec(memory_space=pltpu.SMEM),
-            vmem,
-            pl.BlockSpec(memory_space=pl.ANY),
-            pl.BlockSpec(memory_space=pl.ANY),
-            vmem,
-            vmem,
-            vmem,
-        ],
+        in_specs=[smem, smem, vmem, hbm, hbm, hbm, hbm, vmem, vmem, vmem],
         out_specs=[vmem, vmem],
         out_shape=[
             jax.ShapeDtypeStruct(cotangent.shape, jnp.float32),
             jax.ShapeDtypeStruct(att.shape, jnp.bfloat16),
         ],
         scratch_shapes=[
-            pltpu.VMEM((2,) + own_rows.shape, jnp.bfloat16),
+            pltpu.VMEM((2,) + near.shape, jnp.bfloat16),
+            pltpu.VMEM((2,) + far.shape, jnp.bfloat16),
+            pltpu.VMEM((tokens, inner // 2), jnp.bfloat16),
+            pltpu.VMEM((tokens, inner // 2), jnp.bfloat16),
             pltpu.VMEM(att.shape, jnp.float32),
             pltpu.VMEM(att.shape, jnp.bfloat16),
-            pltpu.SemaphoreType.DMA((2,)),
+            pltpu.SemaphoreType.DMA((4,)),
         ],
         compiler_params=pltpu.CompilerParams(vmem_limit_bytes=VMEM_LIMIT),
         name="project",
-    )(boundary, position, att, own_rows, other_rows, gain, read_rows, cotangent)
+    )(boundary, position, att, *weights, gain, read_rows, cotangent)
 
 
 def backward_kernel(q_ref, ga_ref, prob_ref, *rest):
@@ -230,107 +273,159 @@
         return pl.BlockSpec(tuple(shape[:-1]) + (width,), lambda g: (0,) * (len(shape) - 1) + (g,))
 
     shapes = [p.shape for p in pieces]
+    blocks, rest = shapes[0], shapes[0][3:]
+    sums = [blocks, (2, 1, BY + 2) + rest, (2, 1, BY + 2) + rest, shapes[-1], shapes[-1]]
     return pl.pallas_call(
         backward_kernel,
         grid=(inner // width,),
         in_specs=[wide(queries.shape), wide(grad_att.shape), pl.BlockSpec((GROUP, KEYS, TOK), lambda g: (g, 0, 0))]
         + [wide(s) for s in shapes],
-        out_specs=[wide(queries.shape)] + [wide(s) for s in shapes],
+        out_specs=[wide(queries.shape)] + [wide(s) for s in sums],
         out_shape=[jax.ShapeDtypeStruct(queries.shape, jnp.bfloat16)]
-        + [jax.ShapeDtypeStruct(s, jnp.float32 if i == 0 else jnp.bfloat16) for i, s in enumerate(shapes)],
+        + [jax.ShapeDtypeStruct(s, jnp.float32 if i == 0 else jnp.bfloat16) for i, s in enumerate(sums)],
         compiler_params=pltpu.CompilerParams(vmem_limit_bytes=VMEM_LIMIT),
         name="attend_back",
     )(queries, grad_att, prob, *pieces)
 
 
-def finish_kernel(own_ref, xlow_ref, xhigh_ref, ylow_ref, yhigh_ref, out_ref):
+def add_rows_kernel(own_ref, low_ref, high_ref, out_ref, edge_ref):
     f32 = jnp.float32
     for which in range(2):
         for x in range(BX):
             for y in range(BY):
                 total = own_ref[which, x, y]
                 if x == 0:
-                    total = total + xlow_ref[which, 0, y].astype(f32)
+                    total = total + low_ref[which, 0, y].astype(f32)
                 if x == BX - 1:
-                    total = total + xhigh_ref[which, 0, y].astype(f32)
-                if y == 0:
-                    total = total + ylow_ref[which, x, 0].astype(f32)
-                if y == BY - 1:
-                    total = total + yhigh_ref[which, x, 0].astype(f32)
-                out_ref[which, x, y] = total.astype(out_ref.dtype)
-
-
-def finish(own, xlow, xhigh, ylow, yhigh):
+                    total = total + high_ref[which, 0, y].astype(f32)
+                if y in (0, BY - 1):
+                    edge_ref[which, x, y // (BY - 1)] = total
+                else:
+                    out_ref[which, x, y] = total.astype(out_ref.dtype)
+
+
+def add_rows(own, low, high):
     inner = own.shape[-1]
     width = inner // 4
 
     def wide(shape):
         return pl.BlockSpec(tuple(shape[:-1]) + (width,), lambda g: (0, 0, 0, 0, g))
 
-    args = (own, xlow, xhigh, ylow, yhigh)
+    edge = own.shape[:2] + (2,) + own.shape[3:]
     return pl.pallas_call(
-        finish_kernel,
+        add_rows_kernel,
         grid=(inner // width,),
-        in_specs=[wide(a.shape) for a in args],
-        out_specs=wide(own.shape),
-        out_shape=jax.ShapeDtypeStruct(own.shape, jnp.bfloat16),
-        compiler_params=pltpu.CompilerParams(vmem_limit_bytes=VMEM_LIMIT),
-        name="finish",
-    )(*args)
-
-
-def gather_weight(out_weight):
-    inner = out_weight.shape[1]
-    cols = inner // 2
-    n_wa = lax.axis_size("wa")
-    n_sy = lax.axis_size("sy")
-    half = lax.axis_index("wa") % 2
-    slab = lax.dynamic_slice_in_dim(out_weight, lax.axis_index("sx") % 2 * cols, cols, axis=1)
-    mirror = [(l * n_wa + w, (n_sy - 1 - l) * n_wa + (w ^ 1)) for l in range(n_sy) for w in range(n_wa)]
-    other = lax.ppermute(slab, ("sy", "wa"), mirror)
-    pair = jnp.where(half == 0, jnp.stack([slab, other]), jnp.stack([other, slab]))
-    groups = [list(range(h, n_wa, 2)) for h in range(2)]
-    rows = lax.all_gather(pair, "wa", axis=0, axis_index_groups=groups)
-    return rows.reshape(-1, cols)
+        in_specs=[wide(own.shape), wide(low.shape), wide(high.shape)],
+        out_specs=[wide(own.shape), wide(edge)],
+        out_shape=[jax.ShapeDtypeStruct(own.shape, jnp.bfloat16), jax.ShapeDtypeStruct(edge, jnp.float32)],
+        compiler_params=pltpu.CompilerParams(vmem_limit_bytes=SMALL_LIMIT),
+        name="add_rows",
+    )(own, low, high)
+
+
+def add_columns_kernel(edge_ref, low_ref, high_ref, partial_hbm, out_ref):
+    del partial_hbm
+    first = pl.program_id(0) == 0
+
+    @pl.when(first)
+    def _():
+        out_ref[...] = (edge_ref[...] + low_ref[...].astype(jnp.float32)).astype(out_ref.dtype)
+
+    @pl.when(jnp.logical_not(first))
+    def _():
+        out_ref[...] = (edge_ref[...] + high_ref[...].astype(jnp.float32)).astype(out_ref.dtype)
+
+
+def add_columns(edge, low, high, partial):
+    block = edge.shape[:2] + (1,) + edge.shape[3:]
+    whole = pl.BlockSpec(block, lambda i: (0, 0, 0, 0, 0))
+    return pl.pallas_call(
+        add_columns_kernel,
+        grid=(2,),
+        in_specs=[
+            pl.BlockSpec(block, lambda i: (0, 0, i, 0, 0)),
+            whole,
+            whole,
+            pl.BlockSpec(memory_space=pl.ANY),
+        ],
+        out_specs=pl.BlockSpec(block, lambda i: (0, 0, i * (BY - 1), 0, 0)),
+        out_shape=jax.ShapeDtypeStruct(partial.shape, partial.dtype),
+        input_output_aliases={3: 0},
+        compiler_params=pltpu.CompilerParams(vmem_limit_bytes=SMALL_LIMIT),
+        name="add_columns",
+    )(edge, low, high, partial)
+
+
+def around(value, axis, step):
+    count = lax.axis_size(axis)
+    return lax.ppermute(value, axis, [(i, (i + step) % count) for i in range(count)])
+
+
+def swap_cores(value):
+    return lax.ppermute(value, "sx", [(i, i ^ 1) for i in range(lax.axis_size("sx"))])
 
 
 def body(queries, keys_values, out_weight, gain, read_weight, adjacency, boundary, cotangent):
     size_x, size_y = queries.shape[1:3]
+    inner = out_weight.shape[1]
+    n_sx, n_sy, n_wa = (lax.axis_size(axis) for axis in ("sx", "sy", "wa"))
+    row, column, case = (lax.axis_index(axis) for axis in ("sx", "sy", "wa"))
+    core, chip, ring, half = row % 2, row // 2, case // 2, case % 2
     kv = keys_values[:, 0]
-    rows = gather_weight(out_weight)
+    cols = inner // 2
+    part = inner // n_sx
+    near_slab = lax.dynamic_slice_in_dim(out_weight, core * cols, cols, axis=1)
+    far_slab = lax.dynamic_slice_in_dim(out_weight, core * cols + chip * part, part, axis=1)
+    def mirrored(value, step):
+        pairs = [
+            (l * n_wa + w, (n_sy - 1 - l) * n_wa + (((w ^ 1) + 2 * step) % n_wa)) for l in range(n_sy) for w in range(n_wa)
+        ]
+        return lax.ppermute(value, ("sy", "wa"), pairs)
+
+    far = (mirrored(far_slab, 0), mirrored(far_slab, n_wa // 4))
+    groups = [list(range(h, n_wa, 2)) for h in range(2)]
+    near = lax.all_gather(near_slab, "wa", axis=0, axis_index_groups=groups)
     ylow = shift(kv[:, :, size_y - 1 :], "sy", 1)
     yhigh = shift(kv[:, :, :1], "sy", -1)
-    xlow = shift(kv[:, size_x - 1 :], "sx", 1)
-    xhigh = shift(kv[:, :1], "sx", -1)
+    far, kv_after = lax.optimization_barrier((far, kv))
+    far = jnp.stack(far)
+    far_y = jnp.concatenate([far] + [around(far, "wa", 2 * k) for k in (1, -1, 2)])
+    xlow = shift(kv_after[:, size_x - 1 :], "sx", 1)
+    xhigh = shift(kv_after[:, :1], "sx", -1)
     clow = shift(jnp.concatenate([ylow[:, size_x - 1 :], yhigh[:, size_x - 1 :]], axis=2), "sx", 1)
     chigh = shift(jnp.concatenate([ylow[:, :1], yhigh[:, :1]], axis=2), "sx", -1)
-    pieces = (kv, xlow, xhigh, ylow, yhigh, clow, chigh)
+    pieces = (kv, xlow, clow, xhigh, chigh, ylow, yhigh)
+    far_x = jnp.stack([far_y] + [around(far_y, "sx", 2 * k) for k in (1, 2, -1)])
     position = jnp.stack(
         [
-            lax.axis_index("sx") * size_x,
-            lax.axis_index("sy") * size_y,
-            jnp.int32(size_x * lax.axis_size("sx")),
-            jnp.int32(size_y * lax.axis_size("sy")),
-            lax.axis_index("sx") % 2,
+            row * size_x,
+            column * size_y,
+            jnp.int32(size_x * n_sx),
+            jnp.int32(size_y * n_sy),
+            core,
+            chip,
+            ring,
+            half,
         ]
     ).astype(jnp.int32)
     att, prob = forward(adjacency, position, queries, pieces)
-    rows, att = lax.optimization_barrier((rows, att))
-    other_rows = lax.ppermute(rows, "sx", [(i, i ^ 1) for i in range(lax.axis_size("sx"))])
-    prediction, grad_att = project(boundary, position, att, rows, other_rows, gain[None], read_weight.T, cotangent)
-    grad_queries, own, gxlow, gxhigh, gylow, gyhigh, gclow, gchigh = backward(queries, grad_att, prob, pieces)
-    to_high = shift(jnp.concatenate([gxhigh, gchigh], axis=2), "sx", 1)
-    to_low = shift(jnp.concatenate([gxlow, gclow], axis=2), "sx", -1)
+    near, att = lax.optimization_barrier((near, att))
+    weights = (near, swap_cores(near), far_x, swap_cores(far_x))
+    prediction, grad_att = project(boundary, position, att, weights, gain[None], read_weight.T, cotangent)
+    grad_queries, own, gxlow, gxhigh, gylow, gyhigh = backward(queries, grad_att, prob, pieces)
+    from_low = shift(gxhigh, "sx", 1)
+    from_high = shift(gxlow, "sx", -1)
     f32 = jnp.float32
 
     def side(rim, y):
-        first = rim[:, :1].astype(f32) + to_high[:, :, size_y + y : size_y + y + 1].astype(f32)
-        last = rim[:, 1:].astype(f32) + to_low[:, :, size_y + y : size_y + y + 1].astype(f32)
+        first = rim[:, :1].astype(f32) + from_low[:, :, size_y + y : size_y + y + 1].astype(f32)
+        last = rim[:, 1:].astype(f32) + from_high[:, :, size_y + y : size_y + y + 1].astype(f32)
         return jnp.concatenate([first, last], axis=1).astype(jnp.bfloat16)
 
-    from_low = shift(side(gyhigh, 1), "sy", 1)
-    from_high = shift(side(gylow, 0), "sy", -1)
-    grad_kv = finish(own, to_high[:, :, :size_y], to_low[:, :, :size_y], from_low, from_high)
+    left = shift(side(gyhigh, 1), "sy", 1)
+    right = shift(side(gylow, 0), "sy", -1)
+    partial, edge = add_rows(own, from_low, from_high)
+    grad_kv = add_columns(edge, left, right, partial)
     return (prediction, grad_queries, grad_kv[:, None])
 
 

time: 159 us -> 163 us (1.025)
  starting transfers between devices: 39.9 us -> 69.2 us
  waiting for transfers between devices: 60.1 us -> 35.6 us
  other arithmetic: 6.03 us -> 4.38 us
    ppermute x2 -> x10, starting transfers between devices: 14.1 us -> 40.6 us  [the longest x2 18.7 us: mirrored(): return lax.ppermute(value, ('sy', 'wa'), pairs)]
    all_gather x1, waiting for transfers between devices: 23.4 us -> 0.02 us  [body(): near = lax.all_gather(near_slab, 'wa', axis=0, axis_index_groups=groups)]
    ppermute x10, waiting for transfers between devices: 18 us -> 14 us  [shift(): return lax.ppermute(value, axis, pairs)]
    ppermute x2 -> x10, waiting for transfers between devices: 18.7 us -> 21.6 us  [the longest x6 17.3 us: around(): lax.ppermute(value, axis, [(i, (i + step) % count) for i in range(count)])]
    ppermute x10, starting transfers between devices: 25.8 us -> 28.6 us  [shift(): return lax.ppermute(value, axis, pairs)]
    concatenate x2 -> x0, other arithmetic: 2.43 us -> none  [the longest x1 1.23 us: body(): to_low = shift(jnp.concatenate([gxlow, gclow], axis=2), 'sx', -1)]
    slice x4 -> x2, local copies, waits for them, and re-layouts: 3.62 us -> 2.11 us  [the longest x1 1.07 us: body(): ylow = shift(kv[:, :, size_y - 1:], 'sy', 1)]
    unnamed x26 -> x34, local copies, waits for them, and re-layouts: 4.8 us -> 6.07 us
  transfers between devices with their start and end apart: 13 -> 21, of which waited for: 8 -> 8; matrix products, arithmetic and copies ran while one was open for 5% -> 5% of each run, Pallas kernels for 4% -> 5%
where the time goes in v1:
time: 163 us; the launch traced here: 160 us
  starting transfers between devices  69.2 us (42%)
  waiting for transfers between devices  35.6 us (22%)
  Pallas kernels  27 us (17%)
  between operations  14.6 us (9%)
  local copies, waits for them, and re-layouts  9.63 us (6%)
  other arithmetic  4.38 us (3%)
    ppermute x10, starting transfers between devices, shift(): return lax.ppermute(value, axis, pairs)  28.6 us
    ppermute x2, starting transfers between devices, mirrored(): return lax.ppermute(value, ('sy', 'wa'), pairs)  18.7 us
    ppermute x6, starting transfers between devices, around(): lax.ppermute(value, axis, [(i, (i + step) % count) for i in range(count)])  17.6 us
    ppermute x6, waiting for transfers between devices, around(): lax.ppermute(value, axis, [(i, (i + step) % count) for i in range(count)])  17.3 us
    ppermute x10, waiting for transfers between devices, shift(): return lax.ppermute(value, axis, pairs)  14 us
    pallas_call x1, Pallas kernels, project(): pl.pallas_call(project_kernel, in_specs=[smem, smem, vmem, hbm, hbm, hbm,...  9.37 us
    pallas_call x1, Pallas kernels, backward(): pl.pallas_call(backward_kernel, grid=(inner // width,), in_specs=[wide(qu...  8.31 us
    unnamed x34, local copies, waits for them, and re-layouts  6.07 us
  transfers between devices with their start and end apart: 21, of which 8 were waited for; matrix products, arithmetic and copies ran while one was open for 5% of the time, Pallas kernels for 5%

profile of v1, /device:TPU:1, one launch (start us, length us, event | category | flops | bytes accessed | tf_op | source)
XLA Modules:
  0.0 160.4 jit_solution(17577328686226023276)
XLA Ops:
  7.2 0.0 copy-start
  7.2 0.0 copy-start.4
  7.2 0.0 all-gather.3.cloned.1.call-start
  7.3 0.9 copy-done
  8.2 16.8 %collective-permute-start.1 = (bf16[128,256]{1,0:T(8,128)(2,1)S(1)}, bf16[128,256]{1,0:T(8,128)(2,1)S(1)}, u32[]{:S(2)}, u32[]{:S(2)}) collective-permute-start(bf16[128,256]{1,0:T(8,128)(2,1)S(1)} %constant_dynamic-slice_fusion), channel_id=1, source_target_pairs={{0,57},{1,56},{2,59},{3,58},{4,61},{5,60},{6,63},{7,62},{8,49},{9,... | collective-permute-start | bytes 196616 | tf_op jit(solution)/shard_map/ppermute | solution.py:383
  25.0 1.9 %collective-permute-start = (bf16[128,256]{1,0:T(8,128)(2,1)S(1)}, bf16[128,256]{1,0:T(8,128)(2,1)S(1)}, u32[]{:S(2)}, u32[]{:S(2)}) collective-permute-start(bf16[128,256]{1,0:T(8,128)(2,1)S(1)} %constant_dynamic-slice_fusion), channel_id=1, source_target_pairs={{0,49},{1,48},{2,51},{3,50},{4,53},{5,52},{6,55},{7,54},{8,57},{9,... | collective-permute-start | bytes 196616 | tf_op jit(solution)/shard_map/ppermute | solution.py:383
  26.9 0.7 constant_dynamic-slice_fusion.1
  27.7 0.0 all-gather.3.cloned.1.call-update
  27.7 1.1 fusion.1
  28.8 3.1 %collective-permute-start.3 = (bf16[2,2,1,16,2048]{4,3,2,1,0:T(8,128)(2,1)S(1)}, bf16[2,2,1,16,2048]{4,3,2,1,0:T(8,128)(2,1)S(1)}, u32[]{:S(2)}, u32[]{:S(2)}) collective-permute-start(bf16[2,2,1,16,2048]{4,3,2,1,0:T(8,128)(2,1)S(1)} %get-tuple-element.42), channel_id=1, source_target_pairs={{0,16},{16,32},{32,48},{1,17},{17,33},{33,49},{2,18},{18,34},{34,5... | collective-permute-start | bytes 786440 | tf_op jit(solution)/shard_map/ppermute | solution.py:32
  31.9 1.3 collective-permute-start.4
  33.2 0.0 collective-permute-done.1
  33.2 0.0 collective-permute-done
  33.2 2.4 %collective-permute-start.11 = (bf16[2,128,256]{2,1,0:T(8,128)(2,1)S(1)}, bf16[2,128,256]{2,1,0:T(8,128)(2,1)S(1)}, u32[]{:S(2)}, u32[]{:S(2)}) collective-permute-start(bf16[2,128,256]{2,1,0:T(8,128)(2,1)S(1)} %pad_maximum_fusion.5), channel_id=1, source_target_pairs={{0,4},{1,5},{2,6},{3,7},{4,8},{5,9},{6,10},{7,11},{8,12},{9,13},{1... | collective-permute-start | bytes 393224 | tf_op jit(solution)/shard_map/ppermute | solution.py:361
  35.6 4.2 %collective-permute-start.10 = (bf16[2,128,256]{2,1,0:T(8,128)(2,1)S(1)}, bf16[2,128,256]{2,1,0:T(8,128)(2,1)S(1)}, u32[]{:S(2)}, u32[]{:S(2)}) collective-permute-start(bf16[2,128,256]{2,1,0:T(8,128)(2,1)S(1)} %pad_maximum_fusion.5), channel_id=1, source_target_pairs={{0,14},{1,15},{2,0},{3,1},{4,2},{5,3},{6,4},{7,5},{8,6},{9,7},{10,... | collective-permute-start | bytes 393224 | tf_op jit(solution)/shard_map/ppermute | solution.py:361
  39.8 1.9 %collective-permute-start.9 = (bf16[2,128,256]{2,1,0:T(8,128)(2,1)S(1)}, bf16[2,128,256]{2,1,0:T(8,128)(2,1)S(1)}, u32[]{:S(2)}, u32[]{:S(2)}) collective-permute-start(bf16[2,128,256]{2,1,0:T(8,128)(2,1)S(1)} %pad_maximum_fusion.5), channel_id=1, source_target_pairs={{0,2},{1,3},{2,4},{3,5},{4,6},{5,7},{6,8},{7,9},{8,10},{9,11},{10,... | collective-permute-start | bytes 393224 | tf_op jit(solution)/shard_map/ppermute | solution.py:361
  41.8 1.0 fusion
  42.8 3.7 %collective-permute-start.6 = (bf16[2,1,4,16,2048]{4,3,2,1,0:T(8,128)(2,1)}, bf16[2,1,4,16,2048]{4,3,2,1,0:T(8,128)(2,1)S(1)}, u32[]{:S(2)}, u32[]{:S(2)}) collective-permute-start(bf16[2,1,4,16,2048]{4,3,2,1,0:T(8,128)(2,1)} %get-tuple-element.40), channel_id=1, source_target_pairs={{64,0},{128,64},{192,128},{256,192},{320,256},{384,320},{448,384},... | collective-permute-start | bytes 1572872 | tf_op jit(solution)/shard_map/ppermute | solution.py:32
  46.7 3.0 %collective-permute-start.5 = (bf16[2,1,2,16,2048]{4,3,2,1,0:T(8,128)(2,1)S(1)}, bf16[2,1,2,16,2048]{4,3,2,1,0:T(8,128)(2,1)S(1)}, u32[]{:S(2)}, u32[]{:S(2)}) collective-permute-start(bf16[2,1,2,16,2048]{4,3,2,1,0:T(8,128)(2,1)S(1)} %pad_maximum_fusion.1), channel_id=1, source_target_pairs={{0,64},{64,128},{128,192},{192,256},{256,320},{320,384},{384,448},... | collective-permute-start | bytes 786440 | tf_op jit(solution)/shard_map/ppermute | solution.py:32
  49.7 2.4 %collective-permute-done.9 = bf16[2,128,256]{2,1,0:T(8,128)(2,1)S(1)} collective-permute-done((bf16[2,128,256]{2,1,0:T(8,128)(2,1)S(1)}, bf16[2,128,256]{2,1,0:T(8,128)(2,1)S(1)}, u32[]{:S(2)}, u32[]{:S(2)}) %collective-permute-start.9) | collective-permute-done | bytes 131104 | tf_op jit(solution)/shard_map/ppermute | solution.py:361
  52.1 3.5 %collective-permute-start.7 = (bf16[2,1,2,16,2048]{4,3,2,1,0:T(8,128)(2,1)S(1)}, bf16[2,1,2,16,2048]{4,3,2,1,0:T(8,128)(2,1)S(1)}, u32[]{:S(2)}, u32[]{:S(2)}) collective-permute-start(bf16[2,1,2,16,2048]{4,3,2,1,0:T(8,128)(2,1)S(1)} %pad_maximum_fusion.2), channel_id=1, source_target_pairs={{64,0},{128,64},{192,128},{256,192},{320,256},{384,320},{448,384},... | collective-permute-start | bytes 786440 | tf_op jit(solution)/shard_map/ppermute | solution.py:32
  55.6 0.0 collective-permute-done.10
  55.6 3.0 %collective-permute-start.2 = (bf16[2,1,4,16,2048]{4,3,2,1,0:T(8,128)(2,1)}, bf16[2,1,4,16,2048]{4,3,2,1,0:T(8,128)(2,1)S(1)}, u32[]{:S(2)}, u32[]{:S(2)}) collective-permute-start(bf16[2,1,4,16,2048]{4,3,2,1,0:T(8,128)(2,1)} %get-tuple-element.41), channel_id=1, source_target_pairs={{0,64},{64,128},{128,192},{192,256},{256,320},{320,384},{384,448},... | collective-permute-start | bytes 1572872 | tf_op jit(solution)/shard_map/ppermute | solution.py:32
  58.7 0.0 collective-permute-done.11
  58.7 2.7 %collective-permute-start.14 = (bf16[8,128,256]{2,1,0:T(8,128)(2,1)S(1)}, bf16[8,128,256]{2,1,0:T(8,128)(2,1)}, u32[]{:S(2)}, u32[]{:S(2)}) collective-permute-start(bf16[8,128,256]{2,1,0:T(8,128)(2,1)S(1)} %constant_dynamic-update-slice_fusion), channel_id=1, source_target_pairs={{0,384},{64,448},{128,0},{192,64},{256,128},{320,192},{384,256},{4... | collective-permute-start | bytes 1572872 | tf_op jit(solution)/shard_map/ppermute | solution.py:361
  61.4 0.0 collective-permute-done.5.rest_2_
  61.4 4.1 %collective-permute-start.13 = (bf16[8,128,256]{2,1,0:T(8,128)(2,1)S(1)}, bf16[8,128,256]{2,1,0:T(8,128)(2,1)}, u32[]{:S(2)}, u32[]{:S(2)}) collective-permute-start(bf16[8,128,256]{2,1,0:T(8,128)(2,1)S(1)} %constant_dynamic-update-slice_fusion), channel_id=1, source_target_pairs={{0,256},{64,320},{128,384},{192,448},{256,0},{320,64},{384,128},{4... | collective-permute-start | bytes 1572872 | tf_op jit(solution)/shard_map/ppermute | solution.py:361
  65.6 0.0 collective-permute-done.7.rest_4_
  65.6 2.2 %collective-permute-start.12 = (bf16[8,128,256]{2,1,0:T(8,128)(2,1)S(1)}, bf16[8,128,256]{2,1,0:T(8,128)(2,1)}, u32[]{:S(2)}, u32[]{:S(2)}) collective-permute-start(bf16[8,128,256]{2,1,0:T(8,128)(2,1)S(1)} %constant_dynamic-update-slice_fusion), channel_id=1, source_target_pairs={{0,128},{64,192},{128,256},{192,320},{256,384},{320,448},{384,0},{... | collective-permute-start | bytes 1572872 | tf_op jit(solution)/shard_map/ppermute | solution.py:361
  67.9 0.7 stack.51.pos_ref
  68.5 0.0 collective-permute-done.6.rest_3_
  68.5 0.0 collective-permute-done.2.rest_1_
  68.6 0.8 copy-done.8
  69.3 0.8 copy-done.9
  70.1 5.6 %attend.1 = (bf16[128,2048]{1,0:T(8,128)(2,1)}, f32[16,384,128]{2,1,0:T(8,128)}) custom-call(s32[1,2,4,4]{3,2,1,0:T(4,128)} %adj_ref.1, s32[8]{0:T(128)} %stack.51.pos_ref, bf16[1,2,4,16,2048]{4,3,2,1,0:T(8,128)(2,1)} %q_ref.3, bf16[2,2,4,16,2048]{4,3,2,1,0:T(8,128)(2,1)} %bitcast.22, bf16[2,1,4,16,2048]{4,3,2,1,0:T(8,128)(2,1)} %copy-done.9, ...), custom_call_target="tpu_custom_call" | custom-call | tf_op jit(solution)/shard_map/attend/pallas_call | solution.py:106
  75.7 0.0 collective-permute-done.14
  75.8 2.5 %collective-permute-done.13 = bf16[8,128,256]{2,1,0:T(8,128)(2,1)} collective-permute-done((bf16[8,128,256]{2,1,0:T(8,128)(2,1)S(1)}, bf16[8,128,256]{2,1,0:T(8,128)(2,1)}, u32[]{:S(2)}, u32[]{:S(2)}) %collective-permute-start.13) | collective-permute-done | bytes 524320 | tf_op jit(solution)/shard_map/ppermute | solution.py:361
  78.3 12.4 %collective-permute-done.12 = bf16[8,128,256]{2,1,0:T(8,128)(2,1)} collective-permute-done((bf16[8,128,256]{2,1,0:T(8,128)(2,1)S(1)}, bf16[8,128,256]{2,1,0:T(8,128)(2,1)}, u32[]{:S(2)}, u32[]{:S(2)}) %collective-permute-start.12) | collective-permute-done | bytes 524320 | tf_op jit(solution)/shard_map/ppermute | solution.py:361
  90.7 1.6 %pad_maximum_fusion.far_hbm = bf16[4,8,128,256]{3,2,1,0:T(8,128)(2,1)S(1)} fusion(bf16[1,8,128,256]{3,2,1,0:T(8,128)(2,1)} %bitcast.13, bf16[1,8,128,256]{3,2,1,0:T(8,128)(2,1)} %bitcast.12, bf16[1,8,128,256]{3,2,1,0:T(8,128)(2,1)} %bitcast.11, bf16[1,8,128,256]{3,2,1,0:T(8,128)(2,1)S(1)} %bitcast.28), kind=kLoop, calls=%fused_computation | loop fusion | flops 3145728 | bytes 4194304 | tf_op jit(solution)/shard_map/stack | solution.py:398
  92.4 2.3 %collective-permute-start.15 = (bf16[4,8,128,256]{3,2,1,0:T(8,128)(2,1)S(1)}, bf16[4,8,128,256]{3,2,1,0:T(8,128)(2,1)}, u32[]{:S(2)}, u32[]{:S(2)}) collective-permute-start(bf16[4,8,128,256]{3,2,1,0:T(8,128)(2,1)S(1)} %pad_maximum_fusion.far_hbm), channel_id=1, source_target_pairs={{0,64},{64,0},{128,192},{192,128},{256,320},{320,256},{384,448},{4... | collective-permute-start | bytes 6291464 | tf_op jit(solution)/shard_map/ppermute | solution.py:365
  94.7 0.0 all-gather.3.cloned.1.call-done
  94.7 2.0 %collective-permute-start.8 = (bf16[8,128,1024]{2,1,0:T(8,128)(2,1)}, bf16[8,128,1024]{2,1,0:T(8,128)(2,1)}, u32[]{:S(2)}, u32[]{:S(2)}) collective-permute-start(bf16[8,128,1024]{2,1,0:T(8,128)(2,1)} %bitcast.25), channel_id=1, source_target_pairs={{0,64},{64,0},{128,192},{192,128},{256,320},{320,256},{384,448},{4... | collective-permute-start | bytes 6291464 | tf_op jit(solution)/shard_map/ppermute | solution.py:365
  96.7 0.8 copy.12.cot_ref
  97.5 1.1 collective-permute-done.15.far_swap_hbm
  98.6 3.2 %collective-permute-done.8.near_swap_hbm = bf16[8,128,1024]{2,1,0:T(8,128)(2,1)} collective-permute-done((bf16[8,128,1024]{2,1,0:T(8,128)(2,1)}, bf16[8,128,1024]{2,1,0:T(8,128)(2,1)}, u32[]{:S(2)}, u32[]{:S(2)}) %collective-permute-start.8) | collective-permute-done | bytes 2097184 | tf_op jit(solution)/shard_map/ppermute | solution.py:365
  101.8 9.4 %project.1 = (f32[1,2,4,16,2]{4,3,2,1,0:T(8,128)}, bf16[128,2048]{1,0:T(8,128)(2,1)}) custom-call(s32[1,2,4]{2,1,0:T(2,128)} %bound_ref.1, s32[8]{0:T(128)} %stack.51.pos_ref, bf16[128,2048]{1,0:T(8,128)(2,1)} %get-tuple-element.22.att_ref, bf16[8,128,1024]{2,1,0:T(8,128)(2,1)} %bitcast.26, bf16[8,128,1024]{2,1,0:T(8,128)(2,1)} %collective-permute-done.8.near_swap_hbm, ...), custom_call_target="tpu_custom_call" | custom-call | tf_op jit(solution)/shard_map/project/pallas_call | solution.py:219
  111.2 8.3 %attend_back.1 = (bf16[1,2,4,16,2048]{4,3,2,1,0:T(8,128)(2,1)}, f32[2,2,4,16,2048]{4,3,2,1,0:T(8,128)}, bf16[2,1,6,16,2048]{4,3,2,1,0:T(8,128)(2,1)}, bf16[2,1,6...) custom-call(bf16[1,2,4,16,2048]{4,3,2,1,0:T(8,128)(2,1)} %q_ref.3, ...), custom_call_target="tpu_custom_call" | custom-call | tf_op jit(solution)/shard_map/attend_back/pallas_call | solution.py:278
  119.5 2.4 %collective-permute-start.16 = (bf16[2,1,6,16,2048]{4,3,2,1,0:T(8,128)(2,1)}, bf16[2,1,6,16,2048]{4,3,2,1,0:T(8,128)(2,1)S(1)}, u32[]{:S(2)}, u32[]{:S(2)}) collective-permute-start(bf16[2,1,6,16,2048]{4,3,2,1,0:T(8,128)(2,1)} %get-tuple-element.31), channel_id=1, source_target_pairs={{0,64},{64,128},{128,192},{192,256},{256,320},{320,384},{384,448},... | collective-permute-start | bytes 2359304 | tf_op jit(solution)/shard_map/ppermute | solution.py:32
  122.0 2.1 %collective-permute-start.17 = (bf16[2,1,6,16,2048]{4,3,2,1,0:T(8,128)(2,1)}, bf16[2,1,6,16,2048]{4,3,2,1,0:T(8,128)(2,1)S(1)}, u32[]{:S(2)}, u32[]{:S(2)}) collective-permute-start(bf16[2,1,6,16,2048]{4,3,2,1,0:T(8,128)(2,1)} %get-tuple-element.32), channel_id=1, source_target_pairs={{64,0},{128,64},{192,128},{256,192},{320,256},{384,320},{448,384},... | collective-permute-start | bytes 2359304 | tf_op jit(solution)/shard_map/ppermute | solution.py:32
  124.0 7.2 %collective-permute-done.16.low_ref = bf16[2,1,6,16,2048]{4,3,2,1,0:T(8,128)(2,1)S(1)} collective-permute-done((bf16[2,1,6,16,2048]{4,3,2,1,0:T(8,128)(2,1)}, bf16[2,1,6,16,2048]{4,3,2,1,0:T(8,128)(2,1)S(1)}, u32[]{:S(2)}, u32[]{:S(2)}) %collective-permute-start.16) | collective-permute-done | bytes 786464 | tf_op jit(solution)/shard_map/ppermute | solution.py:32
  131.2 4.3 %collective-permute-done.17.high_ref = bf16[2,1,6,16,2048]{4,3,2,1,0:T(8,128)(2,1)S(1)} collective-permute-done((bf16[2,1,6,16,2048]{4,3,2,1,0:T(8,128)(2,1)}, bf16[2,1,6,16,2048]{4,3,2,1,0:T(8,128)(2,1)S(1)}, u32[]{:S(2)}, u32[]{:S(2)}) %collective-permute-start.17) | collective-permute-done | bytes 786464 | tf_op jit(solution)/shard_map/ppermute | solution.py:32
  135.5 1.2 add_convert_fusion
  136.7 0.0 copy-start.2
  136.7 0.9 copy-done.2
  137.6 0.7 pad_maximum_fusion.3
  138.3 5.2 %collective-permute-start.18 = (bf16[2,2,1,16,2048]{4,3,2,1,0:T(8,128)(2,1)}, bf16[2,2,1,16,2048]{4,3,2,1,0:T(8,128)(2,1)}, u32[]{:S(2)}, u32[]{:S(2)}) collective-permute-start(bf16[2,2,1,16,2048]{4,3,2,1,0:T(8,128)(2,1)} %pad_maximum_fusion.3), channel_id=1, source_target_pairs={{0,16},{16,32},{32,48},{1,17},{17,33},{33,49},{2,18},{18,34},{34,5... | collective-permute-start | bytes 786440 | tf_op jit(solution)/shard_map/ppermute | solution.py:32
  143.5 0.7 pad_maximum_fusion.4
  144.2 1.3 collective-permute-start.19
  145.5 0.7 copy.13
  146.3 1.1 copy-done.3
  147.4 1.8 %add_rows.1 = (bf16[2,2,4,16,2048]{4,3,2,1,0:T(8,128)(2,1)}, f32[2,2,2,16,2048]{4,3,2,1,0:T(8,128)S(1)}) custom-call(f32[2,2,4,16,2048]{4,3,2,1,0:T(8,128)S(1)} %copy-done.1, bf16[2,1,6,16,2048]{4,3,2,1,0:T(8,128)(2,1)S(1)} %collective-permute-done.16.low_ref, bf16[2,1,6,16,2048]{4,3,2,1,0:T(8,128)(2,1)S(1)} %copy-done.3), custom_call_target="tpu_custom_call" | custom-call | tf_op jit(solution)/shard_map/add_rows/pallas_call | solution.py:315
  149.2 0.0 collective-permute-done.18.low_ref
  149.2 2.5 %collective-permute-done.19.high_ref = bf16[2,2,1,16,2048]{4,3,2,1,0:T(8,128)(2,1)} collective-permute-done((bf16[2,2,1,16,2048]{4,3,2,1,0:T(8,128)(2,1)}, bf16[2,2,1,16,2048]{4,3,2,1,0:T(8,128)(2,1)}, u32[]{:S(2)}, u32[]{:S(2)}) %collective-permute-start.19) | collective-permute-done | bytes 262176 | tf_op jit(solution)/shard_map/ppermute | solution.py:32
  151.7 1.9 %add_columns.1 = bf16[2,2,4,16,2048]{4,3,2,1,0:T(8,128)(2,1)} custom-call(f32[2,2,2,16,2048]{4,3,2,1,0:T(8,128)S(1)} %get-tuple-element.33.edge_ref, bf16[2,2,1,16,2048]{4,3,2,1,0:T(8,128)(2,1)} %collective-permute-done.18.low_ref, bf16[2,2,1,16,2048]{4,3,2,1,0:T(8,128)(2,1)} %collective-permute-done.19.high_ref, ...), custom_call_target="tpu_custom_call", output_to_operand_aliasing={{}: (3, {})} | custom-call | tf_op jit(solution)/shard_map/add_columns/pallas_call | solution.py:342
  (34 shorter events, 0.2 us)
Async XLA Ops:
  7.2 1.0 copy-start
  7.2 34.6 %copy-start.4 = (bf16[2,1,2,4,16,2048]{5,4,3,2,1,0:T(8,128)(2,1)S(1)}, bf16[2,1,2,4,16,2048]{5,4,3,2,1,0:T(8,128)(2,1)}, u32[]{:S(2)}) copy-start(bf16[2,1,2,4,16,2048]{5,4,3,2,1,0:T(8,128)(2,1)} %param.9) | copy-start | bytes 3145732
  7.2 87.5 %all-gather.3.cloned.1.call-start = ((), (), s32[]{:S(2)}) async-start(), calls=%async_computation | async-start | bytes 2359296 | tf_op jit(solution)/shard_map/all_gather | solution.py:387
  8.2 24.9 %collective-permute-start.1 = (bf16[128,256]{1,0:T(8,128)(2,1)S(1)}, bf16[128,256]{1,0:T(8,128)(2,1)S(1)}, u32[]{:S(2)}, u32[]{:S(2)}) collective-permute-start(bf16[128,256]{1,0:T(8,128)(2,1)S(1)} %constant_dynamic-slice_fusion), channel_id=1, source_target_pairs={{0,57},{1,56},{2,59},{3,58},{4,61},{5,60},{6,63},{7,62},{8,49},{9,... | collective-permute-start | bytes 196616 | tf_op jit(solution)/shard_map/ppermute | solution.py:383
  25.0 8.2 %collective-permute-start = (bf16[128,256]{1,0:T(8,128)(2,1)S(1)}, bf16[128,256]{1,0:T(8,128)(2,1)S(1)}, u32[]{:S(2)}, u32[]{:S(2)}) collective-permute-start(bf16[128,256]{1,0:T(8,128)(2,1)S(1)} %constant_dynamic-slice_fusion), channel_id=1, source_target_pairs={{0,49},{1,48},{2,51},{3,50},{4,53},{5,52},{6,55},{7,54},{8,57},{9,... | collective-permute-start | bytes 196616 | tf_op jit(solution)/shard_map/ppermute | solution.py:383
  28.8 14.1 %collective-permute-start.3 = (bf16[2,2,1,16,2048]{4,3,2,1,0:T(8,128)(2,1)S(1)}, bf16[2,2,1,16,2048]{4,3,2,1,0:T(8,128)(2,1)S(1)}, u32[]{:S(2)}, u32[]{:S(2)}) collective-permute-start(bf16[2,2,1,16,2048]{4,3,2,1,0:T(8,128)(2,1)S(1)} %get-tuple-element.42), channel_id=1, source_target_pairs={{0,16},{16,32},{32,48},{1,17},{17,33},{33,49},{2,18},{18,34},{34,5... | collective-permute-start | bytes 786440 | tf_op jit(solution)/shard_map/ppermute | solution.py:32
  31.9 14.7 %collective-permute-start.4 = (bf16[2,2,1,16,2048]{4,3,2,1,0:T(8,128)(2,1)S(1)}, bf16[2,2,1,16,2048]{4,3,2,1,0:T(8,128)(2,1)S(1)}, u32[]{:S(2)}, u32[]{:S(2)}) collective-permute-start(bf16[2,2,1,16,2048]{4,3,2,1,0:T(8,128)(2,1)S(1)} %get-tuple-element.43), channel_id=1, source_target_pairs={{16,0},{32,16},{48,32},{17,1},{33,17},{49,33},{18,2},{34,18},{50,3... | collective-permute-start | bytes 786440 | tf_op jit(solution)/shard_map/ppermute | solution.py:32
  33.2 25.5 %collective-permute-start.11 = (bf16[2,128,256]{2,1,0:T(8,128)(2,1)S(1)}, bf16[2,128,256]{2,1,0:T(8,128)(2,1)S(1)}, u32[]{:S(2)}, u32[]{:S(2)}) collective-permute-start(bf16[2,128,256]{2,1,0:T(8,128)(2,1)S(1)} %pad_maximum_fusion.5), channel_id=1, source_target_pairs={{0,4},{1,5},{2,6},{3,7},{4,8},{5,9},{6,10},{7,11},{8,12},{9,13},{1... | collective-permute-start | bytes 393224 | tf_op jit(solution)/shard_map/ppermute | solution.py:361
  35.6 20.0 %collective-permute-start.10 = (bf16[2,128,256]{2,1,0:T(8,128)(2,1)S(1)}, bf16[2,128,256]{2,1,0:T(8,128)(2,1)S(1)}, u32[]{:S(2)}, u32[]{:S(2)}) collective-permute-start(bf16[2,128,256]{2,1,0:T(8,128)(2,1)S(1)} %pad_maximum_fusion.5), channel_id=1, source_target_pairs={{0,14},{1,15},{2,0},{3,1},{4,2},{5,3},{6,4},{7,5},{8,6},{9,7},{10,... | collective-permute-start | bytes 393224 | tf_op jit(solution)/shard_map/ppermute | solution.py:361
  39.8 12.3 %collective-permute-start.9 = (bf16[2,128,256]{2,1,0:T(8,128)(2,1)S(1)}, bf16[2,128,256]{2,1,0:T(8,128)(2,1)S(1)}, u32[]{:S(2)}, u32[]{:S(2)}) collective-permute-start(bf16[2,128,256]{2,1,0:T(8,128)(2,1)S(1)} %pad_maximum_fusion.5), channel_id=1, source_target_pairs={{0,2},{1,3},{2,4},{3,5},{4,6},{5,7},{6,8},{7,9},{8,10},{9,11},{10,... | collective-permute-start | bytes 393224 | tf_op jit(solution)/shard_map/ppermute | solution.py:361
  42.8 25.7 %copy-start.6 = (bf16[2,2,1,16,2048]{4,3,2,1,0:T(8,128)(2,1)}, bf16[2,2,1,16,2048]{4,3,2,1,0:T(8,128)(2,1)S(1)}, u32[]{:S(2)}) copy-start(bf16[2,2,1,16,2048]{4,3,2,1,0:T(8,128)(2,1)S(1)} %collective-permute-done.3.rest_5_) | copy-start | bytes 786436
  42.8 25.7 %collective-permute-start.6 = (bf16[2,1,4,16,2048]{4,3,2,1,0:T(8,128)(2,1)}, bf16[2,1,4,16,2048]{4,3,2,1,0:T(8,128)(2,1)S(1)}, u32[]{:S(2)}, u32[]{:S(2)}) collective-permute-start(bf16[2,1,4,16,2048]{4,3,2,1,0:T(8,128)(2,1)} %get-tuple-element.40), channel_id=1, source_target_pairs={{64,0},{128,64},{192,128},{256,192},{320,256},{384,320},{448,384},... | collective-permute-start | bytes 1572872 | tf_op jit(solution)/shard_map/ppermute | solution.py:32
  46.6 21.9 %copy-start.7 = (bf16[2,2,1,16,2048]{4,3,2,1,0:T(8,128)(2,1)}, bf16[2,2,1,16,2048]{4,3,2,1,0:T(8,128)(2,1)S(1)}, u32[]{:S(2)}) copy-start(bf16[2,2,1,16,2048]{4,3,2,1,0:T(8,128)(2,1)S(1)} %collective-permute-done.4.rest_6_) | copy-start | bytes 786436
  46.7 14.7 %collective-permute-start.5 = (bf16[2,1,2,16,2048]{4,3,2,1,0:T(8,128)(2,1)S(1)}, bf16[2,1,2,16,2048]{4,3,2,1,0:T(8,128)(2,1)S(1)}, u32[]{:S(2)}, u32[]{:S(2)}) collective-permute-start(bf16[2,1,2,16,2048]{4,3,2,1,0:T(8,128)(2,1)S(1)} %pad_maximum_fusion.1), channel_id=1, source_target_pairs={{0,64},{64,128},{128,192},{192,256},{256,320},{320,384},{384,448},... | collective-permute-start | bytes 786440 | tf_op jit(solution)/shard_map/ppermute | solution.py:32
  52.1 13.5 %collective-permute-start.7 = (bf16[2,1,2,16,2048]{4,3,2,1,0:T(8,128)(2,1)S(1)}, bf16[2,1,2,16,2048]{4,3,2,1,0:T(8,128)(2,1)S(1)}, u32[]{:S(2)}, u32[]{:S(2)}) collective-permute-start(bf16[2,1,2,16,2048]{4,3,2,1,0:T(8,128)(2,1)S(1)} %pad_maximum_fusion.2), channel_id=1, source_target_pairs={{64,0},{128,64},{192,128},{256,192},{320,256},{384,320},{448,384},... | collective-permute-start | bytes 786440 | tf_op jit(solution)/shard_map/ppermute | solution.py:32
  55.6 12.9 %collective-permute-start.2 = (bf16[2,1,4,16,2048]{4,3,2,1,0:T(8,128)(2,1)}, bf16[2,1,4,16,2048]{4,3,2,1,0:T(8,128)(2,1)S(1)}, u32[]{:S(2)}, u32[]{:S(2)}) collective-permute-start(bf16[2,1,4,16,2048]{4,3,2,1,0:T(8,128)(2,1)} %get-tuple-element.41), channel_id=1, source_target_pairs={{0,64},{64,128},{128,192},{192,256},{256,320},{320,384},{384,448},... | collective-permute-start | bytes 1572872 | tf_op jit(solution)/shard_map/ppermute | solution.py:32
  58.7 17.0 %collective-permute-start.14 = (bf16[8,128,256]{2,1,0:T(8,128)(2,1)S(1)}, bf16[8,128,256]{2,1,0:T(8,128)(2,1)}, u32[]{:S(2)}, u32[]{:S(2)}) collective-permute-start(bf16[8,128,256]{2,1,0:T(8,128)(2,1)S(1)} %constant_dynamic-update-slice_fusion), channel_id=1, source_target_pairs={{0,384},{64,448},{128,0},{192,64},{256,128},{320,192},{384,256},{4... | collective-permute-start | bytes 1572872 | tf_op jit(solution)/shard_map/ppermute | solution.py:361
  61.4 7.1 %copy-start.10 = (bf16[2,1,2,16,2048]{4,3,2,1,0:T(8,128)(2,1)}, bf16[2,1,2,16,2048]{4,3,2,1,0:T(8,128)(2,1)S(1)}, u32[]{:S(2)}) copy-start(bf16[2,1,2,16,2048]{4,3,2,1,0:T(8,128)(2,1)S(1)} %collective-permute-done.5.rest_2_) | copy-start | bytes 786436
  61.4 16.8 %collective-permute-start.13 = (bf16[8,128,256]{2,1,0:T(8,128)(2,1)S(1)}, bf16[8,128,256]{2,1,0:T(8,128)(2,1)}, u32[]{:S(2)}, u32[]{:S(2)}) collective-permute-start(bf16[8,128,256]{2,1,0:T(8,128)(2,1)S(1)} %constant_dynamic-update-slice_fusion), channel_id=1, source_target_pairs={{0,256},{64,320},{128,384},{192,448},{256,0},{320,64},{384,128},{4... | collective-permute-start | bytes 1572872 | tf_op jit(solution)/shard_map/ppermute | solution.py:361
  65.6 3.0 %copy-start.11 = (bf16[2,1,2,16,2048]{4,3,2,1,0:T(8,128)(2,1)}, bf16[2,1,2,16,2048]{4,3,2,1,0:T(8,128)(2,1)S(1)}, u32[]{:S(2)}) copy-start(bf16[2,1,2,16,2048]{4,3,2,1,0:T(8,128)(2,1)S(1)} %collective-permute-done.7.rest_4_) | copy-start | bytes 786436
  65.6 25.1 %collective-permute-start.12 = (bf16[8,128,256]{2,1,0:T(8,128)(2,1)S(1)}, bf16[8,128,256]{2,1,0:T(8,128)(2,1)}, u32[]{:S(2)}, u32[]{:S(2)}) collective-permute-start(bf16[8,128,256]{2,1,0:T(8,128)(2,1)S(1)} %constant_dynamic-update-slice_fusion), channel_id=1, source_target_pairs={{0,128},{64,192},{128,256},{192,320},{256,384},{320,448},{384,0},{... | collective-permute-start | bytes 1572872 | tf_op jit(solution)/shard_map/ppermute | solution.py:361
  68.5 0.8 copy-start.8
  69.3 0.8 copy-start.9
  90.7 6.0 %copy-start.13 = (f32[1,2,4,16,2]{3,4,2,1,0:T(2,128)S(1)}, f32[1,2,4,16,2]{3,4,2,1,0:T(2,128)}, u32[]{:S(2)}) copy-start(f32[1,2,4,16,2]{3,4,2,1,0:T(2,128)} %param.15) | copy-start | bytes 3076
  92.3 9.5 %copy-start.5 = (bf16[4,8,128,256]{3,2,1,0:T(8,128)(2,1)}, bf16[4,8,128,256]{3,2,1,0:T(8,128)(2,1)S(1)}, u32[]{:S(2)}) copy-start(bf16[4,8,128,256]{3,2,1,0:T(8,128)(2,1)S(1)} %pad_maximum_fusion.far_hbm) | copy-start | bytes 6291460
  92.4 6.2 %collective-permute-start.15 = (bf16[4,8,128,256]{3,2,1,0:T(8,128)(2,1)S(1)}, bf16[4,8,128,256]{3,2,1,0:T(8,128)(2,1)}, u32[]{:S(2)}, u32[]{:S(2)}) collective-permute-start(bf16[4,8,128,256]{3,2,1,0:T(8,128)(2,1)S(1)} %pad_maximum_fusion.far_hbm), channel_id=1, source_target_pairs={{0,64},{64,0},{128,192},{192,128},{256,320},{320,256},{384,448},{4... | collective-permute-start | bytes 6291464 | tf_op jit(solution)/shard_map/ppermute | solution.py:365
  94.7 7.1 %collective-permute-start.8 = (bf16[8,128,1024]{2,1,0:T(8,128)(2,1)}, bf16[8,128,1024]{2,1,0:T(8,128)(2,1)}, u32[]{:S(2)}, u32[]{:S(2)}) collective-permute-start(bf16[8,128,1024]{2,1,0:T(8,128)(2,1)} %bitcast.25), channel_id=1, source_target_pairs={{0,64},{64,0},{128,192},{192,128},{256,320},{320,256},{384,448},{4... | collective-permute-start | bytes 6291464 | tf_op jit(solution)/shard_map/ppermute | solution.py:365
  119.5 26.0 %copy-start.12 = (f32[1,2,4,16,2]{4,3,2,1,0:T(8,128)S(1)}, f32[1,2,4,16,2]{4,3,2,1,0:T(8,128)}, u32[]{:S(2)}) copy-start(f32[1,2,4,16,2]{4,3,2,1,0:T(8,128)} %get-tuple-element.37) | copy-start | bytes 3076
  119.5 26.8 %copy-start.1 = (f32[2,2,4,16,2048]{4,3,2,1,0:T(8,128)S(1)}, f32[2,2,4,16,2048]{4,3,2,1,0:T(8,128)}, u32[]{:S(2)}) copy-start(f32[2,2,4,16,2048]{4,3,2,1,0:T(8,128)} %get-tuple-element.30.own_ref) | copy-start | bytes 6291460
  119.5 11.7 %collective-permute-start.16 = (bf16[2,1,6,16,2048]{4,3,2,1,0:T(8,128)(2,1)}, bf16[2,1,6,16,2048]{4,3,2,1,0:T(8,128)(2,1)S(1)}, u32[]{:S(2)}, u32[]{:S(2)}) collective-permute-start(bf16[2,1,6,16,2048]{4,3,2,1,0:T(8,128)(2,1)} %get-tuple-element.31), channel_id=1, source_target_pairs={{0,64},{64,128},{128,192},{192,256},{256,320},{320,384},{384,448},... | collective-permute-start | bytes 2359304 | tf_op jit(solution)/shard_map/ppermute | solution.py:32
  122.0 13.5 %collective-permute-start.17 = (bf16[2,1,6,16,2048]{4,3,2,1,0:T(8,128)(2,1)}, bf16[2,1,6,16,2048]{4,3,2,1,0:T(8,128)(2,1)S(1)}, u32[]{:S(2)}, u32[]{:S(2)}) collective-permute-start(bf16[2,1,6,16,2048]{4,3,2,1,0:T(8,128)(2,1)} %get-tuple-element.32), channel_id=1, source_target_pairs={{64,0},{128,64},{192,128},{256,192},{320,256},{384,320},{448,384},... | collective-permute-start | bytes 2359304 | tf_op jit(solution)/shard_map/ppermute | solution.py:32
  136.7 0.9 copy-start.2
  138.3 10.8 %collective-permute-start.18 = (bf16[2,2,1,16,2048]{4,3,2,1,0:T(8,128)(2,1)}, bf16[2,2,1,16,2048]{4,3,2,1,0:T(8,128)(2,1)}, u32[]{:S(2)}, u32[]{:S(2)}) collective-permute-start(bf16[2,2,1,16,2048]{4,3,2,1,0:T(8,128)(2,1)} %pad_maximum_fusion.3), channel_id=1, source_target_pairs={{0,16},{16,32},{32,48},{1,17},{17,33},{33,49},{2,18},{18,34},{34,5... | collective-permute-start | bytes 786440 | tf_op jit(solution)/shard_map/ppermute | solution.py:32
  144.2 7.4 %collective-permute-start.19 = (bf16[2,2,1,16,2048]{4,3,2,1,0:T(8,128)(2,1)}, bf16[2,2,1,16,2048]{4,3,2,1,0:T(8,128)(2,1)}, u32[]{:S(2)}, u32[]{:S(2)}) collective-permute-start(bf16[2,2,1,16,2048]{4,3,2,1,0:T(8,128)(2,1)} %pad_maximum_fusion.4), channel_id=1, source_target_pairs={{16,0},{32,16},{48,32},{17,1},{33,17},{49,33},{18,2},{34,18},{50,3... | collective-permute-start | bytes 786440 | tf_op jit(solution)/shard_map/ppermute | solution.py:32
  146.3 1.1 copy-start.3
Sparse Core Ops, SparseCore 0:
  27.8 40.5 all-gather.2

commit v2 on v1

--- a/solution.py
+++ b/solution.py
@@ -129,51 +129,82 @@
     return (0, 1, 7, 2)[k // 2] + 4 * (k % 2)
 
 
-def project_kernel(
-    bound_ref, pos_ref, att_ref, near_hbm, near_swap_hbm, far_hbm, far_swap_hbm, gain_ref, read_ref, cot_ref,
-    pred_ref, ga_ref, near_ref, far_ref, own_att_ref, far_att_ref, proj_ref, gp_ref, sems,
-):
+def weight_lanes(pos_ref, n_ring, cols):
+    core = pos_ref[4]
+    ring = pos_ref[5]
+    half = pos_ref[6]
+
+    def near_head(k):
+        return head_lanes(k * 2 + half)
+
+    def far_head(k):
+        return head_lanes(lax.rem(ring + 2 * n_ring - far_step(k), n_ring) * 2 + 1 - half)
+
+    def side_cols(side):
+        return pl.ds(pl.multiple_of((core if side == 0 else 1 - core) * cols, cols), cols)
+
+    return near_head, far_head, side_cols
+
+
+def project_near_kernel(pos_ref, att_ref, own_hbm, swap_hbm, proj_ref, w_ref, part_ref, sems):
     copies = [
-        pltpu.make_async_copy(near_hbm, near_ref.at[0], sems.at[0]),
-        pltpu.make_async_copy(near_swap_hbm, near_ref.at[1], sems.at[1]),
-        pltpu.make_async_copy(far_hbm, far_ref.at[0], sems.at[2]),
-        pltpu.make_async_copy(far_swap_hbm, far_ref.at[1], sems.at[3]),
+        pltpu.make_async_copy(own_hbm, w_ref.at[0], sems.at[0]),
+        pltpu.make_async_copy(swap_hbm, w_ref.at[1], sems.at[1]),
     ]
     for copy in copies:
         copy.start()
-    core = pos_ref[4]
-    chip = pos_ref[5]
-    ring = pos_ref[6]
-    half = pos_ref[7]
+    n_ring, _, cols = w_ref.shape[1:]
+    near_head, _, side_cols = weight_lanes(pos_ref, n_ring, cols)
+    for k in range(n_ring):
+        part_ref[:, k * HS : (k + 1) * HS] = att_ref[:, near_head(k)]
+    for side in range(2):
+        copies[side].wait()
+        proj_ref[:, side_cols(side)] = dot(part_ref[...], w_ref[side].reshape(n_ring * HS, cols), ((1,), (0,)))
+
+
+def project_near(position, att, own, swapped):
+    vmem = pl.BlockSpec(memory_space=pltpu.VMEM)
+    hbm = pl.BlockSpec(memory_space=pl.ANY)
+    tokens, inner = att.shape
+    return pl.pallas_call(
+        project_near_kernel,
+        in_specs=[pl.BlockSpec(memory_space=pltpu.SMEM), vmem, hbm, hbm],
+        out_specs=vmem,
+        out_shape=jax.ShapeDtypeStruct(att.shape, jnp.float32),
+        scratch_shapes=[
+            pltpu.VMEM((2,) + own.shape, jnp.bfloat16),
+            pltpu.VMEM((tokens, inner // 2), jnp.bfloat16),
+            pltpu.SemaphoreType.DMA((2,)),
+        ],
+        compiler_params=pltpu.CompilerParams(vmem_limit_bytes=VMEM_LIMIT),
+        name="project_near",
+    )(position, att, own, swapped)
+
+
+def project_kernel(
+    bound_ref, pos_ref, att_ref, part_ref, near_hbm, near_swap_hbm, far_hbm, far_swap_hbm, gain_ref, read_ref, cot_ref,
+    pred_ref, ga_ref, near_ref, far_ref, far_att_ref, proj_ref, gp_ref, sems,
+):
+    far_copies = [
+        pltpu.make_async_copy(far_hbm, far_ref.at[0], sems.at[0]),
+        pltpu.make_async_copy(far_swap_hbm, far_ref.at[1], sems.at[1]),
+    ]
+    near_copies = [
+        pltpu.make_async_copy(near_hbm, near_ref.at[0], sems.at[2]),
+        pltpu.make_async_copy(near_swap_hbm, near_ref.at[1], sems.at[3]),
+    ]
+    for copy in far_copies + near_copies:
+        copy.start()
     n_ring, _, cols = near_ref.shape[1:]
-    n_chip = far_ref.shape[1]
-    part = cols // n_chip
-
-    def near_head(k):
-        return head_lanes(k * 2 + half)
-
-    def far_head(k):
-        return head_lanes(lax.rem(ring + 2 * n_ring - far_step(k), n_ring) * 2 + 1 - half)
-
-    def near_cols(side):
-        return pl.ds(pl.multiple_of((core if side == 0 else 1 - core) * cols, cols), cols)
-
-    def far_cols(side, j):
-        start = (core if side == 0 else 1 - core) * cols + lax.rem(chip + n_chip - j, n_chip) * part
-        return pl.ds(pl.multiple_of(start, part), part)
-
+    near_head, far_head, side_cols = weight_lanes(pos_ref, n_ring, cols)
     for k in range(n_ring):
-        own_att_ref[:, k * HS : (k + 1) * HS] = att_ref[:, near_head(k)]
         far_att_ref[:, k * HS : (k + 1) * HS] = att_ref[:, far_head(k)]
     rows = n_ring * HS
     for side in range(2):
-        copies[side].wait()
-        proj_ref[:, near_cols(side)] = dot(own_att_ref[...], near_ref[side].reshape(rows, cols), ((1,), (0,)))
-    for side in range(2):
-        copies[2 + side].wait()
-        for j in range(n_chip):
-            lanes = far_cols(side, j)
-            proj_ref[:, lanes] += dot(far_att_ref[...], far_ref[side, j].reshape(rows, part), ((1,), (0,)))
+        far_copies[side].wait()
+        lanes = side_cols(side)
+        term = dot(far_att_ref[...], far_ref[side].reshape(rows, cols), ((1,), (0,)))
+        proj_ref[:, lanes] = part_ref[:, lanes] + term
     inner = proj_ref.shape[1]
     for pair in range(TOK // (2 * BS)):
         rows_of = slice(pair * 2 * BS, (pair + 1) * 2 * BS)
@@ -195,22 +226,25 @@
         gained = (cot[:, 0:1] * read_ref[0:1, :] + cot[:, 1:2] * read_ref[1:2, :]) * gain
         inner_mean = jnp.sum(gained * proj, axis=1, keepdims=True) * (1.0 / inner)
         gp_ref[rows_of, :] = (inv_rms * gained - proj * (inv_rms * inv_rms * inv_rms * inner_mean)).astype(jnp.bfloat16)
-    near = None
-    far = None
-    for side in range(2):
-        term = dot(gp_ref[:, near_cols(side)], near_ref[side].reshape(rows, cols), ((1,), (1,)))
-        near = term if near is None else near + term
-        for j in range(n_chip):
-            term = dot(gp_ref[:, far_cols(side, j)], far_ref[side, j].reshape(rows, part), ((1,), (1,)))
-            far = term if far is None else far + term
-    near = near.astype(jnp.bfloat16)
-    far = far.astype(jnp.bfloat16)
+
+    def grad(w_ref):
+        total = None
+        for side in range(2):
+            term = dot(gp_ref[:, side_cols(side)], w_ref[side].reshape(rows, cols), ((1,), (1,)))
+            total = term if total is None else total + term
+        return total.astype(jnp.bfloat16)
+
+    far = grad(far_ref)
+    for k in range(n_ring):
+        ga_ref[:, far_head(k)] = far[:, k * HS : (k + 1) * HS]
+    for copy in near_copies:
+        copy.wait()
+    near = grad(near_ref)
     for k in range(n_ring):
         ga_ref[:, near_head(k)] = near[:, k * HS : (k + 1) * HS]
-        ga_ref[:, far_head(k)] = far[:, k * HS : (k + 1) * HS]
-
-
-def project(boundary, position, att, weights, gain, read_rows, cotangent):
+
+
+def project(boundary, position, att, part, weights, gain, read_rows, cotangent):
     vmem = pl.BlockSpec(memory_space=pltpu.VMEM)
     smem = pl.BlockSpec(memory_space=pltpu.SMEM)
     hbm = pl.BlockSpec(memory_space=pl.ANY)
@@ -218,7 +252,7 @@
     tokens, inner = att.shape
     return pl.pallas_call(
         project_kernel,
-        in_specs=[smem, smem, vmem, hbm, hbm, hbm, hbm, vmem, vmem, vmem],
+        in_specs=[smem, smem, vmem, vmem, hbm, hbm, hbm, hbm, vmem, vmem, vmem],
         out_specs=[vmem, vmem],
         out_shape=[
             jax.ShapeDtypeStruct(cotangent.shape, jnp.float32),
@@ -228,14 +262,13 @@
             pltpu.VMEM((2,) + near.shape, jnp.bfloat16),
             pltpu.VMEM((2,) + far.shape, jnp.bfloat16),
             pltpu.VMEM((tokens, inner // 2), jnp.bfloat16),
-            pltpu.VMEM((tokens, inner // 2), jnp.bfloat16),
             pltpu.VMEM(att.shape, jnp.float32),
             pltpu.VMEM(att.shape, jnp.bfloat16),
             pltpu.SemaphoreType.DMA((4,)),
         ],
         compiler_params=pltpu.CompilerParams(vmem_limit_bytes=VMEM_LIMIT),
         name="project",
-    )(boundary, position, att, *weights, gain, read_rows, cotangent)
+    )(boundary, position, att, part, *weights, gain, read_rows, cotangent)
 
 
 def backward_kernel(q_ref, ga_ref, prob_ref, *rest):
@@ -370,32 +403,30 @@
     inner = out_weight.shape[1]
     n_sx, n_sy, n_wa = (lax.axis_size(axis) for axis in ("sx", "sy", "wa"))
     row, column, case = (lax.axis_index(axis) for axis in ("sx", "sy", "wa"))
-    core, chip, ring, half = row % 2, row // 2, case // 2, case % 2
+    core, ring, half = row % 2, case // 2, case % 2
     kv = keys_values[:, 0]
     cols = inner // 2
-    part = inner // n_sx
-    near_slab = lax.dynamic_slice_in_dim(out_weight, core * cols, cols, axis=1)
-    far_slab = lax.dynamic_slice_in_dim(out_weight, core * cols + chip * part, part, axis=1)
+    slab = lax.dynamic_slice_in_dim(out_weight, core * cols, cols, axis=1)
+    groups = [list(range(h, n_wa, 2)) for h in range(2)]
+    near = lax.all_gather(slab, "wa", axis=0, axis_index_groups=groups)
+
     def mirrored(value, step):
         pairs = [
             (l * n_wa + w, (n_sy - 1 - l) * n_wa + (((w ^ 1) + 2 * step) % n_wa)) for l in range(n_sy) for w in range(n_wa)
         ]
         return lax.ppermute(value, ("sy", "wa"), pairs)
 
-    far = (mirrored(far_slab, 0), mirrored(far_slab, n_wa // 4))
-    groups = [list(range(h, n_wa, 2)) for h in range(2)]
-    near = lax.all_gather(near_slab, "wa", axis=0, axis_index_groups=groups)
+    far = (mirrored(slab, 0), mirrored(slab, n_wa // 4))
     ylow = shift(kv[:, :, size_y - 1 :], "sy", 1)
     yhigh = shift(kv[:, :, :1], "sy", -1)
-    far, kv_after = lax.optimization_barrier((far, kv))
+    xlow = shift(kv[:, size_x - 1 :], "sx", 1)
+    xhigh = shift(kv[:, :1], "sx", -1)
+    far, xlow, xhigh, ylow, yhigh = lax.optimization_barrier((far, xlow, xhigh, ylow, yhigh))
     far = jnp.stack(far)
-    far_y = jnp.concatenate([far] + [around(far, "wa", 2 * k) for k in (1, -1, 2)])
-    xlow = shift(kv_after[:, size_x - 1 :], "sx", 1)
-    xhigh = shift(kv_after[:, :1], "sx", -1)
+    far = jnp.concatenate([far] + [around(far, "wa", 2 * k) for k in (1, -1, 2)])
     clow = shift(jnp.concatenate([ylow[:, size_x - 1 :], yhigh[:, size_x - 1 :]], axis=2), "sx", 1)
     chigh = shift(jnp.concatenate([ylow[:, :1], yhigh[:, :1]], axis=2), "sx", -1)
     pieces = (kv, xlow, clow, xhigh, chigh, ylow, yhigh)
-    far_x = jnp.stack([far_y] + [around(far_y, "sx", 2 * k) for k in (1, 2, -1)])
     position = jnp.stack(
         [
             row * size_x,
@@ -403,15 +434,16 @@
             jnp.int32(size_x * n_sx),
             jnp.int32(size_y * n_sy),
             core,
-            chip,
             ring,
             half,
         ]
     ).astype(jnp.int32)
     att, prob = forward(adjacency, position, queries, pieces)
     near, att = lax.optimization_barrier((near, att))
-    weights = (near, swap_cores(near), far_x, swap_cores(far_x))
-    prediction, grad_att = project(boundary, position, att, weights, gain[None], read_weight.T, cotangent)
+    near_swap = swap_cores(near)
+    part = project_near(position, att, near, near_swap)
+    weights = (near, near_swap, far, swap_cores(far))
+    prediction, grad_att = project(boundary, position, att, part, weights, gain[None], read_weight.T, cotangent)
     grad_queries, own, gxlow, gxhigh, gylow, gyhigh = backward(queries, grad_att, prob, pieces)
     from_low = shift(gxhigh, "sx", 1)
     from_high = shift(gxlow, "sx", -1)

time: 163 us -> 171 us (1.049)
  local copies, waits for them, and re-layouts: 9.63 us -> 17 us
  starting transfers between devices: 69.2 us -> 61.9 us
  waiting for transfers between devices: 35.6 us -> 40.9 us
  Pallas kernels: 27 us -> 31 us
    ppermute x6 -> x3, starting transfers between devices: 17.6 us -> 9.49 us  [around(): lax.ppermute(value, axis, [(i, (i + step) % count) for i in range(count)])]
    ppermute x2, waiting for transfers between devices: 0.01 us -> 6.59 us  [mirrored(): return lax.ppermute(value, ('sy', 'wa'), pairs)]
    ppermute x10, waiting for transfers between devices: 14 us -> 18.8 us  [shift(): return lax.ppermute(value, axis, pairs)]
    unnamed x34, local copies, waits for them, and re-layouts: 6.07 us -> 10.6 us
    ppermute x2, waiting for transfers between devices: 4.32 us -> 0.01 us  [swap_cores(): lax.ppermute(value, 'sx', [(i, i ^ 1) for i in range(lax.axis_size('sx'))])]
    pallas_call x1 -> x2, Pallas kernels: 9.37 us -> 13.4 us  [the longest x1 8.64 us: project(): pl.pallas_call(project_kernel, in_specs=[smem, smem, vmem, vmem, hbm, hbm...]
    concatenate x1, local copies, waits for them, and re-layouts: 0.01 us -> 1.87 us  [body(): jnp.concatenate([far] + [around(far, 'wa', 2 * k) for k in (1, -1, 2)])]
    ppermute x6 -> x3, waiting for transfers between devices: 17.3 us -> 15.5 us  [around(): lax.ppermute(value, axis, [(i, (i + step) % count) for i in range(count)])]
  transfers between devices with their start and end apart: 21 -> 18, of which waited for: 8 -> 6; matrix products, arithmetic and copies ran while one was open for 5% -> 8% of each run, Pallas kernels for 5% -> 7%
where the time goes in v2:
time: 171 us; the launch traced here: 169 us
  starting transfers between devices  61.9 us (36%)
  waiting for transfers between devices  40.9 us (24%)
  Pallas kernels  31 us (18%)
  local copies, waits for them, and re-layouts  17 us (10%)
  between operations  14.4 us (8%)
  other arithmetic  3.65 us (2%)
    ppermute x10, starting transfers between devices, shift(): return lax.ppermute(value, axis, pairs)  29.4 us
    ppermute x10, waiting for transfers between devices, shift(): return lax.ppermute(value, axis, pairs)  18.8 us
    ppermute x2, starting transfers between devices, mirrored(): return lax.ppermute(value, ('sy', 'wa'), pairs)  18.7 us
    ppermute x3, waiting for transfers between devices, around(): lax.ppermute(value, axis, [(i, (i + step) % count) for i in range(count)])  15.5 us
    unnamed x34, local copies, waits for them, and re-layouts  10.6 us
    ppermute x3, starting transfers between devices, around(): lax.ppermute(value, axis, [(i, (i + step) % count) for i in range(count)])  9.49 us
    pallas_call x1, Pallas kernels, project(): pl.pallas_call(project_kernel, in_specs=[smem, smem, vmem, vmem, hbm, hbm...  8.64 us
    pallas_call x1, Pallas kernels, backward(): pl.pallas_call(backward_kernel, grid=(inner // width,), in_specs=[wide(qu...  8.3 us
  transfers between devices with their start and end apart: 18, of which 6 were waited for; matrix products, arithmetic and copies ran while one was open for 8% of the time, Pallas kernels for 7%

profile of v2, /device:TPU:1, one launch (start us, length us, event | category | flops | bytes accessed | tf_op | source)
XLA Modules:
  0.0 168.8 jit_solution(6525001559072102489)
XLA Ops:
  7.2 0.0 copy-start
  7.2 0.0 copy-start.4
  7.2 0.0 all-gather.3.cloned.1.call-start
  7.3 1.0 copy-done
  8.2 0.7 constant_dynamic-slice_fusion
  9.0 0.0 all-gather.3.cloned.1.call-update
  9.0 16.8 %collective-permute-start.1 = (bf16[128,1024]{1,0:T(8,128)(2,1)}, bf16[128,1024]{1,0:T(8,128)(2,1)S(1)}, u32[]{:S(2)}, u32[]{:S(2)}) collective-permute-start(bf16[128,1024]{1,0:T(8,128)(2,1)} %constant_dynamic-slice_fusion), channel_id=1, source_target_pairs={{0,57},{1,56},{2,59},{3,58},{4,61},{5,60},{6,63},{7,62},{8,49},{9,... | collective-permute-start | bytes 786440 | tf_op jit(solution)/shard_map/ppermute | solution.py:417
  25.7 1.9 %collective-permute-start = (bf16[128,1024]{1,0:T(8,128)(2,1)}, bf16[128,1024]{1,0:T(8,128)(2,1)S(1)}, u32[]{:S(2)}, u32[]{:S(2)}) collective-permute-start(bf16[128,1024]{1,0:T(8,128)(2,1)} %constant_dynamic-slice_fusion), channel_id=1, source_target_pairs={{0,49},{1,48},{2,51},{3,50},{4,53},{5,52},{6,55},{7,54},{8,57},{9,... | collective-permute-start | bytes 786440 | tf_op jit(solution)/shard_map/ppermute | solution.py:417
  27.7 2.3 %fusion.1 = (bf16[2,1,4,16,2048]{4,3,2,1,0:T(8,128)(2,1)}, bf16[2,1,4,16,2048]{4,3,2,1,0:T(8,128)(2,1)}) fusion(bf16[2,2,4,16,2048]{4,3,2,1,0:T(8,128)(2,1)} %bitcast.16), kind=kLoop, calls=%fused_computation.16 | loop fusion | bytes 2097152 | tf_op jit(solution)/shard_map/slice | solution.py:423
  30.0 2.9 %collective-permute-start.3 = (bf16[2,1,4,16,2048]{4,3,2,1,0:T(8,128)(2,1)}, bf16[2,1,4,16,2048]{4,3,2,1,0:T(8,128)(2,1)S(1)}, u32[]{:S(2)}, u32[]{:S(2)}) collective-permute-start(bf16[2,1,4,16,2048]{4,3,2,1,0:T(8,128)(2,1)} %get-tuple-element.48), channel_id=1, source_target_pairs={{64,0},{128,64},{192,128},{256,192},{320,256},{384,320},{448,384},... | collective-permute-start | bytes 1572872 | tf_op jit(solution)/shard_map/ppermute | solution.py:32
  32.8 3.0 %collective-permute-start.2 = (bf16[2,1,4,16,2048]{4,3,2,1,0:T(8,128)(2,1)}, bf16[2,1,4,16,2048]{4,3,2,1,0:T(8,128)(2,1)S(1)}, u32[]{:S(2)}, u32[]{:S(2)}) collective-permute-start(bf16[2,1,4,16,2048]{4,3,2,1,0:T(8,128)(2,1)} %get-tuple-element.49), channel_id=1, source_target_pairs={{0,64},{64,128},{128,192},{192,256},{256,320},{320,384},{384,448},... | collective-permute-start | bytes 1572872 | tf_op jit(solution)/shard_map/ppermute | solution.py:32
  35.9 0.7 fusion
  36.6 1.3 collective-permute-start.5
  37.9 0.0 collective-permute-done.1
  37.9 4.4 %collective-permute-start.4 = (bf16[2,2,1,16,2048]{4,3,2,1,0:T(8,128)(2,1)S(1)}, bf16[2,2,1,16,2048]{4,3,2,1,0:T(8,128)(2,1)S(1)}, u32[]{:S(2)}, u32[]{:S(2)}) collective-permute-start(bf16[2,2,1,16,2048]{4,3,2,1,0:T(8,128)(2,1)S(1)} %get-tuple-element.47), channel_id=1, source_target_pairs={{0,16},{16,32},{32,48},{1,17},{17,33},{33,49},{2,18},{18,34},{34,5... | collective-permute-start | bytes 786440 | tf_op jit(solution)/shard_map/ppermute | solution.py:32
  42.4 0.7 stack.32.pos_ref
  43.0 6.6 %collective-permute-done = bf16[128,1024]{1,0:T(8,128)(2,1)S(1)} collective-permute-done((bf16[128,1024]{1,0:T(8,128)(2,1)}, bf16[128,1024]{1,0:T(8,128)(2,1)S(1)}, u32[]{:S(2)}, u32[]{:S(2)}) %collective-permute-start) | collective-permute-done | bytes 262176 | tf_op jit(solution)/shard_map/ppermute | solution.py:417
  49.6 0.0 collective-permute-done.5.rest_6_
  49.6 0.0 collective-permute-done.4.rest_5_
  49.7 0.0 collective-permute-done.3.rest_3_
  49.7 0.0 collective-permute-done.2.rest_1_
  49.7 0.9 pad_maximum_fusion
  50.6 4.2 %collective-permute-start.11 = (bf16[2,128,1024]{2,1,0:T(8,128)(2,1)}, bf16[2,128,1024]{2,1,0:T(8,128)(2,1)}, u32[]{:S(2)}, u32[]{:S(2)}) collective-permute-start(bf16[2,128,1024]{2,1,0:T(8,128)(2,1)} %pad_maximum_fusion), channel_id=1, source_target_pairs={{0,4},{1,5},{2,6},{3,7},{4,8},{5,9},{6,10},{7,11},{8,12},{9,13},{1... | collective-permute-start | bytes 1572872 | tf_op jit(solution)/shard_map/ppermute | solution.py:394
  54.8 3.2 %collective-permute-start.10 = (bf16[2,128,1024]{2,1,0:T(8,128)(2,1)}, bf16[2,128,1024]{2,1,0:T(8,128)(2,1)S(1)}, u32[]{:S(2)}, u32[]{:S(2)}) collective-permute-start(bf16[2,128,1024]{2,1,0:T(8,128)(2,1)} %pad_maximum_fusion), channel_id=1, source_target_pairs={{0,14},{1,15},{2,0},{3,1},{4,2},{5,3},{6,4},{7,5},{8,6},{9,7},{10,... | collective-permute-start | bytes 1572872 | tf_op jit(solution)/shard_map/ppermute | solution.py:394
  58.1 2.1 %collective-permute-start.9 = (bf16[2,128,1024]{2,1,0:T(8,128)(2,1)}, bf16[2,128,1024]{2,1,0:T(8,128)(2,1)}, u32[]{:S(2)}, u32[]{:S(2)}) collective-permute-start(bf16[2,128,1024]{2,1,0:T(8,128)(2,1)} %pad_maximum_fusion), channel_id=1, source_target_pairs={{0,2},{1,3},{2,4},{3,5},{4,6},{5,7},{6,8},{7,9},{8,10},{9,11},{10,... | collective-permute-start | bytes 1572872 | tf_op jit(solution)/shard_map/ppermute | solution.py:394
  60.2 5.1 %collective-permute-start.6 = (bf16[2,1,2,16,2048]{4,3,2,1,0:T(8,128)(2,1)S(1)}, bf16[2,1,2,16,2048]{4,3,2,1,0:T(8,128)(2,1)S(1)}, u32[]{:S(2)}, u32[]{:S(2)}) collective-permute-start(bf16[2,1,2,16,2048]{4,3,2,1,0:T(8,128)(2,1)S(1)} %pad_maximum_fusion.1), channel_id=1, source_target_pairs={{0,64},{64,128},{128,192},{192,256},{256,320},{320,384},{384,448},... | collective-permute-start | bytes 786440 | tf_op jit(solution)/shard_map/ppermute | solution.py:32
  65.3 1.9 %collective-permute-start.7 = (bf16[2,1,2,16,2048]{4,3,2,1,0:T(8,128)(2,1)S(1)}, bf16[2,1,2,16,2048]{4,3,2,1,0:T(8,128)(2,1)S(1)}, u32[]{:S(2)}, u32[]{:S(2)}) collective-permute-start(bf16[2,1,2,16,2048]{4,3,2,1,0:T(8,128)(2,1)S(1)} %pad_maximum_fusion.2), channel_id=1, source_target_pairs={{64,0},{128,64},{192,128},{256,192},{320,256},{384,320},{448,384},... | collective-permute-start | bytes 786440 | tf_op jit(solution)/shard_map/ppermute | solution.py:32
  67.2 0.7 constant_dynamic-update-slice_fusion.4
  68.0 0.7 constant_dynamic-update-slice_fusion.3
  68.7 0.0 collective-permute-done.6.rest_2_
  68.7 4.7 %collective-permute-done.7.rest_4_ = bf16[2,1,2,16,2048]{4,3,2,1,0:T(8,128)(2,1)S(1)} collective-permute-done((bf16[2,1,2,16,2048]{4,3,2,1,0:T(8,128)(2,1)S(1)}, bf16[2,1,2,16,2048]{4,3,2,1,0:T(8,128)(2,1)S(1)}, u32[]{:S(2)}, u32[]{:S(2)}) %collective-permute-start.7) | collective-permute-done | bytes 262176 | tf_op jit(solution)/shard_map/ppermute | solution.py:32
  73.4 0.7 copy-done.11
  74.1 5.6 %attend.1 = (bf16[128,2048]{1,0:T(8,128)(2,1)}, f32[16,384,128]{2,1,0:T(8,128)}) custom-call(s32[1,2,4,4]{3,2,1,0:T(4,128)} %adj_ref.1, s32[7]{0:T(128)} %stack.32.pos_ref, bf16[1,2,4,16,2048]{4,3,2,1,0:T(8,128)(2,1)} %q_ref.3, bf16[2,2,4,16,2048]{4,3,2,1,0:T(8,128)(2,1)} %bitcast.17, bf16[2,1,4,16,2048]{4,3,2,1,0:T(8,128)(2,1)} %copy-done.9, ...), custom_call_target="tpu_custom_call" | custom-call | tf_op jit(solution)/shard_map/attend/pallas_call | solution.py:106
  79.7 0.0 copy-start.13
  79.7 15.5 %collective-permute-done.9 = bf16[2,128,1024]{2,1,0:T(8,128)(2,1)} collective-permute-done((bf16[2,128,1024]{2,1,0:T(8,128)(2,1)}, bf16[2,128,1024]{2,1,0:T(8,128)(2,1)}, u32[]{:S(2)}, u32[]{:S(2)}) %collective-permute-start.9) | collective-permute-done | bytes 524320 | tf_op jit(solution)/shard_map/ppermute | solution.py:394
  95.2 1.9 %constant_dynamic-update-slice_fusion.2 = bf16[8,128,1024]{2,1,0:T(8,128)(2,1)} fusion(bf16[8,128,1024]{2,1,0:T(8,128)(2,1)} %constant_dynamic-update-slice_fusion.3, bf16[2,128,1024]{2,1,0:T(8,128)(2,1)} %collective-permute-done.9), kind=kLoop, calls=%fused_computation.11 | loop fusion | bytes 1048576
  97.1 0.0 collective-permute-done.10
  97.1 0.8 constant_dynamic-update-slice_fusion.1
  97.9 2.3 %collective-permute-start.8 = (bf16[8,128,1024]{2,1,0:T(8,128)(2,1)}, bf16[8,128,1024]{2,1,0:T(8,128)(2,1)S(1)}, u32[]{:S(2)}, u32[]{:S(2)}) collective-permute-start(bf16[8,128,1024]{2,1,0:T(8,128)(2,1)} %bitcast.20), channel_id=1, source_target_pairs={{0,64},{64,0},{128,192},{192,128},{256,320},{320,256},{384,448},{4... | collective-permute-start | bytes 6291464 | tf_op jit(solution)/shard_map/ppermute | solution.py:398
  100.3 1.9 %constant_dynamic-update-slice_fusion.far_hbm = bf16[8,128,1024]{2,1,0:T(8,128)(2,1)} fusion(bf16[8,128,1024]{2,1,0:T(8,128)(2,1)} %constant_dynamic-update-slice_fusion.1, bf16[2,128,1024]{2,1,0:T(8,128)(2,1)} %collective-permute-done.11), kind=kLoop, calls=%fused_computation.9 | loop fusion | bytes 1048576 | tf_op jit(solution)/shard_map/concatenate | solution.py:426
  102.1 2.0 %collective-permute-start.12 = (bf16[8,128,1024]{2,1,0:T(8,128)(2,1)}, bf16[8,128,1024]{2,1,0:T(8,128)(2,1)}, u32[]{:S(2)}, u32[]{:S(2)}) collective-permute-start(bf16[8,128,1024]{2,1,0:T(8,128)(2,1)} %constant_dynamic-update-slice_fusion.far_hbm), channel_id=1, source_target_pairs={{0,64},{64,0},{128,192},{192,128},{256,320},{320,256},{384,448},{4... | collective-permute-start | bytes 6291464 | tf_op jit(solution)/shard_map/ppermute | solution.py:398
  104.2 0.8 copy.12.cot_ref
  104.9 0.0 collective-permute-done.8.swap_hbm.near_swap_hbm
  104.9 1.3 copy-done.5
  106.2 4.7 %project_near.1.part_ref = f32[128,2048]{1,0:T(8,128)} custom-call(s32[7]{0:T(128)} %stack.32.pos_ref, bf16[128,2048]{1,0:T(8,128)(2,1)} %get-tuple-element.28.att_ref, bf16[8,128,1024]{2,1,0:T(8,128)(2,1)} %bitcast.21, bf16[8,128,1024]{2,1,0:T(8,128)(2,1)} %copy-done.5), custom_call_target="tpu_custom_call" | custom-call | tf_op jit(solution)/shard_map/project_near/pallas_call | solution.py:169
  111.0 8.6 %project.1 = (f32[1,2,4,16,2]{4,3,2,1,0:T(8,128)}, bf16[128,2048]{1,0:T(8,128)(2,1)}) custom-call(s32[1,2,4]{2,1,0:T(2,128)} %bound_ref.1, s32[7]{0:T(128)} %stack.32.pos_ref, bf16[128,2048]{1,0:T(8,128)(2,1)} %get-tuple-element.28.att_ref, f32[128,2048]{1,0:T(8,128)} %project_near.1.part_ref, bf16[8,128,1024]{2,1,0:T(8,128)(2,1)} %bitcast.22, ...), custom_call_target="tpu_custom_call" | custom-call | tf_op jit(solution)/shard_map/project/pallas_call | solution.py:253
  119.6 8.3 %attend_back.1 = (bf16[1,2,4,16,2048]{4,3,2,1,0:T(8,128)(2,1)}, f32[2,2,4,16,2048]{4,3,2,1,0:T(8,128)}, bf16[2,1,6,16,2048]{4,3,2,1,0:T(8,128)(2,1)}, bf16[2,1,6...) custom-call(bf16[1,2,4,16,2048]{4,3,2,1,0:T(8,128)(2,1)} %q_ref.3, ...), custom_call_target="tpu_custom_call" | custom-call | tf_op jit(solution)/shard_map/attend_back/pallas_call | solution.py:311
  127.9 3.5 %collective-permute-start.13 = (bf16[2,1,6,16,2048]{4,3,2,1,0:T(8,128)(2,1)}, bf16[2,1,6,16,2048]{4,3,2,1,0:T(8,128)(2,1)S(1)}, u32[]{:S(2)}, u32[]{:S(2)}) collective-permute-start(bf16[2,1,6,16,2048]{4,3,2,1,0:T(8,128)(2,1)} %get-tuple-element.37), channel_id=1, source_target_pairs={{0,64},{64,128},{128,192},{192,256},{256,320},{320,384},{384,448},... | collective-permute-start | bytes 2359304 | tf_op jit(solution)/shard_map/ppermute | solution.py:32
  131.5 1.9 %collective-permute-start.14 = (bf16[2,1,6,16,2048]{4,3,2,1,0:T(8,128)(2,1)}, bf16[2,1,6,16,2048]{4,3,2,1,0:T(8,128)(2,1)S(1)}, u32[]{:S(2)}, u32[]{:S(2)}) collective-permute-start(bf16[2,1,6,16,2048]{4,3,2,1,0:T(8,128)(2,1)} %get-tuple-element.38), channel_id=1, source_target_pairs={{64,0},{128,64},{192,128},{256,192},{320,256},{384,320},{448,384},... | collective-permute-start | bytes 2359304 | tf_op jit(solution)/shard_map/ppermute | solution.py:32
  133.4 7.3 %collective-permute-done.13.low_ref = bf16[2,1,6,16,2048]{4,3,2,1,0:T(8,128)(2,1)S(1)} collective-permute-done((bf16[2,1,6,16,2048]{4,3,2,1,0:T(8,128)(2,1)}, bf16[2,1,6,16,2048]{4,3,2,1,0:T(8,128)(2,1)S(1)}, u32[]{:S(2)}, u32[]{:S(2)}) %collective-permute-start.13) | collective-permute-done | bytes 786464 | tf_op jit(solution)/shard_map/ppermute | solution.py:32
  140.7 4.3 %collective-permute-done.14.high_ref = bf16[2,1,6,16,2048]{4,3,2,1,0:T(8,128)(2,1)S(1)} collective-permute-done((bf16[2,1,6,16,2048]{4,3,2,1,0:T(8,128)(2,1)}, bf16[2,1,6,16,2048]{4,3,2,1,0:T(8,128)(2,1)S(1)}, u32[]{:S(2)}, u32[]{:S(2)}) %collective-permute-start.14) | collective-permute-done | bytes 786464 | tf_op jit(solution)/shard_map/ppermute | solution.py:32
  145.0 1.2 add_convert_fusion
  146.2 0.0 copy-start.2
  146.2 0.9 copy-done.2
  147.1 0.7 pad_maximum_fusion.3
  147.8 4.1 %collective-permute-start.15 = (bf16[2,2,1,16,2048]{4,3,2,1,0:T(8,128)(2,1)}, bf16[2,2,1,16,2048]{4,3,2,1,0:T(8,128)(2,1)}, u32[]{:S(2)}, u32[]{:S(2)}) collective-permute-start(bf16[2,2,1,16,2048]{4,3,2,1,0:T(8,128)(2,1)} %pad_maximum_fusion.3), channel_id=1, source_target_pairs={{0,16},{16,32},{32,48},{1,17},{17,33},{33,49},{2,18},{18,34},{34,5... | collective-permute-start | bytes 786440 | tf_op jit(solution)/shard_map/ppermute | solution.py:32
  151.9 0.7 pad_maximum_fusion.4
  152.6 1.3 collective-permute-start.16
  153.9 0.7 copy.13
  154.7 1.1 copy-done.3
  155.8 1.8 %add_rows.1 = (bf16[2,2,4,16,2048]{4,3,2,1,0:T(8,128)(2,1)}, f32[2,2,2,16,2048]{4,3,2,1,0:T(8,128)S(1)}) custom-call(f32[2,2,4,16,2048]{4,3,2,1,0:T(8,128)S(1)} %copy-done.1, bf16[2,1,6,16,2048]{4,3,2,1,0:T(8,128)(2,1)S(1)} %collective-permute-done.13.low_ref, bf16[2,1,6,16,2048]{4,3,2,1,0:T(8,128)(2,1)S(1)} %copy-done.3), custom_call_target="tpu_custom_call" | custom-call | tf_op jit(solution)/shard_map/add_rows/pallas_call | solution.py:348
  157.6 0.0 collective-permute-done.15.low_ref
  157.6 2.5 %collective-permute-done.16.high_ref = bf16[2,2,1,16,2048]{4,3,2,1,0:T(8,128)(2,1)} collective-permute-done((bf16[2,2,1,16,2048]{4,3,2,1,0:T(8,128)(2,1)}, bf16[2,2,1,16,2048]{4,3,2,1,0:T(8,128)(2,1)}, u32[]{:S(2)}, u32[]{:S(2)}) %collective-permute-start.16) | collective-permute-done | bytes 262176 | tf_op jit(solution)/shard_map/ppermute | solution.py:32
  160.1 1.9 %add_columns.1 = bf16[2,2,4,16,2048]{4,3,2,1,0:T(8,128)(2,1)} custom-call(f32[2,2,2,16,2048]{4,3,2,1,0:T(8,128)S(1)} %get-tuple-element.39.edge_ref, bf16[2,2,1,16,2048]{4,3,2,1,0:T(8,128)(2,1)} %collective-permute-done.15.low_ref, bf16[2,2,1,16,2048]{4,3,2,1,0:T(8,128)(2,1)} %collective-permute-done.16.high_ref, ...), custom_call_target="tpu_custom_call", output_to_operand_aliasing={{}: (3, {})} | custom-call | tf_op jit(solution)/shard_map/add_columns/pallas_call | solution.py:375
  (26 shorter events, 0.1 us)
Async XLA Ops:
  7.2 1.0 copy-start
  7.2 28.7 %copy-start.4 = (bf16[2,1,2,4,16,2048]{5,4,3,2,1,0:T(8,128)(2,1)S(1)}, bf16[2,1,2,4,16,2048]{5,4,3,2,1,0:T(8,128)(2,1)}, u32[]{:S(2)}) copy-start(bf16[2,1,2,4,16,2048]{5,4,3,2,1,0:T(8,128)(2,1)} %param.9) | copy-start | bytes 3145732
  7.2 90.8 %all-gather.3.cloned.1.call-start = ((), (), s32[]{:S(2)}) async-start(), calls=%async_computation | async-start | bytes 2359296 | tf_op jit(solution)/shard_map/all_gather | solution.py:411
  9.0 28.9 %collective-permute-start.1 = (bf16[128,1024]{1,0:T(8,128)(2,1)}, bf16[128,1024]{1,0:T(8,128)(2,1)S(1)}, u32[]{:S(2)}, u32[]{:S(2)}) collective-permute-start(bf16[128,1024]{1,0:T(8,128)(2,1)} %constant_dynamic-slice_fusion), channel_id=1, source_target_pairs={{0,57},{1,56},{2,59},{3,58},{4,61},{5,60},{6,63},{7,62},{8,49},{9,... | collective-permute-start | bytes 786440 | tf_op jit(solution)/shard_map/ppermute | solution.py:417
  25.7 23.9 %collective-permute-start = (bf16[128,1024]{1,0:T(8,128)(2,1)}, bf16[128,1024]{1,0:T(8,128)(2,1)S(1)}, u32[]{:S(2)}, u32[]{:S(2)}) collective-permute-start(bf16[128,1024]{1,0:T(8,128)(2,1)} %constant_dynamic-slice_fusion), channel_id=1, source_target_pairs={{0,49},{1,48},{2,51},{3,50},{4,53},{5,52},{6,55},{7,54},{8,57},{9,... | collective-permute-start | bytes 786440 | tf_op jit(solution)/shard_map/ppermute | solution.py:417
  30.0 19.7 %collective-permute-start.3 = (bf16[2,1,4,16,2048]{4,3,2,1,0:T(8,128)(2,1)}, bf16[2,1,4,16,2048]{4,3,2,1,0:T(8,128)(2,1)S(1)}, u32[]{:S(2)}, u32[]{:S(2)}) collective-permute-start(bf16[2,1,4,16,2048]{4,3,2,1,0:T(8,128)(2,1)} %get-tuple-element.48), channel_id=1, source_target_pairs={{64,0},{128,64},{192,128},{256,192},{320,256},{384,320},{448,384},... | collective-permute-start | bytes 1572872 | tf_op jit(solution)/shard_map/ppermute | solution.py:32
  32.8 16.9 %collective-permute-start.2 = (bf16[2,1,4,16,2048]{4,3,2,1,0:T(8,128)(2,1)}, bf16[2,1,4,16,2048]{4,3,2,1,0:T(8,128)(2,1)S(1)}, u32[]{:S(2)}, u32[]{:S(2)}) collective-permute-start(bf16[2,1,4,16,2048]{4,3,2,1,0:T(8,128)(2,1)} %get-tuple-element.49), channel_id=1, source_target_pairs={{0,64},{64,128},{128,192},{192,256},{256,320},{320,384},{384,448},... | collective-permute-start | bytes 1572872 | tf_op jit(solution)/shard_map/ppermute | solution.py:32
  36.6 13.0 %collective-permute-start.5 = (bf16[2,2,1,16,2048]{4,3,2,1,0:T(8,128)(2,1)}, bf16[2,2,1,16,2048]{4,3,2,1,0:T(8,128)(2,1)S(1)}, u32[]{:S(2)}, u32[]{:S(2)}) collective-permute-start(bf16[2,2,1,16,2048]{4,3,2,1,0:T(8,128)(2,1)} %get-tuple-element.46), channel_id=1, source_target_pairs={{16,0},{32,16},{48,32},{17,1},{33,17},{49,33},{18,2},{34,18},{50,3... | collective-permute-start | bytes 786440 | tf_op jit(solution)/shard_map/ppermute | solution.py:32
  37.9 11.7 %collective-permute-start.4 = (bf16[2,2,1,16,2048]{4,3,2,1,0:T(8,128)(2,1)S(1)}, bf16[2,2,1,16,2048]{4,3,2,1,0:T(8,128)(2,1)S(1)}, u32[]{:S(2)}, u32[]{:S(2)}) collective-permute-start(bf16[2,2,1,16,2048]{4,3,2,1,0:T(8,128)(2,1)S(1)} %get-tuple-element.47), channel_id=1, source_target_pairs={{0,16},{16,32},{32,48},{1,17},{17,33},{33,49},{2,18},{18,34},{34,5... | collective-permute-start | bytes 786440 | tf_op jit(solution)/shard_map/ppermute | solution.py:32
  49.6 19.1 %copy-start.6 = (bf16[2,2,1,16,2048]{4,3,2,1,0:T(8,128)(2,1)}, bf16[2,2,1,16,2048]{4,3,2,1,0:T(8,128)(2,1)S(1)}, u32[]{:S(2)}) copy-start(bf16[2,2,1,16,2048]{4,3,2,1,0:T(8,128)(2,1)S(1)} %collective-permute-done.5.rest_6_) | copy-start | bytes 786436
  49.6 19.0 %copy-start.7 = (bf16[2,2,1,16,2048]{4,3,2,1,0:T(8,128)(2,1)}, bf16[2,2,1,16,2048]{4,3,2,1,0:T(8,128)(2,1)S(1)}, u32[]{:S(2)}) copy-start(bf16[2,2,1,16,2048]{4,3,2,1,0:T(8,128)(2,1)S(1)} %collective-permute-done.4.rest_5_) | copy-start | bytes 786436
  49.7 19.0 %copy-start.8 = (bf16[2,1,4,16,2048]{4,3,2,1,0:T(8,128)(2,1)}, bf16[2,1,4,16,2048]{4,3,2,1,0:T(8,128)(2,1)S(1)}, u32[]{:S(2)}) copy-start(bf16[2,1,4,16,2048]{4,3,2,1,0:T(8,128)(2,1)S(1)} %collective-permute-done.3.rest_3_) | copy-start | bytes 1572868
  49.7 19.0 %copy-start.9 = (bf16[2,1,4,16,2048]{4,3,2,1,0:T(8,128)(2,1)}, bf16[2,1,4,16,2048]{4,3,2,1,0:T(8,128)(2,1)S(1)}, u32[]{:S(2)}) copy-start(bf16[2,1,4,16,2048]{4,3,2,1,0:T(8,128)(2,1)S(1)} %collective-permute-done.2.rest_1_) | copy-start | bytes 1572868
  50.6 49.6 %collective-permute-start.11 = (bf16[2,128,1024]{2,1,0:T(8,128)(2,1)}, bf16[2,128,1024]{2,1,0:T(8,128)(2,1)}, u32[]{:S(2)}, u32[]{:S(2)}) collective-permute-start(bf16[2,128,1024]{2,1,0:T(8,128)(2,1)} %pad_maximum_fusion), channel_id=1, source_target_pairs={{0,4},{1,5},{2,6},{3,7},{4,8},{5,9},{6,10},{7,11},{8,12},{9,13},{1... | collective-permute-start | bytes 1572872 | tf_op jit(solution)/shard_map/ppermute | solution.py:394
  54.8 42.3 %collective-permute-start.10 = (bf16[2,128,1024]{2,1,0:T(8,128)(2,1)}, bf16[2,128,1024]{2,1,0:T(8,128)(2,1)S(1)}, u32[]{:S(2)}, u32[]{:S(2)}) collective-permute-start(bf16[2,128,1024]{2,1,0:T(8,128)(2,1)} %pad_maximum_fusion), channel_id=1, source_target_pairs={{0,14},{1,15},{2,0},{3,1},{4,2},{5,3},{6,4},{7,5},{8,6},{9,7},{10,... | collective-permute-start | bytes 1572872 | tf_op jit(solution)/shard_map/ppermute | solution.py:394
  58.1 37.2 %collective-permute-start.9 = (bf16[2,128,1024]{2,1,0:T(8,128)(2,1)}, bf16[2,128,1024]{2,1,0:T(8,128)(2,1)}, u32[]{:S(2)}, u32[]{:S(2)}) collective-permute-start(bf16[2,128,1024]{2,1,0:T(8,128)(2,1)} %pad_maximum_fusion), channel_id=1, source_target_pairs={{0,2},{1,3},{2,4},{3,5},{4,6},{5,7},{6,8},{7,9},{8,10},{9,11},{10,... | collective-permute-start | bytes 1572872 | tf_op jit(solution)/shard_map/ppermute | solution.py:394
  60.2 8.5 %collective-permute-start.6 = (bf16[2,1,2,16,2048]{4,3,2,1,0:T(8,128)(2,1)S(1)}, bf16[2,1,2,16,2048]{4,3,2,1,0:T(8,128)(2,1)S(1)}, u32[]{:S(2)}, u32[]{:S(2)}) collective-permute-start(bf16[2,1,2,16,2048]{4,3,2,1,0:T(8,128)(2,1)S(1)} %pad_maximum_fusion.1), channel_id=1, source_target_pairs={{0,64},{64,128},{128,192},{192,256},{256,320},{320,384},{384,448},... | collective-permute-start | bytes 786440 | tf_op jit(solution)/shard_map/ppermute | solution.py:32
  65.3 8.1 %collective-permute-start.7 = (bf16[2,1,2,16,2048]{4,3,2,1,0:T(8,128)(2,1)S(1)}, bf16[2,1,2,16,2048]{4,3,2,1,0:T(8,128)(2,1)S(1)}, u32[]{:S(2)}, u32[]{:S(2)}) collective-permute-start(bf16[2,1,2,16,2048]{4,3,2,1,0:T(8,128)(2,1)S(1)} %pad_maximum_fusion.2), channel_id=1, source_target_pairs={{64,0},{128,64},{192,128},{256,192},{320,256},{384,320},{448,384},... | collective-permute-start | bytes 786440 | tf_op jit(solution)/shard_map/ppermute | solution.py:32
  68.7 4.7 %copy-start.10 = (bf16[2,1,2,16,2048]{4,3,2,1,0:T(8,128)(2,1)}, bf16[2,1,2,16,2048]{4,3,2,1,0:T(8,128)(2,1)S(1)}, u32[]{:S(2)}) copy-start(bf16[2,1,2,16,2048]{4,3,2,1,0:T(8,128)(2,1)S(1)} %collective-permute-done.6.rest_2_) | copy-start | bytes 786436
  73.4 0.7 copy-start.11
  79.7 24.4 %copy-start.13 = (f32[1,2,4,16,2]{3,4,2,1,0:T(2,128)S(1)}, f32[1,2,4,16,2]{3,4,2,1,0:T(2,128)}, u32[]{:S(2)}) copy-start(f32[1,2,4,16,2]{3,4,2,1,0:T(2,128)} %param.15) | copy-start | bytes 3076
  97.9 7.0 %collective-permute-start.8 = (bf16[8,128,1024]{2,1,0:T(8,128)(2,1)}, bf16[8,128,1024]{2,1,0:T(8,128)(2,1)S(1)}, u32[]{:S(2)}, u32[]{:S(2)}) collective-permute-start(bf16[8,128,1024]{2,1,0:T(8,128)(2,1)} %bitcast.20), channel_id=1, source_target_pairs={{0,64},{64,0},{128,192},{192,128},{256,320},{320,256},{384,448},{4... | collective-permute-start | bytes 6291464 | tf_op jit(solution)/shard_map/ppermute | solution.py:398
  102.1 8.8 %collective-permute-start.12 = (bf16[8,128,1024]{2,1,0:T(8,128)(2,1)}, bf16[8,128,1024]{2,1,0:T(8,128)(2,1)}, u32[]{:S(2)}, u32[]{:S(2)}) collective-permute-start(bf16[8,128,1024]{2,1,0:T(8,128)(2,1)} %constant_dynamic-update-slice_fusion.far_hbm), channel_id=1, source_target_pairs={{0,64},{64,0},{128,192},{192,128},{256,320},{320,256},{384,448},{4... | collective-permute-start | bytes 6291464 | tf_op jit(solution)/shard_map/ppermute | solution.py:398
  104.9 1.3 copy-start.5
  127.9 26.0 %copy-start.12 = (f32[1,2,4,16,2]{4,3,2,1,0:T(8,128)S(1)}, f32[1,2,4,16,2]{4,3,2,1,0:T(8,128)}, u32[]{:S(2)}) copy-start(f32[1,2,4,16,2]{4,3,2,1,0:T(8,128)} %get-tuple-element.43) | copy-start | bytes 3076
  127.9 26.7 %copy-start.1 = (f32[2,2,4,16,2048]{4,3,2,1,0:T(8,128)S(1)}, f32[2,2,4,16,2048]{4,3,2,1,0:T(8,128)}, u32[]{:S(2)}) copy-start(f32[2,2,4,16,2048]{4,3,2,1,0:T(8,128)} %get-tuple-element.36.own_ref) | copy-start | bytes 6291460
  127.9 12.7 %collective-permute-start.13 = (bf16[2,1,6,16,2048]{4,3,2,1,0:T(8,128)(2,1)}, bf16[2,1,6,16,2048]{4,3,2,1,0:T(8,128)(2,1)S(1)}, u32[]{:S(2)}, u32[]{:S(2)}) collective-permute-start(bf16[2,1,6,16,2048]{4,3,2,1,0:T(8,128)(2,1)} %get-tuple-element.37), channel_id=1, source_target_pairs={{0,64},{64,128},{128,192},{192,256},{256,320},{320,384},{384,448},... | collective-permute-start | bytes 2359304 | tf_op jit(solution)/shard_map/ppermute | solution.py:32
  131.5 13.5 %collective-permute-start.14 = (bf16[2,1,6,16,2048]{4,3,2,1,0:T(8,128)(2,1)}, bf16[2,1,6,16,2048]{4,3,2,1,0:T(8,128)(2,1)S(1)}, u32[]{:S(2)}, u32[]{:S(2)}) collective-permute-start(bf16[2,1,6,16,2048]{4,3,2,1,0:T(8,128)(2,1)} %get-tuple-element.38), channel_id=1, source_target_pairs={{64,0},{128,64},{192,128},{256,192},{320,256},{384,320},{448,384},... | collective-permute-start | bytes 2359304 | tf_op jit(solution)/shard_map/ppermute | solution.py:32
  146.2 0.9 copy-start.2
  147.8 9.8 %collective-permute-start.15 = (bf16[2,2,1,16,2048]{4,3,2,1,0:T(8,128)(2,1)}, bf16[2,2,1,16,2048]{4,3,2,1,0:T(8,128)(2,1)}, u32[]{:S(2)}, u32[]{:S(2)}) collective-permute-start(bf16[2,2,1,16,2048]{4,3,2,1,0:T(8,128)(2,1)} %pad_maximum_fusion.3), channel_id=1, source_target_pairs={{0,16},{16,32},{32,48},{1,17},{17,33},{33,49},{2,18},{18,34},{34,5... | collective-permute-start | bytes 786440 | tf_op jit(solution)/shard_map/ppermute | solution.py:32
  152.6 7.4 %collective-permute-start.16 = (bf16[2,2,1,16,2048]{4,3,2,1,0:T(8,128)(2,1)}, bf16[2,2,1,16,2048]{4,3,2,1,0:T(8,128)(2,1)}, u32[]{:S(2)}, u32[]{:S(2)}) collective-permute-start(bf16[2,2,1,16,2048]{4,3,2,1,0:T(8,128)(2,1)} %pad_maximum_fusion.4), channel_id=1, source_target_pairs={{16,0},{32,16},{48,32},{17,1},{33,17},{49,33},{18,2},{34,18},{50,3... | collective-permute-start | bytes 786440 | tf_op jit(solution)/shard_map/ppermute | solution.py:32
  154.7 1.1 copy-start.3
Sparse Core Ops, SparseCore 0:
  10.1 56.6 all-gather.2

commit v3 on v1

--- a/solution.py
+++ b/solution.py
@@ -121,59 +121,61 @@
     )(adjacency, position, queries, *pieces)
 
 
-def head_lanes(index):
-    return pl.ds(pl.multiple_of(index * HS, HS), HS)
-
-
-def far_step(k):
-    return (0, 1, 7, 2)[k // 2] + 4 * (k % 2)
-
-
-def project_kernel(
-    bound_ref, pos_ref, att_ref, near_hbm, near_swap_hbm, far_hbm, far_swap_hbm, gain_ref, read_ref, cot_ref,
-    pred_ref, ga_ref, near_ref, far_ref, own_att_ref, far_att_ref, proj_ref, gp_ref, sems,
-):
-    copies = [
-        pltpu.make_async_copy(near_hbm, near_ref.at[0], sems.at[0]),
-        pltpu.make_async_copy(near_swap_hbm, near_ref.at[1], sems.at[1]),
-        pltpu.make_async_copy(far_hbm, far_ref.at[0], sems.at[2]),
-        pltpu.make_async_copy(far_swap_hbm, far_ref.at[1], sems.at[3]),
-    ]
+def side_cols(pos_ref, side, cols):
+    core = pos_ref[4]
+    return pl.ds(pl.multiple_of((core if side == 0 else 1 - core) * cols, cols), cols)
+
+
+def project_own_kernel(att_ref, w_hbm, part_ref, w_ref, sems):
+    chunks = w_ref.shape[0]
+    rows = w_ref.shape[1]
+    copies = [pltpu.make_async_copy(w_hbm.at[pl.ds(k * rows, rows)], w_ref.at[k], sems.at[k]) for k in range(chunks)]
     for copy in copies:
         copy.start()
-    core = pos_ref[4]
-    chip = pos_ref[5]
-    ring = pos_ref[6]
-    half = pos_ref[7]
-    n_ring, _, cols = near_ref.shape[1:]
-    n_chip = far_ref.shape[1]
-    part = cols // n_chip
-
-    def near_head(k):
-        return head_lanes(k * 2 + half)
-
-    def far_head(k):
-        return head_lanes(lax.rem(ring + 2 * n_ring - far_step(k), n_ring) * 2 + 1 - half)
-
-    def near_cols(side):
-        return pl.ds(pl.multiple_of((core if side == 0 else 1 - core) * cols, cols), cols)
-
-    def far_cols(side, j):
-        start = (core if side == 0 else 1 - core) * cols + lax.rem(chip + n_chip - j, n_chip) * part
-        return pl.ds(pl.multiple_of(start, part), part)
-
-    for k in range(n_ring):
-        own_att_ref[:, k * HS : (k + 1) * HS] = att_ref[:, near_head(k)]
-        far_att_ref[:, k * HS : (k + 1) * HS] = att_ref[:, far_head(k)]
-    rows = n_ring * HS
-    for side in range(2):
-        copies[side].wait()
-        proj_ref[:, near_cols(side)] = dot(own_att_ref[...], near_ref[side].reshape(rows, cols), ((1,), (0,)))
-    for side in range(2):
-        copies[2 + side].wait()
-        for j in range(n_chip):
-            lanes = far_cols(side, j)
-            proj_ref[:, lanes] += dot(far_att_ref[...], far_ref[side, j].reshape(rows, part), ((1,), (0,)))
+    total = None
+    for k in range(chunks):
+        copies[k].wait()
+        term = dot(att_ref[:, k * rows : (k + 1) * rows], w_ref[k], ((1,), (0,)))
+        total = term if total is None else total + term
+    part_ref[...] = total
+
+
+def project_own(att, own):
+    vmem = pl.BlockSpec(memory_space=pltpu.VMEM)
+    tokens = att.shape[0]
+    inner, cols = own.shape
+    chunks = 2
+    return pl.pallas_call(
+        project_own_kernel,
+        in_specs=[vmem, pl.BlockSpec(memory_space=pl.ANY)],
+        out_specs=vmem,
+        out_shape=jax.ShapeDtypeStruct((tokens, cols), jnp.float32),
+        scratch_shapes=[
+            pltpu.VMEM((chunks, inner // chunks, cols), jnp.bfloat16),
+            pltpu.SemaphoreType.DMA((chunks,)),
+        ],
+        compiler_params=pltpu.CompilerParams(vmem_limit_bytes=VMEM_LIMIT),
+        name="project_own",
+    )(att, own)
+
+
+def project_kernel(
+    bound_ref, pos_ref, att_ref, part_ref, own_hbm, swap_hbm, gain_ref, read_ref, cot_ref,
+    pred_ref, ga_ref, swap_ref, own_ref, proj_ref, gp_ref, sems,
+):
+    chunks, rows, cols = swap_ref.shape
+    copies = [pltpu.make_async_copy(swap_hbm.at[pl.ds(k * rows, rows)], swap_ref.at[k], sems.at[k]) for k in range(chunks)]
+    own_copy = pltpu.make_async_copy(own_hbm, own_ref, sems.at[chunks])
+    for copy in copies:
+        copy.start()
+    own_copy.start()
+    total = None
+    for k in range(chunks):
+        copies[k].wait()
+        term = dot(att_ref[:, k * rows : (k + 1) * rows], swap_ref[k], ((1,), (0,)))
+        total = term if total is None else total + term
+    proj_ref[:, side_cols(pos_ref, 0, cols)] = part_ref[...]
+    proj_ref[:, side_cols(pos_ref, 1, cols)] = total
     inner = proj_ref.shape[1]
     for pair in range(TOK // (2 * BS)):
         rows_of = slice(pair * 2 * BS, (pair + 1) * 2 * BS)
@@ -195,47 +197,39 @@
         gained = (cot[:, 0:1] * read_ref[0:1, :] + cot[:, 1:2] * read_ref[1:2, :]) * gain
         inner_mean = jnp.sum(gained * proj, axis=1, keepdims=True) * (1.0 / inner)
         gp_ref[rows_of, :] = (inv_rms * gained - proj * (inv_rms * inv_rms * inv_rms * inner_mean)).astype(jnp.bfloat16)
-    near = None
-    far = None
-    for side in range(2):
-        term = dot(gp_ref[:, near_cols(side)], near_ref[side].reshape(rows, cols), ((1,), (1,)))
-        near = term if near is None else near + term
-        for j in range(n_chip):
-            term = dot(gp_ref[:, far_cols(side, j)], far_ref[side, j].reshape(rows, part), ((1,), (1,)))
-            far = term if far is None else far + term
-    near = near.astype(jnp.bfloat16)
-    far = far.astype(jnp.bfloat16)
-    for k in range(n_ring):
-        ga_ref[:, near_head(k)] = near[:, k * HS : (k + 1) * HS]
-        ga_ref[:, far_head(k)] = far[:, k * HS : (k + 1) * HS]
-
-
-def project(boundary, position, att, weights, gain, read_rows, cotangent):
+    gp_own = gp_ref[:, side_cols(pos_ref, 0, cols)]
+    gp_swap = gp_ref[:, side_cols(pos_ref, 1, cols)]
+    own_copy.wait()
+    for k in range(chunks):
+        lanes = slice(k * rows, (k + 1) * rows)
+        total = dot(gp_swap, swap_ref[k], ((1,), (1,))) + dot(gp_own, own_ref[lanes, :], ((1,), (1,)))
+        ga_ref[:, lanes] = total.astype(jnp.bfloat16)
+
+
+def project(boundary, position, att, part, own, swapped, gain, read_rows, cotangent):
     vmem = pl.BlockSpec(memory_space=pltpu.VMEM)
     smem = pl.BlockSpec(memory_space=pltpu.SMEM)
     hbm = pl.BlockSpec(memory_space=pl.ANY)
-    near, _, far, _ = weights
-    tokens, inner = att.shape
+    inner, cols = own.shape
+    chunks = 4
     return pl.pallas_call(
         project_kernel,
-        in_specs=[smem, smem, vmem, hbm, hbm, hbm, hbm, vmem, vmem, vmem],
+        in_specs=[smem, smem, vmem, vmem, hbm, hbm, vmem, vmem, vmem],
         out_specs=[vmem, vmem],
         out_shape=[
             jax.ShapeDtypeStruct(cotangent.shape, jnp.float32),
             jax.ShapeDtypeStruct(att.shape, jnp.bfloat16),
         ],
         scratch_shapes=[
-            pltpu.VMEM((2,) + near.shape, jnp.bfloat16),
-            pltpu.VMEM((2,) + far.shape, jnp.bfloat16),
-            pltpu.VMEM((tokens, inner // 2), jnp.bfloat16),
-            pltpu.VMEM((tokens, inner // 2), jnp.bfloat16),
+            pltpu.VMEM((chunks, inner // chunks, cols), jnp.bfloat16),
+            pltpu.VMEM(own.shape, jnp.bfloat16),
             pltpu.VMEM(att.shape, jnp.float32),
             pltpu.VMEM(att.shape, jnp.bfloat16),
-            pltpu.SemaphoreType.DMA((4,)),
+            pltpu.SemaphoreType.DMA((chunks + 1,)),
         ],
         compiler_params=pltpu.CompilerParams(vmem_limit_bytes=VMEM_LIMIT),
         name="project",
-    )(boundary, position, att, *weights, gain, read_rows, cotangent)
+    )(boundary, position, att, part, own, swapped, gain, read_rows, cotangent)
 
 
 def backward_kernel(q_ref, ga_ref, prob_ref, *rest):
@@ -288,6 +282,31 @@
     )(queries, grad_att, prob, *pieces)
 
 
+def sides_kernel(from_low_ref, from_high_ref, low_ref, high_ref, left_ref, right_ref):
+    f32 = jnp.float32
+    for which in range(2):
+        for y, rim, out in ((0, low_ref, left_ref), (1, high_ref, right_ref)):
+            first = rim[which, 0, 0].astype(f32) + from_low_ref[which, 0, y].astype(f32)
+            last = rim[which, BX - 1, 0].astype(f32) + from_high_ref[which, 0, y].astype(f32)
+            out[which, 0, 0] = first.astype(out.dtype)
+            out[which, BX - 1, 0] = last.astype(out.dtype)
+
+
+def sides(from_low, from_high, low, high):
+    corner = pl.BlockSpec(from_low.shape[:2] + (2,) + from_low.shape[3:], lambda i: (0, 0, BY // 2, 0, 0))
+    rim = pl.BlockSpec(low.shape, lambda i: (0, 0, 0, 0, 0))
+    shape = jax.ShapeDtypeStruct(low.shape, low.dtype)
+    return pl.pallas_call(
+        sides_kernel,
+        grid=(1,),
+        in_specs=[corner, corner, rim, rim],
+        out_specs=[rim, rim],
+        out_shape=[shape, shape],
+        compiler_params=pltpu.CompilerParams(vmem_limit_bytes=SMALL_LIMIT),
+        name="sides",
+    )(from_low, from_high, low, high)
+
+
 def add_rows_kernel(own_ref, low_ref, high_ref, out_ref, edge_ref):
     f32 = jnp.float32
     for which in range(2):
@@ -356,11 +375,6 @@
     )(edge, low, high, partial)
 
 
-def around(value, axis, step):
-    count = lax.axis_size(axis)
-    return lax.ppermute(value, axis, [(i, (i + step) % count) for i in range(count)])
-
-
 def swap_cores(value):
     return lax.ppermute(value, "sx", [(i, i ^ 1) for i in range(lax.axis_size("sx"))])
 
@@ -370,32 +384,21 @@
     inner = out_weight.shape[1]
     n_sx, n_sy, n_wa = (lax.axis_size(axis) for axis in ("sx", "sy", "wa"))
     row, column, case = (lax.axis_index(axis) for axis in ("sx", "sy", "wa"))
-    core, chip, ring, half = row % 2, row // 2, case // 2, case % 2
+    core = row % 2
     kv = keys_values[:, 0]
     cols = inner // 2
-    part = inner // n_sx
-    near_slab = lax.dynamic_slice_in_dim(out_weight, core * cols, cols, axis=1)
-    far_slab = lax.dynamic_slice_in_dim(out_weight, core * cols + chip * part, part, axis=1)
-    def mirrored(value, step):
-        pairs = [
-            (l * n_wa + w, (n_sy - 1 - l) * n_wa + (((w ^ 1) + 2 * step) % n_wa)) for l in range(n_sy) for w in range(n_wa)
-        ]
-        return lax.ppermute(value, ("sy", "wa"), pairs)
-
-    far = (mirrored(far_slab, 0), mirrored(far_slab, n_wa // 4))
-    groups = [list(range(h, n_wa, 2)) for h in range(2)]
-    near = lax.all_gather(near_slab, "wa", axis=0, axis_index_groups=groups)
+    slab = lax.dynamic_slice_in_dim(out_weight, core * cols, cols, axis=1)
+    pairs = [[w, w + 1] for w in range(0, n_wa, 2)]
+    rings = [list(range(h, n_wa, 2)) for h in range(2)]
+    both = lax.all_gather(slab, "wa", axis=0, axis_index_groups=pairs)
+    own_cols = lax.all_gather(both, "wa", axis=0, axis_index_groups=rings).reshape(-1, cols)
     ylow = shift(kv[:, :, size_y - 1 :], "sy", 1)
     yhigh = shift(kv[:, :, :1], "sy", -1)
-    far, kv_after = lax.optimization_barrier((far, kv))
-    far = jnp.stack(far)
-    far_y = jnp.concatenate([far] + [around(far, "wa", 2 * k) for k in (1, -1, 2)])
-    xlow = shift(kv_after[:, size_x - 1 :], "sx", 1)
-    xhigh = shift(kv_after[:, :1], "sx", -1)
+    xlow = shift(kv[:, size_x - 1 :], "sx", 1)
+    xhigh = shift(kv[:, :1], "sx", -1)
     clow = shift(jnp.concatenate([ylow[:, size_x - 1 :], yhigh[:, size_x - 1 :]], axis=2), "sx", 1)
     chigh = shift(jnp.concatenate([ylow[:, :1], yhigh[:, :1]], axis=2), "sx", -1)
     pieces = (kv, xlow, clow, xhigh, chigh, ylow, yhigh)
-    far_x = jnp.stack([far_y] + [around(far_y, "sx", 2 * k) for k in (1, 2, -1)])
     position = jnp.stack(
         [
             row * size_x,
@@ -403,27 +406,21 @@
             jnp.int32(size_x * n_sx),
             jnp.int32(size_y * n_sy),
             core,
-            chip,
-            ring,
-            half,
         ]
     ).astype(jnp.int32)
     att, prob = forward(adjacency, position, queries, pieces)
-    near, att = lax.optimization_barrier((near, att))
-    weights = (near, swap_cores(near), far_x, swap_cores(far_x))
-    prediction, grad_att = project(boundary, position, att, weights, gain[None], read_weight.T, cotangent)
+    own_cols, att = lax.optimization_barrier((own_cols, att))
+    swapped = swap_cores(own_cols)
+    part = project_own(att, own_cols)
+    prediction, grad_att = project(
+        boundary, position, att, part, own_cols, swapped, gain[None], read_weight.T, cotangent
+    )
     grad_queries, own, gxlow, gxhigh, gylow, gyhigh = backward(queries, grad_att, prob, pieces)
     from_low = shift(gxhigh, "sx", 1)
     from_high = shift(gxlow, "sx", -1)
-    f32 = jnp.float32
-
-    def side(rim, y):
-        first = rim[:, :1].astype(f32) + from_low[:, :, size_y + y : size_y + y + 1].astype(f32)
-        last = rim[:, 1:].astype(f32) + from_high[:, :, size_y + y : size_y + y + 1].astype(f32)
-        return jnp.concatenate([first, last], axis=1).astype(jnp.bfloat16)
-
-    left = shift(side(gyhigh, 1), "sy", 1)
-    right = shift(side(gylow, 0), "sy", -1)
+    to_left, to_right = sides(from_low, from_high, gylow, gyhigh)
+    left = shift(to_right, "sy", 1)
+    right = shift(to_left, "sy", -1)
     partial, edge = add_rows(own, from_low, from_high)
     grad_kv = add_columns(edge, left, right, partial)
     return (prediction, grad_queries, grad_kv[:, None])

time: 163 us -> 155 us (0.951)
  starting transfers between devices: 69.2 us -> 36 us
  blocking collectives: 0 us -> 15.6 us
  waiting for transfers between devices: 35.6 us -> 45.1 us
  other arithmetic: 4.38 us -> 1.34 us
  Pallas kernels: 27 us -> 30 us
    ppermute x8 -> x0, starting transfers between devices: 36.2 us -> none  [the longest x2 18.7 us: mirrored(): return lax.ppermute(value, ('sy', 'wa'), pairs)]
    all_gather x1, waiting for transfers between devices: 0.02 us -> 24.5 us  [body(): lax.all_gather(both, 'wa', axis=0, axis_index_groups=rings)]
    ppermute x8 -> x0, waiting for transfers between devices: 17.3 us -> none  [the longest x6 17.3 us: around(): lax.ppermute(value, axis, [(i, (i + step) % count) for i in range(count)])]
    all_gather x0 -> x1, blocking collectives: none -> 15.6 us  [body(): both = lax.all_gather(slab, 'wa', axis=0, axis_index_groups=pairs)]
    ppermute x10, waiting for transfers between devices: 14 us -> 19.1 us  [shift(): return lax.ppermute(value, axis, pairs)]
    ppermute x10, starting transfers between devices: 28.6 us -> 33.4 us  [shift(): return lax.ppermute(value, axis, pairs)]
    pallas_call x1 -> x3, Pallas kernels: 9.37 us -> 13.3 us  [the longest x1 8.43 us: project(): pl.pallas_call(project_kernel, in_specs=[smem, smem, vmem, vmem, hbm, hbm...]
    ppermute x2 -> x1, waiting for transfers between devices: 4.32 us -> 1.54 us  [swap_cores(): lax.ppermute(value, 'sx', [(i, i ^ 1) for i in range(lax.axis_size('sx'))])]
  transfers between devices with their start and end apart: 21 -> 12, of which waited for: 8 -> 7; matrix products, arithmetic and copies ran while one was open for 5% -> 4% of each run, Pallas kernels for 5% -> 8%
where the time goes in v3:
time: 155 us; the launch traced here: 153 us
  waiting for transfers between devices  45.1 us (29%)
  starting transfers between devices  36 us (23%)
  Pallas kernels  30 us (19%)
  blocking collectives  15.6 us (10%)
  between operations  14.3 us (9%)
  local copies, waits for them, and re-layouts  10.8 us (7%)
    ppermute x10, starting transfers between devices, shift(): return lax.ppermute(value, axis, pairs)  33.4 us
    all_gather x1, waiting for transfers between devices, body(): lax.all_gather(both, 'wa', axis=0, axis_index_groups=rings)  24.5 us
    ppermute x10, waiting for transfers between devices, shift(): return lax.ppermute(value, axis, pairs)  19.1 us
    all_gather x1, blocking collectives, body(): both = lax.all_gather(slab, 'wa', axis=0, axis_index_groups=pairs)  15.6 us
    pallas_call x1, Pallas kernels, project(): pl.pallas_call(project_kernel, in_specs=[smem, smem, vmem, vmem, hbm, hbm...  8.43 us
    pallas_call x1, Pallas kernels, backward(): pl.pallas_call(backward_kernel, grid=(inner // width,), in_specs=[wide(qu...  8.31 us
    unnamed x26, local copies, waits for them, and re-layouts  7.61 us
    pallas_call x1, Pallas kernels, forward(): pl.pallas_call(forward_kernel, grid=(inner // width,), in_specs=[smem, sm...  5.61 us
  transfers between devices with their start and end apart: 12, of which 7 were waited for; matrix products, arithmetic and copies ran while one was open for 4% of the time, Pallas kernels for 8%

profile of v3, /device:TPU:1, one launch (start us, length us, event | category | flops | bytes accessed | tf_op | source)
XLA Modules:
  0.0 153.2 jit_solution(15073691258202453431)
XLA Ops:
  7.2 0.0 copy-start
  7.2 0.0 all-gather.4.cloned.1.call-start
  7.2 1.0 copy-done
  8.2 15.6 %all-gather = bf16[256,1024]{1,0:T(8,128)(2,1)} all-gather(bf16[128,1024]{1,0:T(8,128)(2,1)S(1)} %constant_dynamic-slice_fusion), channel_id=2, replica_groups={{0,1},{2,3},{4,5},{6,7},{8,9},{10,11},{12,13},{14,15},{16,17},{18,19},{..., dimensions={0}, use_global_device_ids=true | all-gather | bytes 786432 | tf_op jit(solution)/shard_map/all_gather | solution.py:393
  23.9 0.0 all-gather.4.cloned.1.call-update
  23.9 1.1 fusion.1
  25.0 0.0 copy-start.11
  25.0 9.5 %collective-permute-start.1 = (bf16[2,2,1,16,2048]{4,3,2,1,0:T(8,128)(2,1)S(1)}, bf16[2,2,1,16,2048]{4,3,2,1,0:T(8,128)(2,1)S(1)}, u32[]{:S(2)}, u32[]{:S(2)}) collective-permute-start(bf16[2,2,1,16,2048]{4,3,2,1,0:T(8,128)(2,1)S(1)} %get-tuple-element.43), channel_id=1, source_target_pairs={{0,16},{16,32},{32,48},{1,17},{17,33},{33,49},{2,18},{18,34},{34,5... | collective-permute-start | bytes 786440 | tf_op jit(solution)/shard_map/ppermute | solution.py:32
  34.4 1.3 collective-permute-start.2
  35.7 2.1 %fusion = (bf16[2,1,4,16,2048]{4,3,2,1,0:T(8,128)(2,1)}, bf16[2,1,4,16,2048]{4,3,2,1,0:T(8,128)(2,1)S(1)}) fusion(bf16[2,2,4,16,2048]{4,3,2,1,0:T(8,128)(2,1)} %bitcast.15), kind=kLoop, calls=%fused_computation.4 | loop fusion | bytes 2097152 | tf_op jit(solution)/shard_map/slice | solution.py:398
  37.8 3.6 %collective-permute-start.4 = (bf16[2,1,4,16,2048]{4,3,2,1,0:T(8,128)(2,1)}, bf16[2,1,4,16,2048]{4,3,2,1,0:T(8,128)(2,1)S(1)}, u32[]{:S(2)}, u32[]{:S(2)}) collective-permute-start(bf16[2,1,4,16,2048]{4,3,2,1,0:T(8,128)(2,1)} %get-tuple-element.41), channel_id=1, source_target_pairs={{64,0},{128,64},{192,128},{256,192},{320,256},{384,320},{448,384},... | collective-permute-start | bytes 1572872 | tf_op jit(solution)/shard_map/ppermute | solution.py:32
  41.4 3.0 %collective-permute-start = (bf16[2,1,4,16,2048]{4,3,2,1,0:T(8,128)(2,1)S(1)}, bf16[2,1,4,16,2048]{4,3,2,1,0:T(8,128)(2,1)S(1)}, u32[]{:S(2)}, u32[]{:S(2)}) collective-permute-start(bf16[2,1,4,16,2048]{4,3,2,1,0:T(8,128)(2,1)S(1)} %get-tuple-element.42), channel_id=1, source_target_pairs={{0,64},{64,128},{128,192},{192,256},{256,320},{320,384},{384,448},... | collective-permute-start | bytes 1572872 | tf_op jit(solution)/shard_map/ppermute | solution.py:32
  44.4 0.0 collective-permute-done.1.rest_5_
  44.4 0.0 copy-start.4
  44.5 0.0 collective-permute-done.2.rest_6_
  44.5 0.0 copy-start.5
  44.5 4.0 %collective-permute-start.3 = (bf16[2,1,2,16,2048]{4,3,2,1,0:T(8,128)(2,1)S(1)}, bf16[2,1,2,16,2048]{4,3,2,1,0:T(8,128)(2,1)S(1)}, u32[]{:S(2)}, u32[]{:S(2)}) collective-permute-start(bf16[2,1,2,16,2048]{4,3,2,1,0:T(8,128)(2,1)S(1)} %pad_maximum_fusion), channel_id=1, source_target_pairs={{0,64},{64,128},{128,192},{192,256},{256,320},{320,384},{384,448},... | collective-permute-start | bytes 786440 | tf_op jit(solution)/shard_map/ppermute | solution.py:32
  48.6 0.7 pad_maximum_fusion.1
  49.3 1.9 %collective-permute-start.5 = (bf16[2,1,2,16,2048]{4,3,2,1,0:T(8,128)(2,1)}, bf16[2,1,2,16,2048]{4,3,2,1,0:T(8,128)(2,1)S(1)}, u32[]{:S(2)}, u32[]{:S(2)}) collective-permute-start(bf16[2,1,2,16,2048]{4,3,2,1,0:T(8,128)(2,1)} %pad_maximum_fusion.1), channel_id=1, source_target_pairs={{64,0},{128,64},{192,128},{256,192},{320,256},{384,320},{448,384},... | collective-permute-start | bytes 786440 | tf_op jit(solution)/shard_map/ppermute | solution.py:32
  51.2 0.6 pad_add_fusion.pos_ref
  51.8 1.5 collective-permute-done.3.rest_2_
  53.3 0.0 copy-start.8
  53.3 4.3 %collective-permute-done.5.rest_4_ = bf16[2,1,2,16,2048]{4,3,2,1,0:T(8,128)(2,1)S(1)} collective-permute-done((bf16[2,1,2,16,2048]{4,3,2,1,0:T(8,128)(2,1)}, bf16[2,1,2,16,2048]{4,3,2,1,0:T(8,128)(2,1)S(1)}, u32[]{:S(2)}, u32[]{:S(2)}) %collective-permute-start.5) | collective-permute-done | bytes 262176 | tf_op jit(solution)/shard_map/ppermute | solution.py:32
  57.6 0.0 copy-start.9
  57.6 0.0 collective-permute-done.4.rest_3_
  57.6 0.0 copy-start.6
  57.6 0.0 collective-permute-done.rest_1_
  57.6 0.0 copy-done.4
  57.6 0.0 copy-done.5
  57.6 0.0 copy-done.8
  57.6 0.7 copy-done.9
  58.3 0.2 copy-done.6
  58.5 0.0 copy-start.7
  58.5 0.8 copy-done.7
  59.3 5.6 %attend.1 = (bf16[128,2048]{1,0:T(8,128)(2,1)}, f32[16,384,128]{2,1,0:T(8,128)}) custom-call(s32[1,2,4,4]{3,2,1,0:T(4,128)} %adj_ref.1, s32[5]{0:T(128)} %pad_add_fusion.pos_ref, bf16[1,2,4,16,2048]{4,3,2,1,0:T(8,128)(2,1)} %q_ref.3, bf16[2,2,4,16,2048]{4,3,2,1,0:T(8,128)(2,1)} %bitcast.16, bf16[2,1,4,16,2048]{4,3,2,1,0:T(8,128)(2,1)} %copy-done.7, ...), custom_call_target="tpu_custom_call" | custom-call | tf_op jit(solution)/shard_map/attend/pallas_call | solution.py:106
  64.9 24.5 %all-gather.4.cloned.1.call-done = bf16[16,128,1024]{2,1,0:T(8,128)(2,1)} async-done(((bf16[2,128,1024]{2,1,0:T(8,128)(2,1)}), bf16[16,128,1024]{2,1,0:T(8,128)(2,1)}) %all-gather.4.cloned.1.call-update) | async-done | bytes 4194320 | tf_op jit(solution)/shard_map/all_gather | solution.py:394
  89.4 2.6 %collective-permute-start.6 = (bf16[2048,1024]{1,0:T(8,128)(2,1)}, bf16[2048,1024]{1,0:T(8,128)(2,1)}, u32[]{:S(2)}, u32[]{:S(2)}) collective-permute-start(bf16[2048,1024]{1,0:T(8,128)(2,1)} %bitcast.11), channel_id=1, source_target_pairs={{0,64},{64,0},{128,192},{192,128},{256,320},{320,256},{384,448},{4... | collective-permute-start | bytes 12582920 | tf_op jit(solution)/shard_map/ppermute | solution.py:379
  91.9 0.0 copy-done.11
  91.9 0.8 copy.15.cot_ref
  92.7 4.8 %project_own.1.part_ref = f32[128,1024]{1,0:T(8,128)} custom-call(bf16[128,2048]{1,0:T(8,128)(2,1)} %get-tuple-element.20.att_ref, bf16[2048,1024]{1,0:T(8,128)(2,1)} %bitcast.12), custom_call_target="tpu_custom_call" | custom-call | tf_op jit(solution)/shard_map/project_own/pallas_call | solution.py:148
  97.5 1.5 %collective-permute-done.6.swap_hbm = bf16[2048,1024]{1,0:T(8,128)(2,1)} collective-permute-done((bf16[2048,1024]{1,0:T(8,128)(2,1)}, bf16[2048,1024]{1,0:T(8,128)(2,1)}, u32[]{:S(2)}, u32[]{:S(2)}) %collective-permute-start.6) | collective-permute-done | bytes 4194336 | tf_op jit(solution)/shard_map/ppermute | solution.py:379
  99.0 8.4 %project.1 = (f32[1,2,4,16,2]{4,3,2,1,0:T(8,128)}, bf16[128,2048]{1,0:T(8,128)(2,1)}) custom-call(s32[1,2,4]{2,1,0:T(2,128)} %bound_ref.1, s32[5]{0:T(128)} %pad_add_fusion.pos_ref, bf16[128,2048]{1,0:T(8,128)(2,1)} %get-tuple-element.20.att_ref, f32[128,1024]{1,0:T(8,128)} %project_own.1.part_ref, bf16[2048,1024]{1,0:T(8,128)(2,1)} %bitcast.13, ...), custom_call_target="tpu_custom_call" | custom-call | tf_op jit(solution)/shard_map/project/pallas_call | solution.py:215
  107.5 0.0 copy-start.10
  107.5 8.3 %attend_back.1 = (bf16[1,2,4,16,2048]{4,3,2,1,0:T(8,128)(2,1)}, f32[2,2,4,16,2048]{4,3,2,1,0:T(8,128)}, bf16[2,1,6,16,2048]{4,3,2,1,0:T(8,128)(2,1)}, bf16[2,1,6...) custom-call(bf16[1,2,4,16,2048]{4,3,2,1,0:T(8,128)(2,1)} %q_ref.3, ...), custom_call_target="tpu_custom_call" | custom-call | tf_op jit(solution)/shard_map/attend_back/pallas_call | solution.py:272
  115.8 3.4 %collective-permute-start.7 = (bf16[2,1,6,16,2048]{4,3,2,1,0:T(8,128)(2,1)}, bf16[2,1,6,16,2048]{4,3,2,1,0:T(8,128)(2,1)S(1)}, u32[]{:S(2)}, u32[]{:S(2)}) collective-permute-start(bf16[2,1,6,16,2048]{4,3,2,1,0:T(8,128)(2,1)} %get-tuple-element.27), channel_id=1, source_target_pairs={{0,64},{64,128},{128,192},{192,256},{256,320},{320,384},{384,448},... | collective-permute-start | bytes 2359304 | tf_op jit(solution)/shard_map/ppermute | solution.py:32
  119.2 1.9 %collective-permute-start.8 = (bf16[2,1,6,16,2048]{4,3,2,1,0:T(8,128)(2,1)}, bf16[2,1,6,16,2048]{4,3,2,1,0:T(8,128)(2,1)S(1)}, u32[]{:S(2)}, u32[]{:S(2)}) collective-permute-start(bf16[2,1,6,16,2048]{4,3,2,1,0:T(8,128)(2,1)} %get-tuple-element.28), channel_id=1, source_target_pairs={{64,0},{128,64},{192,128},{256,192},{320,256},{384,320},{448,384},... | collective-permute-start | bytes 2359304 | tf_op jit(solution)/shard_map/ppermute | solution.py:32
  121.1 7.3 %collective-permute-done.7.low_ref.from_low_ref = bf16[2,1,6,16,2048]{4,3,2,1,0:T(8,128)(2,1)S(1)} collective-permute-done((bf16[2,1,6,16,2048]{4,3,2,1,0:T(8,128)(2,1)}, bf16[2,1,6,16,2048]{4,3,2,1,0:T(8,128)(2,1)S(1)}, u32[]{:S(2)}, u32[]{:S(2)}) %collective-permute-start.7) | collective-permute-done | bytes 786464 | tf_op jit(solution)/shard_map/ppermute | solution.py:32
  128.4 4.3 %collective-permute-done.8.high_ref.from_high_ref = bf16[2,1,6,16,2048]{4,3,2,1,0:T(8,128)(2,1)S(1)} collective-permute-done((bf16[2,1,6,16,2048]{4,3,2,1,0:T(8,128)(2,1)}, bf16[2,1,6,16,2048]{4,3,2,1,0:T(8,128)(2,1)S(1)}, u32[]{:S(2)}, u32[]{:S(2)}) %collective-permute-start.8) | collective-permute-done | bytes 786464 | tf_op jit(solution)/shard_map/ppermute | solution.py:32
  132.7 0.0 copy-start.2
  132.7 0.9 copy-done.2
  133.6 0.0 copy-start.3
  133.6 0.9 copy-done.3
  134.6 0.1 sides.1
  134.7 3.6 %collective-permute-start.9 = (bf16[2,2,1,16,2048]{4,3,2,1,0:T(8,128)(2,1)S(1)}, bf16[2,2,1,16,2048]{4,3,2,1,0:T(8,128)(2,1)S(1)}, u32[]{:S(2)}, u32[]{:S(2)}) collective-permute-start(bf16[2,2,1,16,2048]{4,3,2,1,0:T(8,128)(2,1)S(1)} %get-tuple-element.32), channel_id=1, source_target_pairs={{0,16},{16,32},{32,48},{1,17},{17,33},{33,49},{2,18},{18,34},{34,5... | collective-permute-start | bytes 786440 | tf_op jit(solution)/shard_map/ppermute | solution.py:32
  138.3 1.3 collective-permute-start.10
  139.6 0.0 copy-done.10
  139.6 0.7 copy.16
  140.3 0.0 copy-start.1
  140.3 1.6 %copy-done.1 = f32[2,2,4,16,2048]{4,3,2,1,0:T(8,128)S(1)} copy-done((f32[2,2,4,16,2048]{4,3,2,1,0:T(8,128)S(1)}, f32[2,2,4,16,2048]{4,3,2,1,0:T(8,128)}, u32[]{:S(2)}) %copy-start.1) | copy-done | bytes 2097176
  141.9 1.8 %add_rows.1 = (bf16[2,2,4,16,2048]{4,3,2,1,0:T(8,128)(2,1)}, f32[2,2,2,16,2048]{4,3,2,1,0:T(8,128)S(1)}) custom-call(f32[2,2,4,16,2048]{4,3,2,1,0:T(8,128)S(1)} %copy-done.1, bf16[2,1,6,16,2048]{4,3,2,1,0:T(8,128)(2,1)S(1)} %collective-permute-done.7.low_ref.from_low_ref, bf16[2,1,6,16,2048]{4,3,2,1,0:T(8,128)(2,1)S(1)} %collective-permute-done.8.high_ref.from_high_ref), custom_call_target="tpu_custom_call" | custom-call | tf_op jit(solution)/shard_map/add_rows/pallas_call | solution.py:334
  143.7 0.0 collective-permute-done.9.low_ref
  143.7 1.7 %collective-permute-done.10.high_ref = bf16[2,2,1,16,2048]{4,3,2,1,0:T(8,128)(2,1)S(1)} collective-permute-done((bf16[2,2,1,16,2048]{4,3,2,1,0:T(8,128)(2,1)S(1)}, bf16[2,2,1,16,2048]{4,3,2,1,0:T(8,128)(2,1)S(1)}, u32[]{:S(2)}, u32[]{:S(2)}) %collective-permute-start.10) | collective-permute-done | bytes 262176 | tf_op jit(solution)/shard_map/ppermute | solution.py:32
  145.4 0.9 add_columns.1
  (5 shorter events, 0.1 us)
Async XLA Ops:
  7.2 1.0 copy-start
  7.2 82.2 %all-gather.4.cloned.1.call-start = ((), (), s32[]{:S(2)}) async-start(), calls=%async_computation | async-start | bytes 4718592 | tf_op jit(solution)/shard_map/all_gather | solution.py:394
  25.0 67.0 %copy-start.11 = (f32[1,2,4,16,2]{3,4,2,1,0:T(2,128)S(1)}, f32[1,2,4,16,2]{3,4,2,1,0:T(2,128)}, u32[]{:S(2)}) copy-start(f32[1,2,4,16,2]{3,4,2,1,0:T(2,128)} %param.15) | copy-start | bytes 3076
  25.0 19.5 %collective-permute-start.1 = (bf16[2,2,1,16,2048]{4,3,2,1,0:T(8,128)(2,1)S(1)}, bf16[2,2,1,16,2048]{4,3,2,1,0:T(8,128)(2,1)S(1)}, u32[]{:S(2)}, u32[]{:S(2)}) collective-permute-start(bf16[2,2,1,16,2048]{4,3,2,1,0:T(8,128)(2,1)S(1)} %get-tuple-element.43), channel_id=1, source_target_pairs={{0,16},{16,32},{32,48},{1,17},{17,33},{33,49},{2,18},{18,34},{34,5... | collective-permute-start | bytes 786440 | tf_op jit(solution)/shard_map/ppermute | solution.py:32
  34.4 10.0 %collective-permute-start.2 = (bf16[2,2,1,16,2048]{4,3,2,1,0:T(8,128)(2,1)S(1)}, bf16[2,2,1,16,2048]{4,3,2,1,0:T(8,128)(2,1)S(1)}, u32[]{:S(2)}, u32[]{:S(2)}) collective-permute-start(bf16[2,2,1,16,2048]{4,3,2,1,0:T(8,128)(2,1)S(1)} %get-tuple-element.44), channel_id=1, source_target_pairs={{16,0},{32,16},{48,32},{17,1},{33,17},{49,33},{18,2},{34,18},{50,3... | collective-permute-start | bytes 786440 | tf_op jit(solution)/shard_map/ppermute | solution.py:32
  37.8 19.8 %collective-permute-start.4 = (bf16[2,1,4,16,2048]{4,3,2,1,0:T(8,128)(2,1)}, bf16[2,1,4,16,2048]{4,3,2,1,0:T(8,128)(2,1)S(1)}, u32[]{:S(2)}, u32[]{:S(2)}) collective-permute-start(bf16[2,1,4,16,2048]{4,3,2,1,0:T(8,128)(2,1)} %get-tuple-element.41), channel_id=1, source_target_pairs={{64,0},{128,64},{192,128},{256,192},{320,256},{384,320},{448,384},... | collective-permute-start | bytes 1572872 | tf_op jit(solution)/shard_map/ppermute | solution.py:32
  41.4 16.2 %collective-permute-start = (bf16[2,1,4,16,2048]{4,3,2,1,0:T(8,128)(2,1)S(1)}, bf16[2,1,4,16,2048]{4,3,2,1,0:T(8,128)(2,1)S(1)}, u32[]{:S(2)}, u32[]{:S(2)}) collective-permute-start(bf16[2,1,4,16,2048]{4,3,2,1,0:T(8,128)(2,1)S(1)} %get-tuple-element.42), channel_id=1, source_target_pairs={{0,64},{64,128},{128,192},{192,256},{256,320},{320,384},{384,448},... | collective-permute-start | bytes 1572872 | tf_op jit(solution)/shard_map/ppermute | solution.py:32
  44.4 13.2 %copy-start.4 = (bf16[2,2,1,16,2048]{4,3,2,1,0:T(8,128)(2,1)}, bf16[2,2,1,16,2048]{4,3,2,1,0:T(8,128)(2,1)S(1)}, u32[]{:S(2)}) copy-start(bf16[2,2,1,16,2048]{4,3,2,1,0:T(8,128)(2,1)S(1)} %collective-permute-done.1.rest_5_) | copy-start | bytes 786436
  44.5 13.1 %copy-start.5 = (bf16[2,2,1,16,2048]{4,3,2,1,0:T(8,128)(2,1)}, bf16[2,2,1,16,2048]{4,3,2,1,0:T(8,128)(2,1)S(1)}, u32[]{:S(2)}) copy-start(bf16[2,2,1,16,2048]{4,3,2,1,0:T(8,128)(2,1)S(1)} %collective-permute-done.2.rest_6_) | copy-start | bytes 786436
  44.5 8.8 %collective-permute-start.3 = (bf16[2,1,2,16,2048]{4,3,2,1,0:T(8,128)(2,1)S(1)}, bf16[2,1,2,16,2048]{4,3,2,1,0:T(8,128)(2,1)S(1)}, u32[]{:S(2)}, u32[]{:S(2)}) collective-permute-start(bf16[2,1,2,16,2048]{4,3,2,1,0:T(8,128)(2,1)S(1)} %pad_maximum_fusion), channel_id=1, source_target_pairs={{0,64},{64,128},{128,192},{192,256},{256,320},{320,384},{384,448},... | collective-permute-start | bytes 786440 | tf_op jit(solution)/shard_map/ppermute | solution.py:32
  49.3 8.3 %collective-permute-start.5 = (bf16[2,1,2,16,2048]{4,3,2,1,0:T(8,128)(2,1)}, bf16[2,1,2,16,2048]{4,3,2,1,0:T(8,128)(2,1)S(1)}, u32[]{:S(2)}, u32[]{:S(2)}) collective-permute-start(bf16[2,1,2,16,2048]{4,3,2,1,0:T(8,128)(2,1)} %pad_maximum_fusion.1), channel_id=1, source_target_pairs={{64,0},{128,64},{192,128},{256,192},{320,256},{384,320},{448,384},... | collective-permute-start | bytes 786440 | tf_op jit(solution)/shard_map/ppermute | solution.py:32
  53.3 4.3 %copy-start.8 = (bf16[2,1,2,16,2048]{4,3,2,1,0:T(8,128)(2,1)}, bf16[2,1,2,16,2048]{4,3,2,1,0:T(8,128)(2,1)S(1)}, u32[]{:S(2)}) copy-start(bf16[2,1,2,16,2048]{4,3,2,1,0:T(8,128)(2,1)S(1)} %collective-permute-done.3.rest_2_) | copy-start | bytes 786436
  57.6 0.7 copy-start.9
  57.6 0.9 copy-start.6
  58.5 0.8 copy-start.7
  89.4 9.7 %collective-permute-start.6 = (bf16[2048,1024]{1,0:T(8,128)(2,1)}, bf16[2048,1024]{1,0:T(8,128)(2,1)}, u32[]{:S(2)}, u32[]{:S(2)}) collective-permute-start(bf16[2048,1024]{1,0:T(8,128)(2,1)} %bitcast.11), channel_id=1, source_target_pairs={{0,64},{64,0},{128,192},{192,128},{256,320},{320,256},{384,448},{4... | collective-permute-start | bytes 12582920 | tf_op jit(solution)/shard_map/ppermute | solution.py:379
  107.5 32.1 %copy-start.10 = (f32[1,2,4,16,2]{4,3,2,1,0:T(8,128)S(1)}, f32[1,2,4,16,2]{4,3,2,1,0:T(8,128)}, u32[]{:S(2)}) copy-start(f32[1,2,4,16,2]{4,3,2,1,0:T(8,128)} %get-tuple-element.38) | copy-start | bytes 3076
  115.8 12.6 %collective-permute-start.7 = (bf16[2,1,6,16,2048]{4,3,2,1,0:T(8,128)(2,1)}, bf16[2,1,6,16,2048]{4,3,2,1,0:T(8,128)(2,1)S(1)}, u32[]{:S(2)}, u32[]{:S(2)}) collective-permute-start(bf16[2,1,6,16,2048]{4,3,2,1,0:T(8,128)(2,1)} %get-tuple-element.27), channel_id=1, source_target_pairs={{0,64},{64,128},{128,192},{192,256},{256,320},{320,384},{384,448},... | collective-permute-start | bytes 2359304 | tf_op jit(solution)/shard_map/ppermute | solution.py:32
  119.2 13.5 %collective-permute-start.8 = (bf16[2,1,6,16,2048]{4,3,2,1,0:T(8,128)(2,1)}, bf16[2,1,6,16,2048]{4,3,2,1,0:T(8,128)(2,1)S(1)}, u32[]{:S(2)}, u32[]{:S(2)}) collective-permute-start(bf16[2,1,6,16,2048]{4,3,2,1,0:T(8,128)(2,1)} %get-tuple-element.28), channel_id=1, source_target_pairs={{64,0},{128,64},{192,128},{256,192},{320,256},{384,320},{448,384},... | collective-permute-start | bytes 2359304 | tf_op jit(solution)/shard_map/ppermute | solution.py:32
  132.7 1.0 copy-start.2
  133.6 0.9 copy-start.3
  134.7 9.0 %collective-permute-start.9 = (bf16[2,2,1,16,2048]{4,3,2,1,0:T(8,128)(2,1)S(1)}, bf16[2,2,1,16,2048]{4,3,2,1,0:T(8,128)(2,1)S(1)}, u32[]{:S(2)}, u32[]{:S(2)}) collective-permute-start(bf16[2,2,1,16,2048]{4,3,2,1,0:T(8,128)(2,1)S(1)} %get-tuple-element.32), channel_id=1, source_target_pairs={{0,16},{16,32},{32,48},{1,17},{17,33},{33,49},{2,18},{18,34},{34,5... | collective-permute-start | bytes 786440 | tf_op jit(solution)/shard_map/ppermute | solution.py:32
  138.3 7.1 %collective-permute-start.10 = (bf16[2,2,1,16,2048]{4,3,2,1,0:T(8,128)(2,1)S(1)}, bf16[2,2,1,16,2048]{4,3,2,1,0:T(8,128)(2,1)S(1)}, u32[]{:S(2)}, u32[]{:S(2)}) collective-permute-start(bf16[2,2,1,16,2048]{4,3,2,1,0:T(8,128)(2,1)S(1)} %get-tuple-element.33), channel_id=1, source_target_pairs={{16,0},{32,16},{48,32},{17,1},{33,17},{49,33},{18,2},{34,18},{50,3... | collective-permute-start | bytes 786440 | tf_op jit(solution)/shard_map/ppermute | solution.py:32
  140.3 1.6 %copy-start.1 = (f32[2,2,4,16,2048]{4,3,2,1,0:T(8,128)S(1)}, f32[2,2,4,16,2048]{4,3,2,1,0:T(8,128)}, u32[]{:S(2)}) copy-start(f32[2,2,4,16,2048]{4,3,2,1,0:T(8,128)} %get-tuple-element.26.own_ref) | copy-start | bytes 6291460
Sparse Core Ops, SparseCore 0:
  24.0 65.3 all-gather.3

commit v4 on v3

--- a/solution.py
+++ b/solution.py
@@ -232,54 +232,99 @@
     )(boundary, position, att, part, own, swapped, gain, read_rows, cotangent)
 
 
-def backward_kernel(q_ref, ga_ref, prob_ref, *rest):
+def value_rows(refs, lanes):
+    return jnp.concatenate([ref[0, :, :, :, lanes].reshape(-1, HS) for ref in refs], axis=0)
+
+
+def back_rim_kernel(q_ref, ga_ref, prob_ref, *rest):
     count = len(PIECES)
-    kv_refs = rest[:count]
-    gq_ref = rest[count]
-    gkv_refs = rest[count + 1 :]
+    v_refs = rest[:count]
+    gs_ref = rest[count]
+    rim_refs = rest[count + 1 :]
     for h in range(GROUP):
         lanes = slice(h * HS, (h + 1) * HS)
         query = q_ref[0, :, :, :, lanes].reshape(TOK, HS)
-        keys = piece_rows(kv_refs, 0, lanes)
-        values = piece_rows(kv_refs, 1, lanes)
+        values = value_rows(v_refs, lanes)
         grad_att = ga_ref[:, lanes]
         prob = prob_ref[h]
         grad_prob = dot(values, grad_att, ((1,), (1,)))
         inner_sum = jnp.sum(prob * grad_prob, axis=0, keepdims=True)
         grad_scores = (prob * (grad_prob - inner_sum) * (HS**-0.5)).astype(jnp.bfloat16)
-        grad_query = dot(grad_scores, keys, ((0,), (0,)))
-        gq_ref[0, :, :, :, lanes] = grad_query.reshape(BX, BY, BS, HS).astype(gq_ref.dtype)
-        grads = (dot(grad_scores, query, ((1,), (0,))), dot(prob.astype(jnp.bfloat16), grad_att, ((1,), (0,))))
+        gs_ref[h] = grad_scores
+        half = prob[TOK:].astype(jnp.bfloat16)
+        grads = (dot(grad_scores[TOK:], query, ((1,), (0,))), dot(half, grad_att, ((1,), (0,))))
         for which, grad in enumerate(grads):
             start = 0
-            for ref in gkv_refs:
+            for ref in rim_refs:
                 shape = ref.shape[1:4]
                 rows = shape[0] * shape[1] * shape[2]
                 ref[which, :, :, :, lanes] = grad[start : start + rows].reshape(shape + (HS,)).astype(ref.dtype)
                 start += rows
 
 
-def backward(queries, grad_att, prob, pieces):
+def lane_block(shape, width):
+    return pl.BlockSpec(tuple(shape[:-1]) + (width,), lambda g: (0,) * (len(shape) - 1) + (g,))
+
+
+def half_block(shape, which, width):
+    return pl.BlockSpec((1,) + tuple(shape[1:-1]) + (width,), lambda g: (which,) + (0,) * (len(shape) - 2) + (g,))
+
+
+def back_rim(queries, grad_att, prob, pieces):
     inner = queries.shape[-1]
     width = GROUP * HS
-
-    def wide(shape):
-        return pl.BlockSpec(tuple(shape[:-1]) + (width,), lambda g: (0,) * (len(shape) - 1) + (g,))
-
     shapes = [p.shape for p in pieces]
-    blocks, rest = shapes[0], shapes[0][3:]
-    sums = [blocks, (2, 1, BY + 2) + rest, (2, 1, BY + 2) + rest, shapes[-1], shapes[-1]]
-    return pl.pallas_call(
-        backward_kernel,
+    heads = pl.BlockSpec((GROUP, KEYS, TOK), lambda g: (g, 0, 0))
+    return pl.pallas_call(
+        back_rim_kernel,
         grid=(inner // width,),
-        in_specs=[wide(queries.shape), wide(grad_att.shape), pl.BlockSpec((GROUP, KEYS, TOK), lambda g: (g, 0, 0))]
-        + [wide(s) for s in shapes],
-        out_specs=[wide(queries.shape)] + [wide(s) for s in sums],
-        out_shape=[jax.ShapeDtypeStruct(queries.shape, jnp.bfloat16)]
-        + [jax.ShapeDtypeStruct(s, jnp.float32 if i == 0 else jnp.bfloat16) for i, s in enumerate(sums)],
+        in_specs=[lane_block(queries.shape, width), lane_block(grad_att.shape, width), heads]
+        + [half_block(s, 1, width) for s in shapes],
+        out_specs=[heads] + [lane_block(s, width) for s in shapes[1:]],
+        out_shape=[jax.ShapeDtypeStruct(prob.shape, jnp.bfloat16)]
+        + [jax.ShapeDtypeStruct(s, jnp.bfloat16) for s in shapes[1:]],
         compiler_params=pltpu.CompilerParams(vmem_limit_bytes=VMEM_LIMIT),
-        name="attend_back",
+        name="back_rim",
     )(queries, grad_att, prob, *pieces)
+
+
+def back_own_kernel(q_ref, ga_ref, prob_ref, gs_ref, *rest):
+    count = len(PIECES)
+    k_refs = rest[:count]
+    gq_ref, own_ref = rest[count:]
+    for h in range(GROUP):
+        lanes = slice(h * HS, (h + 1) * HS)
+        query = q_ref[0, :, :, :, lanes].reshape(TOK, HS)
+        grad_scores = gs_ref[h]
+        grad_query = dot(grad_scores, value_rows(k_refs, lanes), ((0,), (0,)))
+        gq_ref[0, :, :, :, lanes] = grad_query.reshape(BX, BY, BS, HS).astype(gq_ref.dtype)
+        own_ref[0, :, :, :, lanes] = dot(grad_scores[:TOK], query, ((1,), (0,))).reshape(BX, BY, BS, HS)
+        half = prob_ref[h].astype(jnp.bfloat16)
+        own_ref[1, :, :, :, lanes] = dot(half, ga_ref[:, lanes], ((1,), (0,))).reshape(BX, BY, BS, HS)
+
+
+def back_own(queries, grad_att, prob, grad_scores, pieces):
+    inner = queries.shape[-1]
+    width = GROUP * HS
+    shapes = [p.shape for p in pieces]
+    return pl.pallas_call(
+        back_own_kernel,
+        grid=(inner // width,),
+        in_specs=[
+            lane_block(queries.shape, width),
+            lane_block(grad_att.shape, width),
+            pl.BlockSpec((GROUP, TOK, TOK), lambda g: (g, 0, 0)),
+            pl.BlockSpec((GROUP, KEYS, TOK), lambda g: (g, 0, 0)),
+        ]
+        + [half_block(s, 0, width) for s in shapes],
+        out_specs=[lane_block(queries.shape, width), lane_block(shapes[0], width)],
+        out_shape=[
+            jax.ShapeDtypeStruct(queries.shape, jnp.bfloat16),
+            jax.ShapeDtypeStruct(shapes[0], jnp.float32),
+        ],
+        compiler_params=pltpu.CompilerParams(vmem_limit_bytes=VMEM_LIMIT),
+        name="back_own",
+    )(queries, grad_att, prob, grad_scores, *pieces)
 
 
 def sides_kernel(from_low_ref, from_high_ref, low_ref, high_ref, left_ref, right_ref):
@@ -293,7 +338,7 @@
 
 
 def sides(from_low, from_high, low, high):
-    corner = pl.BlockSpec(from_low.shape[:2] + (2,) + from_low.shape[3:], lambda i: (0, 0, BY // 2, 0, 0))
+    corner = pl.BlockSpec(from_low.shape, lambda i: (0, 0, 0, 0, 0))
     rim = pl.BlockSpec(low.shape, lambda i: (0, 0, 0, 0, 0))
     shape = jax.ShapeDtypeStruct(low.shape, low.dtype)
     return pl.pallas_call(
@@ -415,10 +460,13 @@
     prediction, grad_att = project(
         boundary, position, att, part, own_cols, swapped, gain[None], read_weight.T, cotangent
     )
-    grad_queries, own, gxlow, gxhigh, gylow, gyhigh = backward(queries, grad_att, prob, pieces)
+    grad_scores, gxlow, gclow, gxhigh, gchigh, gylow, gyhigh = back_rim(queries, grad_att, prob, pieces)
+    corner_low = shift(gchigh, "sx", 1)
+    corner_high = shift(gclow, "sx", -1)
     from_low = shift(gxhigh, "sx", 1)
     from_high = shift(gxlow, "sx", -1)
-    to_left, to_right = sides(from_low, from_high, gylow, gyhigh)
+    grad_queries, own = back_own(queries, grad_att, prob, grad_scores, pieces)
+    to_left, to_right = sides(corner_low, corner_high, gylow, gyhigh)
     left = shift(to_right, "sy", 1)
     right = shift(to_left, "sy", -1)
     partial, edge = add_rows(own, from_low, from_high)

time: 155 us -> 150 us (0.968)
  waiting for transfers between devices: 45.1 us -> 32.1 us
  starting transfers between devices: 36 us -> 42.5 us
  Pallas kernels: 30 us -> 33 us
    ppermute x10 -> x12, waiting for transfers between devices: 19.1 us -> 6.09 us  [shift(): return lax.ppermute(value, axis, pairs)]
    ppermute x10 -> x12, starting transfers between devices: 33.4 us -> 39.9 us  [shift(): return lax.ppermute(value, axis, pairs)]
    pallas_call x1 -> x2, Pallas kernels: 8.31 us -> 11.4 us  [the longest x1 6.2 us: back_rim(): pl.pallas_call(back_rim_kernel, grid=(inner // width,), in_specs=[lane_bl...]
    unnamed x26 -> x28, local copies, waits for them, and re-layouts: 7.61 us -> 7.6 us
  transfers between devices with their start and end apart: 12 -> 14, of which waited for: 7 -> 5; matrix products, arithmetic and copies ran while one was open for 4% -> 3% of each run, Pallas kernels for 8% -> 12%
where the time goes in v4:
time: 150 us; the launch traced here: 149 us
  starting transfers between devices  42.5 us (28%)
  Pallas kernels  33 us (22%)
  waiting for transfers between devices  32.1 us (21%)
  blocking collectives  15.6 us (10%)
  between operations  14.4 us (10%)
  local copies, waits for them, and re-layouts  9.61 us (6%)
    ppermute x12, starting transfers between devices, shift(): return lax.ppermute(value, axis, pairs)  39.9 us
    all_gather x1, waiting for transfers between devices, body(): lax.all_gather(both, 'wa', axis=0, axis_index_groups=rings)  24.5 us
    all_gather x1, blocking collectives, body(): both = lax.all_gather(slab, 'wa', axis=0, axis_index_groups=pairs)  15.6 us
    pallas_call x1, Pallas kernels, project(): pl.pallas_call(project_kernel, in_specs=[smem, smem, vmem, vmem, hbm, hbm...  8.4 us
    unnamed x28, local copies, waits for them, and re-layouts  7.6 us
    pallas_call x1, Pallas kernels, back_rim(): pl.pallas_call(back_rim_kernel, grid=(inner // width,), in_specs=[lane_bl...  6.2 us
    ppermute x12, waiting for transfers between devices, shift(): return lax.ppermute(value, axis, pairs)  6.09 us
    pallas_call x1, Pallas kernels, forward(): pl.pallas_call(forward_kernel, grid=(inner // width,), in_specs=[smem, sm...  5.61 us
  transfers between devices with their start and end apart: 14, of which 5 were waited for; matrix products, arithmetic and copies ran while one was open for 3% of the time, Pallas kernels for 12%

profile of v4, /device:TPU:1, one launch (start us, length us, event | category | flops | bytes accessed | tf_op | source)
XLA Modules:
  0.0 148.6 jit_solution(9821599962008204417)
XLA Ops:
  7.2 0.0 copy-start
  7.2 0.0 copy-start.4
  7.2 0.0 all-gather.4.cloned.1.call-start
  7.3 1.0 copy-done
  8.2 15.6 %all-gather = bf16[256,1024]{1,0:T(8,128)(2,1)} all-gather(bf16[128,1024]{1,0:T(8,128)(2,1)S(1)} %constant_dynamic-slice_fusion), channel_id=2, replica_groups={{0,1},{2,3},{4,5},{6,7},{8,9},{10,11},{12,13},{14,15},{16,17},{18,19},{..., dimensions={0}, use_global_device_ids=true | all-gather | bytes 786432 | tf_op jit(solution)/shard_map/all_gather | solution.py:438
  23.9 0.0 all-gather.4.cloned.1.call-update
  23.9 1.1 fusion.1
  25.0 9.5 %collective-permute-start.1 = (bf16[2,2,1,16,2048]{4,3,2,1,0:T(8,128)(2,1)S(1)}, bf16[2,2,1,16,2048]{4,3,2,1,0:T(8,128)(2,1)S(1)}, u32[]{:S(2)}, u32[]{:S(2)}) collective-permute-start(bf16[2,2,1,16,2048]{4,3,2,1,0:T(8,128)(2,1)S(1)} %get-tuple-element.49), channel_id=1, source_target_pairs={{0,16},{16,32},{32,48},{1,17},{17,33},{33,49},{2,18},{18,34},{34,5... | collective-permute-start | bytes 786440 | tf_op jit(solution)/shard_map/ppermute | solution.py:32
  34.4 1.3 collective-permute-start.2
  35.7 0.0 copy-done.4
  35.7 0.9 fusion
  36.6 0.0 copy-start.12
  36.6 3.7 %collective-permute-start.4 = (bf16[2,1,4,16,2048]{4,3,2,1,0:T(8,128)(2,1)}, bf16[2,1,4,16,2048]{4,3,2,1,0:T(8,128)(2,1)S(1)}, u32[]{:S(2)}, u32[]{:S(2)}) collective-permute-start(bf16[2,1,4,16,2048]{4,3,2,1,0:T(8,128)(2,1)} %get-tuple-element.47), channel_id=1, source_target_pairs={{64,0},{128,64},{192,128},{256,192},{320,256},{384,320},{448,384},... | collective-permute-start | bytes 1572872 | tf_op jit(solution)/shard_map/ppermute | solution.py:32
  40.3 3.0 %collective-permute-start = (bf16[2,1,4,16,2048]{4,3,2,1,0:T(8,128)(2,1)S(1)}, bf16[2,1,4,16,2048]{4,3,2,1,0:T(8,128)(2,1)S(1)}, u32[]{:S(2)}, u32[]{:S(2)}) collective-permute-start(bf16[2,1,4,16,2048]{4,3,2,1,0:T(8,128)(2,1)S(1)} %get-tuple-element.48), channel_id=1, source_target_pairs={{0,64},{64,128},{128,192},{192,256},{256,320},{320,384},{384,448},... | collective-permute-start | bytes 1572872 | tf_op jit(solution)/shard_map/ppermute | solution.py:32
  43.3 0.0 collective-permute-done.1.rest_5_
  43.4 0.0 copy-start.7
  43.4 0.0 collective-permute-done.2.rest_6_
  43.4 0.0 copy-start.8
  43.5 5.1 %collective-permute-start.3 = (bf16[2,1,2,16,2048]{4,3,2,1,0:T(8,128)(2,1)S(1)}, bf16[2,1,2,16,2048]{4,3,2,1,0:T(8,128)(2,1)S(1)}, u32[]{:S(2)}, u32[]{:S(2)}) collective-permute-start(bf16[2,1,2,16,2048]{4,3,2,1,0:T(8,128)(2,1)S(1)} %pad_maximum_fusion), channel_id=1, source_target_pairs={{0,64},{64,128},{128,192},{192,256},{256,320},{320,384},{384,448},... | collective-permute-start | bytes 786440 | tf_op jit(solution)/shard_map/ppermute | solution.py:32
  48.6 0.7 pad_maximum_fusion.1
  49.3 1.9 %collective-permute-start.5 = (bf16[2,1,2,16,2048]{4,3,2,1,0:T(8,128)(2,1)}, bf16[2,1,2,16,2048]{4,3,2,1,0:T(8,128)(2,1)S(1)}, u32[]{:S(2)}, u32[]{:S(2)}) collective-permute-start(bf16[2,1,2,16,2048]{4,3,2,1,0:T(8,128)(2,1)} %pad_maximum_fusion.1), channel_id=1, source_target_pairs={{64,0},{128,64},{192,128},{256,192},{320,256},{384,320},{448,384},... | collective-permute-start | bytes 786440 | tf_op jit(solution)/shard_map/ppermute | solution.py:32
  51.2 0.7 pad_add_fusion.pos_ref
  51.9 0.4 collective-permute-done.3.rest_2_
  52.3 5.3 %collective-permute-done.5.rest_4_ = bf16[2,1,2,16,2048]{4,3,2,1,0:T(8,128)(2,1)S(1)} collective-permute-done((bf16[2,1,2,16,2048]{4,3,2,1,0:T(8,128)(2,1)}, bf16[2,1,2,16,2048]{4,3,2,1,0:T(8,128)(2,1)S(1)}, u32[]{:S(2)}, u32[]{:S(2)}) %collective-permute-start.5) | collective-permute-done | bytes 262176 | tf_op jit(solution)/shard_map/ppermute | solution.py:32
  57.6 0.0 collective-permute-done.4.rest_3_
  57.6 0.0 collective-permute-done.rest_1_
  57.6 0.0 copy-done.7
  57.6 0.0 copy-done.8
  57.6 0.0 copy-done.9
  57.6 0.6 copy-done.10
  58.3 0.2 copy-done.5
  58.5 0.8 copy-done.6
  59.3 5.6 %attend.1 = (bf16[128,2048]{1,0:T(8,128)(2,1)}, f32[16,384,128]{2,1,0:T(8,128)}) custom-call(s32[1,2,4,4]{3,2,1,0:T(4,128)} %adj_ref.1, s32[5]{0:T(128)} %pad_add_fusion.pos_ref, bf16[1,2,4,16,2048]{4,3,2,1,0:T(8,128)(2,1)} %q_ref.5, bf16[2,2,4,16,2048]{4,3,2,1,0:T(8,128)(2,1)} %bitcast.12, bf16[2,1,4,16,2048]{4,3,2,1,0:T(8,128)(2,1)} %copy-done.6, ...), custom_call_target="tpu_custom_call" | custom-call | tf_op jit(solution)/shard_map/attend/pallas_call | solution.py:106
  64.9 24.5 %all-gather.4.cloned.1.call-done = bf16[16,128,1024]{2,1,0:T(8,128)(2,1)} async-done(((bf16[2,128,1024]{2,1,0:T(8,128)(2,1)}), bf16[16,128,1024]{2,1,0:T(8,128)(2,1)}) %all-gather.4.cloned.1.call-update) | async-done | bytes 4194320 | tf_op jit(solution)/shard_map/all_gather | solution.py:439
  89.4 2.6 %collective-permute-start.6 = (bf16[2048,1024]{1,0:T(8,128)(2,1)}, bf16[2048,1024]{1,0:T(8,128)(2,1)}, u32[]{:S(2)}, u32[]{:S(2)}) collective-permute-start(bf16[2048,1024]{1,0:T(8,128)(2,1)} %bitcast.16), channel_id=1, source_target_pairs={{0,64},{64,0},{128,192},{192,128},{256,320},{320,256},{384,448},{4... | collective-permute-start | bytes 12582920 | tf_op jit(solution)/shard_map/ppermute | solution.py:424
  91.9 0.0 copy-done.12
  91.9 0.8 copy.15.cot_ref
  92.7 4.8 %project_own.1.part_ref = f32[128,1024]{1,0:T(8,128)} custom-call(bf16[128,2048]{1,0:T(8,128)(2,1)} %get-tuple-element.23.att_ref, bf16[2048,1024]{1,0:T(8,128)(2,1)} %bitcast.17), custom_call_target="tpu_custom_call" | custom-call | tf_op jit(solution)/shard_map/project_own/pallas_call | solution.py:148
  97.5 1.5 %collective-permute-done.6.swap_hbm = bf16[2048,1024]{1,0:T(8,128)(2,1)} collective-permute-done((bf16[2048,1024]{1,0:T(8,128)(2,1)}, bf16[2048,1024]{1,0:T(8,128)(2,1)}, u32[]{:S(2)}, u32[]{:S(2)}) %collective-permute-start.6) | collective-permute-done | bytes 4194336 | tf_op jit(solution)/shard_map/ppermute | solution.py:424
  99.0 8.4 %project.1 = (f32[1,2,4,16,2]{4,3,2,1,0:T(8,128)}, bf16[128,2048]{1,0:T(8,128)(2,1)}) custom-call(s32[1,2,4]{2,1,0:T(2,128)} %bound_ref.1, s32[5]{0:T(128)} %pad_add_fusion.pos_ref, bf16[128,2048]{1,0:T(8,128)(2,1)} %get-tuple-element.23.att_ref, f32[128,1024]{1,0:T(8,128)} %project_own.1.part_ref, bf16[2048,1024]{1,0:T(8,128)(2,1)} %bitcast.18, ...), custom_call_target="tpu_custom_call" | custom-call | tf_op jit(solution)/shard_map/project/pallas_call | solution.py:215
  107.5 0.0 copy-start.11
  107.5 6.2 %back_rim.1 = (bf16[16,384,128]{2,1,0:T(8,128)(2,1)}, bf16[2,1,4,16,2048]{4,3,2,1,0:T(8,128)(2,1)}, bf16[2,1,2,16,2048]{4,3,2,1,0:T(8,128)(2,1)}, bf16[2,1,4,16,...) custom-call(bf16[1,2,4,16,2048]{4,3,2,1,0:T(8,128)(2,1)} %q_ref.5, ...), custom_call_target="tpu_custom_call" | custom-call | tf_op jit(solution)/shard_map/back_rim/pallas_call | solution.py:278
  113.7 3.4 %collective-permute-start.9 = (bf16[2,1,2,16,2048]{4,3,2,1,0:T(8,128)(2,1)}, bf16[2,1,2,16,2048]{4,3,2,1,0:T(8,128)(2,1)S(1)}, u32[]{:S(2)}, u32[]{:S(2)}) collective-permute-start(bf16[2,1,2,16,2048]{4,3,2,1,0:T(8,128)(2,1)} %get-tuple-element.34), channel_id=1, source_target_pairs={{0,64},{64,128},{128,192},{192,256},{256,320},{320,384},{384,448},... | collective-permute-start | bytes 786440 | tf_op jit(solution)/shard_map/ppermute | solution.py:32
  117.0 1.9 %collective-permute-start.10 = (bf16[2,1,2,16,2048]{4,3,2,1,0:T(8,128)(2,1)}, bf16[2,1,2,16,2048]{4,3,2,1,0:T(8,128)(2,1)S(1)}, u32[]{:S(2)}, u32[]{:S(2)}) collective-permute-start(bf16[2,1,2,16,2048]{4,3,2,1,0:T(8,128)(2,1)} %get-tuple-element.35), channel_id=1, source_target_pairs={{64,0},{128,64},{192,128},{256,192},{320,256},{384,320},{448,384},... | collective-permute-start | bytes 786440 | tf_op jit(solution)/shard_map/ppermute | solution.py:32
  119.0 3.6 %collective-permute-start.7 = (bf16[2,1,4,16,2048]{4,3,2,1,0:T(8,128)(2,1)}, bf16[2,1,4,16,2048]{4,3,2,1,0:T(8,128)(2,1)S(1)}, u32[]{:S(2)}, u32[]{:S(2)}) collective-permute-start(bf16[2,1,4,16,2048]{4,3,2,1,0:T(8,128)(2,1)} %get-tuple-element.31), channel_id=1, source_target_pairs={{0,64},{64,128},{128,192},{192,256},{256,320},{320,384},{384,448},... | collective-permute-start | bytes 1572872 | tf_op jit(solution)/shard_map/ppermute | solution.py:32
  122.6 1.9 %collective-permute-start.8 = (bf16[2,1,4,16,2048]{4,3,2,1,0:T(8,128)(2,1)}, bf16[2,1,4,16,2048]{4,3,2,1,0:T(8,128)(2,1)S(1)}, u32[]{:S(2)}, u32[]{:S(2)}) collective-permute-start(bf16[2,1,4,16,2048]{4,3,2,1,0:T(8,128)(2,1)} %get-tuple-element.32), channel_id=1, source_target_pairs={{64,0},{128,64},{192,128},{256,192},{320,256},{384,320},{448,384},... | collective-permute-start | bytes 1572872 | tf_op jit(solution)/shard_map/ppermute | solution.py:32
  124.5 0.0 collective-permute-done.9.from_low_ref
  124.6 0.4 collective-permute-done.10.from_high_ref
  124.9 0.9 copy-done.2
  125.9 0.9 copy-done.3
  126.8 0.1 sides.1
  127.0 3.3 %collective-permute-start.11 = (bf16[2,2,1,16,2048]{4,3,2,1,0:T(8,128)(2,1)S(1)}, bf16[2,2,1,16,2048]{4,3,2,1,0:T(8,128)(2,1)S(1)}, u32[]{:S(2)}, u32[]{:S(2)}) collective-permute-start(bf16[2,2,1,16,2048]{4,3,2,1,0:T(8,128)(2,1)S(1)} %get-tuple-element.38), channel_id=1, source_target_pairs={{0,16},{16,32},{32,48},{1,17},{17,33},{33,49},{2,18},{18,34},{34,5... | collective-permute-start | bytes 786440 | tf_op jit(solution)/shard_map/ppermute | solution.py:32
  130.3 1.3 collective-permute-start.12
  131.6 0.0 copy-done.11
  131.6 0.7 copy.16
  132.3 5.2 %back_own.1 = (bf16[1,2,4,16,2048]{4,3,2,1,0:T(8,128)(2,1)}, f32[2,2,4,16,2048]{4,3,2,1,0:T(8,128)}) custom-call(bf16[1,2,4,16,2048]{4,3,2,1,0:T(8,128)(2,1)} %q_ref.5, bf16[128,2048]{1,0:T(8,128)(2,1)} %get-tuple-element.26.ga_ref, f32[16,384,128]{2,1,0:T(8,128)} %get-tuple-element.27.prob_ref, bf16[16,384,128]{2,1,0:T(8,128)(2,1)} %get-tuple-element.28.gs_ref, ...), custom_call_target="tpu_custom_call" | custom-call | tf_op jit(solution)/shard_map/back_own/pallas_call | solution.py:310
  137.5 0.0 collective-permute-done.7.low_ref
  137.5 0.0 collective-permute-done.8.high_ref
  137.5 0.0 copy-start.1
  137.5 1.6 %copy-done.1 = f32[2,2,4,16,2048]{4,3,2,1,0:T(8,128)S(1)} copy-done((f32[2,2,4,16,2048]{4,3,2,1,0:T(8,128)S(1)}, f32[2,2,4,16,2048]{4,3,2,1,0:T(8,128)}, u32[]{:S(2)}) %copy-start.1) | copy-done | bytes 2097176
  139.1 1.7 %add_rows.1 = (bf16[2,2,4,16,2048]{4,3,2,1,0:T(8,128)(2,1)}, f32[2,2,2,16,2048]{4,3,2,1,0:T(8,128)S(1)}) custom-call(f32[2,2,4,16,2048]{4,3,2,1,0:T(8,128)S(1)} %copy-done.1, bf16[2,1,4,16,2048]{4,3,2,1,0:T(8,128)(2,1)S(1)} %collective-permute-done.7.low_ref, bf16[2,1,4,16,2048]{4,3,2,1,0:T(8,128)(2,1)S(1)} %collective-permute-done.8.high_ref), custom_call_target="tpu_custom_call" | custom-call | tf_op jit(solution)/shard_map/add_rows/pallas_call | solution.py:379
  140.8 0.0 collective-permute-done.11.low_ref
  140.8 0.0 collective-permute-done.12.high_ref
  140.8 0.9 add_columns.1
  (11 shorter events, 0.1 us)
Async XLA Ops:
  7.2 1.0 copy-start
  7.2 28.5 %copy-start.4 = (bf16[2,1,2,4,16,2048]{5,4,3,2,1,0:T(8,128)(2,1)S(1)}, bf16[2,1,2,4,16,2048]{5,4,3,2,1,0:T(8,128)(2,1)}, u32[]{:S(2)}) copy-start(bf16[2,1,2,4,16,2048]{5,4,3,2,1,0:T(8,128)(2,1)} %param.9) | copy-start | bytes 3145732
  7.2 82.2 %all-gather.4.cloned.1.call-start = ((), (), s32[]{:S(2)}) async-start(), calls=%async_computation | async-start | bytes 4718592 | tf_op jit(solution)/shard_map/all_gather | solution.py:439
  25.0 18.4 %collective-permute-start.1 = (bf16[2,2,1,16,2048]{4,3,2,1,0:T(8,128)(2,1)S(1)}, bf16[2,2,1,16,2048]{4,3,2,1,0:T(8,128)(2,1)S(1)}, u32[]{:S(2)}, u32[]{:S(2)}) collective-permute-start(bf16[2,2,1,16,2048]{4,3,2,1,0:T(8,128)(2,1)S(1)} %get-tuple-element.49), channel_id=1, source_target_pairs={{0,16},{16,32},{32,48},{1,17},{17,33},{33,49},{2,18},{18,34},{34,5... | collective-permute-start | bytes 786440 | tf_op jit(solution)/shard_map/ppermute | solution.py:32
  34.4 9.0 %collective-permute-start.2 = (bf16[2,2,1,16,2048]{4,3,2,1,0:T(8,128)(2,1)S(1)}, bf16[2,2,1,16,2048]{4,3,2,1,0:T(8,128)(2,1)S(1)}, u32[]{:S(2)}, u32[]{:S(2)}) collective-permute-start(bf16[2,2,1,16,2048]{4,3,2,1,0:T(8,128)(2,1)S(1)} %get-tuple-element.50), channel_id=1, source_target_pairs={{16,0},{32,16},{48,32},{17,1},{33,17},{49,33},{18,2},{34,18},{50,3... | collective-permute-start | bytes 786440 | tf_op jit(solution)/shard_map/ppermute | solution.py:32
  36.6 55.3 %copy-start.12 = (f32[1,2,4,16,2]{3,4,2,1,0:T(2,128)S(1)}, f32[1,2,4,16,2]{3,4,2,1,0:T(2,128)}, u32[]{:S(2)}) copy-start(f32[1,2,4,16,2]{3,4,2,1,0:T(2,128)} %param.15) | copy-start | bytes 3076
  36.6 21.0 %collective-permute-start.4 = (bf16[2,1,4,16,2048]{4,3,2,1,0:T(8,128)(2,1)}, bf16[2,1,4,16,2048]{4,3,2,1,0:T(8,128)(2,1)S(1)}, u32[]{:S(2)}, u32[]{:S(2)}) collective-permute-start(bf16[2,1,4,16,2048]{4,3,2,1,0:T(8,128)(2,1)} %get-tuple-element.47), channel_id=1, source_target_pairs={{64,0},{128,64},{192,128},{256,192},{320,256},{384,320},{448,384},... | collective-permute-start | bytes 1572872 | tf_op jit(solution)/shard_map/ppermute | solution.py:32
  40.3 17.3 %collective-permute-start = (bf16[2,1,4,16,2048]{4,3,2,1,0:T(8,128)(2,1)S(1)}, bf16[2,1,4,16,2048]{4,3,2,1,0:T(8,128)(2,1)S(1)}, u32[]{:S(2)}, u32[]{:S(2)}) collective-permute-start(bf16[2,1,4,16,2048]{4,3,2,1,0:T(8,128)(2,1)S(1)} %get-tuple-element.48), channel_id=1, source_target_pairs={{0,64},{64,128},{128,192},{192,256},{256,320},{320,384},{384,448},... | collective-permute-start | bytes 1572872 | tf_op jit(solution)/shard_map/ppermute | solution.py:32
  43.4 14.2 %copy-start.7 = (bf16[2,2,1,16,2048]{4,3,2,1,0:T(8,128)(2,1)}, bf16[2,2,1,16,2048]{4,3,2,1,0:T(8,128)(2,1)S(1)}, u32[]{:S(2)}) copy-start(bf16[2,2,1,16,2048]{4,3,2,1,0:T(8,128)(2,1)S(1)} %collective-permute-done.1.rest_5_) | copy-start | bytes 786436
  43.4 14.2 %copy-start.8 = (bf16[2,2,1,16,2048]{4,3,2,1,0:T(8,128)(2,1)}, bf16[2,2,1,16,2048]{4,3,2,1,0:T(8,128)(2,1)S(1)}, u32[]{:S(2)}) copy-start(bf16[2,2,1,16,2048]{4,3,2,1,0:T(8,128)(2,1)S(1)} %collective-permute-done.2.rest_6_) | copy-start | bytes 786436
  43.5 8.8 %collective-permute-start.3 = (bf16[2,1,2,16,2048]{4,3,2,1,0:T(8,128)(2,1)S(1)}, bf16[2,1,2,16,2048]{4,3,2,1,0:T(8,128)(2,1)S(1)}, u32[]{:S(2)}, u32[]{:S(2)}) collective-permute-start(bf16[2,1,2,16,2048]{4,3,2,1,0:T(8,128)(2,1)S(1)} %pad_maximum_fusion), channel_id=1, source_target_pairs={{0,64},{64,128},{128,192},{192,256},{256,320},{320,384},{384,448},... | collective-permute-start | bytes 786440 | tf_op jit(solution)/shard_map/ppermute | solution.py:32
  49.3 8.3 %collective-permute-start.5 = (bf16[2,1,2,16,2048]{4,3,2,1,0:T(8,128)(2,1)}, bf16[2,1,2,16,2048]{4,3,2,1,0:T(8,128)(2,1)S(1)}, u32[]{:S(2)}, u32[]{:S(2)}) collective-permute-start(bf16[2,1,2,16,2048]{4,3,2,1,0:T(8,128)(2,1)} %pad_maximum_fusion.1), channel_id=1, source_target_pairs={{64,0},{128,64},{192,128},{256,192},{320,256},{384,320},{448,384},... | collective-permute-start | bytes 786440 | tf_op jit(solution)/shard_map/ppermute | solution.py:32
  52.3 5.4 %copy-start.9 = (bf16[2,1,2,16,2048]{4,3,2,1,0:T(8,128)(2,1)}, bf16[2,1,2,16,2048]{4,3,2,1,0:T(8,128)(2,1)S(1)}, u32[]{:S(2)}) copy-start(bf16[2,1,2,16,2048]{4,3,2,1,0:T(8,128)(2,1)S(1)} %collective-permute-done.3.rest_2_) | copy-start | bytes 786436
  57.6 0.7 copy-start.10
  57.6 0.9 copy-start.5
  58.5 0.8 copy-start.6
  89.4 9.7 %collective-permute-start.6 = (bf16[2048,1024]{1,0:T(8,128)(2,1)}, bf16[2048,1024]{1,0:T(8,128)(2,1)}, u32[]{:S(2)}, u32[]{:S(2)}) collective-permute-start(bf16[2048,1024]{1,0:T(8,128)(2,1)} %bitcast.16), channel_id=1, source_target_pairs={{0,64},{64,0},{128,192},{192,128},{256,320},{320,256},{384,448},{4... | collective-permute-start | bytes 12582920 | tf_op jit(solution)/shard_map/ppermute | solution.py:424
  107.5 24.1 %copy-start.11 = (f32[1,2,4,16,2]{4,3,2,1,0:T(8,128)S(1)}, f32[1,2,4,16,2]{4,3,2,1,0:T(8,128)}, u32[]{:S(2)}) copy-start(f32[1,2,4,16,2]{4,3,2,1,0:T(8,128)} %get-tuple-element.44) | copy-start | bytes 3076
  113.7 10.9 %collective-permute-start.9 = (bf16[2,1,2,16,2048]{4,3,2,1,0:T(8,128)(2,1)}, bf16[2,1,2,16,2048]{4,3,2,1,0:T(8,128)(2,1)S(1)}, u32[]{:S(2)}, u32[]{:S(2)}) collective-permute-start(bf16[2,1,2,16,2048]{4,3,2,1,0:T(8,128)(2,1)} %get-tuple-element.34), channel_id=1, source_target_pairs={{0,64},{64,128},{128,192},{192,256},{256,320},{320,384},{384,448},... | collective-permute-start | bytes 786440 | tf_op jit(solution)/shard_map/ppermute | solution.py:32
  117.0 7.9 %collective-permute-start.10 = (bf16[2,1,2,16,2048]{4,3,2,1,0:T(8,128)(2,1)}, bf16[2,1,2,16,2048]{4,3,2,1,0:T(8,128)(2,1)S(1)}, u32[]{:S(2)}, u32[]{:S(2)}) collective-permute-start(bf16[2,1,2,16,2048]{4,3,2,1,0:T(8,128)(2,1)} %get-tuple-element.35), channel_id=1, source_target_pairs={{64,0},{128,64},{192,128},{256,192},{320,256},{384,320},{448,384},... | collective-permute-start | bytes 786440 | tf_op jit(solution)/shard_map/ppermute | solution.py:32
  119.0 18.5 %collective-permute-start.7 = (bf16[2,1,4,16,2048]{4,3,2,1,0:T(8,128)(2,1)}, bf16[2,1,4,16,2048]{4,3,2,1,0:T(8,128)(2,1)S(1)}, u32[]{:S(2)}, u32[]{:S(2)}) collective-permute-start(bf16[2,1,4,16,2048]{4,3,2,1,0:T(8,128)(2,1)} %get-tuple-element.31), channel_id=1, source_target_pairs={{0,64},{64,128},{128,192},{192,256},{256,320},{320,384},{384,448},... | collective-permute-start | bytes 1572872 | tf_op jit(solution)/shard_map/ppermute | solution.py:32
  122.6 14.8 %collective-permute-start.8 = (bf16[2,1,4,16,2048]{4,3,2,1,0:T(8,128)(2,1)}, bf16[2,1,4,16,2048]{4,3,2,1,0:T(8,128)(2,1)S(1)}, u32[]{:S(2)}, u32[]{:S(2)}) collective-permute-start(bf16[2,1,4,16,2048]{4,3,2,1,0:T(8,128)(2,1)} %get-tuple-element.32), channel_id=1, source_target_pairs={{64,0},{128,64},{192,128},{256,192},{320,256},{384,320},{448,384},... | collective-permute-start | bytes 1572872 | tf_op jit(solution)/shard_map/ppermute | solution.py:32
  124.9 1.0 copy-start.2
  125.9 0.9 copy-start.3
  127.0 13.8 %collective-permute-start.11 = (bf16[2,2,1,16,2048]{4,3,2,1,0:T(8,128)(2,1)S(1)}, bf16[2,2,1,16,2048]{4,3,2,1,0:T(8,128)(2,1)S(1)}, u32[]{:S(2)}, u32[]{:S(2)}) collective-permute-start(bf16[2,2,1,16,2048]{4,3,2,1,0:T(8,128)(2,1)S(1)} %get-tuple-element.38), channel_id=1, source_target_pairs={{0,16},{16,32},{32,48},{1,17},{17,33},{33,49},{2,18},{18,34},{34,5... | collective-permute-start | bytes 786440 | tf_op jit(solution)/shard_map/ppermute | solution.py:32
  130.3 10.6 %collective-permute-start.12 = (bf16[2,2,1,16,2048]{4,3,2,1,0:T(8,128)(2,1)S(1)}, bf16[2,2,1,16,2048]{4,3,2,1,0:T(8,128)(2,1)S(1)}, u32[]{:S(2)}, u32[]{:S(2)}) collective-permute-start(bf16[2,2,1,16,2048]{4,3,2,1,0:T(8,128)(2,1)S(1)} %get-tuple-element.39), channel_id=1, source_target_pairs={{16,0},{32,16},{48,32},{17,1},{33,17},{49,33},{18,2},{34,18},{50,3... | collective-permute-start | bytes 786440 | tf_op jit(solution)/shard_map/ppermute | solution.py:32
  137.5 1.6 %copy-start.1 = (f32[2,2,4,16,2048]{4,3,2,1,0:T(8,128)S(1)}, f32[2,2,4,16,2048]{4,3,2,1,0:T(8,128)}, u32[]{:S(2)}) copy-start(f32[2,2,4,16,2048]{4,3,2,1,0:T(8,128)} %get-tuple-element.30.own_ref) | copy-start | bytes 6291460
Sparse Core Ops, SparseCore 0:
  24.0 65.3 all-gather.3

commit v5 on v4

--- a/solution.py
+++ b/solution.py
@@ -12,7 +12,8 @@
 TOK = BX * BY * BS
 GROUP = 4
 VMEM_LIMIT = 60 * 1024 * 1024
-SMALL_LIMIT = 24 * 1024 * 1024
+SMALL_LIMIT = 12 * 1024 * 1024
+OWN_LIMIT = 57 * 1024 * 1024
 
 LOCAL = [(x, y) for x in range(BX) for y in range(BY)]
 XLOW = [(-1, y) for y in range(BY)]
@@ -144,7 +145,7 @@
     vmem = pl.BlockSpec(memory_space=pltpu.VMEM)
     tokens = att.shape[0]
     inner, cols = own.shape
-    chunks = 2
+    chunks = 4
     return pl.pallas_call(
         project_own_kernel,
         in_specs=[vmem, pl.BlockSpec(memory_space=pl.ANY)],
@@ -191,9 +192,9 @@
         normed = proj * inv_rms * gain
         pred0 = jnp.sum(normed * read_ref[0:1, :], axis=1, keepdims=True) * flag
         pred1 = jnp.sum(normed * read_ref[1:2, :], axis=1, keepdims=True) * flag
-        pred = jnp.where(lax.broadcasted_iota(jnp.int32, (2 * BS, 2), 1) == 0, pred0, pred1)
-        pred_ref[0, x, y] = pred[:BS]
-        pred_ref[0, x, y + 1] = pred[BS:]
+        pred = jnp.where(lax.broadcasted_iota(jnp.int32, (2 * BS, HS), 1) == 0, pred0, pred1).T
+        pred_ref[0, x, y] = pred[:2, :BS]
+        pred_ref[0, x, y + 1] = pred[:2, BS:]
         gained = (cot[:, 0:1] * read_ref[0:1, :] + cot[:, 1:2] * read_ref[1:2, :]) * gain
         inner_mean = jnp.sum(gained * proj, axis=1, keepdims=True) * (1.0 / inner)
         gp_ref[rows_of, :] = (inv_rms * gained - proj * (inv_rms * inv_rms * inv_rms * inner_mean)).astype(jnp.bfloat16)
@@ -217,7 +218,7 @@
         in_specs=[smem, smem, vmem, vmem, hbm, hbm, vmem, vmem, vmem],
         out_specs=[vmem, vmem],
         out_shape=[
-            jax.ShapeDtypeStruct(cotangent.shape, jnp.float32),
+            jax.ShapeDtypeStruct(cotangent.shape[:3] + (2, BS), jnp.float32),
             jax.ShapeDtypeStruct(att.shape, jnp.bfloat16),
         ],
         scratch_shapes=[
@@ -291,22 +292,33 @@
 def back_own_kernel(q_ref, ga_ref, prob_ref, gs_ref, *rest):
     count = len(PIECES)
     k_refs = rest[:count]
-    gq_ref, own_ref = rest[count:]
+    low_ref, high_ref, gq_ref, out_ref, edge_ref = rest[count:]
     for h in range(GROUP):
         lanes = slice(h * HS, (h + 1) * HS)
         query = q_ref[0, :, :, :, lanes].reshape(TOK, HS)
         grad_scores = gs_ref[h]
         grad_query = dot(grad_scores, value_rows(k_refs, lanes), ((0,), (0,)))
         gq_ref[0, :, :, :, lanes] = grad_query.reshape(BX, BY, BS, HS).astype(gq_ref.dtype)
-        own_ref[0, :, :, :, lanes] = dot(grad_scores[:TOK], query, ((1,), (0,))).reshape(BX, BY, BS, HS)
         half = prob_ref[h].astype(jnp.bfloat16)
-        own_ref[1, :, :, :, lanes] = dot(half, ga_ref[:, lanes], ((1,), (0,))).reshape(BX, BY, BS, HS)
-
-
-def back_own(queries, grad_att, prob, grad_scores, pieces):
+        grads = (dot(grad_scores[:TOK], query, ((1,), (0,))), dot(half, ga_ref[:, lanes], ((1,), (0,))))
+        for which, grad in enumerate(grads):
+            for block, (x, y) in enumerate(LOCAL):
+                total = grad[block * BS : (block + 1) * BS]
+                if x == 0:
+                    total = total + low_ref[which, 0, y, :, lanes].astype(jnp.float32)
+                if x == BX - 1:
+                    total = total + high_ref[which, 0, y, :, lanes].astype(jnp.float32)
+                if y in (0, BY - 1):
+                    edge_ref[which, x, y // (BY - 1), :, lanes] = total
+                else:
+                    out_ref[which, x, y, :, lanes] = total.astype(out_ref.dtype)
+
+
+def back_own(queries, grad_att, prob, grad_scores, pieces, low, high):
     inner = queries.shape[-1]
     width = GROUP * HS
     shapes = [p.shape for p in pieces]
+    edge = shapes[0][:2] + (2,) + shapes[0][3:]
     return pl.pallas_call(
         back_own_kernel,
         grid=(inner // width,),
@@ -316,108 +328,98 @@
             pl.BlockSpec((GROUP, TOK, TOK), lambda g: (g, 0, 0)),
             pl.BlockSpec((GROUP, KEYS, TOK), lambda g: (g, 0, 0)),
         ]
-        + [half_block(s, 0, width) for s in shapes],
-        out_specs=[lane_block(queries.shape, width), lane_block(shapes[0], width)],
+        + [half_block(s, 0, width) for s in shapes]
+        + [lane_block(low.shape, width), lane_block(high.shape, width)],
+        out_specs=[lane_block(queries.shape, width), lane_block(shapes[0], width), lane_block(edge, width)],
         out_shape=[
             jax.ShapeDtypeStruct(queries.shape, jnp.bfloat16),
-            jax.ShapeDtypeStruct(shapes[0], jnp.float32),
-        ],
-        compiler_params=pltpu.CompilerParams(vmem_limit_bytes=VMEM_LIMIT),
+            jax.ShapeDtypeStruct(shapes[0], jnp.bfloat16),
+            jax.ShapeDtypeStruct(edge, jnp.float32),
+        ],
+        compiler_params=pltpu.CompilerParams(vmem_limit_bytes=OWN_LIMIT),
         name="back_own",
-    )(queries, grad_att, prob, grad_scores, *pieces)
-
-
-def sides_kernel(from_low_ref, from_high_ref, low_ref, high_ref, left_ref, right_ref):
+    )(
+        queries,
+        grad_att,
+        prob,
+        grad_scores,
+        *pieces,
+        *(pltpu.with_memory_space_constraint(term, pltpu.VMEM) for term in (low, high)),
+    )
+
+
+def sides_kernel(from_low_ref, from_high_ref, low_hbm, high_hbm, left_ref, right_ref, rim_ref, sems):
     f32 = jnp.float32
-    for which in range(2):
-        for y, rim, out in ((0, low_ref, left_ref), (1, high_ref, right_ref)):
-            first = rim[which, 0, 0].astype(f32) + from_low_ref[which, 0, y].astype(f32)
-            last = rim[which, BX - 1, 0].astype(f32) + from_high_ref[which, 0, y].astype(f32)
+    copies = [
+        pltpu.make_async_copy(low_hbm, rim_ref.at[0], sems.at[0]),
+        pltpu.make_async_copy(high_hbm, rim_ref.at[1], sems.at[1]),
+    ]
+    for copy in copies:
+        copy.start()
+    for y, out in ((0, left_ref), (1, right_ref)):
+        copies[y].wait()
+        for which in range(2):
+            first = rim_ref[y, which, 0, 0].astype(f32) + from_low_ref[which, 0, y].astype(f32)
+            last = rim_ref[y, which, BX - 1, 0].astype(f32) + from_high_ref[which, 0, y].astype(f32)
             out[which, 0, 0] = first.astype(out.dtype)
             out[which, BX - 1, 0] = last.astype(out.dtype)
 
 
 def sides(from_low, from_high, low, high):
-    corner = pl.BlockSpec(from_low.shape, lambda i: (0, 0, 0, 0, 0))
-    rim = pl.BlockSpec(low.shape, lambda i: (0, 0, 0, 0, 0))
+    vmem = pl.BlockSpec(memory_space=pltpu.VMEM)
+    hbm = pl.BlockSpec(memory_space=pltpu.HBM)
     shape = jax.ShapeDtypeStruct(low.shape, low.dtype)
     return pl.pallas_call(
         sides_kernel,
-        grid=(1,),
-        in_specs=[corner, corner, rim, rim],
-        out_specs=[rim, rim],
+        in_specs=[vmem, vmem, hbm, hbm],
+        out_specs=[vmem, vmem],
         out_shape=[shape, shape],
+        scratch_shapes=[pltpu.VMEM((2,) + low.shape, low.dtype), pltpu.SemaphoreType.DMA((2,))],
         compiler_params=pltpu.CompilerParams(vmem_limit_bytes=SMALL_LIMIT),
         name="sides",
-    )(from_low, from_high, low, high)
-
-
-def add_rows_kernel(own_ref, low_ref, high_ref, out_ref, edge_ref):
-    f32 = jnp.float32
+    )(from_low, from_high, *(pltpu.with_memory_space_constraint(rim, pltpu.HBM) for rim in (low, high)))
+
+
+def add_columns_kernel(low_ref, high_ref, edge_hbm, partial_hbm, out_hbm, edge_ref, sum_ref, sems):
+    del partial_hbm
+    loads = [pltpu.make_async_copy(edge_hbm.at[i], edge_ref.at[i], sems.at[i]) for i in range(2)]
+    for load in loads:
+        load.start()
+    stores = []
     for which in range(2):
-        for x in range(BX):
-            for y in range(BY):
-                total = own_ref[which, x, y]
-                if x == 0:
-                    total = total + low_ref[which, 0, y].astype(f32)
-                if x == BX - 1:
-                    total = total + high_ref[which, 0, y].astype(f32)
-                if y in (0, BY - 1):
-                    edge_ref[which, x, y // (BY - 1)] = total
-                else:
-                    out_ref[which, x, y] = total.astype(out_ref.dtype)
-
-
-def add_rows(own, low, high):
-    inner = own.shape[-1]
-    width = inner // 4
-
-    def wide(shape):
-        return pl.BlockSpec(tuple(shape[:-1]) + (width,), lambda g: (0, 0, 0, 0, g))
-
-    edge = own.shape[:2] + (2,) + own.shape[3:]
-    return pl.pallas_call(
-        add_rows_kernel,
-        grid=(inner // width,),
-        in_specs=[wide(own.shape), wide(low.shape), wide(high.shape)],
-        out_specs=[wide(own.shape), wide(edge)],
-        out_shape=[jax.ShapeDtypeStruct(own.shape, jnp.bfloat16), jax.ShapeDtypeStruct(edge, jnp.float32)],
-        compiler_params=pltpu.CompilerParams(vmem_limit_bytes=SMALL_LIMIT),
-        name="add_rows",
-    )(own, low, high)
-
-
-def add_columns_kernel(edge_ref, low_ref, high_ref, partial_hbm, out_ref):
-    del partial_hbm
-    first = pl.program_id(0) == 0
-
-    @pl.when(first)
-    def _():
-        out_ref[...] = (edge_ref[...] + low_ref[...].astype(jnp.float32)).astype(out_ref.dtype)
-
-    @pl.when(jnp.logical_not(first))
-    def _():
-        out_ref[...] = (edge_ref[...] + high_ref[...].astype(jnp.float32)).astype(out_ref.dtype)
+        loads[which].wait()
+        for side, ref in enumerate((low_ref, high_ref)):
+            for x in range(BX):
+                total = edge_ref[which, x, side] + ref[which, x, 0].astype(jnp.float32)
+                sum_ref[which, side, x] = total.astype(sum_ref.dtype)
+                y = side * (BY - 1)
+                index = (which * 2 + side) * BX + x
+                store = pltpu.make_async_copy(
+                    sum_ref.at[which, side, x], out_hbm.at[which, x, y], sems.at[2 + index]
+                )
+                store.start()
+                stores.append(store)
+    for store in stores:
+        store.wait()
 
 
 def add_columns(edge, low, high, partial):
-    block = edge.shape[:2] + (1,) + edge.shape[3:]
-    whole = pl.BlockSpec(block, lambda i: (0, 0, 0, 0, 0))
+    vmem = pl.BlockSpec(memory_space=pltpu.VMEM)
+    hbm = pl.BlockSpec(memory_space=pltpu.HBM)
     return pl.pallas_call(
         add_columns_kernel,
-        grid=(2,),
-        in_specs=[
-            pl.BlockSpec(block, lambda i: (0, 0, i, 0, 0)),
-            whole,
-            whole,
-            pl.BlockSpec(memory_space=pl.ANY),
-        ],
-        out_specs=pl.BlockSpec(block, lambda i: (0, 0, i * (BY - 1), 0, 0)),
+        in_specs=[vmem, vmem, hbm, hbm],
+        out_specs=hbm,
         out_shape=jax.ShapeDtypeStruct(partial.shape, partial.dtype),
+        scratch_shapes=[
+            pltpu.VMEM(edge.shape, jnp.float32),
+            pltpu.VMEM((2, 2, BX) + edge.shape[3:], partial.dtype),
+            pltpu.SemaphoreType.DMA((2 + 4 * BX,)),
+        ],
         input_output_aliases={3: 0},
         compiler_params=pltpu.CompilerParams(vmem_limit_bytes=SMALL_LIMIT),
         name="add_columns",
-    )(edge, low, high, partial)
+    )(low, high, *(pltpu.with_memory_space_constraint(term, pltpu.HBM) for term in (edge, partial)))
 
 
 def swap_cores(value):
@@ -465,13 +467,12 @@
     corner_high = shift(gclow, "sx", -1)
     from_low = shift(gxhigh, "sx", 1)
     from_high = shift(gxlow, "sx", -1)
-    grad_queries, own = back_own(queries, grad_att, prob, grad_scores, pieces)
+    grad_queries, partial, edge = back_own(queries, grad_att, prob, grad_scores, pieces, from_low, from_high)
     to_left, to_right = sides(corner_low, corner_high, gylow, gyhigh)
     left = shift(to_right, "sy", 1)
     right = shift(to_left, "sy", -1)
-    partial, edge = add_rows(own, from_low, from_high)
     grad_kv = add_columns(edge, left, right, partial)
-    return (prediction, grad_queries, grad_kv[:, None])
+    return (jnp.swapaxes(prediction, 3, 4), grad_queries, grad_kv[:, None])
 
 
 def solution(mesh):

time: 150 us -> 149 us (level)
  waiting for transfers between devices: 32.1 us -> 35.5 us
  local copies, waits for them, and re-layouts: 9.61 us -> 6.64 us
    unnamed x28 -> x17, local copies, waits for them, and re-layouts: 7.6 us -> 3.42 us
    ppermute x12, waiting for transfers between devices: 6.09 us -> 9.07 us  [shift(): return lax.ppermute(value, axis, pairs)]
    pallas_call x3 -> x2, Pallas kernels: 2.81 us -> 3.1 us  [the longest x1 2 us: add_columns(): pl.pallas_call(add_columns_kernel, in_specs=[vmem, vmem, hbm, hbm], out_s...]
  transfers between devices with their start and end apart: 14 -> 14, of which waited for: 5 -> 6; matrix products, arithmetic and copies ran while one was open for 3% -> 4% of each run, Pallas kernels for 12% -> 11%
where the time goes in v5:
time: 149 us; the launch traced here: 148 us
  starting transfers between devices  41.3 us (28%)
  waiting for transfers between devices  35.5 us (24%)
  Pallas kernels  32.8 us (22%)
  blocking collectives  15.6 us (10%)
  between operations  14.4 us (10%)
  local copies, waits for them, and re-layouts  6.64 us (4%)
    ppermute x12, starting transfers between devices, shift(): return lax.ppermute(value, axis, pairs)  38.7 us
    all_gather x1, waiting for transfers between devices, body(): lax.all_gather(both, 'wa', axis=0, axis_index_groups=rings)  24.4 us
    all_gather x1, blocking collectives, body(): both = lax.all_gather(slab, 'wa', axis=0, axis_index_groups=pairs)  15.6 us
    ppermute x12, waiting for transfers between devices, shift(): return lax.ppermute(value, axis, pairs)  9.07 us
    pallas_call x1, Pallas kernels, project(): pl.pallas_call(project_kernel, in_specs=[smem, smem, vmem, vmem, hbm, hbm...  8.42 us
    pallas_call x1, Pallas kernels, back_rim(): pl.pallas_call(back_rim_kernel, grid=(inner // width,), in_specs=[lane_bl...  6.18 us
    pallas_call x1, Pallas kernels, forward(): pl.pallas_call(forward_kernel, grid=(inner // width,), in_specs=[smem, sm...  5.61 us
    pallas_call x1, Pallas kernels, back_own(): pl.pallas_call(back_own_kernel, grid=(inner // width,), in_specs=[lane_bl...  5.14 us
  transfers between devices with their start and end apart: 14, of which 6 were waited for; matrix products, arithmetic and copies ran while one was open for 4% of the time, Pallas kernels for 11%

profile of v5, /device:TPU:1, one launch (start us, length us, event | category | flops | bytes accessed | tf_op | source)
XLA Modules:
  0.0 147.6 jit_solution(14935639760409646892)
XLA Ops:
  7.2 0.0 copy-start
  7.2 0.0 all-gather.4.cloned.1.call-start
  7.2 1.0 copy-done
  8.2 15.6 %all-gather = bf16[256,1024]{1,0:T(8,128)(2,1)} all-gather(bf16[128,1024]{1,0:T(8,128)(2,1)S(1)} %constant_dynamic-slice_fusion), channel_id=2, replica_groups={{0,1},{2,3},{4,5},{6,7},{8,9},{10,11},{12,13},{14,15},{16,17},{18,19},{..., dimensions={0}, use_global_device_ids=true | all-gather | bytes 786432 | tf_op jit(solution)/shard_map/all_gather | solution.py:440
  23.9 0.0 all-gather.4.cloned.1.call-update
  23.9 1.1 fusion.1
  25.0 0.0 copy-start.7
  25.0 9.5 %collective-permute-start.1 = (bf16[2,2,1,16,2048]{4,3,2,1,0:T(8,128)(2,1)S(1)}, bf16[2,2,1,16,2048]{4,3,2,1,0:T(8,128)(2,1)S(1)}, u32[]{:S(2)}, u32[]{:S(2)}) collective-permute-start(bf16[2,2,1,16,2048]{4,3,2,1,0:T(8,128)(2,1)S(1)} %get-tuple-element.47), channel_id=1, source_target_pairs={{0,16},{16,32},{32,48},{1,17},{17,33},{33,49},{2,18},{18,34},{34,5... | collective-permute-start | bytes 786440 | tf_op jit(solution)/shard_map/ppermute | solution.py:33
  34.4 1.3 collective-permute-start.2
  35.7 2.1 %fusion = (bf16[2,1,4,16,2048]{4,3,2,1,0:T(8,128)(2,1)}, bf16[2,1,4,16,2048]{4,3,2,1,0:T(8,128)(2,1)S(1)}) fusion(bf16[2,2,4,16,2048]{4,3,2,1,0:T(8,128)(2,1)} %bitcast.13), kind=kLoop, calls=%fused_computation.4 | loop fusion | bytes 2097152 | tf_op jit(solution)/shard_map/slice | solution.py:445
  37.8 3.6 %collective-permute-start.4 = (bf16[2,1,4,16,2048]{4,3,2,1,0:T(8,128)(2,1)}, bf16[2,1,4,16,2048]{4,3,2,1,0:T(8,128)(2,1)S(1)}, u32[]{:S(2)}, u32[]{:S(2)}) collective-permute-start(bf16[2,1,4,16,2048]{4,3,2,1,0:T(8,128)(2,1)} %get-tuple-element.45), channel_id=1, source_target_pairs={{64,0},{128,64},{192,128},{256,192},{320,256},{384,320},{448,384},... | collective-permute-start | bytes 1572872 | tf_op jit(solution)/shard_map/ppermute | solution.py:33
  41.4 3.0 %collective-permute-start = (bf16[2,1,4,16,2048]{4,3,2,1,0:T(8,128)(2,1)S(1)}, bf16[2,1,4,16,2048]{4,3,2,1,0:T(8,128)(2,1)S(1)}, u32[]{:S(2)}, u32[]{:S(2)}) collective-permute-start(bf16[2,1,4,16,2048]{4,3,2,1,0:T(8,128)(2,1)S(1)} %get-tuple-element.46), channel_id=1, source_target_pairs={{0,64},{64,128},{128,192},{192,256},{256,320},{320,384},{384,448},... | collective-permute-start | bytes 1572872 | tf_op jit(solution)/shard_map/ppermute | solution.py:33
  44.4 0.0 collective-permute-done.1.rest_5_
  44.4 0.0 copy-start.3
  44.5 0.0 collective-permute-done.2.rest_6_
  44.5 0.0 copy-start.4
  44.5 4.0 %collective-permute-start.3 = (bf16[2,1,2,16,2048]{4,3,2,1,0:T(8,128)(2,1)S(1)}, bf16[2,1,2,16,2048]{4,3,2,1,0:T(8,128)(2,1)S(1)}, u32[]{:S(2)}, u32[]{:S(2)}) collective-permute-start(bf16[2,1,2,16,2048]{4,3,2,1,0:T(8,128)(2,1)S(1)} %pad_maximum_fusion), channel_id=1, source_target_pairs={{0,64},{64,128},{128,192},{192,256},{256,320},{320,384},{384,448},... | collective-permute-start | bytes 786440 | tf_op jit(solution)/shard_map/ppermute | solution.py:33
  48.6 0.7 pad_maximum_fusion.1
  49.3 1.9 %collective-permute-start.5 = (bf16[2,1,2,16,2048]{4,3,2,1,0:T(8,128)(2,1)}, bf16[2,1,2,16,2048]{4,3,2,1,0:T(8,128)(2,1)S(1)}, u32[]{:S(2)}, u32[]{:S(2)}) collective-permute-start(bf16[2,1,2,16,2048]{4,3,2,1,0:T(8,128)(2,1)} %pad_maximum_fusion.1), channel_id=1, source_target_pairs={{64,0},{128,64},{192,128},{256,192},{320,256},{384,320},{448,384},... | collective-permute-start | bytes 786440 | tf_op jit(solution)/shard_map/ppermute | solution.py:33
  51.2 0.7 pad_add_fusion.pos_ref
  51.9 1.4 collective-permute-done.3.rest_2_
  53.3 0.0 copy-start.5
  53.3 4.3 %collective-permute-done.5.rest_4_ = bf16[2,1,2,16,2048]{4,3,2,1,0:T(8,128)(2,1)S(1)} collective-permute-done((bf16[2,1,2,16,2048]{4,3,2,1,0:T(8,128)(2,1)}, bf16[2,1,2,16,2048]{4,3,2,1,0:T(8,128)(2,1)S(1)}, u32[]{:S(2)}, u32[]{:S(2)}) %collective-permute-start.5) | collective-permute-done | bytes 262176 | tf_op jit(solution)/shard_map/ppermute | solution.py:33
  57.6 0.0 copy-start.6
  57.6 0.0 collective-permute-done.4.rest_3_
  57.6 0.0 copy-start.1
  57.6 0.0 collective-permute-done.rest_1_
  57.6 0.0 copy-done.3
  57.6 0.0 copy-done.4
  57.6 0.0 copy-done.5
  57.6 0.7 copy-done.6
  58.3 0.2 copy-done.1
  58.5 0.0 copy-start.2
  58.5 0.8 copy-done.2
  59.3 5.6 %attend.1 = (bf16[128,2048]{1,0:T(8,128)(2,1)}, f32[16,384,128]{2,1,0:T(8,128)}) custom-call(s32[1,2,4,4]{3,2,1,0:T(4,128)} %adj_ref.1, s32[5]{0:T(128)} %pad_add_fusion.pos_ref, bf16[1,2,4,16,2048]{4,3,2,1,0:T(8,128)(2,1)} %q_ref.5, bf16[2,2,4,16,2048]{4,3,2,1,0:T(8,128)(2,1)} %bitcast.14, bf16[2,1,4,16,2048]{4,3,2,1,0:T(8,128)(2,1)} %copy-done.2, ...), custom_call_target="tpu_custom_call" | custom-call | tf_op jit(solution)/shard_map/attend/pallas_call | solution.py:107
  64.9 24.4 %all-gather.4.cloned.1.call-done = bf16[16,128,1024]{2,1,0:T(8,128)(2,1)} async-done(((bf16[2,128,1024]{2,1,0:T(8,128)(2,1)}), bf16[16,128,1024]{2,1,0:T(8,128)(2,1)}) %all-gather.4.cloned.1.call-update) | async-done | bytes 4194320 | tf_op jit(solution)/shard_map/all_gather | solution.py:441
  89.4 2.6 %collective-permute-start.6 = (bf16[2048,1024]{1,0:T(8,128)(2,1)}, bf16[2048,1024]{1,0:T(8,128)(2,1)}, u32[]{:S(2)}, u32[]{:S(2)}) collective-permute-start(bf16[2048,1024]{1,0:T(8,128)(2,1)} %bitcast.17), channel_id=1, source_target_pairs={{0,64},{64,0},{128,192},{192,128},{256,320},{320,256},{384,448},{4... | collective-permute-start | bytes 12582920 | tf_op jit(solution)/shard_map/ppermute | solution.py:426
  91.9 0.0 copy-done.7
  91.9 0.7 copy.14.cot_ref
  92.7 4.4 %project_own.1.part_ref = f32[128,1024]{1,0:T(8,128)} custom-call(bf16[128,2048]{1,0:T(8,128)(2,1)} %get-tuple-element.22.att_ref, bf16[2048,1024]{1,0:T(8,128)(2,1)} %bitcast.18), custom_call_target="tpu_custom_call" | custom-call | tf_op jit(solution)/shard_map/project_own/pallas_call | solution.py:149
  97.0 2.0 %collective-permute-done.6.swap_hbm = bf16[2048,1024]{1,0:T(8,128)(2,1)} collective-permute-done((bf16[2048,1024]{1,0:T(8,128)(2,1)}, bf16[2048,1024]{1,0:T(8,128)(2,1)}, u32[]{:S(2)}, u32[]{:S(2)}) %collective-permute-start.6) | collective-permute-done | bytes 4194336 | tf_op jit(solution)/shard_map/ppermute | solution.py:426
  99.0 8.4 %project.1 = (f32[1,2,4,2,16]{4,3,2,1,0:T(2,128)}, bf16[128,2048]{1,0:T(8,128)(2,1)}) custom-call(s32[1,2,4]{2,1,0:T(2,128)} %bound_ref.1, s32[5]{0:T(128)} %pad_add_fusion.pos_ref, bf16[128,2048]{1,0:T(8,128)(2,1)} %get-tuple-element.22.att_ref, f32[128,1024]{1,0:T(8,128)} %project_own.1.part_ref, bf16[2048,1024]{1,0:T(8,128)(2,1)} %bitcast.19, ...), custom_call_target="tpu_custom_call" | custom-call | tf_op jit(solution)/shard_map/project/pallas_call | solution.py:216
  107.5 6.2 %back_rim.1 = (bf16[16,384,128]{2,1,0:T(8,128)(2,1)}, bf16[2,1,4,16,2048]{4,3,2,1,0:T(8,128)(2,1)}, bf16[2,1,2,16,2048]{4,3,2,1,0:T(8,128)(2,1)}, bf16[2,1,4,16,...) custom-call(bf16[1,2,4,16,2048]{4,3,2,1,0:T(8,128)(2,1)} %q_ref.5, ...), custom_call_target="tpu_custom_call" | custom-call | tf_op jit(solution)/shard_map/back_rim/pallas_call | solution.py:279
  113.7 3.4 %collective-permute-start.9 = (bf16[2,1,2,16,2048]{4,3,2,1,0:T(8,128)(2,1)}, bf16[2,1,2,16,2048]{4,3,2,1,0:T(8,128)(2,1)S(1)}, u32[]{:S(2)}, u32[]{:S(2)}) collective-permute-start(bf16[2,1,2,16,2048]{4,3,2,1,0:T(8,128)(2,1)} %get-tuple-element.31), channel_id=1, source_target_pairs={{0,64},{64,128},{128,192},{192,256},{256,320},{320,384},{384,448},... | collective-permute-start | bytes 786440 | tf_op jit(solution)/shard_map/ppermute | solution.py:33
  117.0 1.9 %collective-permute-start.10 = (bf16[2,1,2,16,2048]{4,3,2,1,0:T(8,128)(2,1)}, bf16[2,1,2,16,2048]{4,3,2,1,0:T(8,128)(2,1)S(1)}, u32[]{:S(2)}, u32[]{:S(2)}) collective-permute-start(bf16[2,1,2,16,2048]{4,3,2,1,0:T(8,128)(2,1)} %get-tuple-element.32), channel_id=1, source_target_pairs={{64,0},{128,64},{192,128},{256,192},{320,256},{384,320},{448,384},... | collective-permute-start | bytes 786440 | tf_op jit(solution)/shard_map/ppermute | solution.py:33
  119.0 3.6 %collective-permute-start.7 = (bf16[2,1,4,16,2048]{4,3,2,1,0:T(8,128)(2,1)}, bf16[2,1,4,16,2048]{4,3,2,1,0:T(8,128)(2,1)S(1)}, u32[]{:S(2)}, u32[]{:S(2)}) collective-permute-start(bf16[2,1,4,16,2048]{4,3,2,1,0:T(8,128)(2,1)} %get-tuple-element.28), channel_id=1, source_target_pairs={{0,64},{64,128},{128,192},{192,256},{256,320},{320,384},{384,448},... | collective-permute-start | bytes 1572872 | tf_op jit(solution)/shard_map/ppermute | solution.py:33
  122.6 1.9 %collective-permute-start.8 = (bf16[2,1,4,16,2048]{4,3,2,1,0:T(8,128)(2,1)}, bf16[2,1,4,16,2048]{4,3,2,1,0:T(8,128)(2,1)S(1)}, u32[]{:S(2)}, u32[]{:S(2)}) collective-permute-start(bf16[2,1,4,16,2048]{4,3,2,1,0:T(8,128)(2,1)} %get-tuple-element.29), channel_id=1, source_target_pairs={{64,0},{128,64},{192,128},{256,192},{320,256},{384,320},{448,384},... | collective-permute-start | bytes 1572872 | tf_op jit(solution)/shard_map/ppermute | solution.py:33
  124.5 0.0 collective-permute-done.9.from_low_ref
  124.5 0.4 collective-permute-done.10.from_high_ref
  124.9 1.1 sides.1
  126.0 3.3 %collective-permute-start.11 = (bf16[2,2,1,16,2048]{4,3,2,1,0:T(8,128)(2,1)S(1)}, bf16[2,2,1,16,2048]{4,3,2,1,0:T(8,128)(2,1)S(1)}, u32[]{:S(2)}, u32[]{:S(2)}) collective-permute-start(bf16[2,2,1,16,2048]{4,3,2,1,0:T(8,128)(2,1)S(1)} %get-tuple-element.35), channel_id=1, source_target_pairs={{0,16},{16,32},{32,48},{1,17},{17,33},{33,49},{2,18},{18,34},{34,5... | collective-permute-start | bytes 786440 | tf_op jit(solution)/shard_map/ppermute | solution.py:33
  129.3 1.3 collective-permute-start.12
  130.6 0.0 collective-permute-done.7.rest_7_
  130.6 3.0 %collective-permute-done.8.rest_8_ = bf16[2,1,4,16,2048]{4,3,2,1,0:T(8,128)(2,1)S(1)} collective-permute-done((bf16[2,1,4,16,2048]{4,3,2,1,0:T(8,128)(2,1)}, bf16[2,1,4,16,2048]{4,3,2,1,0:T(8,128)(2,1)S(1)}, u32[]{:S(2)}, u32[]{:S(2)}) %collective-permute-start.8) | collective-permute-done | bytes 524320 | tf_op jit(solution)/shard_map/ppermute | solution.py:33
  133.6 5.1 %back_own.1 = (bf16[1,2,4,16,2048]{4,3,2,1,0:T(8,128)(2,1)}, bf16[2,2,4,16,2048]{4,3,2,1,0:T(8,128)(2,1)}, f32[2,2,2,16,2048]{4,3,2,1,0:T(8,128)}) custom-call(bf16[1,2,4,16,2048]{4,3,2,1,0:T(8,128)(2,1)} %q_ref.5, bf16[128,2048]{1,0:T(8,128)(2,1)} %get-tuple-element.25.ga_ref, f32[16,384,128]{2,1,0:T(8,128)} %get-tuple-element.26.prob_ref, ...), custom_call_target="tpu_custom_call" | custom-call | tf_op jit(solution)/shard_map/back_own/pallas_call | solution.py:322
  138.7 0.0 collective-permute-done.11.low_ref
  138.8 0.0 collective-permute-done.12.high_ref
  138.8 2.0 %add_columns.1 = bf16[2,2,4,16,2048]{4,3,2,1,0:T(8,128)(2,1)} custom-call(bf16[2,2,1,16,2048]{4,3,2,1,0:T(8,128)(2,1)S(1)} %collective-permute-done.11.low_ref, bf16[2,2,1,16,2048]{4,3,2,1,0:T(8,128)(2,1)S(1)} %collective-permute-done.12.high_ref, f32[2,2,2,16,2048]{4,3,2,1,0:T(8,128)} %get-tuple-element.37.edge_hbm, ...), custom_call_target="tpu_custom_call", output_to_operand_aliasing={{}: (3, {})} | custom-call | tf_op jit(solution)/shard_map/add_columns/pallas_call | solution.py:409
  (5 shorter events, 0.1 us)
Async XLA Ops:
  7.2 1.0 copy-start
  7.2 82.2 %all-gather.4.cloned.1.call-start = ((), (), s32[]{:S(2)}) async-start(), calls=%async_computation | async-start | bytes 4718592 | tf_op jit(solution)/shard_map/all_gather | solution.py:441
  25.0 67.0 %copy-start.7 = (f32[1,2,4,16,2]{3,4,2,1,0:T(2,128)S(1)}, f32[1,2,4,16,2]{3,4,2,1,0:T(2,128)}, u32[]{:S(2)}) copy-start(f32[1,2,4,16,2]{3,4,2,1,0:T(2,128)} %param.15) | copy-start | bytes 3076
  25.0 19.5 %collective-permute-start.1 = (bf16[2,2,1,16,2048]{4,3,2,1,0:T(8,128)(2,1)S(1)}, bf16[2,2,1,16,2048]{4,3,2,1,0:T(8,128)(2,1)S(1)}, u32[]{:S(2)}, u32[]{:S(2)}) collective-permute-start(bf16[2,2,1,16,2048]{4,3,2,1,0:T(8,128)(2,1)S(1)} %get-tuple-element.47), channel_id=1, source_target_pairs={{0,16},{16,32},{32,48},{1,17},{17,33},{33,49},{2,18},{18,34},{34,5... | collective-permute-start | bytes 786440 | tf_op jit(solution)/shard_map/ppermute | solution.py:33
  34.4 10.0 %collective-permute-start.2 = (bf16[2,2,1,16,2048]{4,3,2,1,0:T(8,128)(2,1)S(1)}, bf16[2,2,1,16,2048]{4,3,2,1,0:T(8,128)(2,1)S(1)}, u32[]{:S(2)}, u32[]{:S(2)}) collective-permute-start(bf16[2,2,1,16,2048]{4,3,2,1,0:T(8,128)(2,1)S(1)} %get-tuple-element.48), channel_id=1, source_target_pairs={{16,0},{32,16},{48,32},{17,1},{33,17},{49,33},{18,2},{34,18},{50,3... | collective-permute-start | bytes 786440 | tf_op jit(solution)/shard_map/ppermute | solution.py:33
  37.8 19.8 %collective-permute-start.4 = (bf16[2,1,4,16,2048]{4,3,2,1,0:T(8,128)(2,1)}, bf16[2,1,4,16,2048]{4,3,2,1,0:T(8,128)(2,1)S(1)}, u32[]{:S(2)}, u32[]{:S(2)}) collective-permute-start(bf16[2,1,4,16,2048]{4,3,2,1,0:T(8,128)(2,1)} %get-tuple-element.45), channel_id=1, source_target_pairs={{64,0},{128,64},{192,128},{256,192},{320,256},{384,320},{448,384},... | collective-permute-start | bytes 1572872 | tf_op jit(solution)/shard_map/ppermute | solution.py:33
  41.4 16.2 %collective-permute-start = (bf16[2,1,4,16,2048]{4,3,2,1,0:T(8,128)(2,1)S(1)}, bf16[2,1,4,16,2048]{4,3,2,1,0:T(8,128)(2,1)S(1)}, u32[]{:S(2)}, u32[]{:S(2)}) collective-permute-start(bf16[2,1,4,16,2048]{4,3,2,1,0:T(8,128)(2,1)S(1)} %get-tuple-element.46), channel_id=1, source_target_pairs={{0,64},{64,128},{128,192},{192,256},{256,320},{320,384},{384,448},... | collective-permute-start | bytes 1572872 | tf_op jit(solution)/shard_map/ppermute | solution.py:33
  44.4 13.2 %copy-start.3 = (bf16[2,2,1,16,2048]{4,3,2,1,0:T(8,128)(2,1)}, bf16[2,2,1,16,2048]{4,3,2,1,0:T(8,128)(2,1)S(1)}, u32[]{:S(2)}) copy-start(bf16[2,2,1,16,2048]{4,3,2,1,0:T(8,128)(2,1)S(1)} %collective-permute-done.1.rest_5_) | copy-start | bytes 786436
  44.5 13.1 %copy-start.4 = (bf16[2,2,1,16,2048]{4,3,2,1,0:T(8,128)(2,1)}, bf16[2,2,1,16,2048]{4,3,2,1,0:T(8,128)(2,1)S(1)}, u32[]{:S(2)}) copy-start(bf16[2,2,1,16,2048]{4,3,2,1,0:T(8,128)(2,1)S(1)} %collective-permute-done.2.rest_6_) | copy-start | bytes 786436
  44.5 8.8 %collective-permute-start.3 = (bf16[2,1,2,16,2048]{4,3,2,1,0:T(8,128)(2,1)S(1)}, bf16[2,1,2,16,2048]{4,3,2,1,0:T(8,128)(2,1)S(1)}, u32[]{:S(2)}, u32[]{:S(2)}) collective-permute-start(bf16[2,1,2,16,2048]{4,3,2,1,0:T(8,128)(2,1)S(1)} %pad_maximum_fusion), channel_id=1, source_target_pairs={{0,64},{64,128},{128,192},{192,256},{256,320},{320,384},{384,448},... | collective-permute-start | bytes 786440 | tf_op jit(solution)/shard_map/ppermute | solution.py:33
  49.3 8.3 %collective-permute-start.5 = (bf16[2,1,2,16,2048]{4,3,2,1,0:T(8,128)(2,1)}, bf16[2,1,2,16,2048]{4,3,2,1,0:T(8,128)(2,1)S(1)}, u32[]{:S(2)}, u32[]{:S(2)}) collective-permute-start(bf16[2,1,2,16,2048]{4,3,2,1,0:T(8,128)(2,1)} %pad_maximum_fusion.1), channel_id=1, source_target_pairs={{64,0},{128,64},{192,128},{256,192},{320,256},{384,320},{448,384},... | collective-permute-start | bytes 786440 | tf_op jit(solution)/shard_map/ppermute | solution.py:33
  53.3 4.3 %copy-start.5 = (bf16[2,1,2,16,2048]{4,3,2,1,0:T(8,128)(2,1)}, bf16[2,1,2,16,2048]{4,3,2,1,0:T(8,128)(2,1)S(1)}, u32[]{:S(2)}) copy-start(bf16[2,1,2,16,2048]{4,3,2,1,0:T(8,128)(2,1)S(1)} %collective-permute-done.3.rest_2_) | copy-start | bytes 786436
  57.6 0.7 copy-start.6
  57.6 0.9 copy-start.1
  58.5 0.8 copy-start.2
  89.4 9.7 %collective-permute-start.6 = (bf16[2048,1024]{1,0:T(8,128)(2,1)}, bf16[2048,1024]{1,0:T(8,128)(2,1)}, u32[]{:S(2)}, u32[]{:S(2)}) collective-permute-start(bf16[2048,1024]{1,0:T(8,128)(2,1)} %bitcast.17), channel_id=1, source_target_pairs={{0,64},{64,0},{128,192},{192,128},{256,320},{320,256},{384,448},{4... | collective-permute-start | bytes 12582920 | tf_op jit(solution)/shard_map/ppermute | solution.py:426
  113.7 10.9 %collective-permute-start.9 = (bf16[2,1,2,16,2048]{4,3,2,1,0:T(8,128)(2,1)}, bf16[2,1,2,16,2048]{4,3,2,1,0:T(8,128)(2,1)S(1)}, u32[]{:S(2)}, u32[]{:S(2)}) collective-permute-start(bf16[2,1,2,16,2048]{4,3,2,1,0:T(8,128)(2,1)} %get-tuple-element.31), channel_id=1, source_target_pairs={{0,64},{64,128},{128,192},{192,256},{256,320},{320,384},{384,448},... | collective-permute-start | bytes 786440 | tf_op jit(solution)/shard_map/ppermute | solution.py:33
  117.0 7.9 %collective-permute-start.10 = (bf16[2,1,2,16,2048]{4,3,2,1,0:T(8,128)(2,1)}, bf16[2,1,2,16,2048]{4,3,2,1,0:T(8,128)(2,1)S(1)}, u32[]{:S(2)}, u32[]{:S(2)}) collective-permute-start(bf16[2,1,2,16,2048]{4,3,2,1,0:T(8,128)(2,1)} %get-tuple-element.32), channel_id=1, source_target_pairs={{64,0},{128,64},{192,128},{256,192},{320,256},{384,320},{448,384},... | collective-permute-start | bytes 786440 | tf_op jit(solution)/shard_map/ppermute | solution.py:33
  119.0 11.7 %collective-permute-start.7 = (bf16[2,1,4,16,2048]{4,3,2,1,0:T(8,128)(2,1)}, bf16[2,1,4,16,2048]{4,3,2,1,0:T(8,128)(2,1)S(1)}, u32[]{:S(2)}, u32[]{:S(2)}) collective-permute-start(bf16[2,1,4,16,2048]{4,3,2,1,0:T(8,128)(2,1)} %get-tuple-element.28), channel_id=1, source_target_pairs={{0,64},{64,128},{128,192},{192,256},{256,320},{320,384},{384,448},... | collective-permute-start | bytes 1572872 | tf_op jit(solution)/shard_map/ppermute | solution.py:33
  122.6 11.0 %collective-permute-start.8 = (bf16[2,1,4,16,2048]{4,3,2,1,0:T(8,128)(2,1)}, bf16[2,1,4,16,2048]{4,3,2,1,0:T(8,128)(2,1)S(1)}, u32[]{:S(2)}, u32[]{:S(2)}) collective-permute-start(bf16[2,1,4,16,2048]{4,3,2,1,0:T(8,128)(2,1)} %get-tuple-element.29), channel_id=1, source_target_pairs={{64,0},{128,64},{192,128},{256,192},{320,256},{384,320},{448,384},... | collective-permute-start | bytes 1572872 | tf_op jit(solution)/shard_map/ppermute | solution.py:33
  126.0 12.7 %collective-permute-start.11 = (bf16[2,2,1,16,2048]{4,3,2,1,0:T(8,128)(2,1)S(1)}, bf16[2,2,1,16,2048]{4,3,2,1,0:T(8,128)(2,1)S(1)}, u32[]{:S(2)}, u32[]{:S(2)}) collective-permute-start(bf16[2,2,1,16,2048]{4,3,2,1,0:T(8,128)(2,1)S(1)} %get-tuple-element.35), channel_id=1, source_target_pairs={{0,16},{16,32},{32,48},{1,17},{17,33},{33,49},{2,18},{18,34},{34,5... | collective-permute-start | bytes 786440 | tf_op jit(solution)/shard_map/ppermute | solution.py:33
  129.3 9.4 %collective-permute-start.12 = (bf16[2,2,1,16,2048]{4,3,2,1,0:T(8,128)(2,1)S(1)}, bf16[2,2,1,16,2048]{4,3,2,1,0:T(8,128)(2,1)S(1)}, u32[]{:S(2)}, u32[]{:S(2)}) collective-permute-start(bf16[2,2,1,16,2048]{4,3,2,1,0:T(8,128)(2,1)S(1)} %get-tuple-element.36), channel_id=1, source_target_pairs={{16,0},{32,16},{48,32},{17,1},{33,17},{49,33},{18,2},{34,18},{50,3... | collective-permute-start | bytes 786440 | tf_op jit(solution)/shard_map/ppermute | solution.py:33
Sparse Core Ops, SparseCore 0:
  24.0 65.3 all-gather.3

commit v6 on v5

--- a/solution.py
+++ b/solution.py
@@ -11,9 +11,8 @@
 BY = 4
 TOK = BX * BY * BS
 GROUP = 4
-VMEM_LIMIT = 60 * 1024 * 1024
+VMEM_LIMIT = 24 * 1024 * 1024
 SMALL_LIMIT = 12 * 1024 * 1024
-OWN_LIMIT = 57 * 1024 * 1024
 
 LOCAL = [(x, y) for x in range(BX) for y in range(BY)]
 XLOW = [(-1, y) for y in range(BY)]
@@ -31,6 +30,10 @@
     count = lax.axis_size(axis)
     pairs = [(i, i + step) for i in range(count) if 0 <= i + step < count]
     return lax.ppermute(value, axis, pairs)
+
+
+def in_vmem(*values):
+    return tuple(pltpu.with_memory_space_constraint(value, pltpu.VMEM) for value in values)
 
 
 def dot(a, b, dims):
@@ -128,15 +131,17 @@
 
 
 def project_own_kernel(att_ref, w_hbm, part_ref, w_ref, sems):
-    chunks = w_ref.shape[0]
-    rows = w_ref.shape[1]
-    copies = [pltpu.make_async_copy(w_hbm.at[pl.ds(k * rows, rows)], w_ref.at[k], sems.at[k]) for k in range(chunks)]
+    chunks = 4
+    rows = w_ref.shape[0] // chunks
+    parts = [pl.ds(k * rows, rows) for k in range(chunks)]
+    copies = [pltpu.make_async_copy(w_hbm.at[part], w_ref.at[part], sems.at[k]) for k, part in enumerate(parts)]
     for copy in copies:
         copy.start()
     total = None
     for k in range(chunks):
         copies[k].wait()
-        term = dot(att_ref[:, k * rows : (k + 1) * rows], w_ref[k], ((1,), (0,)))
+        lanes = slice(k * rows, (k + 1) * rows)
+        term = dot(att_ref[:, lanes], w_ref[lanes, :], ((1,), (0,)))
         total = term if total is None else total + term
     part_ref[...] = total
 
@@ -144,36 +149,34 @@
 def project_own(att, own):
     vmem = pl.BlockSpec(memory_space=pltpu.VMEM)
     tokens = att.shape[0]
-    inner, cols = own.shape
-    chunks = 4
+    cols = own.shape[1]
     return pl.pallas_call(
         project_own_kernel,
         in_specs=[vmem, pl.BlockSpec(memory_space=pl.ANY)],
-        out_specs=vmem,
-        out_shape=jax.ShapeDtypeStruct((tokens, cols), jnp.float32),
-        scratch_shapes=[
-            pltpu.VMEM((chunks, inner // chunks, cols), jnp.bfloat16),
-            pltpu.SemaphoreType.DMA((chunks,)),
-        ],
+        out_specs=[vmem, vmem],
+        out_shape=[jax.ShapeDtypeStruct((tokens, cols), jnp.float32), jax.ShapeDtypeStruct(own.shape, own.dtype)],
+        scratch_shapes=[pltpu.SemaphoreType.DMA((4,))],
         compiler_params=pltpu.CompilerParams(vmem_limit_bytes=VMEM_LIMIT),
         name="project_own",
-    )(att, own)
+    )(att, pltpu.with_memory_space_constraint(own, pltpu.HBM))
 
 
 def project_kernel(
-    bound_ref, pos_ref, att_ref, part_ref, own_hbm, swap_hbm, gain_ref, read_ref, cot_ref,
-    pred_ref, ga_ref, swap_ref, own_ref, proj_ref, gp_ref, sems,
+    bound_ref, pos_ref, att_ref, part_ref, own_ref, swap_hbm, gain_ref, read_ref, cot_ref,
+    pred_ref, ga_ref, swap_ref, proj_ref, gp_ref, sems,
 ):
-    chunks, rows, cols = swap_ref.shape
-    copies = [pltpu.make_async_copy(swap_hbm.at[pl.ds(k * rows, rows)], swap_ref.at[k], sems.at[k]) for k in range(chunks)]
-    own_copy = pltpu.make_async_copy(own_hbm, own_ref, sems.at[chunks])
+    cols = swap_ref.shape[1]
+    chunks = 4
+    rows = swap_ref.shape[0] // chunks
+    parts = [pl.ds(k * rows, rows) for k in range(chunks)]
+    copies = [pltpu.make_async_copy(swap_hbm.at[part], swap_ref.at[part], sems.at[k]) for k, part in enumerate(parts)]
     for copy in copies:
         copy.start()
-    own_copy.start()
     total = None
     for k in range(chunks):
         copies[k].wait()
-        term = dot(att_ref[:, k * rows : (k + 1) * rows], swap_ref[k], ((1,), (0,)))
+        lanes = slice(k * rows, (k + 1) * rows)
+        term = dot(att_ref[:, lanes], swap_ref[lanes, :], ((1,), (0,)))
         total = term if total is None else total + term
     proj_ref[:, side_cols(pos_ref, 0, cols)] = part_ref[...]
     proj_ref[:, side_cols(pos_ref, 1, cols)] = total
@@ -200,41 +203,44 @@
         gp_ref[rows_of, :] = (inv_rms * gained - proj * (inv_rms * inv_rms * inv_rms * inner_mean)).astype(jnp.bfloat16)
     gp_own = gp_ref[:, side_cols(pos_ref, 0, cols)]
     gp_swap = gp_ref[:, side_cols(pos_ref, 1, cols)]
-    own_copy.wait()
     for k in range(chunks):
         lanes = slice(k * rows, (k + 1) * rows)
-        total = dot(gp_swap, swap_ref[k], ((1,), (1,))) + dot(gp_own, own_ref[lanes, :], ((1,), (1,)))
+        total = dot(gp_swap, swap_ref[lanes, :], ((1,), (1,))) + dot(gp_own, own_ref[lanes, :], ((1,), (1,)))
         ga_ref[:, lanes] = total.astype(jnp.bfloat16)
 
 
 def project(boundary, position, att, part, own, swapped, gain, read_rows, cotangent):
     vmem = pl.BlockSpec(memory_space=pltpu.VMEM)
     smem = pl.BlockSpec(memory_space=pltpu.SMEM)
-    hbm = pl.BlockSpec(memory_space=pl.ANY)
-    inner, cols = own.shape
-    chunks = 4
     return pl.pallas_call(
         project_kernel,
-        in_specs=[smem, smem, vmem, vmem, hbm, hbm, vmem, vmem, vmem],
+        in_specs=[smem, smem, vmem, vmem, vmem, pl.BlockSpec(memory_space=pl.ANY), vmem, vmem, vmem],
         out_specs=[vmem, vmem],
         out_shape=[
             jax.ShapeDtypeStruct(cotangent.shape[:3] + (2, BS), jnp.float32),
             jax.ShapeDtypeStruct(att.shape, jnp.bfloat16),
         ],
         scratch_shapes=[
-            pltpu.VMEM((chunks, inner // chunks, cols), jnp.bfloat16),
-            pltpu.VMEM(own.shape, jnp.bfloat16),
+            pltpu.VMEM(swapped.shape, jnp.bfloat16),
             pltpu.VMEM(att.shape, jnp.float32),
             pltpu.VMEM(att.shape, jnp.bfloat16),
-            pltpu.SemaphoreType.DMA((chunks + 1,)),
+            pltpu.SemaphoreType.DMA((4,)),
         ],
         compiler_params=pltpu.CompilerParams(vmem_limit_bytes=VMEM_LIMIT),
         name="project",
-    )(boundary, position, att, part, own, swapped, gain, read_rows, cotangent)
-
-
-def value_rows(refs, lanes):
-    return jnp.concatenate([ref[0, :, :, :, lanes].reshape(-1, HS) for ref in refs], axis=0)
+    )(
+        boundary,
+        position,
+        *in_vmem(att, part, own),
+        pltpu.with_memory_space_constraint(swapped, pltpu.HBM),
+        gain,
+        read_rows,
+        cotangent,
+    )
+
+
+def kv_rows(refs, which, lanes):
+    return jnp.concatenate([ref[which, :, :, :, lanes].reshape(-1, HS) for ref in refs], axis=0)
 
 
 def back_rim_kernel(q_ref, ga_ref, prob_ref, *rest):
@@ -242,10 +248,10 @@
     v_refs = rest[:count]
     gs_ref = rest[count]
     rim_refs = rest[count + 1 :]
-    for h in range(GROUP):
+    for h in range(prob_ref.shape[0]):
         lanes = slice(h * HS, (h + 1) * HS)
         query = q_ref[0, :, :, :, lanes].reshape(TOK, HS)
-        values = value_rows(v_refs, lanes)
+        values = kv_rows(v_refs, 1, lanes)
         grad_att = ga_ref[:, lanes]
         prob = prob_ref[h]
         grad_prob = dot(values, grad_att, ((1,), (1,)))
@@ -263,43 +269,31 @@
                 start += rows
 
 
-def lane_block(shape, width):
-    return pl.BlockSpec(tuple(shape[:-1]) + (width,), lambda g: (0,) * (len(shape) - 1) + (g,))
-
-
-def half_block(shape, which, width):
-    return pl.BlockSpec((1,) + tuple(shape[1:-1]) + (width,), lambda g: (which,) + (0,) * (len(shape) - 2) + (g,))
-
-
 def back_rim(queries, grad_att, prob, pieces):
-    inner = queries.shape[-1]
-    width = GROUP * HS
+    vmem = pl.BlockSpec(memory_space=pltpu.VMEM)
     shapes = [p.shape for p in pieces]
-    heads = pl.BlockSpec((GROUP, KEYS, TOK), lambda g: (g, 0, 0))
     return pl.pallas_call(
         back_rim_kernel,
-        grid=(inner // width,),
-        in_specs=[lane_block(queries.shape, width), lane_block(grad_att.shape, width), heads]
-        + [half_block(s, 1, width) for s in shapes],
-        out_specs=[heads] + [lane_block(s, width) for s in shapes[1:]],
+        in_specs=[vmem] * (3 + len(pieces)),
+        out_specs=[vmem] * len(pieces),
         out_shape=[jax.ShapeDtypeStruct(prob.shape, jnp.bfloat16)]
         + [jax.ShapeDtypeStruct(s, jnp.bfloat16) for s in shapes[1:]],
         compiler_params=pltpu.CompilerParams(vmem_limit_bytes=VMEM_LIMIT),
         name="back_rim",
-    )(queries, grad_att, prob, *pieces)
+    )(*in_vmem(queries, grad_att, prob, *pieces))
 
 
 def back_own_kernel(q_ref, ga_ref, prob_ref, gs_ref, *rest):
     count = len(PIECES)
     k_refs = rest[:count]
     low_ref, high_ref, gq_ref, out_ref, edge_ref = rest[count:]
-    for h in range(GROUP):
+    for h in range(prob_ref.shape[0]):
         lanes = slice(h * HS, (h + 1) * HS)
         query = q_ref[0, :, :, :, lanes].reshape(TOK, HS)
         grad_scores = gs_ref[h]
-        grad_query = dot(grad_scores, value_rows(k_refs, lanes), ((0,), (0,)))
+        grad_query = dot(grad_scores, kv_rows(k_refs, 0, lanes), ((0,), (0,)))
         gq_ref[0, :, :, :, lanes] = grad_query.reshape(BX, BY, BS, HS).astype(gq_ref.dtype)
-        half = prob_ref[h].astype(jnp.bfloat16)
+        half = prob_ref[h, :TOK, :].astype(jnp.bfloat16)
         grads = (dot(grad_scores[:TOK], query, ((1,), (0,))), dot(half, ga_ref[:, lanes], ((1,), (0,))))
         for which, grad in enumerate(grads):
             for block, (x, y) in enumerate(LOCAL):
@@ -315,88 +309,57 @@
 
 
 def back_own(queries, grad_att, prob, grad_scores, pieces, low, high):
-    inner = queries.shape[-1]
-    width = GROUP * HS
-    shapes = [p.shape for p in pieces]
-    edge = shapes[0][:2] + (2,) + shapes[0][3:]
+    vmem = pl.BlockSpec(memory_space=pltpu.VMEM)
+    own = pieces[0].shape
+    edge = own[:2] + (2,) + own[3:]
     return pl.pallas_call(
         back_own_kernel,
-        grid=(inner // width,),
-        in_specs=[
-            lane_block(queries.shape, width),
-            lane_block(grad_att.shape, width),
-            pl.BlockSpec((GROUP, TOK, TOK), lambda g: (g, 0, 0)),
-            pl.BlockSpec((GROUP, KEYS, TOK), lambda g: (g, 0, 0)),
-        ]
-        + [half_block(s, 0, width) for s in shapes]
-        + [lane_block(low.shape, width), lane_block(high.shape, width)],
-        out_specs=[lane_block(queries.shape, width), lane_block(shapes[0], width), lane_block(edge, width)],
+        in_specs=[vmem] * (6 + len(pieces)),
+        out_specs=[vmem] * 3,
         out_shape=[
             jax.ShapeDtypeStruct(queries.shape, jnp.bfloat16),
-            jax.ShapeDtypeStruct(shapes[0], jnp.bfloat16),
+            jax.ShapeDtypeStruct(own, jnp.bfloat16),
             jax.ShapeDtypeStruct(edge, jnp.float32),
         ],
-        compiler_params=pltpu.CompilerParams(vmem_limit_bytes=OWN_LIMIT),
+        compiler_params=pltpu.CompilerParams(vmem_limit_bytes=VMEM_LIMIT),
         name="back_own",
-    )(
-        queries,
-        grad_att,
-        prob,
-        grad_scores,
-        *pieces,
-        *(pltpu.with_memory_space_constraint(term, pltpu.VMEM) for term in (low, high)),
-    )
-
-
-def sides_kernel(from_low_ref, from_high_ref, low_hbm, high_hbm, left_ref, right_ref, rim_ref, sems):
+    )(*in_vmem(queries, grad_att, prob, grad_scores, *pieces, low, high))
+
+
+def sides_kernel(from_low_ref, from_high_ref, low_ref, high_ref, left_ref, right_ref):
     f32 = jnp.float32
-    copies = [
-        pltpu.make_async_copy(low_hbm, rim_ref.at[0], sems.at[0]),
-        pltpu.make_async_copy(high_hbm, rim_ref.at[1], sems.at[1]),
-    ]
-    for copy in copies:
-        copy.start()
-    for y, out in ((0, left_ref), (1, right_ref)):
-        copies[y].wait()
+    for y, rim, out in ((0, low_ref, left_ref), (1, high_ref, right_ref)):
         for which in range(2):
-            first = rim_ref[y, which, 0, 0].astype(f32) + from_low_ref[which, 0, y].astype(f32)
-            last = rim_ref[y, which, BX - 1, 0].astype(f32) + from_high_ref[which, 0, y].astype(f32)
+            first = rim[which, 0, 0].astype(f32) + from_low_ref[which, 0, y].astype(f32)
+            last = rim[which, BX - 1, 0].astype(f32) + from_high_ref[which, 0, y].astype(f32)
             out[which, 0, 0] = first.astype(out.dtype)
             out[which, BX - 1, 0] = last.astype(out.dtype)
 
 
 def sides(from_low, from_high, low, high):
     vmem = pl.BlockSpec(memory_space=pltpu.VMEM)
-    hbm = pl.BlockSpec(memory_space=pltpu.HBM)
     shape = jax.ShapeDtypeStruct(low.shape, low.dtype)
     return pl.pallas_call(
         sides_kernel,
-        in_specs=[vmem, vmem, hbm, hbm],
+        in_specs=[vmem] * 4,
         out_specs=[vmem, vmem],
         out_shape=[shape, shape],
-        scratch_shapes=[pltpu.VMEM((2,) + low.shape, low.dtype), pltpu.SemaphoreType.DMA((2,))],
         compiler_params=pltpu.CompilerParams(vmem_limit_bytes=SMALL_LIMIT),
         name="sides",
-    )(from_low, from_high, *(pltpu.with_memory_space_constraint(rim, pltpu.HBM) for rim in (low, high)))
-
-
-def add_columns_kernel(low_ref, high_ref, edge_hbm, partial_hbm, out_hbm, edge_ref, sum_ref, sems):
+    )(*in_vmem(from_low, from_high, low, high))
+
+
+def add_columns_kernel(low_ref, high_ref, edge_ref, partial_hbm, out_hbm, sum_ref, sems):
     del partial_hbm
-    loads = [pltpu.make_async_copy(edge_hbm.at[i], edge_ref.at[i], sems.at[i]) for i in range(2)]
-    for load in loads:
-        load.start()
     stores = []
     for which in range(2):
-        loads[which].wait()
         for side, ref in enumerate((low_ref, high_ref)):
             for x in range(BX):
                 total = edge_ref[which, x, side] + ref[which, x, 0].astype(jnp.float32)
                 sum_ref[which, side, x] = total.astype(sum_ref.dtype)
                 y = side * (BY - 1)
                 index = (which * 2 + side) * BX + x
-                store = pltpu.make_async_copy(
-                    sum_ref.at[which, side, x], out_hbm.at[which, x, y], sems.at[2 + index]
-                )
+                store = pltpu.make_async_copy(sum_ref.at[which, side, x], out_hbm.at[which, x, y], sems.at[index])
                 store.start()
                 stores.append(store)
     for store in stores:
@@ -408,18 +371,17 @@
     hbm = pl.BlockSpec(memory_space=pltpu.HBM)
     return pl.pallas_call(
         add_columns_kernel,
-        in_specs=[vmem, vmem, hbm, hbm],
+        in_specs=[vmem, vmem, vmem, hbm],
         out_specs=hbm,
         out_shape=jax.ShapeDtypeStruct(partial.shape, partial.dtype),
         scratch_shapes=[
-            pltpu.VMEM(edge.shape, jnp.float32),
             pltpu.VMEM((2, 2, BX) + edge.shape[3:], partial.dtype),
-            pltpu.SemaphoreType.DMA((2 + 4 * BX,)),
+            pltpu.SemaphoreType.DMA((4 * BX,)),
         ],
         input_output_aliases={3: 0},
         compiler_params=pltpu.CompilerParams(vmem_limit_bytes=SMALL_LIMIT),
         name="add_columns",
-    )(low, high, *(pltpu.with_memory_space_constraint(term, pltpu.HBM) for term in (edge, partial)))
+    )(*in_vmem(low, high, edge), pltpu.with_memory_space_constraint(partial, pltpu.HBM))
 
 
 def swap_cores(value):
@@ -458,7 +420,7 @@
     att, prob = forward(adjacency, position, queries, pieces)
     own_cols, att = lax.optimization_barrier((own_cols, att))
     swapped = swap_cores(own_cols)
-    part = project_own(att, own_cols)
+    part, own_cols = project_own(att, own_cols)
     prediction, grad_att = project(
         boundary, position, att, part, own_cols, swapped, gain[None], read_weight.T, cotangent
     )

time: 149 us -> 143 us (0.960)
  Pallas kernels: 32.8 us -> 23 us
  local copies, waits for them, and re-layouts: 6.64 us -> 9.61 us
  waiting for transfers between devices: 35.5 us -> 37.9 us
    pallas_call x5, Pallas kernels: 22.8 us -> 16 us  [the longest x1 7.4 us: project(): pl.pallas_call(project_kernel, in_specs=[smem, smem, vmem, vmem, vmem, pl...]
    ppermute x12, waiting for transfers between devices: 9.07 us -> 12 us  [shift(): return lax.ppermute(value, axis, pairs)]
    unnamed x17 -> x33, local copies, waits for them, and re-layouts: 3.42 us -> 6.19 us
    all_gather x1, waiting for transfers between devices: 24.4 us -> 22.6 us  [body(): lax.all_gather(both, 'wa', axis=0, axis_index_groups=rings)]
    pallas_call x1, Pallas kernels: 4.35 us -> 2.58 us  [project_own(): pl.pallas_call(project_own_kernel, in_specs=[vmem, pl.BlockSpec(memory_sp...]
  transfers between devices with their start and end apart: 14 -> 14, of which waited for: 6 -> 6; matrix products, arithmetic and copies ran while one was open for 4% -> 4% of each run, Pallas kernels for 11% -> 7%
where the time goes in v6:
time: 143 us; the launch traced here: 142 us
  starting transfers between devices  40.2 us (28%)
  waiting for transfers between devices  37.9 us (27%)
  Pallas kernels  23 us (16%)
  blocking collectives  15.6 us (11%)
  between operations  14.4 us (10%)
  local copies, waits for them, and re-layouts  9.61 us (7%)
  other arithmetic  1.55 us (1%)
    ppermute x12, starting transfers between devices, shift(): return lax.ppermute(value, axis, pairs)  37.6 us
    all_gather x1, waiting for transfers between devices, body(): lax.all_gather(both, 'wa', axis=0, axis_index_groups=rings)  22.6 us
    all_gather x1, blocking collectives, body(): both = lax.all_gather(slab, 'wa', axis=0, axis_index_groups=pairs)  15.6 us
    ppermute x12, waiting for transfers between devices, shift(): return lax.ppermute(value, axis, pairs)  12 us
    pallas_call x1, Pallas kernels, project(): pl.pallas_call(project_kernel, in_specs=[smem, smem, vmem, vmem, vmem, pl...  7.4 us
    unnamed x33, local copies, waits for them, and re-layouts  6.19 us
    pallas_call x1, Pallas kernels, back_rim(): pl.pallas_call(back_rim_kernel, in_specs=[vmem] * (3 + len(pieces)), out_...  4.55 us
    pallas_call x1, Pallas kernels, forward(): pl.pallas_call(forward_kernel, grid=(inner // width,), in_specs=[smem, sm...  4.34 us
  transfers between devices with their start and end apart: 14, of which 6 were waited for; matrix products, arithmetic and copies ran while one was open for 4% of the time, Pallas kernels for 7%

profile of v6, /device:TPU:1, one launch (start us, length us, event | category | flops | bytes accessed | tf_op | source)
XLA Modules:
  0.0 142.3 jit_solution(8445271801517525519)
XLA Ops:
  7.2 0.0 copy-start
  7.2 0.0 copy-start.1
  7.2 0.0 copy-start.13
  7.2 0.0 copy-start.4
  7.2 0.0 all-gather.4.cloned.1.call-start
  7.3 0.9 copy-done
  8.2 15.6 %all-gather = bf16[256,1024]{1,0:T(8,128)(2,1)} all-gather(bf16[128,1024]{1,0:T(8,128)(2,1)S(1)} %constant_dynamic-slice_fusion), channel_id=2, replica_groups={{0,1},{2,3},{4,5},{6,7},{8,9},{10,11},{12,13},{14,15},{16,17},{18,19},{..., dimensions={0}, use_global_device_ids=true | all-gather | bytes 786432 | tf_op jit(solution)/shard_map/all_gather | solution.py:402
  23.9 0.0 all-gather.4.cloned.1.call-update
  23.9 1.1 fusion.1
  25.0 0.0 copy-start.15
  25.0 9.5 %collective-permute-start.1 = (bf16[2,2,1,16,2048]{4,3,2,1,0:T(8,128)(2,1)S(1)}, bf16[2,2,1,16,2048]{4,3,2,1,0:T(8,128)(2,1)S(1)}, u32[]{:S(2)}, u32[]{:S(2)}) collective-permute-start(bf16[2,2,1,16,2048]{4,3,2,1,0:T(8,128)(2,1)S(1)} %get-tuple-element.51), channel_id=1, source_target_pairs={{0,16},{16,32},{32,48},{1,17},{17,33},{33,49},{2,18},{18,34},{34,5... | collective-permute-start | bytes 786440 | tf_op jit(solution)/shard_map/ppermute | solution.py:32
  34.4 1.3 collective-permute-start.2
  35.7 2.3 %fusion = (bf16[2,1,4,16,2048]{4,3,2,1,0:T(8,128)(2,1)}, bf16[2,1,4,16,2048]{4,3,2,1,0:T(8,128)(2,1)}) fusion(bf16[2,2,4,16,2048]{4,3,2,1,0:T(8,128)(2,1)} %bitcast.13), kind=kLoop, calls=%fused_computation.4 | loop fusion | bytes 2097152 | tf_op jit(solution)/shard_map/slice | solution.py:407
  38.0 4.7 %collective-permute-start = (bf16[2,1,4,16,2048]{4,3,2,1,0:T(8,128)(2,1)}, bf16[2,1,4,16,2048]{4,3,2,1,0:T(8,128)(2,1)S(1)}, u32[]{:S(2)}, u32[]{:S(2)}) collective-permute-start(bf16[2,1,4,16,2048]{4,3,2,1,0:T(8,128)(2,1)} %get-tuple-element.50), channel_id=1, source_target_pairs={{0,64},{64,128},{128,192},{192,256},{256,320},{320,384},{384,448},... | collective-permute-start | bytes 1572872 | tf_op jit(solution)/shard_map/ppermute | solution.py:32
  42.7 1.9 %collective-permute-start.4 = (bf16[2,1,4,16,2048]{4,3,2,1,0:T(8,128)(2,1)}, bf16[2,1,4,16,2048]{4,3,2,1,0:T(8,128)(2,1)S(1)}, u32[]{:S(2)}, u32[]{:S(2)}) collective-permute-start(bf16[2,1,4,16,2048]{4,3,2,1,0:T(8,128)(2,1)} %get-tuple-element.49), channel_id=1, source_target_pairs={{64,0},{128,64},{192,128},{256,192},{320,256},{384,320},{448,384},... | collective-permute-start | bytes 1572872 | tf_op jit(solution)/shard_map/ppermute | solution.py:32
  44.6 0.0 collective-permute-done.1.rest_5_
  44.6 0.0 collective-permute-done.2.rest_6_
  44.7 0.0 copy-start.5
  44.7 0.7 copy-done.5
  45.4 0.7 pad_maximum_fusion
  46.1 3.8 %collective-permute-start.3 = (bf16[2,1,2,16,2048]{4,3,2,1,0:T(8,128)(2,1)}, bf16[2,1,2,16,2048]{4,3,2,1,0:T(8,128)(2,1)}, u32[]{:S(2)}, u32[]{:S(2)}) collective-permute-start(bf16[2,1,2,16,2048]{4,3,2,1,0:T(8,128)(2,1)} %pad_maximum_fusion), channel_id=1, source_target_pairs={{0,64},{64,128},{128,192},{192,256},{256,320},{320,384},{384,448},... | collective-permute-start | bytes 786440 | tf_op jit(solution)/shard_map/ppermute | solution.py:32
  50.0 0.7 pad_maximum_fusion.1
  50.7 1.9 %collective-permute-start.5 = (bf16[2,1,2,16,2048]{4,3,2,1,0:T(8,128)(2,1)}, bf16[2,1,2,16,2048]{4,3,2,1,0:T(8,128)(2,1)}, u32[]{:S(2)}, u32[]{:S(2)}) collective-permute-start(bf16[2,1,2,16,2048]{4,3,2,1,0:T(8,128)(2,1)} %pad_maximum_fusion.1), channel_id=1, source_target_pairs={{64,0},{128,64},{192,128},{256,192},{320,256},{384,320},{448,384},... | collective-permute-start | bytes 786440 | tf_op jit(solution)/shard_map/ppermute | solution.py:32
  52.6 0.0 copy-start.14
  52.6 0.1 pad_add_fusion.pos_ref
  52.7 0.9 collective-permute-done.3.rest_2_
  53.6 5.4 %collective-permute-done.5.rest_4_ = bf16[2,1,2,16,2048]{4,3,2,1,0:T(8,128)(2,1)} collective-permute-done((bf16[2,1,2,16,2048]{4,3,2,1,0:T(8,128)(2,1)}, bf16[2,1,2,16,2048]{4,3,2,1,0:T(8,128)(2,1)}, u32[]{:S(2)}, u32[]{:S(2)}) %collective-permute-start.5) | collective-permute-done | bytes 262176 | tf_op jit(solution)/shard_map/ppermute | solution.py:32
  59.0 0.0 collective-permute-done.rest_1_
  59.0 0.0 collective-permute-done.4.rest_3_
  59.0 0.0 copy-done.1
  59.0 0.0 copy-done.13
  59.0 0.0 copy-done.4
  59.0 0.0 copy-start.6
  59.0 0.9 copy-done.6
  60.0 4.3 %attend.1 = (bf16[128,2048]{1,0:T(8,128)(2,1)S(1)}, f32[16,384,128]{2,1,0:T(8,128)S(1)}) custom-call(s32[1,2,4,4]{3,2,1,0:T(4,128)S(1)} %copy-done.13, s32[5]{0:T(128)S(1)} %pad_add_fusion.pos_ref, bf16[1,2,4,16,2048]{4,3,2,1,0:T(8,128)(2,1)S(1)} %copy-done.4, bf16[2,2,4,16,2048]{4,3,2,1,0:T(8,128)(2,1)S(1)} %bitcast.14, ...), custom_call_target="tpu_custom_call" | custom-call | tf_op jit(solution)/shard_map/attend/pallas_call | solution.py:110
  64.3 0.0 copy-start.2
  64.3 1.6 %copy-done.2 = f32[16,384,128]{2,1,0:T(8,128)} copy-done((f32[16,384,128]{2,1,0:T(8,128)}, f32[16,384,128]{2,1,0:T(8,128)S(1)}, u32[]{:S(2)}) %copy-start.2) | copy-done | bytes 3145752
  66.0 0.8 copy-done.8
  66.7 22.6 %all-gather.4.cloned.1.call-done = bf16[16,128,1024]{2,1,0:T(8,128)(2,1)} async-done(((bf16[2,128,1024]{2,1,0:T(8,128)(2,1)}), bf16[16,128,1024]{2,1,0:T(8,128)(2,1)}) %all-gather.4.cloned.1.call-update) | async-done | bytes 4194320 | tf_op jit(solution)/shard_map/all_gather | solution.py:403
  89.4 2.6 %collective-permute-start.6 = (bf16[2048,1024]{1,0:T(8,128)(2,1)}, bf16[2048,1024]{1,0:T(8,128)(2,1)}, u32[]{:S(2)}, u32[]{:S(2)}) collective-permute-start(bf16[2048,1024]{1,0:T(8,128)(2,1)} %bitcast.19), channel_id=1, source_target_pairs={{0,64},{64,0},{128,192},{192,128},{256,320},{320,256},{384,448},{4... | collective-permute-start | bytes 12582920 | tf_op jit(solution)/shard_map/ppermute | solution.py:388
  91.9 0.0 copy-done.15
  91.9 0.1 copy.14.cot_ref
  92.1 1.0 copy-done.9
  93.1 2.6 %project_own.1 = (f32[128,1024]{1,0:T(8,128)S(1)}, bf16[2048,1024]{1,0:T(8,128)(2,1)S(1)}) custom-call(bf16[128,2048]{1,0:T(8,128)(2,1)S(1)} %copy-done.9, bf16[2048,1024]{1,0:T(8,128)(2,1)} %bitcast.20), custom_call_target="tpu_custom_call" | custom-call | tf_op jit(solution)/shard_map/project_own/pallas_call | solution.py:153
  95.7 3.3 %collective-permute-done.6.swap_hbm = bf16[2048,1024]{1,0:T(8,128)(2,1)} collective-permute-done((bf16[2048,1024]{1,0:T(8,128)(2,1)}, bf16[2048,1024]{1,0:T(8,128)(2,1)}, u32[]{:S(2)}, u32[]{:S(2)}) %collective-permute-start.6) | collective-permute-done | bytes 4194336 | tf_op jit(solution)/shard_map/ppermute | solution.py:388
  99.0 0.0 copy-done.14
  99.1 0.0 copy-done.10
  99.1 7.4 %project.1 = (f32[1,2,4,2,16]{4,3,2,1,0:T(2,128)}, bf16[128,2048]{1,0:T(8,128)(2,1)S(1)}) custom-call(s32[1,2,4]{2,1,0:T(2,128)S(1)} %copy-done.14, s32[5]{0:T(128)S(1)} %pad_add_fusion.pos_ref, bf16[128,2048]{1,0:T(8,128)(2,1)S(1)} %copy-done.10, f32[128,1024]{1,0:T(8,128)S(1)} %get-tuple-element.26.part_ref, ...), custom_call_target="tpu_custom_call" | custom-call | tf_op jit(solution)/shard_map/project/pallas_call | solution.py:215
  106.5 4.5 %back_rim.1 = (bf16[16,384,128]{2,1,0:T(8,128)(2,1)S(1)}, bf16[2,1,4,16,2048]{4,3,2,1,0:T(8,128)(2,1)S(1)}, bf16[2,1,2,16,2048]{4,3,2,1,0:T(8,128)(2,1)S(1)}, bf...) custom-call(bf16[1,2,4,16,2048]{4,3,2,1,0:T(8,128)(2,1)S(1)} %copy-d, ...), custom_call_target="tpu_custom_call" | custom-call | tf_op jit(solution)/shard_map/back_rim/pallas_call | solution.py:275
  111.1 2.3 %collective-permute-start.10 = (bf16[2,1,2,16,2048]{4,3,2,1,0:T(8,128)(2,1)S(1)}, bf16[2,1,2,16,2048]{4,3,2,1,0:T(8,128)(2,1)S(1)}, u32[]{:S(2)}, u32[]{:S(2)}) collective-permute-start(bf16[2,1,2,16,2048]{4,3,2,1,0:T(8,128)(2,1)S(1)} %get-tuple-element.36), channel_id=1, source_target_pairs={{64,0},{128,64},{192,128},{256,192},{320,256},{384,320},{448,384},... | collective-permute-start | bytes 786440 | tf_op jit(solution)/shard_map/ppermute | solution.py:32
  113.4 3.3 %collective-permute-start.9 = (bf16[2,1,2,16,2048]{4,3,2,1,0:T(8,128)(2,1)S(1)}, bf16[2,1,2,16,2048]{4,3,2,1,0:T(8,128)(2,1)S(1)}, u32[]{:S(2)}, u32[]{:S(2)}) collective-permute-start(bf16[2,1,2,16,2048]{4,3,2,1,0:T(8,128)(2,1)S(1)} %get-tuple-element.35), channel_id=1, source_target_pairs={{0,64},{64,128},{128,192},{192,256},{256,320},{320,384},{384,448},... | collective-permute-start | bytes 786440 | tf_op jit(solution)/shard_map/ppermute | solution.py:32
  116.6 2.1 %collective-permute-start.7 = (bf16[2,1,4,16,2048]{4,3,2,1,0:T(8,128)(2,1)S(1)}, bf16[2,1,4,16,2048]{4,3,2,1,0:T(8,128)(2,1)S(1)}, u32[]{:S(2)}, u32[]{:S(2)}) collective-permute-start(bf16[2,1,4,16,2048]{4,3,2,1,0:T(8,128)(2,1)S(1)} %get-tuple-element.32), channel_id=1, source_target_pairs={{0,64},{64,128},{128,192},{192,256},{256,320},{320,384},{384,448},... | collective-permute-start | bytes 1572872 | tf_op jit(solution)/shard_map/ppermute | solution.py:32
  118.8 2.2 %collective-permute-start.8 = (bf16[2,1,4,16,2048]{4,3,2,1,0:T(8,128)(2,1)S(1)}, bf16[2,1,4,16,2048]{4,3,2,1,0:T(8,128)(2,1)S(1)}, u32[]{:S(2)}, u32[]{:S(2)}) collective-permute-start(bf16[2,1,4,16,2048]{4,3,2,1,0:T(8,128)(2,1)S(1)} %get-tuple-element.33), channel_id=1, source_target_pairs={{64,0},{128,64},{192,128},{256,192},{320,256},{384,320},{448,384},... | collective-permute-start | bytes 1572872 | tf_op jit(solution)/shard_map/ppermute | solution.py:32
  121.0 0.0 collective-permute-done.10.from_high_ref
  121.0 0.0 collective-permute-done.9.from_low_ref
  121.0 0.1 sides.1
  121.2 3.3 %collective-permute-start.11 = (bf16[2,2,1,16,2048]{4,3,2,1,0:T(8,128)(2,1)S(1)}, bf16[2,2,1,16,2048]{4,3,2,1,0:T(8,128)(2,1)S(1)}, u32[]{:S(2)}, u32[]{:S(2)}) collective-permute-start(bf16[2,2,1,16,2048]{4,3,2,1,0:T(8,128)(2,1)S(1)} %get-tuple-element.39), channel_id=1, source_target_pairs={{0,16},{16,32},{32,48},{1,17},{17,33},{33,49},{2,18},{18,34},{34,5... | collective-permute-start | bytes 786440 | tf_op jit(solution)/shard_map/ppermute | solution.py:32
  124.5 1.3 collective-permute-start.12
  125.8 0.0 collective-permute-done.7.rest_7_
  125.8 3.8 %collective-permute-done.8.rest_8_ = bf16[2,1,4,16,2048]{4,3,2,1,0:T(8,128)(2,1)S(1)} collective-permute-done((bf16[2,1,4,16,2048]{4,3,2,1,0:T(8,128)(2,1)S(1)}, bf16[2,1,4,16,2048]{4,3,2,1,0:T(8,128)(2,1)S(1)}, u32[]{:S(2)}, u32[]{:S(2)}) %collective-permute-start.8) | collective-permute-done | bytes 524320 | tf_op jit(solution)/shard_map/ppermute | solution.py:32
  129.6 3.1 %back_own.1 = (bf16[1,2,4,16,2048]{4,3,2,1,0:T(8,128)(2,1)}, bf16[2,2,4,16,2048]{4,3,2,1,0:T(8,128)(2,1)}, f32[2,2,2,16,2048]{4,3,2,1,0:T(8,128)S(1)}) custom-call(bf16[1,2,4,16,2048]{4,3,2,1,0:T(8,128)(2,1)S(1)} %copy-done.4, bf16[128,2048]{1,0:T(8,128)(2,1)S(1)} %get-tuple-element.29.ga_ref, f32[16,384,128]{2,1,0:T(8,128)S(1)} %copy-done.3, ...), custom_call_target="tpu_custom_call" | custom-call | tf_op jit(solution)/shard_map/back_own/pallas_call | solution.py:315
  132.7 0.0 collective-permute-done.11.low_ref
  132.7 1.9 %collective-permute-done.12.high_ref = bf16[2,2,1,16,2048]{4,3,2,1,0:T(8,128)(2,1)S(1)} collective-permute-done((bf16[2,2,1,16,2048]{4,3,2,1,0:T(8,128)(2,1)S(1)}, bf16[2,2,1,16,2048]{4,3,2,1,0:T(8,128)(2,1)S(1)}, u32[]{:S(2)}, u32[]{:S(2)}) %collective-permute-start.12) | collective-permute-done | bytes 262176 | tf_op jit(solution)/shard_map/ppermute | solution.py:32
  134.6 0.9 add_columns.1
  (15 shorter events, 0.1 us)
Async XLA Ops:
  7.2 1.0 copy-start
  7.2 51.8 %copy-start.1 = (bf16[2,1,2,4,16,2048]{5,4,3,2,1,0:T(8,128)(2,1)S(1)}, bf16[2,1,2,4,16,2048]{5,4,3,2,1,0:T(8,128)(2,1)}, u32[]{:S(2)}) copy-start(bf16[2,1,2,4,16,2048]{5,4,3,2,1,0:T(8,128)(2,1)} %param.9) | copy-start | bytes 3145732
  7.2 51.8 %copy-start.13 = (s32[1,2,4,4]{3,2,1,0:T(4,128)S(1)}, s32[1,2,4,4]{3,2,1,0:T(4,128)}, u32[]{:S(2)}) copy-start(s32[1,2,4,4]{3,2,1,0:T(4,128)} %adj_ref.1) | copy-start | bytes 388
  7.2 51.8 %copy-start.4 = (bf16[1,2,4,16,2048]{4,3,2,1,0:T(8,128)(2,1)S(1)}, bf16[1,2,4,16,2048]{4,3,2,1,0:T(8,128)(2,1)}, u32[]{:S(2)}) copy-start(bf16[1,2,4,16,2048]{4,3,2,1,0:T(8,128)(2,1)} %q_ref.5) | copy-start | bytes 1572868
  7.2 82.1 %all-gather.4.cloned.1.call-start = ((), (), s32[]{:S(2)}) async-start(), calls=%async_computation | async-start | bytes 4718592 | tf_op jit(solution)/shard_map/all_gather | solution.py:403
  25.0 67.0 %copy-start.15 = (f32[1,2,4,16,2]{3,4,2,1,0:T(2,128)S(1)}, f32[1,2,4,16,2]{3,4,2,1,0:T(2,128)}, u32[]{:S(2)}) copy-start(f32[1,2,4,16,2]{3,4,2,1,0:T(2,128)} %param.15) | copy-start | bytes 3076
  25.0 19.6 %collective-permute-start.1 = (bf16[2,2,1,16,2048]{4,3,2,1,0:T(8,128)(2,1)S(1)}, bf16[2,2,1,16,2048]{4,3,2,1,0:T(8,128)(2,1)S(1)}, u32[]{:S(2)}, u32[]{:S(2)}) collective-permute-start(bf16[2,2,1,16,2048]{4,3,2,1,0:T(8,128)(2,1)S(1)} %get-tuple-element.51), channel_id=1, source_target_pairs={{0,16},{16,32},{32,48},{1,17},{17,33},{33,49},{2,18},{18,34},{34,5... | collective-permute-start | bytes 786440 | tf_op jit(solution)/shard_map/ppermute | solution.py:32
  34.4 10.2 %collective-permute-start.2 = (bf16[2,2,1,16,2048]{4,3,2,1,0:T(8,128)(2,1)S(1)}, bf16[2,2,1,16,2048]{4,3,2,1,0:T(8,128)(2,1)S(1)}, u32[]{:S(2)}, u32[]{:S(2)}) collective-permute-start(bf16[2,2,1,16,2048]{4,3,2,1,0:T(8,128)(2,1)S(1)} %get-tuple-element.52), channel_id=1, source_target_pairs={{16,0},{32,16},{48,32},{17,1},{33,17},{49,33},{18,2},{34,18},{50,3... | collective-permute-start | bytes 786440 | tf_op jit(solution)/shard_map/ppermute | solution.py:32
  38.0 21.0 %collective-permute-start = (bf16[2,1,4,16,2048]{4,3,2,1,0:T(8,128)(2,1)}, bf16[2,1,4,16,2048]{4,3,2,1,0:T(8,128)(2,1)S(1)}, u32[]{:S(2)}, u32[]{:S(2)}) collective-permute-start(bf16[2,1,4,16,2048]{4,3,2,1,0:T(8,128)(2,1)} %get-tuple-element.50), channel_id=1, source_target_pairs={{0,64},{64,128},{128,192},{192,256},{256,320},{320,384},{384,448},... | collective-permute-start | bytes 1572872 | tf_op jit(solution)/shard_map/ppermute | solution.py:32
  42.7 16.3 %collective-permute-start.4 = (bf16[2,1,4,16,2048]{4,3,2,1,0:T(8,128)(2,1)}, bf16[2,1,4,16,2048]{4,3,2,1,0:T(8,128)(2,1)S(1)}, u32[]{:S(2)}, u32[]{:S(2)}) collective-permute-start(bf16[2,1,4,16,2048]{4,3,2,1,0:T(8,128)(2,1)} %get-tuple-element.49), channel_id=1, source_target_pairs={{64,0},{128,64},{192,128},{256,192},{320,256},{384,320},{448,384},... | collective-permute-start | bytes 1572872 | tf_op jit(solution)/shard_map/ppermute | solution.py:32
  44.7 0.7 copy-start.5
  46.1 7.5 %collective-permute-start.3 = (bf16[2,1,2,16,2048]{4,3,2,1,0:T(8,128)(2,1)}, bf16[2,1,2,16,2048]{4,3,2,1,0:T(8,128)(2,1)}, u32[]{:S(2)}, u32[]{:S(2)}) collective-permute-start(bf16[2,1,2,16,2048]{4,3,2,1,0:T(8,128)(2,1)} %pad_maximum_fusion), channel_id=1, source_target_pairs={{0,64},{64,128},{128,192},{192,256},{256,320},{320,384},{384,448},... | collective-permute-start | bytes 786440 | tf_op jit(solution)/shard_map/ppermute | solution.py:32
  50.7 8.3 %collective-permute-start.5 = (bf16[2,1,2,16,2048]{4,3,2,1,0:T(8,128)(2,1)}, bf16[2,1,2,16,2048]{4,3,2,1,0:T(8,128)(2,1)}, u32[]{:S(2)}, u32[]{:S(2)}) collective-permute-start(bf16[2,1,2,16,2048]{4,3,2,1,0:T(8,128)(2,1)} %pad_maximum_fusion.1), channel_id=1, source_target_pairs={{64,0},{128,64},{192,128},{256,192},{320,256},{384,320},{448,384},... | collective-permute-start | bytes 786440 | tf_op jit(solution)/shard_map/ppermute | solution.py:32
  52.6 46.4 %copy-start.14 = (s32[1,2,4]{2,1,0:T(2,128)S(1)}, s32[1,2,4]{2,1,0:T(2,128)}, u32[]{:S(2)}) copy-start(s32[1,2,4]{2,1,0:T(2,128)} %bound_ref.1) | copy-start | bytes 100
  59.0 1.0 copy-start.6
  60.0 39.1 %copy-start.11 = (f32[2048,2]{0,1:T(2,128)S(1)}, f32[2048,2]{0,1:T(2,128)}, u32[]{:S(2)}) copy-start(f32[2048,2]{0,1:T(2,128)} %param.12) | copy-start | bytes 49156
  60.0 39.1 %copy-start.12 = (f32[2048]{0:T(1024)S(1)}, f32[2048]{0:T(1024)}, u32[]{:S(2)}) copy-start(f32[2048]{0:T(1024)} %param.11) | copy-start | bytes 24580
  64.3 1.6 %copy-start.2 = (f32[16,384,128]{2,1,0:T(8,128)}, f32[16,384,128]{2,1,0:T(8,128)S(1)}, u32[]{:S(2)}) copy-start(f32[16,384,128]{2,1,0:T(8,128)S(1)} %get-tuple-element.30.prob_ref) | copy-start | bytes 9437188
  65.9 0.8 copy-start.8
  89.4 9.7 %collective-permute-start.6 = (bf16[2048,1024]{1,0:T(8,128)(2,1)}, bf16[2048,1024]{1,0:T(8,128)(2,1)}, u32[]{:S(2)}, u32[]{:S(2)}) collective-permute-start(bf16[2048,1024]{1,0:T(8,128)(2,1)} %bitcast.19), channel_id=1, source_target_pairs={{0,64},{64,0},{128,192},{192,128},{256,320},{320,256},{384,448},{4... | collective-permute-start | bytes 12582920 | tf_op jit(solution)/shard_map/ppermute | solution.py:388
  92.1 1.0 copy-start.9
  93.1 5.9 %copy-start.10 = (bf16[128,2048]{1,0:T(8,128)(2,1)S(1)}, bf16[128,2048]{1,0:T(8,128)(2,1)}, u32[]{:S(2)}) copy-start(bf16[128,2048]{1,0:T(8,128)(2,1)} %copy-done.8) | copy-start | bytes 1572868
  99.1 7.4 %copy-start.3 = (f32[16,384,128]{2,1,0:T(8,128)S(1)}, f32[16,384,128]{2,1,0:T(8,128)}, u32[]{:S(2)}) copy-start(f32[16,384,128]{2,1,0:T(8,128)} %copy-done.2) | copy-start | bytes 9437188
  99.1 7.4 %copy-start.7 = (bf16[2,2,1,16,2048]{4,3,2,1,0:T(8,128)(2,1)S(1)}, bf16[2,2,1,16,2048]{4,3,2,1,0:T(8,128)(2,1)}, u32[]{:S(2)}) copy-start(bf16[2,2,1,16,2048]{4,3,2,1,0:T(8,128)(2,1)} %copy-done.5) | copy-start | bytes 786436
  111.1 10.0 %collective-permute-start.10 = (bf16[2,1,2,16,2048]{4,3,2,1,0:T(8,128)(2,1)S(1)}, bf16[2,1,2,16,2048]{4,3,2,1,0:T(8,128)(2,1)S(1)}, u32[]{:S(2)}, u32[]{:S(2)}) collective-permute-start(bf16[2,1,2,16,2048]{4,3,2,1,0:T(8,128)(2,1)S(1)} %get-tuple-element.36), channel_id=1, source_target_pairs={{64,0},{128,64},{192,128},{256,192},{320,256},{384,320},{448,384},... | collective-permute-start | bytes 786440 | tf_op jit(solution)/shard_map/ppermute | solution.py:32
  113.4 7.7 %collective-permute-start.9 = (bf16[2,1,2,16,2048]{4,3,2,1,0:T(8,128)(2,1)S(1)}, bf16[2,1,2,16,2048]{4,3,2,1,0:T(8,128)(2,1)S(1)}, u32[]{:S(2)}, u32[]{:S(2)}) collective-permute-start(bf16[2,1,2,16,2048]{4,3,2,1,0:T(8,128)(2,1)S(1)} %get-tuple-element.35), channel_id=1, source_target_pairs={{0,64},{64,128},{128,192},{192,256},{256,320},{320,384},{384,448},... | collective-permute-start | bytes 786440 | tf_op jit(solution)/shard_map/ppermute | solution.py:32
  116.6 9.1 %collective-permute-start.7 = (bf16[2,1,4,16,2048]{4,3,2,1,0:T(8,128)(2,1)S(1)}, bf16[2,1,4,16,2048]{4,3,2,1,0:T(8,128)(2,1)S(1)}, u32[]{:S(2)}, u32[]{:S(2)}) collective-permute-start(bf16[2,1,4,16,2048]{4,3,2,1,0:T(8,128)(2,1)S(1)} %get-tuple-element.32), channel_id=1, source_target_pairs={{0,64},{64,128},{128,192},{192,256},{256,320},{320,384},{384,448},... | collective-permute-start | bytes 1572872 | tf_op jit(solution)/shard_map/ppermute | solution.py:32
  118.8 10.8 %collective-permute-start.8 = (bf16[2,1,4,16,2048]{4,3,2,1,0:T(8,128)(2,1)S(1)}, bf16[2,1,4,16,2048]{4,3,2,1,0:T(8,128)(2,1)S(1)}, u32[]{:S(2)}, u32[]{:S(2)}) collective-permute-start(bf16[2,1,4,16,2048]{4,3,2,1,0:T(8,128)(2,1)S(1)} %get-tuple-element.33), channel_id=1, source_target_pairs={{64,0},{128,64},{192,128},{256,192},{320,256},{384,320},{448,384},... | collective-permute-start | bytes 1572872 | tf_op jit(solution)/shard_map/ppermute | solution.py:32
  121.2 11.5 %collective-permute-start.11 = (bf16[2,2,1,16,2048]{4,3,2,1,0:T(8,128)(2,1)S(1)}, bf16[2,2,1,16,2048]{4,3,2,1,0:T(8,128)(2,1)S(1)}, u32[]{:S(2)}, u32[]{:S(2)}) collective-permute-start(bf16[2,2,1,16,2048]{4,3,2,1,0:T(8,128)(2,1)S(1)} %get-tuple-element.39), channel_id=1, source_target_pairs={{0,16},{16,32},{32,48},{1,17},{17,33},{33,49},{2,18},{18,34},{34,5... | collective-permute-start | bytes 786440 | tf_op jit(solution)/shard_map/ppermute | solution.py:32
  124.5 10.1 %collective-permute-start.12 = (bf16[2,2,1,16,2048]{4,3,2,1,0:T(8,128)(2,1)S(1)}, bf16[2,2,1,16,2048]{4,3,2,1,0:T(8,128)(2,1)S(1)}, u32[]{:S(2)}, u32[]{:S(2)}) collective-permute-start(bf16[2,2,1,16,2048]{4,3,2,1,0:T(8,128)(2,1)S(1)} %get-tuple-element.40), channel_id=1, source_target_pairs={{16,0},{32,16},{48,32},{17,1},{33,17},{49,33},{18,2},{34,18},{50,3... | collective-permute-start | bytes 786440 | tf_op jit(solution)/shard_map/ppermute | solution.py:32
Sparse Core Ops, SparseCore 0:
  24.0 65.3 all-gather.3

commit v7 on v6

--- a/solution.py
+++ b/solution.py
@@ -24,6 +24,7 @@
 PIECES = [LOCAL, XLOW, CLOW, XHIGH, CHIGH, YLOW, YHIGH]
 KEY_BLOCKS = [block for piece in PIECES for block in piece]
 KEYS = len(KEY_BLOCKS) * BS
+SENT_STEPS = (0, 4, 1, 5, 7, 3, 6, 2)
 
 
 def shift(value, axis, step):
@@ -125,61 +126,83 @@
     )(adjacency, position, queries, *pieces)
 
 
-def side_cols(pos_ref, side, cols):
+def side_cols(pos_ref, side, cols, start=0, size=None):
     core = pos_ref[4]
-    return pl.ds(pl.multiple_of((core if side == 0 else 1 - core) * cols, cols), cols)
-
-
-def project_own_kernel(att_ref, w_hbm, part_ref, w_ref, sems):
+    first = (core if side == 0 else 1 - core) * cols + start
+    return pl.ds(pl.multiple_of(first, HS), cols - start if size is None else size)
+
+
+def sent_heads(pos_ref, n_ring):
+    return [
+        pl.ds(pl.multiple_of((lax.rem(pos_ref[5] + 2 * n_ring - step, n_ring) * 2 + half) * HS, HS), HS)
+        for step in SENT_STEPS
+        for half in range(2)
+    ]
+
+
+def project_own_kernel(pos_ref, att_ref, w_hbm, sent_ref, part_ref, w_ref, mixed_ref, sems):
     chunks = 4
     rows = w_ref.shape[0] // chunks
     parts = [pl.ds(k * rows, rows) for k in range(chunks)]
     copies = [pltpu.make_async_copy(w_hbm.at[part], w_ref.at[part], sems.at[k]) for k, part in enumerate(parts)]
     for copy in copies:
         copy.start()
+    for k, lanes in enumerate(sent_heads(pos_ref, sent_ref.shape[0])):
+        mixed_ref[:, k * HS : (k + 1) * HS] = att_ref[:, lanes]
+    ring_cols = w_ref.shape[1]
+    inner = w_ref.shape[0]
+    part_ref[:, ring_cols:] = dot(mixed_ref[...], sent_ref[...].reshape(inner, -1), ((1,), (0,)))
     total = None
     for k in range(chunks):
         copies[k].wait()
         lanes = slice(k * rows, (k + 1) * rows)
         term = dot(att_ref[:, lanes], w_ref[lanes, :], ((1,), (0,)))
         total = term if total is None else total + term
-    part_ref[...] = total
-
-
-def project_own(att, own):
+    part_ref[:, :ring_cols] = total
+
+
+def project_own(position, att, own, sent):
     vmem = pl.BlockSpec(memory_space=pltpu.VMEM)
-    tokens = att.shape[0]
-    cols = own.shape[1]
+    smem = pl.BlockSpec(memory_space=pltpu.SMEM)
+    tokens, inner = att.shape
     return pl.pallas_call(
         project_own_kernel,
-        in_specs=[vmem, pl.BlockSpec(memory_space=pl.ANY)],
-        out_specs=[vmem, vmem],
-        out_shape=[jax.ShapeDtypeStruct((tokens, cols), jnp.float32), jax.ShapeDtypeStruct(own.shape, own.dtype)],
+        in_specs=[smem, vmem, pl.BlockSpec(memory_space=pl.ANY), vmem],
+        out_specs=[vmem, vmem, vmem],
+        out_shape=[
+            jax.ShapeDtypeStruct((tokens, inner // 2), jnp.float32),
+            jax.ShapeDtypeStruct(own.shape, own.dtype),
+            jax.ShapeDtypeStruct(att.shape, att.dtype),
+        ],
         scratch_shapes=[pltpu.SemaphoreType.DMA((4,))],
         compiler_params=pltpu.CompilerParams(vmem_limit_bytes=VMEM_LIMIT),
         name="project_own",
-    )(att, pltpu.with_memory_space_constraint(own, pltpu.HBM))
+    )(position, att, pltpu.with_memory_space_constraint(own, pltpu.HBM), *in_vmem(sent))
 
 
 def project_kernel(
-    bound_ref, pos_ref, att_ref, part_ref, own_ref, swap_hbm, gain_ref, read_ref, cot_ref,
-    pred_ref, ga_ref, swap_ref, proj_ref, gp_ref, sems,
+    bound_ref, pos_ref, att_ref, mixed_ref, part_ref, own_ref, swap_hbm, sent_ref, sent_swap_ref, gain_ref, read_ref,
+    cot_ref, pred_ref, ga_ref, swap_ref, proj_ref, gp_ref, sum_ref, sems,
 ):
-    cols = swap_ref.shape[1]
+    inner, ring_cols = swap_ref.shape
+    cols = inner // 2
     chunks = 4
-    rows = swap_ref.shape[0] // chunks
+    rows = inner // chunks
     parts = [pl.ds(k * rows, rows) for k in range(chunks)]
     copies = [pltpu.make_async_copy(swap_hbm.at[part], swap_ref.at[part], sems.at[k]) for k, part in enumerate(parts)]
     for copy in copies:
         copy.start()
+    sent = sent_ref[...].reshape(inner, cols - ring_cols)
+    sent_swap = sent_swap_ref[...].reshape(inner, cols - ring_cols)
+    proj_ref[:, side_cols(pos_ref, 0, cols)] = part_ref[...]
+    proj_ref[:, side_cols(pos_ref, 1, cols, ring_cols)] = dot(mixed_ref[...], sent_swap, ((1,), (0,)))
     total = None
     for k in range(chunks):
         copies[k].wait()
         lanes = slice(k * rows, (k + 1) * rows)
         term = dot(att_ref[:, lanes], swap_ref[lanes, :], ((1,), (0,)))
         total = term if total is None else total + term
-    proj_ref[:, side_cols(pos_ref, 0, cols)] = part_ref[...]
-    proj_ref[:, side_cols(pos_ref, 1, cols)] = total
+    proj_ref[:, side_cols(pos_ref, 1, cols, 0, ring_cols)] = total
     inner = proj_ref.shape[1]
     for pair in range(TOK // (2 * BS)):
         rows_of = slice(pair * 2 * BS, (pair + 1) * 2 * BS)
@@ -205,16 +228,21 @@
     gp_swap = gp_ref[:, side_cols(pos_ref, 1, cols)]
     for k in range(chunks):
         lanes = slice(k * rows, (k + 1) * rows)
-        total = dot(gp_swap, swap_ref[lanes, :], ((1,), (1,))) + dot(gp_own, own_ref[lanes, :], ((1,), (1,)))
-        ga_ref[:, lanes] = total.astype(jnp.bfloat16)
-
-
-def project(boundary, position, att, part, own, swapped, gain, read_rows, cotangent):
+        sum_ref[:, lanes] = dot(gp_swap[:, :ring_cols], swap_ref[lanes, :], ((1,), (1,))) + dot(
+            gp_own[:, :ring_cols], own_ref[lanes, :], ((1,), (1,))
+        )
+    mixed = dot(gp_swap[:, ring_cols:], sent_swap, ((1,), (1,))) + dot(gp_own[:, ring_cols:], sent, ((1,), (1,)))
+    for k, lanes in enumerate(sent_heads(pos_ref, sent_ref.shape[0])):
+        ga_ref[:, lanes] = (sum_ref[:, lanes] + mixed[:, k * HS : (k + 1) * HS]).astype(jnp.bfloat16)
+
+
+def project(boundary, position, att, mixed, part, own, swapped, sent, sent_swap, gain, read_rows, cotangent):
     vmem = pl.BlockSpec(memory_space=pltpu.VMEM)
     smem = pl.BlockSpec(memory_space=pltpu.SMEM)
+    hbm = pl.BlockSpec(memory_space=pl.ANY)
     return pl.pallas_call(
         project_kernel,
-        in_specs=[smem, smem, vmem, vmem, vmem, pl.BlockSpec(memory_space=pl.ANY), vmem, vmem, vmem],
+        in_specs=[smem, smem, vmem, vmem, vmem, vmem, hbm, vmem, vmem, vmem, vmem, vmem],
         out_specs=[vmem, vmem],
         out_shape=[
             jax.ShapeDtypeStruct(cotangent.shape[:3] + (2, BS), jnp.float32),
@@ -224,6 +252,7 @@
             pltpu.VMEM(swapped.shape, jnp.bfloat16),
             pltpu.VMEM(att.shape, jnp.float32),
             pltpu.VMEM(att.shape, jnp.bfloat16),
+            pltpu.VMEM(att.shape, jnp.float32),
             pltpu.SemaphoreType.DMA((4,)),
         ],
         compiler_params=pltpu.CompilerParams(vmem_limit_bytes=VMEM_LIMIT),
@@ -231,8 +260,9 @@
     )(
         boundary,
         position,
-        *in_vmem(att, part, own),
+        *in_vmem(att, mixed, part, own),
         pltpu.with_memory_space_constraint(swapped, pltpu.HBM),
+        *in_vmem(sent, sent_swap),
         gain,
         read_rows,
         cotangent,
@@ -384,6 +414,11 @@
     )(*in_vmem(low, high, edge), pltpu.with_memory_space_constraint(partial, pltpu.HBM))
 
 
+def around(value, axis, step):
+    count = lax.axis_size(axis)
+    return lax.ppermute(value, axis, [(i, (i + step) % count) for i in range(count)])
+
+
 def swap_cores(value):
     return lax.ppermute(value, "sx", [(i, i ^ 1) for i in range(lax.axis_size("sx"))])
 
@@ -400,13 +435,20 @@
     pairs = [[w, w + 1] for w in range(0, n_wa, 2)]
     rings = [list(range(h, n_wa, 2)) for h in range(2)]
     both = lax.all_gather(slab, "wa", axis=0, axis_index_groups=pairs)
-    own_cols = lax.all_gather(both, "wa", axis=0, axis_index_groups=rings).reshape(-1, cols)
+    ring_cols = 3 * cols // 4
+    own_cols = lax.all_gather(both[:, :, :ring_cols], "wa", axis=0, axis_index_groups=rings).reshape(-1, ring_cols)
+    sent = both[None, :, :, ring_cols:]
+    sent = jnp.concatenate([sent, around(sent, "wa", n_wa // 2)])
     ylow = shift(kv[:, :, size_y - 1 :], "sy", 1)
     yhigh = shift(kv[:, :, :1], "sy", -1)
     xlow = shift(kv[:, size_x - 1 :], "sx", 1)
     xhigh = shift(kv[:, :1], "sx", -1)
     clow = shift(jnp.concatenate([ylow[:, size_x - 1 :], yhigh[:, size_x - 1 :]], axis=2), "sx", 1)
     chigh = shift(jnp.concatenate([ylow[:, :1], yhigh[:, :1]], axis=2), "sx", -1)
+    sent, xlow = lax.optimization_barrier((sent, xlow))
+    sent = jnp.concatenate([sent] + [around(sent, "wa", 2 * k) for k in (1, -1, -2)])
+    queries, sent = lax.optimization_barrier((queries, sent))
+    sent_swap = swap_cores(sent)
     pieces = (kv, xlow, clow, xhigh, chigh, ylow, yhigh)
     position = jnp.stack(
         [
@@ -415,14 +457,26 @@
             jnp.int32(size_x * n_sx),
             jnp.int32(size_y * n_sy),
             core,
+            case // 2,
         ]
     ).astype(jnp.int32)
     att, prob = forward(adjacency, position, queries, pieces)
-    own_cols, att = lax.optimization_barrier((own_cols, att))
+    own_cols, att, sent_swap = lax.optimization_barrier((own_cols, att, sent_swap))
     swapped = swap_cores(own_cols)
-    part, own_cols = project_own(att, own_cols)
+    part, own_cols, mixed = project_own(position, att, own_cols, sent)
     prediction, grad_att = project(
-        boundary, position, att, part, own_cols, swapped, gain[None], read_weight.T, cotangent
+        boundary,
+        position,
+        att,
+        mixed,
+        part,
+        own_cols,
+        swapped,
+        sent,
+        sent_swap,
+        gain[None],
+        read_weight.T,
+        cotangent,
     )
     grad_scores, gxlow, gclow, gxhigh, gchigh, gylow, gyhigh = back_rim(queries, grad_att, prob, pieces)
     corner_low = shift(gchigh, "sx", 1)

time: 143 us -> 172 us (1.20)
  the two profiles are of different devices: /device:TPU:1 before, /device:TPU:18 now
where the time goes in v7:
time: 172 us; the launch traced here: 171 us
  starting transfers between devices  58 us (34%)
  waiting for transfers between devices  46.8 us (27%)
  Pallas kernels  24.8 us (14%)
  blocking collectives  16.1 us (9%)
  between operations  14.5 us (8%)
  local copies, waits for them, and re-layouts  9.21 us (5%)
    ppermute x4, waiting for transfers between devices, around(): lax.ppermute(value, axis, [(i, (i + step) % count) for i in range(count)])  37.1 us
    ppermute x12, starting transfers between devices, shift(): return lax.ppermute(value, axis, pairs)  36.8 us
    all_gather x1, blocking collectives, body(): both = lax.all_gather(slab, 'wa', axis=0, axis_index_groups=pairs)  16.1 us
    ppermute x4, starting transfers between devices, around(): lax.ppermute(value, axis, [(i, (i + step) % count) for i in range(count)])  15.5 us
    ppermute x12, waiting for transfers between devices, shift(): return lax.ppermute(value, axis, pairs)  8.31 us
    pallas_call x1, Pallas kernels, project(): pl.pallas_call(project_kernel, in_specs=[smem, smem, vmem, vmem, vmem, vm...  8.24 us
    unnamed x37, local copies, waits for them, and re-layouts  7.32 us
    ppermute x2, starting transfers between devices, swap_cores(): lax.ppermute(value, 'sx', [(i, i ^ 1) for i in range(lax.axis_size('sx'))])  5.61 us
  transfers between devices with their start and end apart: 19, of which 10 were waited for; matrix products, arithmetic and copies ran while one was open for 2% of the time, Pallas kernels for 6%

profile of v7, /device:TPU:18, one launch (start us, length us, event | category | flops | bytes accessed | tf_op | source)
XLA Modules:
  0.0 170.9 jit_solution(14455282508162980229)
XLA Ops:
  7.2 0.0 copy-start
  7.2 0.0 all-gather.4.cloned.1.call-start
  7.3 1.0 copy-done
  8.2 16.1 %all-gather = bf16[256,1024]{1,0:T(8,128)(2,1)S(1)} all-gather(bf16[128,1024]{1,0:T(8,128)(2,1)S(1)} %constant_dynamic-slice_fusion), channel_id=2, replica_groups={{0,1},{2,3},{4,5},{6,7},{8,9},{10,11},{12,13},{14,15},{16,17},{18,19},{..., dimensions={0}, use_global_device_ids=true | all-gather | bytes 786432 | tf_op jit(solution)/shard_map/all_gather | solution.py:437
  24.3 0.8 slice.40
  25.1 0.0 all-gather.4.cloned.1.call-update
  25.1 0.9 fusion
  26.0 2.0 %collective-permute-start.1 = (bf16[2,1,4,16,2048]{4,3,2,1,0:T(8,128)(2,1)S(1)}, bf16[2,1,4,16,2048]{4,3,2,1,0:T(8,128)(2,1)S(1)}, u32[]{:S(2)}, u32[]{:S(2)}) collective-permute-start(bf16[2,1,4,16,2048]{4,3,2,1,0:T(8,128)(2,1)S(1)} %get-tuple-element.62), channel_id=1, source_target_pairs={{0,64},{64,128},{128,192},{192,256},{256,320},{320,384},{384,448},... | collective-permute-start | bytes 1572872 | tf_op jit(solution)/shard_map/ppermute | solution.py:33
  28.1 9.1 %collective-permute-start.5 = (bf16[2,2,1,16,2048]{4,3,2,1,0:T(8,128)(2,1)S(1)}, bf16[2,2,1,16,2048]{4,3,2,1,0:T(8,128)(2,1)S(1)}, u32[]{:S(2)}, u32[]{:S(2)}) collective-permute-start(bf16[2,2,1,16,2048]{4,3,2,1,0:T(8,128)(2,1)S(1)} %get-tuple-element.63), channel_id=1, source_target_pairs={{0,16},{16,32},{32,48},{1,17},{17,33},{33,49},{2,18},{18,34},{34,5... | collective-permute-start | bytes 786440 | tf_op jit(solution)/shard_map/ppermute | solution.py:33
  37.2 5.9 %collective-permute-start = (bf16[1,2,128,256]{3,2,1,0:T(8,128)(2,1)S(1)}, bf16[1,2,128,256]{3,2,1,0:T(8,128)(2,1)S(1)}, u32[]{:S(2)}, u32[]{:S(2)}) collective-permute-start(bf16[1,2,128,256]{3,2,1,0:T(8,128)(2,1)S(1)} %slice_bitcast_fusion), channel_id=1, source_target_pairs={{0,8},{1,9},{2,10},{3,11},{4,12},{5,13},{6,14},{7,15},{8,0},{9,1},... | collective-permute-start | bytes 393224 | tf_op jit(solution)/shard_map/ppermute | solution.py:419
  43.2 1.3 collective-permute-start.6
  44.5 3.1 %collective-permute-start.8 = (bf16[2,1,4,16,2048]{4,3,2,1,0:T(8,128)(2,1)}, bf16[2,1,4,16,2048]{4,3,2,1,0:T(8,128)(2,1)}, u32[]{:S(2)}, u32[]{:S(2)}) collective-permute-start(bf16[2,1,4,16,2048]{4,3,2,1,0:T(8,128)(2,1)} %get-tuple-element.61), channel_id=1, source_target_pairs={{64,0},{128,64},{192,128},{256,192},{320,256},{384,320},{448,384},... | collective-permute-start | bytes 1572872 | tf_op jit(solution)/shard_map/ppermute | solution.py:33
  47.6 6.4 %collective-permute-done = bf16[1,2,128,256]{3,2,1,0:T(8,128)(2,1)S(1)} collective-permute-done((bf16[1,2,128,256]{3,2,1,0:T(8,128)(2,1)S(1)}, bf16[1,2,128,256]{3,2,1,0:T(8,128)(2,1)S(1)}, u32[]{:S(2)}, u32[]{:S(2)}) %collective-permute-start) | collective-permute-done | bytes 131104 | tf_op jit(solution)/shard_map/ppermute | solution.py:419
  54.0 0.0 collective-permute-done.1.rest_1_
  54.0 0.0 copy-start.5
  54.1 1.9 %collective-permute-start.2 = (bf16[2,2,128,256]{3,2,1,0:T(8,128)(2,1)S(1)}, bf16[2,2,128,256]{3,2,1,0:T(8,128)(2,1)S(1)}, u32[]{:S(2)}, u32[]{:S(2)}) collective-permute-start(bf16[2,2,128,256]{3,2,1,0:T(8,128)(2,1)S(1)} %pad_maximum_fusion.1), channel_id=1, source_target_pairs={{0,2},{1,3},{2,4},{3,5},{4,6},{5,7},{6,8},{7,9},{8,10},{9,11},{10,... | collective-permute-start | bytes 786440 | tf_op jit(solution)/shard_map/ppermute | solution.py:419
  56.0 3.9 %collective-permute-start.3 = (bf16[2,2,128,256]{3,2,1,0:T(8,128)(2,1)S(1)}, bf16[2,2,128,256]{3,2,1,0:T(8,128)(2,1)S(1)}, u32[]{:S(2)}, u32[]{:S(2)}) collective-permute-start(bf16[2,2,128,256]{3,2,1,0:T(8,128)(2,1)S(1)} %pad_maximum_fusion.1), channel_id=1, source_target_pairs={{0,14},{1,15},{2,0},{3,1},{4,2},{5,3},{6,4},{7,5},{8,6},{9,7},{10,... | collective-permute-start | bytes 786440 | tf_op jit(solution)/shard_map/ppermute | solution.py:419
  59.9 0.0 collective-permute-done.5.rest_5_
  59.9 3.8 %collective-permute-start.4 = (bf16[2,2,128,256]{3,2,1,0:T(8,128)(2,1)S(1)}, bf16[2,2,128,256]{3,2,1,0:T(8,128)(2,1)S(1)}, u32[]{:S(2)}, u32[]{:S(2)}) collective-permute-start(bf16[2,2,128,256]{3,2,1,0:T(8,128)(2,1)S(1)} %pad_maximum_fusion.1), channel_id=1, source_target_pairs={{0,12},{1,13},{2,14},{3,15},{4,0},{5,1},{6,2},{7,3},{8,4},{9,5},{1... | collective-permute-start | bytes 786440 | tf_op jit(solution)/shard_map/ppermute | solution.py:419
  63.7 6.7 %collective-permute-done.2 = bf16[2,2,128,256]{3,2,1,0:T(8,128)(2,1)S(1)} collective-permute-done((bf16[2,2,128,256]{3,2,1,0:T(8,128)(2,1)S(1)}, bf16[2,2,128,256]{3,2,1,0:T(8,128)(2,1)S(1)}, u32[]{:S(2)}, u32[]{:S(2)}) %collective-permute-start.2) | collective-permute-done | bytes 262176 | tf_op jit(solution)/shard_map/ppermute | solution.py:419
  70.4 4.9 %collective-permute-done.3 = bf16[2,2,128,256]{3,2,1,0:T(8,128)(2,1)S(1)} collective-permute-done((bf16[2,2,128,256]{3,2,1,0:T(8,128)(2,1)S(1)}, bf16[2,2,128,256]{3,2,1,0:T(8,128)(2,1)S(1)}, u32[]{:S(2)}, u32[]{:S(2)}) %collective-permute-start.3) | collective-permute-done | bytes 262176 | tf_op jit(solution)/shard_map/ppermute | solution.py:419
  75.3 19.1 %collective-permute-done.4 = bf16[2,2,128,256]{3,2,1,0:T(8,128)(2,1)S(1)} collective-permute-done((bf16[2,2,128,256]{3,2,1,0:T(8,128)(2,1)S(1)}, bf16[2,2,128,256]{3,2,1,0:T(8,128)(2,1)S(1)}, u32[]{:S(2)}, u32[]{:S(2)}) %collective-permute-start.4) | collective-permute-done | bytes 262176 | tf_op jit(solution)/shard_map/ppermute | solution.py:419
  94.4 0.1 pad_maximum_fusion.sent_ref
  94.6 0.0 copy-start.17
  94.6 1.9 %collective-permute-start.10 = (bf16[8,2,128,256]{3,2,1,0:T(8,128)(2,1)S(1)}, bf16[8,2,128,256]{3,2,1,0:T(8,128)(2,1)}, u32[]{:S(2)}, u32[]{:S(2)}) collective-permute-start(bf16[8,2,128,256]{3,2,1,0:T(8,128)(2,1)S(1)} %pad_maximum_fusion.sent_ref), channel_id=1, source_target_pairs={{0,64},{64,0},{128,192},{192,128},{256,320},{320,256},{384,448},{4... | collective-permute-start | bytes 3145736 | tf_op jit(solution)/shard_map/ppermute | solution.py:423
  96.5 0.0 collective-permute-done.6.rest_6_
  96.6 0.7 copy-done.8
  97.3 0.7 pad_maximum_fusion.2
  98.0 2.4 %collective-permute-start.7 = (bf16[2,1,2,16,2048]{4,3,2,1,0:T(8,128)(2,1)}, bf16[2,1,2,16,2048]{4,3,2,1,0:T(8,128)(2,1)}, u32[]{:S(2)}, u32[]{:S(2)}) collective-permute-start(bf16[2,1,2,16,2048]{4,3,2,1,0:T(8,128)(2,1)} %pad_maximum_fusion.2), channel_id=1, source_target_pairs={{0,64},{64,128},{128,192},{192,256},{256,320},{320,384},{384,448},... | collective-permute-start | bytes 786440 | tf_op jit(solution)/shard_map/ppermute | solution.py:33
  100.4 0.7 pad_maximum_fusion.3
  101.1 3.1 %collective-permute-start.9 = (bf16[2,1,2,16,2048]{4,3,2,1,0:T(8,128)(2,1)}, bf16[2,1,2,16,2048]{4,3,2,1,0:T(8,128)(2,1)}, u32[]{:S(2)}, u32[]{:S(2)}) collective-permute-start(bf16[2,1,2,16,2048]{4,3,2,1,0:T(8,128)(2,1)} %pad_maximum_fusion.3), channel_id=1, source_target_pairs={{64,0},{128,64},{192,128},{256,192},{320,256},{384,320},{448,384},... | collective-permute-start | bytes 786440 | tf_op jit(solution)/shard_map/ppermute | solution.py:33
  104.3 0.1 stack.19.pos_ref
  104.4 1.6 collective-permute-done.7.rest_2_
  106.0 2.5 %collective-permute-done.9.rest_4_ = bf16[2,1,2,16,2048]{4,3,2,1,0:T(8,128)(2,1)} collective-permute-done((bf16[2,1,2,16,2048]{4,3,2,1,0:T(8,128)(2,1)}, bf16[2,1,2,16,2048]{4,3,2,1,0:T(8,128)(2,1)}, u32[]{:S(2)}, u32[]{:S(2)}) %collective-permute-start.9) | collective-permute-done | bytes 262176 | tf_op jit(solution)/shard_map/ppermute | solution.py:33
  108.4 0.0 collective-permute-done.8.rest_3_
  108.5 1.0 copy-done.6
  109.5 0.9 copy-done.9
  110.4 4.5 %attend.1 = (bf16[128,2048]{1,0:T(8,128)(2,1)S(1)}, f32[16,384,128]{2,1,0:T(8,128)S(1)}) custom-call(s32[1,2,4,4]{3,2,1,0:T(4,128)S(1)} %copy-done.15, s32[6]{0:T(128)S(1)} %stack.19.pos_ref, bf16[1,2,4,16,2048]{4,3,2,1,0:T(8,128)(2,1)S(1)} %copy-done.4, bf16[2,2,4,16,2048]{4,3,2,1,0:T(8,128)(2,1)S(1)} %bitcast.17, ...), custom_call_target="tpu_custom_call" | custom-call | tf_op jit(solution)/shard_map/attend/pallas_call | solution.py:111
  114.9 1.7 copy-done.2
  116.6 0.8 copy-done.11
  117.4 0.0 collective-permute-done.10.sent_swap_ref
  117.4 0.0 all-gather.4.cloned.1.call-done
  117.4 3.7 %collective-permute-start.11 = (bf16[2048,768]{1,0:T(8,128)(2,1)}, bf16[2048,768]{1,0:T(8,128)(2,1)}, u32[]{:S(2)}, u32[]{:S(2)}) collective-permute-start(bf16[2048,768]{1,0:T(8,128)(2,1)} %bitcast.22), channel_id=1, source_target_pairs={{0,64},{64,0},{128,192},{192,128},{256,320},{320,256},{384,448},{4... | collective-permute-start | bytes 9437192 | tf_op jit(solution)/shard_map/ppermute | solution.py:423
  121.1 0.1 copy.14.cot_ref
  121.3 1.0 copy-done.12
  122.3 3.1 %project_own.1 = (f32[128,1024]{1,0:T(8,128)S(1)}, bf16[2048,768]{1,0:T(8,128)(2,1)S(1)}, bf16[128,2048]{1,0:T(8,128)(2,1)S(1)}) custom-call(s32[6]{0:T(128)S(1)} %stack.19.pos_ref, bf16[128,2048]{1,0:T(8,128)(2,1)S(1)} %copy-done.12, bf16[2048,768]{1,0:T(8,128)(2,1)} %bitcast.23, bf16[8,2,128,256]{3,2,1,0:T(8,128)(2,1)S(1)} %pad_maximum_fusion.sent_ref), custom_call_target="tpu_custom_call" | custom-call | tf_op jit(solution)/shard_map/project_own/pallas_call | solution.py:168
  125.4 1.3 collective-permute-done.11.swap_hbm
  126.7 0.0 copy-start.7
  126.8 8.2 %project.1 = (f32[1,2,4,2,16]{4,3,2,1,0:T(2,128)}, bf16[128,2048]{1,0:T(8,128)(2,1)S(1)}) custom-call(s32[1,2,4]{2,1,0:T(2,128)S(1)} %copy-done.16, s32[6]{0:T(128)S(1)} %stack.19.pos_ref, bf16[128,2048]{1,0:T(8,128)(2,1)S(1)} %copy-done.12, bf16[128,2048]{1,0:T(8,128)(2,1)S(1)} %get-tuple-element.36.mixed_ref, f32[128,1024]{1,0:T(8,128)S(1)} %get-tuple-element.37.part_ref, ...), custom_call_target="tpu_custom_call" | custom-call | tf_op jit(solution)/shard_map/project/pallas_call | solution.py:243
  135.0 4.7 %back_rim.1 = (bf16[16,384,128]{2,1,0:T(8,128)(2,1)S(1)}, bf16[2,1,4,16,2048]{4,3,2,1,0:T(8,128)(2,1)S(1)}, bf16[2,1,2,16,2048]{4,3,2,1,0:T(8,128)(2,1)S(1)}, bf...) custom-call(bf16[1,2,4,16,2048]{4,3,2,1,0:T(8,128)(2,1)S(1)} %copy-d, ...), custom_call_target="tpu_custom_call" | custom-call | tf_op jit(solution)/shard_map/back_rim/pallas_call | solution.py:305
  139.7 2.3 %collective-permute-start.14 = (bf16[2,1,2,16,2048]{4,3,2,1,0:T(8,128)(2,1)S(1)}, bf16[2,1,2,16,2048]{4,3,2,1,0:T(8,128)(2,1)S(1)}, u32[]{:S(2)}, u32[]{:S(2)}) collective-permute-start(bf16[2,1,2,16,2048]{4,3,2,1,0:T(8,128)(2,1)S(1)} %get-tuple-element.47), channel_id=1, source_target_pairs={{0,64},{64,128},{128,192},{192,256},{256,320},{320,384},{384,448},... | collective-permute-start | bytes 786440 | tf_op jit(solution)/shard_map/ppermute | solution.py:33
  142.0 3.3 %collective-permute-start.15 = (bf16[2,1,2,16,2048]{4,3,2,1,0:T(8,128)(2,1)S(1)}, bf16[2,1,2,16,2048]{4,3,2,1,0:T(8,128)(2,1)S(1)}, u32[]{:S(2)}, u32[]{:S(2)}) collective-permute-start(bf16[2,1,2,16,2048]{4,3,2,1,0:T(8,128)(2,1)S(1)} %get-tuple-element.48), channel_id=1, source_target_pairs={{64,0},{128,64},{192,128},{256,192},{320,256},{384,320},{448,384},... | collective-permute-start | bytes 786440 | tf_op jit(solution)/shard_map/ppermute | solution.py:33
  145.3 1.9 %collective-permute-start.12 = (bf16[2,1,4,16,2048]{4,3,2,1,0:T(8,128)(2,1)S(1)}, bf16[2,1,4,16,2048]{4,3,2,1,0:T(8,128)(2,1)S(1)}, u32[]{:S(2)}, u32[]{:S(2)}) collective-permute-start(bf16[2,1,4,16,2048]{4,3,2,1,0:T(8,128)(2,1)S(1)} %get-tuple-element.44), channel_id=1, source_target_pairs={{0,64},{64,128},{128,192},{192,256},{256,320},{320,384},{384,448},... | collective-permute-start | bytes 1572872 | tf_op jit(solution)/shard_map/ppermute | solution.py:33
  147.3 3.6 %collective-permute-start.13 = (bf16[2,1,4,16,2048]{4,3,2,1,0:T(8,128)(2,1)S(1)}, bf16[2,1,4,16,2048]{4,3,2,1,0:T(8,128)(2,1)S(1)}, u32[]{:S(2)}, u32[]{:S(2)}) collective-permute-start(bf16[2,1,4,16,2048]{4,3,2,1,0:T(8,128)(2,1)S(1)} %get-tuple-element.45), channel_id=1, source_target_pairs={{64,0},{128,64},{192,128},{256,192},{320,256},{384,320},{448,384},... | collective-permute-start | bytes 1572872 | tf_op jit(solution)/shard_map/ppermute | solution.py:33
  150.9 0.0 collective-permute-done.14.from_low_ref
  150.9 0.1 sides.1
  151.1 3.3 %collective-permute-start.16 = (bf16[2,2,1,16,2048]{4,3,2,1,0:T(8,128)(2,1)S(1)}, bf16[2,2,1,16,2048]{4,3,2,1,0:T(8,128)(2,1)S(1)}, u32[]{:S(2)}, u32[]{:S(2)}) collective-permute-start(bf16[2,2,1,16,2048]{4,3,2,1,0:T(8,128)(2,1)S(1)} %get-tuple-element.51), channel_id=1, source_target_pairs={{0,16},{16,32},{32,48},{1,17},{17,33},{33,49},{2,18},{18,34},{34,5... | collective-permute-start | bytes 786440 | tf_op jit(solution)/shard_map/ppermute | solution.py:33
  154.4 1.3 collective-permute-start.17
  155.7 0.1 collective-permute-done.12.rest_7_
  155.8 1.8 %collective-permute-done.13.rest_8_ = bf16[2,1,4,16,2048]{4,3,2,1,0:T(8,128)(2,1)S(1)} collective-permute-done((bf16[2,1,4,16,2048]{4,3,2,1,0:T(8,128)(2,1)S(1)}, bf16[2,1,4,16,2048]{4,3,2,1,0:T(8,128)(2,1)S(1)}, u32[]{:S(2)}, u32[]{:S(2)}) %collective-permute-start.13) | collective-permute-done | bytes 524320 | tf_op jit(solution)/shard_map/ppermute | solution.py:33
  157.6 3.2 %back_own.1 = (bf16[1,2,4,16,2048]{4,3,2,1,0:T(8,128)(2,1)}, bf16[2,2,4,16,2048]{4,3,2,1,0:T(8,128)(2,1)}, f32[2,2,2,16,2048]{4,3,2,1,0:T(8,128)S(1)}) custom-call(bf16[1,2,4,16,2048]{4,3,2,1,0:T(8,128)(2,1)S(1)} %copy-done.4, bf16[128,2048]{1,0:T(8,128)(2,1)S(1)} %get-tuple-element.41.ga_ref, f32[16,384,128]{2,1,0:T(8,128)S(1)} %copy-done.3, ...), custom_call_target="tpu_custom_call" | custom-call | tf_op jit(solution)/shard_map/back_own/pallas_call | solution.py:345
  160.8 0.0 collective-permute-done.16.low_ref
  160.8 2.3 %collective-permute-done.17.high_ref = bf16[2,2,1,16,2048]{4,3,2,1,0:T(8,128)(2,1)S(1)} collective-permute-done((bf16[2,2,1,16,2048]{4,3,2,1,0:T(8,128)(2,1)S(1)}, bf16[2,2,1,16,2048]{4,3,2,1,0:T(8,128)(2,1)S(1)}, u32[]{:S(2)}, u32[]{:S(2)}) %collective-permute-start.17) | collective-permute-done | bytes 262176 | tf_op jit(solution)/shard_map/ppermute | solution.py:33
  163.2 0.9 add_columns.1
  (33 shorter events, 0.2 us)
Async XLA Ops:
  7.2 1.0 copy-start
  7.2 18.0 %copy-start.1 = (bf16[2,1,2,4,16,2048]{5,4,3,2,1,0:T(8,128)(2,1)S(1)}, bf16[2,1,2,4,16,2048]{5,4,3,2,1,0:T(8,128)(2,1)}, u32[]{:S(2)}) copy-start(bf16[2,1,2,4,16,2048]{5,4,3,2,1,0:T(8,128)(2,1)} %param.9) | copy-start | bytes 3145732
  7.2 110.2 %all-gather.4.cloned.1.call-start = ((), (), s32[]{:S(2)}) async-start(), calls=%async_computation | async-start | bytes 3538944 | tf_op jit(solution)/shard_map/all_gather | solution.py:439
  26.0 82.4 %copy-start.4 = (bf16[1,2,4,16,2048]{4,3,2,1,0:T(8,128)(2,1)S(1)}, bf16[1,2,4,16,2048]{4,3,2,1,0:T(8,128)(2,1)}, u32[]{:S(2)}) copy-start(bf16[1,2,4,16,2048]{4,3,2,1,0:T(8,128)(2,1)} %q_ref.2) | copy-start | bytes 1572868
  26.0 82.4 %copy-start.15 = (s32[1,2,4,4]{3,2,1,0:T(4,128)S(1)}, s32[1,2,4,4]{3,2,1,0:T(4,128)}, u32[]{:S(2)}) copy-start(s32[1,2,4,4]{3,2,1,0:T(4,128)} %adj_ref.1) | copy-start | bytes 388
  26.0 28.0 %collective-permute-start.1 = (bf16[2,1,4,16,2048]{4,3,2,1,0:T(8,128)(2,1)S(1)}, bf16[2,1,4,16,2048]{4,3,2,1,0:T(8,128)(2,1)S(1)}, u32[]{:S(2)}, u32[]{:S(2)}) collective-permute-start(bf16[2,1,4,16,2048]{4,3,2,1,0:T(8,128)(2,1)S(1)} %get-tuple-element.62), channel_id=1, source_target_pairs={{0,64},{64,128},{128,192},{192,256},{256,320},{320,384},{384,448},... | collective-permute-start | bytes 1572872 | tf_op jit(solution)/shard_map/ppermute | solution.py:33
  28.1 31.8 %collective-permute-start.5 = (bf16[2,2,1,16,2048]{4,3,2,1,0:T(8,128)(2,1)S(1)}, bf16[2,2,1,16,2048]{4,3,2,1,0:T(8,128)(2,1)S(1)}, u32[]{:S(2)}, u32[]{:S(2)}) collective-permute-start(bf16[2,2,1,16,2048]{4,3,2,1,0:T(8,128)(2,1)S(1)} %get-tuple-element.63), channel_id=1, source_target_pairs={{0,16},{16,32},{32,48},{1,17},{17,33},{33,49},{2,18},{18,34},{34,5... | collective-permute-start | bytes 786440 | tf_op jit(solution)/shard_map/ppermute | solution.py:33
  37.2 16.8 %collective-permute-start = (bf16[1,2,128,256]{3,2,1,0:T(8,128)(2,1)S(1)}, bf16[1,2,128,256]{3,2,1,0:T(8,128)(2,1)S(1)}, u32[]{:S(2)}, u32[]{:S(2)}) collective-permute-start(bf16[1,2,128,256]{3,2,1,0:T(8,128)(2,1)S(1)} %slice_bitcast_fusion), channel_id=1, source_target_pairs={{0,8},{1,9},{2,10},{3,11},{4,12},{5,13},{6,14},{7,15},{8,0},{9,1},... | collective-permute-start | bytes 393224 | tf_op jit(solution)/shard_map/ppermute | solution.py:419
  43.2 53.3 %collective-permute-start.6 = (bf16[2,2,1,16,2048]{4,3,2,1,0:T(8,128)(2,1)S(1)}, bf16[2,2,1,16,2048]{4,3,2,1,0:T(8,128)(2,1)S(1)}, u32[]{:S(2)}, u32[]{:S(2)}) collective-permute-start(bf16[2,2,1,16,2048]{4,3,2,1,0:T(8,128)(2,1)S(1)} %get-tuple-element.64), channel_id=1, source_target_pairs={{16,0},{32,16},{48,32},{17,1},{33,17},{49,33},{18,2},{34,18},{50,3... | collective-permute-start | bytes 786440 | tf_op jit(solution)/shard_map/ppermute | solution.py:33
  44.5 64.0 %collective-permute-start.8 = (bf16[2,1,4,16,2048]{4,3,2,1,0:T(8,128)(2,1)}, bf16[2,1,4,16,2048]{4,3,2,1,0:T(8,128)(2,1)}, u32[]{:S(2)}, u32[]{:S(2)}) collective-permute-start(bf16[2,1,4,16,2048]{4,3,2,1,0:T(8,128)(2,1)} %get-tuple-element.61), channel_id=1, source_target_pairs={{64,0},{128,64},{192,128},{256,192},{320,256},{384,320},{448,384},... | collective-permute-start | bytes 1572872 | tf_op jit(solution)/shard_map/ppermute | solution.py:33
  54.0 21.2 %copy-start.5 = (bf16[2,1,4,16,2048]{4,3,2,1,0:T(8,128)(2,1)}, bf16[2,1,4,16,2048]{4,3,2,1,0:T(8,128)(2,1)S(1)}, u32[]{:S(2)}) copy-start(bf16[2,1,4,16,2048]{4,3,2,1,0:T(8,128)(2,1)S(1)} %collective-permute-done.1.rest_1_) | copy-start | bytes 1572868
  54.1 16.4 %collective-permute-start.2 = (bf16[2,2,128,256]{3,2,1,0:T(8,128)(2,1)S(1)}, bf16[2,2,128,256]{3,2,1,0:T(8,128)(2,1)S(1)}, u32[]{:S(2)}, u32[]{:S(2)}) collective-permute-start(bf16[2,2,128,256]{3,2,1,0:T(8,128)(2,1)S(1)} %pad_maximum_fusion.1), channel_id=1, source_target_pairs={{0,2},{1,3},{2,4},{3,5},{4,6},{5,7},{6,8},{7,9},{8,10},{9,11},{10,... | collective-permute-start | bytes 786440 | tf_op jit(solution)/shard_map/ppermute | solution.py:419
  56.0 19.3 %collective-permute-start.3 = (bf16[2,2,128,256]{3,2,1,0:T(8,128)(2,1)S(1)}, bf16[2,2,128,256]{3,2,1,0:T(8,128)(2,1)S(1)}, u32[]{:S(2)}, u32[]{:S(2)}) collective-permute-start(bf16[2,2,128,256]{3,2,1,0:T(8,128)(2,1)S(1)} %pad_maximum_fusion.1), channel_id=1, source_target_pairs={{0,14},{1,15},{2,0},{3,1},{4,2},{5,3},{6,4},{7,5},{8,6},{9,7},{10,... | collective-permute-start | bytes 786440 | tf_op jit(solution)/shard_map/ppermute | solution.py:419
  59.9 34.5 %collective-permute-start.4 = (bf16[2,2,128,256]{3,2,1,0:T(8,128)(2,1)S(1)}, bf16[2,2,128,256]{3,2,1,0:T(8,128)(2,1)S(1)}, u32[]{:S(2)}, u32[]{:S(2)}) collective-permute-start(bf16[2,2,128,256]{3,2,1,0:T(8,128)(2,1)S(1)} %pad_maximum_fusion.1), channel_id=1, source_target_pairs={{0,12},{1,13},{2,14},{3,15},{4,0},{5,1},{6,2},{7,3},{8,4},{9,5},{1... | collective-permute-start | bytes 786440 | tf_op jit(solution)/shard_map/ppermute | solution.py:419
  94.6 26.5 %copy-start.17 = (f32[1,2,4,16,2]{3,4,2,1,0:T(2,128)S(1)}, f32[1,2,4,16,2]{3,4,2,1,0:T(2,128)}, u32[]{:S(2)}) copy-start(f32[1,2,4,16,2]{3,4,2,1,0:T(2,128)} %param.15) | copy-start | bytes 3076
  94.6 22.8 %collective-permute-start.10 = (bf16[8,2,128,256]{3,2,1,0:T(8,128)(2,1)S(1)}, bf16[8,2,128,256]{3,2,1,0:T(8,128)(2,1)}, u32[]{:S(2)}, u32[]{:S(2)}) collective-permute-start(bf16[8,2,128,256]{3,2,1,0:T(8,128)(2,1)S(1)} %pad_maximum_fusion.sent_ref), channel_id=1, source_target_pairs={{0,64},{64,0},{128,192},{192,128},{256,320},{320,256},{384,448},{4... | collective-permute-start | bytes 3145736 | tf_op jit(solution)/shard_map/ppermute | solution.py:423
  96.6 0.7 copy-start.8
  98.0 8.0 %collective-permute-start.7 = (bf16[2,1,2,16,2048]{4,3,2,1,0:T(8,128)(2,1)}, bf16[2,1,2,16,2048]{4,3,2,1,0:T(8,128)(2,1)}, u32[]{:S(2)}, u32[]{:S(2)}) collective-permute-start(bf16[2,1,2,16,2048]{4,3,2,1,0:T(8,128)(2,1)} %pad_maximum_fusion.2), channel_id=1, source_target_pairs={{0,64},{64,128},{128,192},{192,256},{256,320},{320,384},{384,448},... | collective-permute-start | bytes 786440 | tf_op jit(solution)/shard_map/ppermute | solution.py:33
  101.1 7.3 %collective-permute-start.9 = (bf16[2,1,2,16,2048]{4,3,2,1,0:T(8,128)(2,1)}, bf16[2,1,2,16,2048]{4,3,2,1,0:T(8,128)(2,1)}, u32[]{:S(2)}, u32[]{:S(2)}) collective-permute-start(bf16[2,1,2,16,2048]{4,3,2,1,0:T(8,128)(2,1)} %pad_maximum_fusion.3), channel_id=1, source_target_pairs={{64,0},{128,64},{192,128},{256,192},{320,256},{384,320},{448,384},... | collective-permute-start | bytes 786440 | tf_op jit(solution)/shard_map/ppermute | solution.py:33
  108.4 1.0 copy-start.6
  109.5 0.9 copy-start.9
  114.9 1.7 copy-start.2
  116.6 0.8 copy-start.11
  117.4 9.3 %copy-start.13 = (f32[2048,2]{0,1:T(2,128)S(1)}, f32[2048,2]{0,1:T(2,128)}, u32[]{:S(2)}) copy-start(f32[2048,2]{0,1:T(2,128)} %param.12) | copy-start | bytes 49156
  117.4 9.3 %copy-start.14 = (f32[2048]{0:T(1024)S(1)}, f32[2048]{0:T(1024)}, u32[]{:S(2)}) copy-start(f32[2048]{0:T(1024)} %param.11) | copy-start | bytes 24580
  117.4 9.3 %copy-start.16 = (s32[1,2,4]{2,1,0:T(2,128)S(1)}, s32[1,2,4]{2,1,0:T(2,128)}, u32[]{:S(2)}) copy-start(s32[1,2,4]{2,1,0:T(2,128)} %bound_ref.1) | copy-start | bytes 100
  117.4 9.3 %collective-permute-start.11 = (bf16[2048,768]{1,0:T(8,128)(2,1)}, bf16[2048,768]{1,0:T(8,128)(2,1)}, u32[]{:S(2)}, u32[]{:S(2)}) collective-permute-start(bf16[2048,768]{1,0:T(8,128)(2,1)} %bitcast.22), channel_id=1, source_target_pairs={{0,64},{64,0},{128,192},{192,128},{256,320},{320,256},{384,448},{4... | collective-permute-start | bytes 9437192 | tf_op jit(solution)/shard_map/ppermute | solution.py:423
  121.3 1.0 copy-start.12
  126.7 8.3 %copy-start.3 = (f32[16,384,128]{2,1,0:T(8,128)S(1)}, f32[16,384,128]{2,1,0:T(8,128)}, u32[]{:S(2)}) copy-start(f32[16,384,128]{2,1,0:T(8,128)} %copy-done.2) | copy-start | bytes 9437188
  126.7 8.3 %copy-start.7 = (bf16[2,1,4,16,2048]{4,3,2,1,0:T(8,128)(2,1)S(1)}, bf16[2,1,4,16,2048]{4,3,2,1,0:T(8,128)(2,1)}, u32[]{:S(2)}) copy-start(bf16[2,1,4,16,2048]{4,3,2,1,0:T(8,128)(2,1)} %copy-done.5) | copy-start | bytes 1572868
  126.8 8.3 %copy-start.10 = (bf16[2,2,1,16,2048]{4,3,2,1,0:T(8,128)(2,1)S(1)}, bf16[2,2,1,16,2048]{4,3,2,1,0:T(8,128)(2,1)}, u32[]{:S(2)}) copy-start(bf16[2,2,1,16,2048]{4,3,2,1,0:T(8,128)(2,1)} %copy-done.8) | copy-start | bytes 786436
  139.7 11.2 %collective-permute-start.14 = (bf16[2,1,2,16,2048]{4,3,2,1,0:T(8,128)(2,1)S(1)}, bf16[2,1,2,16,2048]{4,3,2,1,0:T(8,128)(2,1)S(1)}, u32[]{:S(2)}, u32[]{:S(2)}) collective-permute-start(bf16[2,1,2,16,2048]{4,3,2,1,0:T(8,128)(2,1)S(1)} %get-tuple-element.47), channel_id=1, source_target_pairs={{0,64},{64,128},{128,192},{192,256},{256,320},{320,384},{384,448},... | collective-permute-start | bytes 786440 | tf_op jit(solution)/shard_map/ppermute | solution.py:33
  142.0 8.9 %collective-permute-start.15 = (bf16[2,1,2,16,2048]{4,3,2,1,0:T(8,128)(2,1)S(1)}, bf16[2,1,2,16,2048]{4,3,2,1,0:T(8,128)(2,1)S(1)}, u32[]{:S(2)}, u32[]{:S(2)}) collective-permute-start(bf16[2,1,2,16,2048]{4,3,2,1,0:T(8,128)(2,1)S(1)} %get-tuple-element.48), channel_id=1, source_target_pairs={{64,0},{128,64},{192,128},{256,192},{320,256},{384,320},{448,384},... | collective-permute-start | bytes 786440 | tf_op jit(solution)/shard_map/ppermute | solution.py:33
  145.3 10.5 %collective-permute-start.12 = (bf16[2,1,4,16,2048]{4,3,2,1,0:T(8,128)(2,1)S(1)}, bf16[2,1,4,16,2048]{4,3,2,1,0:T(8,128)(2,1)S(1)}, u32[]{:S(2)}, u32[]{:S(2)}) collective-permute-start(bf16[2,1,4,16,2048]{4,3,2,1,0:T(8,128)(2,1)S(1)} %get-tuple-element.44), channel_id=1, source_target_pairs={{0,64},{64,128},{128,192},{192,256},{256,320},{320,384},{384,448},... | collective-permute-start | bytes 1572872 | tf_op jit(solution)/shard_map/ppermute | solution.py:33
  147.3 10.3 %collective-permute-start.13 = (bf16[2,1,4,16,2048]{4,3,2,1,0:T(8,128)(2,1)S(1)}, bf16[2,1,4,16,2048]{4,3,2,1,0:T(8,128)(2,1)S(1)}, u32[]{:S(2)}, u32[]{:S(2)}) collective-permute-start(bf16[2,1,4,16,2048]{4,3,2,1,0:T(8,128)(2,1)S(1)} %get-tuple-element.45), channel_id=1, source_target_pairs={{64,0},{128,64},{192,128},{256,192},{320,256},{384,320},{448,384},... | collective-permute-start | bytes 1572872 | tf_op jit(solution)/shard_map/ppermute | solution.py:33
  151.1 9.8 %collective-permute-start.16 = (bf16[2,2,1,16,2048]{4,3,2,1,0:T(8,128)(2,1)S(1)}, bf16[2,2,1,16,2048]{4,3,2,1,0:T(8,128)(2,1)S(1)}, u32[]{:S(2)}, u32[]{:S(2)}) collective-permute-start(bf16[2,2,1,16,2048]{4,3,2,1,0:T(8,128)(2,1)S(1)} %get-tuple-element.51), channel_id=1, source_target_pairs={{0,16},{16,32},{32,48},{1,17},{17,33},{33,49},{2,18},{18,34},{34,5... | collective-permute-start | bytes 786440 | tf_op jit(solution)/shard_map/ppermute | solution.py:33
  154.4 8.8 %collective-permute-start.17 = (bf16[2,2,1,16,2048]{4,3,2,1,0:T(8,128)(2,1)S(1)}, bf16[2,2,1,16,2048]{4,3,2,1,0:T(8,128)(2,1)S(1)}, u32[]{:S(2)}, u32[]{:S(2)}) collective-permute-start(bf16[2,2,1,16,2048]{4,3,2,1,0:T(8,128)(2,1)S(1)} %get-tuple-element.52), channel_id=1, source_target_pairs={{16,0},{32,16},{48,32},{17,1},{33,17},{49,33},{18,2},{34,18},{50,3... | collective-permute-start | bytes 786440 | tf_op jit(solution)/shard_map/ppermute | solution.py:33
Sparse Core Ops, SparseCore 0:
  25.3 73.8 all-gather.3

commit v8 on v6

--- a/solution.py
+++ b/solution.py
@@ -130,13 +130,15 @@
     return pl.ds(pl.multiple_of((core if side == 0 else 1 - core) * cols, cols), cols)
 
 
-def project_own_kernel(att_ref, w_hbm, part_ref, w_ref, sems):
+def project_own_kernel(att_ref, w_hbm, prob_hbm, part_ref, w_ref, prob_ref, sems):
     chunks = 4
     rows = w_ref.shape[0] // chunks
     parts = [pl.ds(k * rows, rows) for k in range(chunks)]
     copies = [pltpu.make_async_copy(w_hbm.at[part], w_ref.at[part], sems.at[k]) for k, part in enumerate(parts)]
     for copy in copies:
         copy.start()
+    prob_copy = pltpu.make_async_copy(prob_hbm, prob_ref, sems.at[chunks])
+    prob_copy.start()
     total = None
     for k in range(chunks):
         copies[k].wait()
@@ -144,21 +146,27 @@
         term = dot(att_ref[:, lanes], w_ref[lanes, :], ((1,), (0,)))
         total = term if total is None else total + term
     part_ref[...] = total
-
-
-def project_own(att, own):
-    vmem = pl.BlockSpec(memory_space=pltpu.VMEM)
+    prob_copy.wait()
+
+
+def project_own(att, own, prob):
+    vmem = pl.BlockSpec(memory_space=pltpu.VMEM)
+    hbm = pl.BlockSpec(memory_space=pl.ANY)
     tokens = att.shape[0]
     cols = own.shape[1]
     return pl.pallas_call(
         project_own_kernel,
-        in_specs=[vmem, pl.BlockSpec(memory_space=pl.ANY)],
-        out_specs=[vmem, vmem],
-        out_shape=[jax.ShapeDtypeStruct((tokens, cols), jnp.float32), jax.ShapeDtypeStruct(own.shape, own.dtype)],
-        scratch_shapes=[pltpu.SemaphoreType.DMA((4,))],
+        in_specs=[vmem, hbm, hbm],
+        out_specs=[vmem, vmem, vmem],
+        out_shape=[
+            jax.ShapeDtypeStruct((tokens, cols), jnp.float32),
+            jax.ShapeDtypeStruct(own.shape, own.dtype),
+            jax.ShapeDtypeStruct(prob.shape, prob.dtype),
+        ],
+        scratch_shapes=[pltpu.SemaphoreType.DMA((5,))],
         compiler_params=pltpu.CompilerParams(vmem_limit_bytes=VMEM_LIMIT),
         name="project_own",
-    )(att, pltpu.with_memory_space_constraint(own, pltpu.HBM))
+    )(att, *(pltpu.with_memory_space_constraint(value, pltpu.HBM) for value in (own, prob)))
 
 
 def project_kernel(
@@ -166,7 +174,7 @@
     pred_ref, ga_ref, swap_ref, proj_ref, gp_ref, sems,
 ):
     cols = swap_ref.shape[1]
-    chunks = 4
+    chunks = 8
     rows = swap_ref.shape[0] // chunks
     parts = [pl.ds(k * rows, rows) for k in range(chunks)]
     copies = [pltpu.make_async_copy(swap_hbm.at[part], swap_ref.at[part], sems.at[k]) for k, part in enumerate(parts)]
@@ -224,7 +232,7 @@
             pltpu.VMEM(swapped.shape, jnp.bfloat16),
             pltpu.VMEM(att.shape, jnp.float32),
             pltpu.VMEM(att.shape, jnp.bfloat16),
-            pltpu.SemaphoreType.DMA((4,)),
+            pltpu.SemaphoreType.DMA((8,)),
         ],
         compiler_params=pltpu.CompilerParams(vmem_limit_bytes=VMEM_LIMIT),
         name="project",
@@ -420,7 +428,7 @@
     att, prob = forward(adjacency, position, queries, pieces)
     own_cols, att = lax.optimization_barrier((own_cols, att))
     swapped = swap_cores(own_cols)
-    part, own_cols = project_own(att, own_cols)
+    part, own_cols, prob = project_own(att, own_cols, prob)
     prediction, grad_att = project(
         boundary, position, att, part, own_cols, swapped, gain[None], read_weight.T, cotangent
     )

time: 143 us -> 143 us (level)
    unnamed x33 -> x31, local copies, waits for them, and re-layouts: 6.19 us -> 6.19 us
  transfers between devices with their start and end apart: 14 -> 14, of which waited for: 6 -> 6; matrix products, arithmetic and copies ran while one was open for 4% -> 4% of each run, Pallas kernels for 7% -> 8%
where the time goes in v8:
time: 143 us; the launch traced here: 142 us
  starting transfers between devices  40.2 us (28%)
  waiting for transfers between devices  37.2 us (26%)
  Pallas kernels  23.3 us (16%)
  blocking collectives  15.6 us (11%)
  between operations  14.4 us (10%)
  local copies, waits for them, and re-layouts  9.61 us (7%)
  other arithmetic  1.56 us (1%)
    ppermute x12, starting transfers between devices, shift(): return lax.ppermute(value, axis, pairs)  37.6 us
    all_gather x1, waiting for transfers between devices, body(): lax.all_gather(both, 'wa', axis=0, axis_index_groups=rings)  22.6 us
    all_gather x1, blocking collectives, body(): both = lax.all_gather(slab, 'wa', axis=0, axis_index_groups=pairs)  15.6 us
    ppermute x12, waiting for transfers between devices, shift(): return lax.ppermute(value, axis, pairs)  12 us
    pallas_call x1, Pallas kernels, project(): pl.pallas_call(project_kernel, in_specs=[smem, smem, vmem, vmem, vmem, pl...  7.03 us
    unnamed x31, local copies, waits for them, and re-layouts  6.19 us
    pallas_call x1, Pallas kernels, back_rim(): pl.pallas_call(back_rim_kernel, in_specs=[vmem] * (3 + len(pieces)), out_...  4.58 us
    pallas_call x1, Pallas kernels, forward(): pl.pallas_call(forward_kernel, grid=(inner // width,), in_specs=[smem, sm...  4.37 us
  transfers between devices with their start and end apart: 14, of which 6 were waited for; matrix products, arithmetic and copies ran while one was open for 4% of the time, Pallas kernels for 8%

profile of v8, /device:TPU:1, one launch (start us, length us, event | category | flops | bytes accessed | tf_op | source)
XLA Modules:
  0.0 141.9 jit_solution(9188600348676437985)
XLA Ops:
  7.2 0.0 copy-start
  7.2 0.0 copy-start.1
  7.2 0.0 copy-start.12
  7.2 0.0 copy-start.2
  7.2 0.0 all-gather.4.cloned.1.call-start
  7.3 0.9 copy-done
  8.2 15.6 %all-gather = bf16[256,1024]{1,0:T(8,128)(2,1)} all-gather(bf16[128,1024]{1,0:T(8,128)(2,1)S(1)} %constant_dynamic-slice_fusion), channel_id=2, replica_groups={{0,1},{2,3},{4,5},{6,7},{8,9},{10,11},{12,13},{14,15},{16,17},{18,19},{..., dimensions={0}, use_global_device_ids=true | all-gather | bytes 786432 | tf_op jit(solution)/shard_map/all_gather | solution.py:410
  23.9 0.0 all-gather.4.cloned.1.call-update
  23.9 1.1 fusion.1
  25.0 0.0 copy-start.14
  25.0 9.5 %collective-permute-start.1 = (bf16[2,2,1,16,2048]{4,3,2,1,0:T(8,128)(2,1)S(1)}, bf16[2,2,1,16,2048]{4,3,2,1,0:T(8,128)(2,1)S(1)}, u32[]{:S(2)}, u32[]{:S(2)}) collective-permute-start(bf16[2,2,1,16,2048]{4,3,2,1,0:T(8,128)(2,1)S(1)} %get-tuple-element.53), channel_id=1, source_target_pairs={{0,16},{16,32},{32,48},{1,17},{17,33},{33,49},{2,18},{18,34},{34,5... | collective-permute-start | bytes 786440 | tf_op jit(solution)/shard_map/ppermute | solution.py:32
  34.4 1.3 collective-permute-start.2
  35.7 2.3 %fusion = (bf16[2,1,4,16,2048]{4,3,2,1,0:T(8,128)(2,1)}, bf16[2,1,4,16,2048]{4,3,2,1,0:T(8,128)(2,1)}) fusion(bf16[2,2,4,16,2048]{4,3,2,1,0:T(8,128)(2,1)} %bitcast.13), kind=kLoop, calls=%fused_computation.4 | loop fusion | bytes 2097152 | tf_op jit(solution)/shard_map/slice | solution.py:415
  38.0 4.7 %collective-permute-start = (bf16[2,1,4,16,2048]{4,3,2,1,0:T(8,128)(2,1)}, bf16[2,1,4,16,2048]{4,3,2,1,0:T(8,128)(2,1)S(1)}, u32[]{:S(2)}, u32[]{:S(2)}) collective-permute-start(bf16[2,1,4,16,2048]{4,3,2,1,0:T(8,128)(2,1)} %get-tuple-element.52), channel_id=1, source_target_pairs={{0,64},{64,128},{128,192},{192,256},{256,320},{320,384},{384,448},... | collective-permute-start | bytes 1572872 | tf_op jit(solution)/shard_map/ppermute | solution.py:32
  42.7 1.9 %collective-permute-start.4 = (bf16[2,1,4,16,2048]{4,3,2,1,0:T(8,128)(2,1)}, bf16[2,1,4,16,2048]{4,3,2,1,0:T(8,128)(2,1)S(1)}, u32[]{:S(2)}, u32[]{:S(2)}) collective-permute-start(bf16[2,1,4,16,2048]{4,3,2,1,0:T(8,128)(2,1)} %get-tuple-element.51), channel_id=1, source_target_pairs={{64,0},{128,64},{192,128},{256,192},{320,256},{384,320},{448,384},... | collective-permute-start | bytes 1572872 | tf_op jit(solution)/shard_map/ppermute | solution.py:32
  44.6 0.0 collective-permute-done.1.rest_5_
  44.6 0.0 collective-permute-done.2.rest_6_
  44.7 0.0 copy-start.3
  44.7 0.7 copy-done.3
  45.4 0.8 pad_maximum_fusion
  46.1 3.8 %collective-permute-start.3 = (bf16[2,1,2,16,2048]{4,3,2,1,0:T(8,128)(2,1)}, bf16[2,1,2,16,2048]{4,3,2,1,0:T(8,128)(2,1)}, u32[]{:S(2)}, u32[]{:S(2)}) collective-permute-start(bf16[2,1,2,16,2048]{4,3,2,1,0:T(8,128)(2,1)} %pad_maximum_fusion), channel_id=1, source_target_pairs={{0,64},{64,128},{128,192},{192,256},{256,320},{320,384},{384,448},... | collective-permute-start | bytes 786440 | tf_op jit(solution)/shard_map/ppermute | solution.py:32
  50.0 0.7 pad_maximum_fusion.1
  50.7 1.9 %collective-permute-start.5 = (bf16[2,1,2,16,2048]{4,3,2,1,0:T(8,128)(2,1)}, bf16[2,1,2,16,2048]{4,3,2,1,0:T(8,128)(2,1)}, u32[]{:S(2)}, u32[]{:S(2)}) collective-permute-start(bf16[2,1,2,16,2048]{4,3,2,1,0:T(8,128)(2,1)} %pad_maximum_fusion.1), channel_id=1, source_target_pairs={{64,0},{128,64},{192,128},{256,192},{320,256},{384,320},{448,384},... | collective-permute-start | bytes 786440 | tf_op jit(solution)/shard_map/ppermute | solution.py:32
  52.6 0.1 pad_add_fusion.pos_ref
  52.7 0.9 collective-permute-done.3.rest_2_
  53.6 5.4 %collective-permute-done.5.rest_4_ = bf16[2,1,2,16,2048]{4,3,2,1,0:T(8,128)(2,1)} collective-permute-done((bf16[2,1,2,16,2048]{4,3,2,1,0:T(8,128)(2,1)}, bf16[2,1,2,16,2048]{4,3,2,1,0:T(8,128)(2,1)}, u32[]{:S(2)}, u32[]{:S(2)}) %collective-permute-start.5) | collective-permute-done | bytes 262176 | tf_op jit(solution)/shard_map/ppermute | solution.py:32
  59.0 0.0 collective-permute-done.rest_1_
  59.0 0.0 collective-permute-done.4.rest_3_
  59.0 0.0 copy-done.1
  59.0 0.0 copy-done.12
  59.0 0.0 copy-done.2
  59.0 0.0 copy-start.4
  59.0 0.9 copy-done.4
  60.0 4.4 %attend.1 = (bf16[128,2048]{1,0:T(8,128)(2,1)S(1)}, f32[16,384,128]{2,1,0:T(8,128)S(1)}) custom-call(s32[1,2,4,4]{3,2,1,0:T(4,128)S(1)} %copy-done.12, s32[5]{0:T(128)S(1)} %pad_add_fusion.pos_ref, bf16[1,2,4,16,2048]{4,3,2,1,0:T(8,128)(2,1)S(1)} %copy-done.2, bf16[2,2,4,16,2048]{4,3,2,1,0:T(8,128)(2,1)S(1)} %bitcast.14, ...), custom_call_target="tpu_custom_call" | custom-call | tf_op jit(solution)/shard_map/attend/pallas_call | solution.py:110
  64.4 0.0 copy-start.6
  64.4 1.6 %copy-done.6 = f32[16,384,128]{2,1,0:T(8,128)} copy-done((f32[16,384,128]{2,1,0:T(8,128)}, f32[16,384,128]{2,1,0:T(8,128)S(1)}, u32[]{:S(2)}) %copy-start.6) | copy-done | bytes 3145752
  66.0 0.8 copy-done.7
  66.8 22.6 %all-gather.4.cloned.1.call-done = bf16[16,128,1024]{2,1,0:T(8,128)(2,1)} async-done(((bf16[2,128,1024]{2,1,0:T(8,128)(2,1)}), bf16[16,128,1024]{2,1,0:T(8,128)(2,1)}) %all-gather.4.cloned.1.call-update) | async-done | bytes 4194320 | tf_op jit(solution)/shard_map/all_gather | solution.py:411
  89.4 2.6 %collective-permute-start.6 = (bf16[2048,1024]{1,0:T(8,128)(2,1)}, bf16[2048,1024]{1,0:T(8,128)(2,1)}, u32[]{:S(2)}, u32[]{:S(2)}) collective-permute-start(bf16[2048,1024]{1,0:T(8,128)(2,1)} %bitcast.19), channel_id=1, source_target_pairs={{0,64},{64,0},{128,192},{192,128},{256,320},{320,256},{384,448},{4... | collective-permute-start | bytes 12582920 | tf_op jit(solution)/shard_map/ppermute | solution.py:396
  91.9 0.0 copy-done.14
  91.9 0.1 copy.14.cot_ref
  92.1 1.0 copy-done.8
  93.1 3.3 %project_own.1 = (f32[128,1024]{1,0:T(8,128)S(1)}, bf16[2048,1024]{1,0:T(8,128)(2,1)S(1)}, f32[16,384,128]{2,1,0:T(8,128)S(1)}) custom-call(bf16[128,2048]{1,0:T(8,128)(2,1)S(1)} %copy-done.8, bf16[2048,1024]{1,0:T(8,128)(2,1)} %bitcast.20, f32[16,384,128]{2,1,0:T(8,128)} %copy-done.6), custom_call_target="tpu_custom_call" | custom-call | tf_op jit(solution)/shard_map/project_own/pallas_call | solution.py:157
  96.4 2.7 %collective-permute-done.6.swap_hbm = bf16[2048,1024]{1,0:T(8,128)(2,1)} collective-permute-done((bf16[2048,1024]{1,0:T(8,128)(2,1)}, bf16[2048,1024]{1,0:T(8,128)(2,1)}, u32[]{:S(2)}, u32[]{:S(2)}) %collective-permute-start.6) | collective-permute-done | bytes 4194336 | tf_op jit(solution)/shard_map/ppermute | solution.py:396
  99.0 0.0 copy-done.10
  99.0 0.0 copy-done.11
  99.1 0.0 copy-done.13
  99.1 7.0 %project.1 = (f32[1,2,4,2,16]{4,3,2,1,0:T(2,128)}, bf16[128,2048]{1,0:T(8,128)(2,1)S(1)}) custom-call(s32[1,2,4]{2,1,0:T(2,128)S(1)} %copy-done.13, s32[5]{0:T(128)S(1)} %pad_add_fusion.pos_ref, bf16[128,2048]{1,0:T(8,128)(2,1)S(1)} %copy-done.9, f32[128,1024]{1,0:T(8,128)S(1)} %get-tuple-element.28.part_ref, ...), custom_call_target="tpu_custom_call" | custom-call | tf_op jit(solution)/shard_map/project/pallas_call | solution.py:223
  106.1 4.6 %back_rim.1 = (bf16[16,384,128]{2,1,0:T(8,128)(2,1)S(1)}, bf16[2,1,4,16,2048]{4,3,2,1,0:T(8,128)(2,1)S(1)}, bf16[2,1,2,16,2048]{4,3,2,1,0:T(8,128)(2,1)S(1)}, bf...) custom-call(bf16[1,2,4,16,2048]{4,3,2,1,0:T(8,128)(2,1)S(1)} %copy-d, ...), custom_call_target="tpu_custom_call" | custom-call | tf_op jit(solution)/shard_map/back_rim/pallas_call | solution.py:283
  110.7 2.3 %collective-permute-start.10 = (bf16[2,1,2,16,2048]{4,3,2,1,0:T(8,128)(2,1)S(1)}, bf16[2,1,2,16,2048]{4,3,2,1,0:T(8,128)(2,1)S(1)}, u32[]{:S(2)}, u32[]{:S(2)}) collective-permute-start(bf16[2,1,2,16,2048]{4,3,2,1,0:T(8,128)(2,1)S(1)} %get-tuple-element.38), channel_id=1, source_target_pairs={{64,0},{128,64},{192,128},{256,192},{320,256},{384,320},{448,384},... | collective-permute-start | bytes 786440 | tf_op jit(solution)/shard_map/ppermute | solution.py:32
  113.0 3.3 %collective-permute-start.9 = (bf16[2,1,2,16,2048]{4,3,2,1,0:T(8,128)(2,1)S(1)}, bf16[2,1,2,16,2048]{4,3,2,1,0:T(8,128)(2,1)S(1)}, u32[]{:S(2)}, u32[]{:S(2)}) collective-permute-start(bf16[2,1,2,16,2048]{4,3,2,1,0:T(8,128)(2,1)S(1)} %get-tuple-element.37), channel_id=1, source_target_pairs={{0,64},{64,128},{128,192},{192,256},{256,320},{320,384},{384,448},... | collective-permute-start | bytes 786440 | tf_op jit(solution)/shard_map/ppermute | solution.py:32
  116.3 2.1 %collective-permute-start.7 = (bf16[2,1,4,16,2048]{4,3,2,1,0:T(8,128)(2,1)S(1)}, bf16[2,1,4,16,2048]{4,3,2,1,0:T(8,128)(2,1)S(1)}, u32[]{:S(2)}, u32[]{:S(2)}) collective-permute-start(bf16[2,1,4,16,2048]{4,3,2,1,0:T(8,128)(2,1)S(1)} %get-tuple-element.34), channel_id=1, source_target_pairs={{0,64},{64,128},{128,192},{192,256},{256,320},{320,384},{384,448},... | collective-permute-start | bytes 1572872 | tf_op jit(solution)/shard_map/ppermute | solution.py:32
  118.4 2.2 %collective-permute-start.8 = (bf16[2,1,4,16,2048]{4,3,2,1,0:T(8,128)(2,1)S(1)}, bf16[2,1,4,16,2048]{4,3,2,1,0:T(8,128)(2,1)S(1)}, u32[]{:S(2)}, u32[]{:S(2)}) collective-permute-start(bf16[2,1,4,16,2048]{4,3,2,1,0:T(8,128)(2,1)S(1)} %get-tuple-element.35), channel_id=1, source_target_pairs={{64,0},{128,64},{192,128},{256,192},{320,256},{384,320},{448,384},... | collective-permute-start | bytes 1572872 | tf_op jit(solution)/shard_map/ppermute | solution.py:32
  120.7 0.0 collective-permute-done.10.from_high_ref
  120.7 0.0 collective-permute-done.9.from_low_ref
  120.7 0.1 sides.1
  120.8 3.3 %collective-permute-start.11 = (bf16[2,2,1,16,2048]{4,3,2,1,0:T(8,128)(2,1)S(1)}, bf16[2,2,1,16,2048]{4,3,2,1,0:T(8,128)(2,1)S(1)}, u32[]{:S(2)}, u32[]{:S(2)}) collective-permute-start(bf16[2,2,1,16,2048]{4,3,2,1,0:T(8,128)(2,1)S(1)} %get-tuple-element.41), channel_id=1, source_target_pairs={{0,16},{16,32},{32,48},{1,17},{17,33},{33,49},{2,18},{18,34},{34,5... | collective-permute-start | bytes 786440 | tf_op jit(solution)/shard_map/ppermute | solution.py:32
  124.1 1.3 collective-permute-start.12
  125.4 0.0 collective-permute-done.7.rest_7_
  125.4 3.8 %collective-permute-done.8.rest_8_ = bf16[2,1,4,16,2048]{4,3,2,1,0:T(8,128)(2,1)S(1)} collective-permute-done((bf16[2,1,4,16,2048]{4,3,2,1,0:T(8,128)(2,1)S(1)}, bf16[2,1,4,16,2048]{4,3,2,1,0:T(8,128)(2,1)S(1)}, u32[]{:S(2)}, u32[]{:S(2)}) %collective-permute-start.8) | collective-permute-done | bytes 524320 | tf_op jit(solution)/shard_map/ppermute | solution.py:32
  129.2 3.1 %back_own.1 = (bf16[1,2,4,16,2048]{4,3,2,1,0:T(8,128)(2,1)}, bf16[2,2,4,16,2048]{4,3,2,1,0:T(8,128)(2,1)}, f32[2,2,2,16,2048]{4,3,2,1,0:T(8,128)S(1)}) custom-call(bf16[1,2,4,16,2048]{4,3,2,1,0:T(8,128)(2,1)S(1)} %copy-done.2, bf16[128,2048]{1,0:T(8,128)(2,1)S(1)} %get-tuple-element.31.ga_ref, f32[16,384,128]{2,1,0:T(8,128)S(1)} %get-tuple-element.32.prob_ref, ...), custom_call_target="tpu_custom_call" | custom-call | tf_op jit(solution)/shard_map/back_own/pallas_call | solution.py:323
  132.3 0.0 collective-permute-done.11.low_ref
  132.3 1.9 %collective-permute-done.12.high_ref = bf16[2,2,1,16,2048]{4,3,2,1,0:T(8,128)(2,1)S(1)} collective-permute-done((bf16[2,2,1,16,2048]{4,3,2,1,0:T(8,128)(2,1)S(1)}, bf16[2,2,1,16,2048]{4,3,2,1,0:T(8,128)(2,1)S(1)}, u32[]{:S(2)}, u32[]{:S(2)}) %collective-permute-start.12) | collective-permute-done | bytes 262176 | tf_op jit(solution)/shard_map/ppermute | solution.py:32
  134.2 0.9 add_columns.1
  (13 shorter events, 0.1 us)
Async XLA Ops:
  7.2 1.0 copy-start
  7.2 51.8 %copy-start.1 = (bf16[2,1,2,4,16,2048]{5,4,3,2,1,0:T(8,128)(2,1)S(1)}, bf16[2,1,2,4,16,2048]{5,4,3,2,1,0:T(8,128)(2,1)}, u32[]{:S(2)}) copy-start(bf16[2,1,2,4,16,2048]{5,4,3,2,1,0:T(8,128)(2,1)} %param.9) | copy-start | bytes 3145732
  7.2 51.8 %copy-start.12 = (s32[1,2,4,4]{3,2,1,0:T(4,128)S(1)}, s32[1,2,4,4]{3,2,1,0:T(4,128)}, u32[]{:S(2)}) copy-start(s32[1,2,4,4]{3,2,1,0:T(4,128)} %adj_ref.1) | copy-start | bytes 388
  7.2 51.8 %copy-start.2 = (bf16[1,2,4,16,2048]{4,3,2,1,0:T(8,128)(2,1)S(1)}, bf16[1,2,4,16,2048]{4,3,2,1,0:T(8,128)(2,1)}, u32[]{:S(2)}) copy-start(bf16[1,2,4,16,2048]{4,3,2,1,0:T(8,128)(2,1)} %q_ref.5) | copy-start | bytes 1572868
  7.2 82.1 %all-gather.4.cloned.1.call-start = ((), (), s32[]{:S(2)}) async-start(), calls=%async_computation | async-start | bytes 4718592 | tf_op jit(solution)/shard_map/all_gather | solution.py:411
  25.0 67.0 %copy-start.14 = (f32[1,2,4,16,2]{3,4,2,1,0:T(2,128)S(1)}, f32[1,2,4,16,2]{3,4,2,1,0:T(2,128)}, u32[]{:S(2)}) copy-start(f32[1,2,4,16,2]{3,4,2,1,0:T(2,128)} %param.15) | copy-start | bytes 3076
  25.0 19.6 %collective-permute-start.1 = (bf16[2,2,1,16,2048]{4,3,2,1,0:T(8,128)(2,1)S(1)}, bf16[2,2,1,16,2048]{4,3,2,1,0:T(8,128)(2,1)S(1)}, u32[]{:S(2)}, u32[]{:S(2)}) collective-permute-start(bf16[2,2,1,16,2048]{4,3,2,1,0:T(8,128)(2,1)S(1)} %get-tuple-element.53), channel_id=1, source_target_pairs={{0,16},{16,32},{32,48},{1,17},{17,33},{33,49},{2,18},{18,34},{34,5... | collective-permute-start | bytes 786440 | tf_op jit(solution)/shard_map/ppermute | solution.py:32
  34.4 10.2 %collective-permute-start.2 = (bf16[2,2,1,16,2048]{4,3,2,1,0:T(8,128)(2,1)S(1)}, bf16[2,2,1,16,2048]{4,3,2,1,0:T(8,128)(2,1)S(1)}, u32[]{:S(2)}, u32[]{:S(2)}) collective-permute-start(bf16[2,2,1,16,2048]{4,3,2,1,0:T(8,128)(2,1)S(1)} %get-tuple-element.54), channel_id=1, source_target_pairs={{16,0},{32,16},{48,32},{17,1},{33,17},{49,33},{18,2},{34,18},{50,3... | collective-permute-start | bytes 786440 | tf_op jit(solution)/shard_map/ppermute | solution.py:32
  38.0 21.0 %collective-permute-start = (bf16[2,1,4,16,2048]{4,3,2,1,0:T(8,128)(2,1)}, bf16[2,1,4,16,2048]{4,3,2,1,0:T(8,128)(2,1)S(1)}, u32[]{:S(2)}, u32[]{:S(2)}) collective-permute-start(bf16[2,1,4,16,2048]{4,3,2,1,0:T(8,128)(2,1)} %get-tuple-element.52), channel_id=1, source_target_pairs={{0,64},{64,128},{128,192},{192,256},{256,320},{320,384},{384,448},... | collective-permute-start | bytes 1572872 | tf_op jit(solution)/shard_map/ppermute | solution.py:32
  42.7 16.3 %collective-permute-start.4 = (bf16[2,1,4,16,2048]{4,3,2,1,0:T(8,128)(2,1)}, bf16[2,1,4,16,2048]{4,3,2,1,0:T(8,128)(2,1)S(1)}, u32[]{:S(2)}, u32[]{:S(2)}) collective-permute-start(bf16[2,1,4,16,2048]{4,3,2,1,0:T(8,128)(2,1)} %get-tuple-element.51), channel_id=1, source_target_pairs={{64,0},{128,64},{192,128},{256,192},{320,256},{384,320},{448,384},... | collective-permute-start | bytes 1572872 | tf_op jit(solution)/shard_map/ppermute | solution.py:32
  44.7 0.7 copy-start.3
  46.1 7.5 %collective-permute-start.3 = (bf16[2,1,2,16,2048]{4,3,2,1,0:T(8,128)(2,1)}, bf16[2,1,2,16,2048]{4,3,2,1,0:T(8,128)(2,1)}, u32[]{:S(2)}, u32[]{:S(2)}) collective-permute-start(bf16[2,1,2,16,2048]{4,3,2,1,0:T(8,128)(2,1)} %pad_maximum_fusion), channel_id=1, source_target_pairs={{0,64},{64,128},{128,192},{192,256},{256,320},{320,384},{384,448},... | collective-permute-start | bytes 786440 | tf_op jit(solution)/shard_map/ppermute | solution.py:32
  50.7 8.3 %collective-permute-start.5 = (bf16[2,1,2,16,2048]{4,3,2,1,0:T(8,128)(2,1)}, bf16[2,1,2,16,2048]{4,3,2,1,0:T(8,128)(2,1)}, u32[]{:S(2)}, u32[]{:S(2)}) collective-permute-start(bf16[2,1,2,16,2048]{4,3,2,1,0:T(8,128)(2,1)} %pad_maximum_fusion.1), channel_id=1, source_target_pairs={{64,0},{128,64},{192,128},{256,192},{320,256},{384,320},{448,384},... | collective-permute-start | bytes 786440 | tf_op jit(solution)/shard_map/ppermute | solution.py:32
  59.0 1.0 copy-start.4
  64.4 1.6 %copy-start.6 = (f32[16,384,128]{2,1,0:T(8,128)}, f32[16,384,128]{2,1,0:T(8,128)S(1)}, u32[]{:S(2)}) copy-start(f32[16,384,128]{2,1,0:T(8,128)S(1)} %get-tuple-element.27.prob_hbm) | copy-start | bytes 9437188
  66.0 0.8 copy-start.7
  66.8 32.3 %copy-start.10 = (f32[2048,2]{0,1:T(2,128)S(1)}, f32[2048,2]{0,1:T(2,128)}, u32[]{:S(2)}) copy-start(f32[2048,2]{0,1:T(2,128)} %param.12) | copy-start | bytes 49156
  66.8 32.3 %copy-start.11 = (f32[2048]{0:T(1024)S(1)}, f32[2048]{0:T(1024)}, u32[]{:S(2)}) copy-start(f32[2048]{0:T(1024)} %param.11) | copy-start | bytes 24580
  66.8 32.3 %copy-start.13 = (s32[1,2,4]{2,1,0:T(2,128)S(1)}, s32[1,2,4]{2,1,0:T(2,128)}, u32[]{:S(2)}) copy-start(s32[1,2,4]{2,1,0:T(2,128)} %bound_ref.1) | copy-start | bytes 100
  89.4 9.7 %collective-permute-start.6 = (bf16[2048,1024]{1,0:T(8,128)(2,1)}, bf16[2048,1024]{1,0:T(8,128)(2,1)}, u32[]{:S(2)}, u32[]{:S(2)}) collective-permute-start(bf16[2048,1024]{1,0:T(8,128)(2,1)} %bitcast.19), channel_id=1, source_target_pairs={{0,64},{64,0},{128,192},{192,128},{256,320},{320,256},{384,448},{4... | collective-permute-start | bytes 12582920 | tf_op jit(solution)/shard_map/ppermute | solution.py:396
  92.1 1.0 copy-start.8
  93.1 5.9 %copy-start.9 = (bf16[128,2048]{1,0:T(8,128)(2,1)S(1)}, bf16[128,2048]{1,0:T(8,128)(2,1)}, u32[]{:S(2)}) copy-start(bf16[128,2048]{1,0:T(8,128)(2,1)} %copy-done.7) | copy-start | bytes 1572868
  99.1 7.0 %copy-start.5 = (bf16[2,2,1,16,2048]{4,3,2,1,0:T(8,128)(2,1)S(1)}, bf16[2,2,1,16,2048]{4,3,2,1,0:T(8,128)(2,1)}, u32[]{:S(2)}) copy-start(bf16[2,2,1,16,2048]{4,3,2,1,0:T(8,128)(2,1)} %copy-done.3) | copy-start | bytes 786436
  110.7 10.0 %collective-permute-start.10 = (bf16[2,1,2,16,2048]{4,3,2,1,0:T(8,128)(2,1)S(1)}, bf16[2,1,2,16,2048]{4,3,2,1,0:T(8,128)(2,1)S(1)}, u32[]{:S(2)}, u32[]{:S(2)}) collective-permute-start(bf16[2,1,2,16,2048]{4,3,2,1,0:T(8,128)(2,1)S(1)} %get-tuple-element.38), channel_id=1, source_target_pairs={{64,0},{128,64},{192,128},{256,192},{320,256},{384,320},{448,384},... | collective-permute-start | bytes 786440 | tf_op jit(solution)/shard_map/ppermute | solution.py:32
  113.0 7.7 %collective-permute-start.9 = (bf16[2,1,2,16,2048]{4,3,2,1,0:T(8,128)(2,1)S(1)}, bf16[2,1,2,16,2048]{4,3,2,1,0:T(8,128)(2,1)S(1)}, u32[]{:S(2)}, u32[]{:S(2)}) collective-permute-start(bf16[2,1,2,16,2048]{4,3,2,1,0:T(8,128)(2,1)S(1)} %get-tuple-element.37), channel_id=1, source_target_pairs={{0,64},{64,128},{128,192},{192,256},{256,320},{320,384},{384,448},... | collective-permute-start | bytes 786440 | tf_op jit(solution)/shard_map/ppermute | solution.py:32
  116.3 9.1 %collective-permute-start.7 = (bf16[2,1,4,16,2048]{4,3,2,1,0:T(8,128)(2,1)S(1)}, bf16[2,1,4,16,2048]{4,3,2,1,0:T(8,128)(2,1)S(1)}, u32[]{:S(2)}, u32[]{:S(2)}) collective-permute-start(bf16[2,1,4,16,2048]{4,3,2,1,0:T(8,128)(2,1)S(1)} %get-tuple-element.34), channel_id=1, source_target_pairs={{0,64},{64,128},{128,192},{192,256},{256,320},{320,384},{384,448},... | collective-permute-start | bytes 1572872 | tf_op jit(solution)/shard_map/ppermute | solution.py:32
  118.4 10.8 %collective-permute-start.8 = (bf16[2,1,4,16,2048]{4,3,2,1,0:T(8,128)(2,1)S(1)}, bf16[2,1,4,16,2048]{4,3,2,1,0:T(8,128)(2,1)S(1)}, u32[]{:S(2)}, u32[]{:S(2)}) collective-permute-start(bf16[2,1,4,16,2048]{4,3,2,1,0:T(8,128)(2,1)S(1)} %get-tuple-element.35), channel_id=1, source_target_pairs={{64,0},{128,64},{192,128},{256,192},{320,256},{384,320},{448,384},... | collective-permute-start | bytes 1572872 | tf_op jit(solution)/shard_map/ppermute | solution.py:32
  120.8 11.5 %collective-permute-start.11 = (bf16[2,2,1,16,2048]{4,3,2,1,0:T(8,128)(2,1)S(1)}, bf16[2,2,1,16,2048]{4,3,2,1,0:T(8,128)(2,1)S(1)}, u32[]{:S(2)}, u32[]{:S(2)}) collective-permute-start(bf16[2,2,1,16,2048]{4,3,2,1,0:T(8,128)(2,1)S(1)} %get-tuple-element.41), channel_id=1, source_target_pairs={{0,16},{16,32},{32,48},{1,17},{17,33},{33,49},{2,18},{18,34},{34,5... | collective-permute-start | bytes 786440 | tf_op jit(solution)/shard_map/ppermute | solution.py:32
  124.1 10.1 %collective-permute-start.12 = (bf16[2,2,1,16,2048]{4,3,2,1,0:T(8,128)(2,1)S(1)}, bf16[2,2,1,16,2048]{4,3,2,1,0:T(8,128)(2,1)S(1)}, u32[]{:S(2)}, u32[]{:S(2)}) collective-permute-start(bf16[2,2,1,16,2048]{4,3,2,1,0:T(8,128)(2,1)S(1)} %get-tuple-element.42), channel_id=1, source_target_pairs={{16,0},{32,16},{48,32},{17,1},{33,17},{49,33},{18,2},{34,18},{50,3... | collective-permute-start | bytes 786440 | tf_op jit(solution)/shard_map/ppermute | solution.py:32
Sparse Core Ops, SparseCore 0:
  24.0 65.3 all-gather.3

commit v9 on v8

--- a/solution.py
+++ b/solution.py
@@ -174,20 +174,21 @@
     pred_ref, ga_ref, swap_ref, proj_ref, gp_ref, sems,
 ):
     cols = swap_ref.shape[1]
-    chunks = 8
+    chunks = 4
     rows = swap_ref.shape[0] // chunks
-    parts = [pl.ds(k * rows, rows) for k in range(chunks)]
-    copies = [pltpu.make_async_copy(swap_hbm.at[part], swap_ref.at[part], sems.at[k]) for k, part in enumerate(parts)]
+    width = cols // chunks
+    parts = [pl.ds(k * width, width) for k in range(chunks)]
+    copies = [
+        pltpu.make_async_copy(swap_hbm.at[:, part], swap_ref.at[:, part], sems.at[k]) for k, part in enumerate(parts)
+    ]
     for copy in copies:
         copy.start()
-    total = None
+    proj_ref[:, side_cols(pos_ref, 0, cols)] = part_ref[...]
+    first = pos_ref[4] * -cols + cols
     for k in range(chunks):
         copies[k].wait()
-        lanes = slice(k * rows, (k + 1) * rows)
-        term = dot(att_ref[:, lanes], swap_ref[lanes, :], ((1,), (0,)))
-        total = term if total is None else total + term
-    proj_ref[:, side_cols(pos_ref, 0, cols)] = part_ref[...]
-    proj_ref[:, side_cols(pos_ref, 1, cols)] = total
+        lanes = pl.ds(pl.multiple_of(first + k * width, width), width)
+        proj_ref[:, lanes] = dot(att_ref[...], swap_ref[:, k * width : (k + 1) * width], ((1,), (0,)))
     inner = proj_ref.shape[1]
     for pair in range(TOK // (2 * BS)):
         rows_of = slice(pair * 2 * BS, (pair + 1) * 2 * BS)
@@ -232,7 +233,7 @@
             pltpu.VMEM(swapped.shape, jnp.bfloat16),
             pltpu.VMEM(att.shape, jnp.float32),
             pltpu.VMEM(att.shape, jnp.bfloat16),
-            pltpu.SemaphoreType.DMA((8,)),
+            pltpu.SemaphoreType.DMA((4,)),
         ],
         compiler_params=pltpu.CompilerParams(vmem_limit_bytes=VMEM_LIMIT),
         name="project",

time: 143 us -> 143 us (level)
  no operation moved by 1% of the time
where the time goes in v9:
time: 143 us; the launch traced here: 142 us
  starting transfers between devices  40.2 us (28%)
  waiting for transfers between devices  37.2 us (26%)
  Pallas kernels  23.8 us (17%)
  blocking collectives  15.6 us (11%)
  between operations  14.4 us (10%)
  local copies, waits for them, and re-layouts  9.61 us (7%)
  other arithmetic  1.56 us (1%)
    ppermute x12, starting transfers between devices, shift(): return lax.ppermute(value, axis, pairs)  37.6 us
    all_gather x1, waiting for transfers between devices, body(): lax.all_gather(both, 'wa', axis=0, axis_index_groups=rings)  22.6 us
    all_gather x1, blocking collectives, body(): both = lax.all_gather(slab, 'wa', axis=0, axis_index_groups=pairs)  15.6 us
    ppermute x12, waiting for transfers between devices, shift(): return lax.ppermute(value, axis, pairs)  12 us
    pallas_call x1, Pallas kernels, project(): pl.pallas_call(project_kernel, in_specs=[smem, smem, vmem, vmem, vmem, pl...  7.54 us
    unnamed x31, local copies, waits for them, and re-layouts  6.19 us
    pallas_call x1, Pallas kernels, back_rim(): pl.pallas_call(back_rim_kernel, in_specs=[vmem] * (3 + len(pieces)), out_...  4.58 us
    pallas_call x1, Pallas kernels, forward(): pl.pallas_call(forward_kernel, grid=(inner // width,), in_specs=[smem, sm...  4.37 us
  transfers between devices with their start and end apart: 14, of which 6 were waited for; matrix products, arithmetic and copies ran while one was open for 4% of the time, Pallas kernels for 8%

profile of v9, /device:TPU:1, one launch (start us, length us, event | category | flops | bytes accessed | tf_op | source)
XLA Modules:
  0.0 142.4 jit_solution(17183823942418877680)
XLA Ops:
  7.2 0.0 copy-start
  7.2 0.0 copy-start.1
  7.2 0.0 copy-start.12
  7.2 0.0 copy-start.2
  7.2 0.0 all-gather.4.cloned.1.call-start
  7.3 0.9 copy-done
  8.2 15.6 %all-gather = bf16[256,1024]{1,0:T(8,128)(2,1)} all-gather(bf16[128,1024]{1,0:T(8,128)(2,1)S(1)} %constant_dynamic-slice_fusion), channel_id=2, replica_groups={{0,1},{2,3},{4,5},{6,7},{8,9},{10,11},{12,13},{14,15},{16,17},{18,19},{..., dimensions={0}, use_global_device_ids=true | all-gather | bytes 786432 | tf_op jit(solution)/shard_map/all_gather | solution.py:411
  23.9 0.0 all-gather.4.cloned.1.call-update
  23.9 1.1 fusion.1
  25.0 0.0 copy-start.14
  25.0 9.5 %collective-permute-start.1 = (bf16[2,2,1,16,2048]{4,3,2,1,0:T(8,128)(2,1)S(1)}, bf16[2,2,1,16,2048]{4,3,2,1,0:T(8,128)(2,1)S(1)}, u32[]{:S(2)}, u32[]{:S(2)}) collective-permute-start(bf16[2,2,1,16,2048]{4,3,2,1,0:T(8,128)(2,1)S(1)} %get-tuple-element.53), channel_id=1, source_target_pairs={{0,16},{16,32},{32,48},{1,17},{17,33},{33,49},{2,18},{18,34},{34,5... | collective-permute-start | bytes 786440 | tf_op jit(solution)/shard_map/ppermute | solution.py:32
  34.4 1.3 collective-permute-start.2
  35.7 2.3 %fusion = (bf16[2,1,4,16,2048]{4,3,2,1,0:T(8,128)(2,1)}, bf16[2,1,4,16,2048]{4,3,2,1,0:T(8,128)(2,1)}) fusion(bf16[2,2,4,16,2048]{4,3,2,1,0:T(8,128)(2,1)} %bitcast.13), kind=kLoop, calls=%fused_computation.4 | loop fusion | bytes 2097152 | tf_op jit(solution)/shard_map/slice | solution.py:416
  38.0 4.7 %collective-permute-start = (bf16[2,1,4,16,2048]{4,3,2,1,0:T(8,128)(2,1)}, bf16[2,1,4,16,2048]{4,3,2,1,0:T(8,128)(2,1)S(1)}, u32[]{:S(2)}, u32[]{:S(2)}) collective-permute-start(bf16[2,1,4,16,2048]{4,3,2,1,0:T(8,128)(2,1)} %get-tuple-element.52), channel_id=1, source_target_pairs={{0,64},{64,128},{128,192},{192,256},{256,320},{320,384},{384,448},... | collective-permute-start | bytes 1572872 | tf_op jit(solution)/shard_map/ppermute | solution.py:32
  42.7 1.9 %collective-permute-start.4 = (bf16[2,1,4,16,2048]{4,3,2,1,0:T(8,128)(2,1)}, bf16[2,1,4,16,2048]{4,3,2,1,0:T(8,128)(2,1)S(1)}, u32[]{:S(2)}, u32[]{:S(2)}) collective-permute-start(bf16[2,1,4,16,2048]{4,3,2,1,0:T(8,128)(2,1)} %get-tuple-element.51), channel_id=1, source_target_pairs={{64,0},{128,64},{192,128},{256,192},{320,256},{384,320},{448,384},... | collective-permute-start | bytes 1572872 | tf_op jit(solution)/shard_map/ppermute | solution.py:32
  44.6 0.0 collective-permute-done.1.rest_5_
  44.6 0.0 collective-permute-done.2.rest_6_
  44.7 0.0 copy-start.3
  44.7 0.7 copy-done.3
  45.4 0.8 pad_maximum_fusion
  46.1 3.8 %collective-permute-start.3 = (bf16[2,1,2,16,2048]{4,3,2,1,0:T(8,128)(2,1)}, bf16[2,1,2,16,2048]{4,3,2,1,0:T(8,128)(2,1)}, u32[]{:S(2)}, u32[]{:S(2)}) collective-permute-start(bf16[2,1,2,16,2048]{4,3,2,1,0:T(8,128)(2,1)} %pad_maximum_fusion), channel_id=1, source_target_pairs={{0,64},{64,128},{128,192},{192,256},{256,320},{320,384},{384,448},... | collective-permute-start | bytes 786440 | tf_op jit(solution)/shard_map/ppermute | solution.py:32
  50.0 0.7 pad_maximum_fusion.1
  50.7 1.9 %collective-permute-start.5 = (bf16[2,1,2,16,2048]{4,3,2,1,0:T(8,128)(2,1)}, bf16[2,1,2,16,2048]{4,3,2,1,0:T(8,128)(2,1)}, u32[]{:S(2)}, u32[]{:S(2)}) collective-permute-start(bf16[2,1,2,16,2048]{4,3,2,1,0:T(8,128)(2,1)} %pad_maximum_fusion.1), channel_id=1, source_target_pairs={{64,0},{128,64},{192,128},{256,192},{320,256},{384,320},{448,384},... | collective-permute-start | bytes 786440 | tf_op jit(solution)/shard_map/ppermute | solution.py:32
  52.6 0.1 pad_add_fusion.pos_ref
  52.7 0.9 collective-permute-done.3.rest_2_
  53.6 5.4 %collective-permute-done.5.rest_4_ = bf16[2,1,2,16,2048]{4,3,2,1,0:T(8,128)(2,1)} collective-permute-done((bf16[2,1,2,16,2048]{4,3,2,1,0:T(8,128)(2,1)}, bf16[2,1,2,16,2048]{4,3,2,1,0:T(8,128)(2,1)}, u32[]{:S(2)}, u32[]{:S(2)}) %collective-permute-start.5) | collective-permute-done | bytes 262176 | tf_op jit(solution)/shard_map/ppermute | solution.py:32
  59.0 0.0 collective-permute-done.rest_1_
  59.0 0.0 collective-permute-done.4.rest_3_
  59.0 0.0 copy-done.1
  59.0 0.0 copy-done.12
  59.0 0.0 copy-done.2
  59.0 0.0 copy-start.4
  59.0 0.9 copy-done.4
  60.0 4.4 %attend.1 = (bf16[128,2048]{1,0:T(8,128)(2,1)S(1)}, f32[16,384,128]{2,1,0:T(8,128)S(1)}) custom-call(s32[1,2,4,4]{3,2,1,0:T(4,128)S(1)} %copy-done.12, s32[5]{0:T(128)S(1)} %pad_add_fusion.pos_ref, bf16[1,2,4,16,2048]{4,3,2,1,0:T(8,128)(2,1)S(1)} %copy-done.2, bf16[2,2,4,16,2048]{4,3,2,1,0:T(8,128)(2,1)S(1)} %bitcast.14, ...), custom_call_target="tpu_custom_call" | custom-call | tf_op jit(solution)/shard_map/attend/pallas_call | solution.py:110
  64.4 0.0 copy-start.6
  64.4 1.6 %copy-done.6 = f32[16,384,128]{2,1,0:T(8,128)} copy-done((f32[16,384,128]{2,1,0:T(8,128)}, f32[16,384,128]{2,1,0:T(8,128)S(1)}, u32[]{:S(2)}) %copy-start.6) | copy-done | bytes 3145752
  66.0 0.8 copy-done.7
  66.8 22.6 %all-gather.4.cloned.1.call-done = bf16[16,128,1024]{2,1,0:T(8,128)(2,1)} async-done(((bf16[2,128,1024]{2,1,0:T(8,128)(2,1)}), bf16[16,128,1024]{2,1,0:T(8,128)(2,1)}) %all-gather.4.cloned.1.call-update) | async-done | bytes 4194320 | tf_op jit(solution)/shard_map/all_gather | solution.py:412
  89.4 2.6 %collective-permute-start.6 = (bf16[2048,1024]{1,0:T(8,128)(2,1)}, bf16[2048,1024]{1,0:T(8,128)(2,1)}, u32[]{:S(2)}, u32[]{:S(2)}) collective-permute-start(bf16[2048,1024]{1,0:T(8,128)(2,1)} %bitcast.19), channel_id=1, source_target_pairs={{0,64},{64,0},{128,192},{192,128},{256,320},{320,256},{384,448},{4... | collective-permute-start | bytes 12582920 | tf_op jit(solution)/shard_map/ppermute | solution.py:397
  91.9 0.0 copy-done.14
  91.9 0.1 copy.14.cot_ref
  92.1 1.0 copy-done.8
  93.1 3.3 %project_own.1 = (f32[128,1024]{1,0:T(8,128)S(1)}, bf16[2048,1024]{1,0:T(8,128)(2,1)S(1)}, f32[16,384,128]{2,1,0:T(8,128)S(1)}) custom-call(bf16[128,2048]{1,0:T(8,128)(2,1)S(1)} %copy-done.8, bf16[2048,1024]{1,0:T(8,128)(2,1)} %bitcast.20, f32[16,384,128]{2,1,0:T(8,128)} %copy-done.6), custom_call_target="tpu_custom_call" | custom-call | tf_op jit(solution)/shard_map/project_own/pallas_call | solution.py:157
  96.4 2.7 %collective-permute-done.6.swap_hbm = bf16[2048,1024]{1,0:T(8,128)(2,1)} collective-permute-done((bf16[2048,1024]{1,0:T(8,128)(2,1)}, bf16[2048,1024]{1,0:T(8,128)(2,1)}, u32[]{:S(2)}, u32[]{:S(2)}) %collective-permute-start.6) | collective-permute-done | bytes 4194336 | tf_op jit(solution)/shard_map/ppermute | solution.py:397
  99.0 0.0 copy-done.10
  99.0 0.0 copy-done.11
  99.1 7.5 %project.1 = (f32[1,2,4,2,16]{4,3,2,1,0:T(2,128)}, bf16[128,2048]{1,0:T(8,128)(2,1)S(1)}) custom-call(s32[1,2,4]{2,1,0:T(2,128)S(1)} %copy-done.13, s32[5]{0:T(128)S(1)} %pad_add_fusion.pos_ref, bf16[128,2048]{1,0:T(8,128)(2,1)S(1)} %copy-done.9, f32[128,1024]{1,0:T(8,128)S(1)} %get-tuple-element.28.part_ref, ...), custom_call_target="tpu_custom_call" | custom-call | tf_op jit(solution)/shard_map/project/pallas_call | solution.py:224
  106.6 0.0 copy-done.5
  106.6 4.6 %back_rim.1 = (bf16[16,384,128]{2,1,0:T(8,128)(2,1)S(1)}, bf16[2,1,4,16,2048]{4,3,2,1,0:T(8,128)(2,1)S(1)}, bf16[2,1,2,16,2048]{4,3,2,1,0:T(8,128)(2,1)S(1)}, bf...) custom-call(bf16[1,2,4,16,2048]{4,3,2,1,0:T(8,128)(2,1)S(1)} %copy-d, ...), custom_call_target="tpu_custom_call" | custom-call | tf_op jit(solution)/shard_map/back_rim/pallas_call | solution.py:284
  111.2 2.3 %collective-permute-start.10 = (bf16[2,1,2,16,2048]{4,3,2,1,0:T(8,128)(2,1)S(1)}, bf16[2,1,2,16,2048]{4,3,2,1,0:T(8,128)(2,1)S(1)}, u32[]{:S(2)}, u32[]{:S(2)}) collective-permute-start(bf16[2,1,2,16,2048]{4,3,2,1,0:T(8,128)(2,1)S(1)} %get-tuple-element.38), channel_id=1, source_target_pairs={{64,0},{128,64},{192,128},{256,192},{320,256},{384,320},{448,384},... | collective-permute-start | bytes 786440 | tf_op jit(solution)/shard_map/ppermute | solution.py:32
  113.5 3.3 %collective-permute-start.9 = (bf16[2,1,2,16,2048]{4,3,2,1,0:T(8,128)(2,1)S(1)}, bf16[2,1,2,16,2048]{4,3,2,1,0:T(8,128)(2,1)S(1)}, u32[]{:S(2)}, u32[]{:S(2)}) collective-permute-start(bf16[2,1,2,16,2048]{4,3,2,1,0:T(8,128)(2,1)S(1)} %get-tuple-element.37), channel_id=1, source_target_pairs={{0,64},{64,128},{128,192},{192,256},{256,320},{320,384},{384,448},... | collective-permute-start | bytes 786440 | tf_op jit(solution)/shard_map/ppermute | solution.py:32
  116.8 2.1 %collective-permute-start.7 = (bf16[2,1,4,16,2048]{4,3,2,1,0:T(8,128)(2,1)S(1)}, bf16[2,1,4,16,2048]{4,3,2,1,0:T(8,128)(2,1)S(1)}, u32[]{:S(2)}, u32[]{:S(2)}) collective-permute-start(bf16[2,1,4,16,2048]{4,3,2,1,0:T(8,128)(2,1)S(1)} %get-tuple-element.34), channel_id=1, source_target_pairs={{0,64},{64,128},{128,192},{192,256},{256,320},{320,384},{384,448},... | collective-permute-start | bytes 1572872 | tf_op jit(solution)/shard_map/ppermute | solution.py:32
  118.9 2.2 %collective-permute-start.8 = (bf16[2,1,4,16,2048]{4,3,2,1,0:T(8,128)(2,1)S(1)}, bf16[2,1,4,16,2048]{4,3,2,1,0:T(8,128)(2,1)S(1)}, u32[]{:S(2)}, u32[]{:S(2)}) collective-permute-start(bf16[2,1,4,16,2048]{4,3,2,1,0:T(8,128)(2,1)S(1)} %get-tuple-element.35), channel_id=1, source_target_pairs={{64,0},{128,64},{192,128},{256,192},{320,256},{384,320},{448,384},... | collective-permute-start | bytes 1572872 | tf_op jit(solution)/shard_map/ppermute | solution.py:32
  121.2 0.0 collective-permute-done.10.from_high_ref
  121.2 0.0 collective-permute-done.9.from_low_ref
  121.2 0.1 sides.1
  121.3 3.3 %collective-permute-start.11 = (bf16[2,2,1,16,2048]{4,3,2,1,0:T(8,128)(2,1)S(1)}, bf16[2,2,1,16,2048]{4,3,2,1,0:T(8,128)(2,1)S(1)}, u32[]{:S(2)}, u32[]{:S(2)}) collective-permute-start(bf16[2,2,1,16,2048]{4,3,2,1,0:T(8,128)(2,1)S(1)} %get-tuple-element.41), channel_id=1, source_target_pairs={{0,16},{16,32},{32,48},{1,17},{17,33},{33,49},{2,18},{18,34},{34,5... | collective-permute-start | bytes 786440 | tf_op jit(solution)/shard_map/ppermute | solution.py:32
  124.6 1.3 collective-permute-start.12
  125.9 0.0 collective-permute-done.7.rest_7_
  125.9 3.8 %collective-permute-done.8.rest_8_ = bf16[2,1,4,16,2048]{4,3,2,1,0:T(8,128)(2,1)S(1)} collective-permute-done((bf16[2,1,4,16,2048]{4,3,2,1,0:T(8,128)(2,1)S(1)}, bf16[2,1,4,16,2048]{4,3,2,1,0:T(8,128)(2,1)S(1)}, u32[]{:S(2)}, u32[]{:S(2)}) %collective-permute-start.8) | collective-permute-done | bytes 524320 | tf_op jit(solution)/shard_map/ppermute | solution.py:32
  129.7 3.1 %back_own.1 = (bf16[1,2,4,16,2048]{4,3,2,1,0:T(8,128)(2,1)}, bf16[2,2,4,16,2048]{4,3,2,1,0:T(8,128)(2,1)}, f32[2,2,2,16,2048]{4,3,2,1,0:T(8,128)S(1)}) custom-call(bf16[1,2,4,16,2048]{4,3,2,1,0:T(8,128)(2,1)S(1)} %copy-done.2, bf16[128,2048]{1,0:T(8,128)(2,1)S(1)} %get-tuple-element.31.ga_ref, f32[16,384,128]{2,1,0:T(8,128)S(1)} %get-tuple-element.32.prob_ref, ...), custom_call_target="tpu_custom_call" | custom-call | tf_op jit(solution)/shard_map/back_own/pallas_call | solution.py:324
  132.8 0.0 collective-permute-done.11.low_ref
  132.8 1.9 %collective-permute-done.12.high_ref = bf16[2,2,1,16,2048]{4,3,2,1,0:T(8,128)(2,1)S(1)} collective-permute-done((bf16[2,2,1,16,2048]{4,3,2,1,0:T(8,128)(2,1)S(1)}, bf16[2,2,1,16,2048]{4,3,2,1,0:T(8,128)(2,1)S(1)}, u32[]{:S(2)}, u32[]{:S(2)}) %collective-permute-start.12) | collective-permute-done | bytes 262176 | tf_op jit(solution)/shard_map/ppermute | solution.py:32
  134.7 0.9 add_columns.1
  (13 shorter events, 0.1 us)
Async XLA Ops:
  7.2 1.0 copy-start
  7.2 51.8 %copy-start.1 = (bf16[2,1,2,4,16,2048]{5,4,3,2,1,0:T(8,128)(2,1)S(1)}, bf16[2,1,2,4,16,2048]{5,4,3,2,1,0:T(8,128)(2,1)}, u32[]{:S(2)}) copy-start(bf16[2,1,2,4,16,2048]{5,4,3,2,1,0:T(8,128)(2,1)} %param.9) | copy-start | bytes 3145732
  7.2 51.8 %copy-start.12 = (s32[1,2,4,4]{3,2,1,0:T(4,128)S(1)}, s32[1,2,4,4]{3,2,1,0:T(4,128)}, u32[]{:S(2)}) copy-start(s32[1,2,4,4]{3,2,1,0:T(4,128)} %adj_ref.1) | copy-start | bytes 388
  7.2 51.8 %copy-start.2 = (bf16[1,2,4,16,2048]{4,3,2,1,0:T(8,128)(2,1)S(1)}, bf16[1,2,4,16,2048]{4,3,2,1,0:T(8,128)(2,1)}, u32[]{:S(2)}) copy-start(bf16[1,2,4,16,2048]{4,3,2,1,0:T(8,128)(2,1)} %q_ref.5) | copy-start | bytes 1572868
  7.2 82.1 %all-gather.4.cloned.1.call-start = ((), (), s32[]{:S(2)}) async-start(), calls=%async_computation | async-start | bytes 4718592 | tf_op jit(solution)/shard_map/all_gather | solution.py:412
  25.0 67.0 %copy-start.14 = (f32[1,2,4,16,2]{3,4,2,1,0:T(2,128)S(1)}, f32[1,2,4,16,2]{3,4,2,1,0:T(2,128)}, u32[]{:S(2)}) copy-start(f32[1,2,4,16,2]{3,4,2,1,0:T(2,128)} %param.15) | copy-start | bytes 3076
  25.0 19.6 %collective-permute-start.1 = (bf16[2,2,1,16,2048]{4,3,2,1,0:T(8,128)(2,1)S(1)}, bf16[2,2,1,16,2048]{4,3,2,1,0:T(8,128)(2,1)S(1)}, u32[]{:S(2)}, u32[]{:S(2)}) collective-permute-start(bf16[2,2,1,16,2048]{4,3,2,1,0:T(8,128)(2,1)S(1)} %get-tuple-element.53), channel_id=1, source_target_pairs={{0,16},{16,32},{32,48},{1,17},{17,33},{33,49},{2,18},{18,34},{34,5... | collective-permute-start | bytes 786440 | tf_op jit(solution)/shard_map/ppermute | solution.py:32
  34.4 10.2 %collective-permute-start.2 = (bf16[2,2,1,16,2048]{4,3,2,1,0:T(8,128)(2,1)S(1)}, bf16[2,2,1,16,2048]{4,3,2,1,0:T(8,128)(2,1)S(1)}, u32[]{:S(2)}, u32[]{:S(2)}) collective-permute-start(bf16[2,2,1,16,2048]{4,3,2,1,0:T(8,128)(2,1)S(1)} %get-tuple-element.54), channel_id=1, source_target_pairs={{16,0},{32,16},{48,32},{17,1},{33,17},{49,33},{18,2},{34,18},{50,3... | collective-permute-start | bytes 786440 | tf_op jit(solution)/shard_map/ppermute | solution.py:32
  38.0 21.0 %collective-permute-start = (bf16[2,1,4,16,2048]{4,3,2,1,0:T(8,128)(2,1)}, bf16[2,1,4,16,2048]{4,3,2,1,0:T(8,128)(2,1)S(1)}, u32[]{:S(2)}, u32[]{:S(2)}) collective-permute-start(bf16[2,1,4,16,2048]{4,3,2,1,0:T(8,128)(2,1)} %get-tuple-element.52), channel_id=1, source_target_pairs={{0,64},{64,128},{128,192},{192,256},{256,320},{320,384},{384,448},... | collective-permute-start | bytes 1572872 | tf_op jit(solution)/shard_map/ppermute | solution.py:32
  42.7 16.3 %collective-permute-start.4 = (bf16[2,1,4,16,2048]{4,3,2,1,0:T(8,128)(2,1)}, bf16[2,1,4,16,2048]{4,3,2,1,0:T(8,128)(2,1)S(1)}, u32[]{:S(2)}, u32[]{:S(2)}) collective-permute-start(bf16[2,1,4,16,2048]{4,3,2,1,0:T(8,128)(2,1)} %get-tuple-element.51), channel_id=1, source_target_pairs={{64,0},{128,64},{192,128},{256,192},{320,256},{384,320},{448,384},... | collective-permute-start | bytes 1572872 | tf_op jit(solution)/shard_map/ppermute | solution.py:32
  44.7 0.7 copy-start.3
  46.1 7.5 %collective-permute-start.3 = (bf16[2,1,2,16,2048]{4,3,2,1,0:T(8,128)(2,1)}, bf16[2,1,2,16,2048]{4,3,2,1,0:T(8,128)(2,1)}, u32[]{:S(2)}, u32[]{:S(2)}) collective-permute-start(bf16[2,1,2,16,2048]{4,3,2,1,0:T(8,128)(2,1)} %pad_maximum_fusion), channel_id=1, source_target_pairs={{0,64},{64,128},{128,192},{192,256},{256,320},{320,384},{384,448},... | collective-permute-start | bytes 786440 | tf_op jit(solution)/shard_map/ppermute | solution.py:32
  50.7 8.3 %collective-permute-start.5 = (bf16[2,1,2,16,2048]{4,3,2,1,0:T(8,128)(2,1)}, bf16[2,1,2,16,2048]{4,3,2,1,0:T(8,128)(2,1)}, u32[]{:S(2)}, u32[]{:S(2)}) collective-permute-start(bf16[2,1,2,16,2048]{4,3,2,1,0:T(8,128)(2,1)} %pad_maximum_fusion.1), channel_id=1, source_target_pairs={{64,0},{128,64},{192,128},{256,192},{320,256},{384,320},{448,384},... | collective-permute-start | bytes 786440 | tf_op jit(solution)/shard_map/ppermute | solution.py:32
  59.0 1.0 copy-start.4
  64.4 1.6 %copy-start.6 = (f32[16,384,128]{2,1,0:T(8,128)}, f32[16,384,128]{2,1,0:T(8,128)S(1)}, u32[]{:S(2)}) copy-start(f32[16,384,128]{2,1,0:T(8,128)S(1)} %get-tuple-element.27.prob_hbm) | copy-start | bytes 9437188
  66.0 0.8 copy-start.7
  66.8 32.3 %copy-start.10 = (f32[2048,2]{0,1:T(2,128)S(1)}, f32[2048,2]{0,1:T(2,128)}, u32[]{:S(2)}) copy-start(f32[2048,2]{0,1:T(2,128)} %param.12) | copy-start | bytes 49156
  66.8 32.3 %copy-start.11 = (f32[2048]{0:T(1024)S(1)}, f32[2048]{0:T(1024)}, u32[]{:S(2)}) copy-start(f32[2048]{0:T(1024)} %param.11) | copy-start | bytes 24580
  66.8 32.3 %copy-start.13 = (s32[1,2,4]{2,1,0:T(2,128)S(1)}, s32[1,2,4]{2,1,0:T(2,128)}, u32[]{:S(2)}) copy-start(s32[1,2,4]{2,1,0:T(2,128)} %bound_ref.1) | copy-start | bytes 100
  89.4 9.7 %collective-permute-start.6 = (bf16[2048,1024]{1,0:T(8,128)(2,1)}, bf16[2048,1024]{1,0:T(8,128)(2,1)}, u32[]{:S(2)}, u32[]{:S(2)}) collective-permute-start(bf16[2048,1024]{1,0:T(8,128)(2,1)} %bitcast.19), channel_id=1, source_target_pairs={{0,64},{64,0},{128,192},{192,128},{256,320},{320,256},{384,448},{4... | collective-permute-start | bytes 12582920 | tf_op jit(solution)/shard_map/ppermute | solution.py:397
  92.1 1.0 copy-start.8
  93.1 5.9 %copy-start.9 = (bf16[128,2048]{1,0:T(8,128)(2,1)S(1)}, bf16[128,2048]{1,0:T(8,128)(2,1)}, u32[]{:S(2)}) copy-start(bf16[128,2048]{1,0:T(8,128)(2,1)} %copy-done.7) | copy-start | bytes 1572868
  99.1 7.6 %copy-start.5 = (bf16[2,2,1,16,2048]{4,3,2,1,0:T(8,128)(2,1)S(1)}, bf16[2,2,1,16,2048]{4,3,2,1,0:T(8,128)(2,1)}, u32[]{:S(2)}) copy-start(bf16[2,2,1,16,2048]{4,3,2,1,0:T(8,128)(2,1)} %copy-done.3) | copy-start | bytes 786436
  111.2 10.0 %collective-permute-start.10 = (bf16[2,1,2,16,2048]{4,3,2,1,0:T(8,128)(2,1)S(1)}, bf16[2,1,2,16,2048]{4,3,2,1,0:T(8,128)(2,1)S(1)}, u32[]{:S(2)}, u32[]{:S(2)}) collective-permute-start(bf16[2,1,2,16,2048]{4,3,2,1,0:T(8,128)(2,1)S(1)} %get-tuple-element.38), channel_id=1, source_target_pairs={{64,0},{128,64},{192,128},{256,192},{320,256},{384,320},{448,384},... | collective-permute-start | bytes 786440 | tf_op jit(solution)/shard_map/ppermute | solution.py:32
  113.5 7.7 %collective-permute-start.9 = (bf16[2,1,2,16,2048]{4,3,2,1,0:T(8,128)(2,1)S(1)}, bf16[2,1,2,16,2048]{4,3,2,1,0:T(8,128)(2,1)S(1)}, u32[]{:S(2)}, u32[]{:S(2)}) collective-permute-start(bf16[2,1,2,16,2048]{4,3,2,1,0:T(8,128)(2,1)S(1)} %get-tuple-element.37), channel_id=1, source_target_pairs={{0,64},{64,128},{128,192},{192,256},{256,320},{320,384},{384,448},... | collective-permute-start | bytes 786440 | tf_op jit(solution)/shard_map/ppermute | solution.py:32
  116.8 9.1 %collective-permute-start.7 = (bf16[2,1,4,16,2048]{4,3,2,1,0:T(8,128)(2,1)S(1)}, bf16[2,1,4,16,2048]{4,3,2,1,0:T(8,128)(2,1)S(1)}, u32[]{:S(2)}, u32[]{:S(2)}) collective-permute-start(bf16[2,1,4,16,2048]{4,3,2,1,0:T(8,128)(2,1)S(1)} %get-tuple-element.34), channel_id=1, source_target_pairs={{0,64},{64,128},{128,192},{192,256},{256,320},{320,384},{384,448},... | collective-permute-start | bytes 1572872 | tf_op jit(solution)/shard_map/ppermute | solution.py:32
  118.9 10.8 %collective-permute-start.8 = (bf16[2,1,4,16,2048]{4,3,2,1,0:T(8,128)(2,1)S(1)}, bf16[2,1,4,16,2048]{4,3,2,1,0:T(8,128)(2,1)S(1)}, u32[]{:S(2)}, u32[]{:S(2)}) collective-permute-start(bf16[2,1,4,16,2048]{4,3,2,1,0:T(8,128)(2,1)S(1)} %get-tuple-element.35), channel_id=1, source_target_pairs={{64,0},{128,64},{192,128},{256,192},{320,256},{384,320},{448,384},... | collective-permute-start | bytes 1572872 | tf_op jit(solution)/shard_map/ppermute | solution.py:32
  121.3 11.5 %collective-permute-start.11 = (bf16[2,2,1,16,2048]{4,3,2,1,0:T(8,128)(2,1)S(1)}, bf16[2,2,1,16,2048]{4,3,2,1,0:T(8,128)(2,1)S(1)}, u32[]{:S(2)}, u32[]{:S(2)}) collective-permute-start(bf16[2,2,1,16,2048]{4,3,2,1,0:T(8,128)(2,1)S(1)} %get-tuple-element.41), channel_id=1, source_target_pairs={{0,16},{16,32},{32,48},{1,17},{17,33},{33,49},{2,18},{18,34},{34,5... | collective-permute-start | bytes 786440 | tf_op jit(solution)/shard_map/ppermute | solution.py:32
  124.6 10.1 %collective-permute-start.12 = (bf16[2,2,1,16,2048]{4,3,2,1,0:T(8,128)(2,1)S(1)}, bf16[2,2,1,16,2048]{4,3,2,1,0:T(8,128)(2,1)S(1)}, u32[]{:S(2)}, u32[]{:S(2)}) collective-permute-start(bf16[2,2,1,16,2048]{4,3,2,1,0:T(8,128)(2,1)S(1)} %get-tuple-element.42), channel_id=1, source_target_pairs={{16,0},{32,16},{48,32},{17,1},{33,17},{49,33},{18,2},{34,18},{50,3... | collective-permute-start | bytes 786440 | tf_op jit(solution)/shard_map/ppermute | solution.py:32
Sparse Core Ops, SparseCore 0:
  24.0 65.3 all-gather.3
